TPU v7x, 32 devices: a whole 2x2x4 slice. The times are simulated.
32 devices in a mesh: dp: 16 (over z, y, x), mp: 2 (over core).
Axes of the slice: x: 2, y: 2, z: 4, core: 2. Of those that a mesh axis runs over, the one named last changes fastest.
Arguments:
- inputs: float32 [64, 256, 768], P('dp'), may hold values from -6 to 6
- segment_ids: int32 [64, 256], P('dp'), may hold values from 0 to 7, never falling along the last dimension, each value on 1 to 64 neighbouring positions
- ln1_gain: float32 [768], replicated, may hold values from 0.1 to 1.9
- ln1_bias: float32 [768], replicated, may hold values from -1.75 to 1.75
- w_query: bfloat16 [768, 768], P(None, 'mp'), may hold values from -0.21875 to 0.21875
- b_query: float32 [768], P('mp'), may hold values from -3 to 3
- w_key: bfloat16 [768, 768], P(None, 'mp'), may hold values from -0.21875 to 0.21875
- w_value: bfloat16 [768, 768], P(None, 'mp'), may hold values from -0.21875 to 0.21875
- b_value: float32 [768], P('mp'), may hold values from -3 to 3
- w_output: bfloat16 [768, 768], P('mp'), may hold values from -1.25 to 1.25
- b_output: float32 [768], replicated, may hold values from -3 to 3
- ln2_gain: float32 [768], replicated, may hold values from 0.1 to 1.9
- ln2_bias: float32 [768], replicated, may hold values from -1.75 to 1.75
- w_up: bfloat16 [768, 3072], P(None, 'mp'), may hold values from -0.21875 to 0.21875
- b_up: float32 [3072], P('mp'), may hold values from -3 to 3
- w_down: bfloat16 [3072, 768], P('mp'), may hold values from -0.109375 to 0.109375
- b_down: float32 [768], replicated, may hold values from -3 to 3
- cotangent: float32 [64, 256, 768], P('dp'), may hold values from -6 to 6
Outputs:
- result: float32 [64, 256, 768], P('dp')
- grad_inputs: float32 [64, 256, 768], P('dp')
- grad_ln1_gain: float32 [768], replicated
- grad_ln1_bias: float32 [768], replicated
- grad_w_query: float32 [768, 768], P('dp', 'mp')
- grad_b_query: float32 [768], P('mp')
- grad_w_key: float32 [768, 768], P('dp', 'mp')
- grad_w_value: float32 [768, 768], P('dp', 'mp')
- grad_b_value: float32 [768], P('mp')
- grad_w_output: float32 [768, 768], P('mp', 'dp')
- grad_b_output: float32 [768], replicated
- grad_ln2_gain: float32 [768], replicated
- grad_ln2_bias: float32 [768], replicated
- grad_w_up: float32 [768, 3072], P('dp', 'mp')
- grad_b_up: float32 [3072], P('mp')
- grad_w_down: float32 [3072, 768], P('mp', 'dp')
- grad_b_down: float32 [768], replicated
Inputs may be any that keep to these rules, and one draw needn't show every extreme that they name: `segment_ids`: along each row the ids never fall; every id of 0 to 7 covers 1 to 64 consecutive positions, some one exactly 64.
All inputs are finite; a program needn't handle non-finite values.
Results may differ from a plain program's by a relative error of at most 0.011.
Values sent between devices are 32-bit elements; how exact they have to be, the bound alone decides.
No kernel may reach another device: no remote copies, remote signals or barrier semaphores. Data moves between devices by JAX's collectives and lax.ppermute only.
A program may use at most 128 MiB of HBM per device.

v0:
```python
from functools import partial
import math

import jax
import jax.numpy as jnp
from jax import lax
from jax.sharding import PartitionSpec as P

HD = 64


EPSILON = 1e-06
MASKED = -1000000000.0


def norm_parts(values, gain_vec, shift_vec):
    row_mean = jnp.mean(values, axis=-1, keepdims=True)
    centered = values - row_mean
    inv_std = lax.rsqrt(jnp.mean(centered * centered, axis=-1, keepdims=True) + EPSILON)
    unit_rows = centered * inv_std
    return (unit_rows * gain_vec + shift_vec, unit_rows, inv_std)


def norm_back(grad_out, unit_rows, inv_std, gain_vec):
    grad_gain = jnp.sum(grad_out * unit_rows, axis=0)
    grad_shift = jnp.sum(grad_out, axis=0)
    grad_unit = grad_out * gain_vec
    grad_in = inv_std * (
        grad_unit
        - jnp.mean(grad_unit, axis=-1, keepdims=True)
        - unit_rows * jnp.mean(grad_unit * unit_rows, axis=-1, keepdims=True)
    )
    return (grad_in, grad_gain, grad_shift)


def matmul(left, right):
    return jnp.dot(left, right, preferred_element_type=jnp.float32)


def left_product(left, right):
    return jnp.einsum("ta,tb->ab", left, right, preferred_element_type=jnp.float32)


def right_product(left, right):
    return jnp.einsum("tb,ab->ta", left, right, preferred_element_type=jnp.float32)


def on_device(
    inputs,
    segment_ids,
    ln1_gain,
    ln1_bias,
    w_query,
    b_query,
    w_key,
    w_value,
    b_value,
    w_output,
    b_output,
    ln2_gain,
    ln2_bias,
    w_up,
    b_up,
    w_down,
    b_down,
    cotangent,
):
    rows, length, width = inputs.shape
    local_cols = w_query.shape[1]
    local_heads = local_cols // HD
    tokens = rows * length
    scale = 1.0 / math.sqrt(HD)
    tokens_flat = inputs.reshape(tokens, width)
    normed, unit_one, inv_one = norm_parts(tokens_flat, ln1_gain, ln1_bias)
    normed_b = normed.astype(jnp.bfloat16)
    queries = (matmul(normed_b, w_query) + b_query).astype(jnp.bfloat16)
    keys_b = matmul(normed_b, w_key).astype(jnp.bfloat16)
    values_b = (matmul(normed_b, w_value) + b_value).astype(jnp.bfloat16)
    head_shape = (rows, length, local_heads, HD)
    query_four = queries.reshape(head_shape)
    key_four = keys_b.reshape(head_shape)
    value_four = values_b.reshape(head_shape)
    same = segment_ids[:, None, :, None] == segment_ids[:, None, None, :]

    def scores_of(first, second):
        raw = jnp.einsum("rqhe,rkhe->rhqk", first, second, preferred_element_type=jnp.float32)
        return jnp.where(same, raw * scale, MASKED)

    scores = scores_of(query_four, key_four)
    highest = jnp.max(scores, axis=-1, keepdims=True)
    expo = jnp.exp(scores - highest)
    totals = jnp.sum(expo, axis=-1, keepdims=True)
    probs = expo / totals
    log_total = highest + jnp.log(totals)
    context = jnp.einsum(
        "rhqk,rkhe->rqhe",
        probs.astype(jnp.bfloat16),
        value_four,
        preferred_element_type=jnp.float32,
    )
    context_b = context.reshape(tokens, local_cols).astype(jnp.bfloat16)
    attn_out = lax.psum(matmul(context_b, w_output), "mp")
    middle = tokens_flat + attn_out + b_output
    normed_two, unit_two, inv_two = norm_parts(middle, ln2_gain, ln2_bias)
    normed_two_b = normed_two.astype(jnp.bfloat16)
    upper = matmul(normed_two_b, w_up) + b_up
    activated, gelu_pull = jax.vjp(partial(jax.nn.gelu, approximate=True), upper)
    activated_b = activated.astype(jnp.bfloat16)
    down_out = lax.psum(matmul(activated_b, w_down), "mp")
    outcome = middle + down_out + b_down
    grad_top = cotangent.reshape(tokens, width)
    grad_top_b = grad_top.astype(jnp.bfloat16)
    grad_w_down = left_product(activated_b, grad_top_b)
    grad_b_down = jnp.sum(grad_top, axis=0)
    grad_act = right_product(grad_top_b, w_down)
    grad_upper = gelu_pull(grad_act)[0].astype(jnp.bfloat16)
    grad_w_up = left_product(normed_two_b, grad_upper)
    grad_b_up = jnp.sum(grad_upper.astype(jnp.float32), axis=0)
    grad_norm_two = lax.psum(right_product(grad_upper, w_up), "mp")
    grad_mid_part, grad_ln2_gain, grad_ln2_bias = norm_back(
        grad_norm_two, unit_two, inv_two, ln2_gain
    )
    grad_middle = grad_top + grad_mid_part
    grad_middle_b = grad_middle.astype(jnp.bfloat16)
    grad_b_output = jnp.sum(grad_middle, axis=0)
    grad_w_output = left_product(context_b, grad_middle_b)
    grad_context = right_product(grad_middle_b, w_output).astype(jnp.bfloat16).reshape(head_shape)
    again = jnp.exp(scores_of(query_four, key_four) - log_total)
    grad_probs = jnp.einsum(
        "rqhe,rkhe->rhqk", grad_context, value_four, preferred_element_type=jnp.float32
    )
    grad_values = jnp.einsum(
        "rhqk,rqhe->rkhe",
        again.astype(jnp.bfloat16),
        grad_context,
        preferred_element_type=jnp.float32,
    ).astype(jnp.bfloat16)
    row_delta = jnp.sum(again * grad_probs, axis=-1, keepdims=True)
    grad_scores = (again * (grad_probs - row_delta) * scale).astype(jnp.bfloat16)
    grad_queries = jnp.einsum(
        "rhqk,rkhe->rqhe", grad_scores, key_four, preferred_element_type=jnp.float32
    ).astype(jnp.bfloat16)
    grad_keys = jnp.einsum(
        "rhqk,rqhe->rkhe", grad_scores, query_four, preferred_element_type=jnp.float32
    ).astype(jnp.bfloat16)
    grad_queries = grad_queries.reshape(tokens, local_cols)
    grad_keys = grad_keys.reshape(tokens, local_cols)
    grad_values = grad_values.reshape(tokens, local_cols)
    grad_w_query = left_product(normed_b, grad_queries)
    grad_w_key = left_product(normed_b, grad_keys)
    grad_w_value = left_product(normed_b, grad_values)
    grad_b_query = jnp.sum(grad_queries.astype(jnp.float32), axis=0)
    grad_b_value = jnp.sum(grad_values.astype(jnp.float32), axis=0)
    partial_norm = (
        right_product(grad_queries, w_query)
        + right_product(grad_keys, w_key)
        + right_product(grad_values, w_value)
    )
    grad_norm_one = lax.psum(partial_norm, "mp")
    grad_in_part, grad_ln1_gain, grad_ln1_bias = norm_back(
        grad_norm_one, unit_one, inv_one, ln1_gain
    )
    grad_inputs = grad_middle + grad_in_part
    reduced = (
        lax.psum_scatter(grad_w_query, "dp", scatter_dimension=0, tiled=True),
        lax.psum_scatter(grad_w_key, "dp", scatter_dimension=0, tiled=True),
        lax.psum_scatter(grad_w_value, "dp", scatter_dimension=0, tiled=True),
        lax.psum_scatter(grad_w_output, "dp", scatter_dimension=1, tiled=True),
        lax.psum_scatter(grad_w_up, "dp", scatter_dimension=0, tiled=True),
        lax.psum_scatter(grad_w_down, "dp", scatter_dimension=1, tiled=True),
    )
    out_query, out_key, out_value, out_output, out_up, out_down = reduced
    smalls = lax.psum(
        (
            grad_ln1_gain,
            grad_ln1_bias,
            grad_b_query,
            grad_b_value,
            grad_b_output,
            grad_ln2_gain,
            grad_ln2_bias,
            grad_b_up,
            grad_b_down,
        ),
        "dp",
    )
    return (
        outcome.reshape(rows, length, width),
        grad_inputs.reshape(rows, length, width),
        smalls[0],
        smalls[1],
        out_query,
        smalls[2],
        out_key,
        out_value,
        smalls[3],
        out_output,
        smalls[4],
        smalls[5],
        smalls[6],
        out_up,
        smalls[7],
        out_down,
        smalls[8],
    )


def solution(mesh):
    return jax.shard_map(
        on_device,
        mesh=mesh,
        in_specs=(
            P("dp", None, None),
            P("dp", None),
            P(),
            P(),
            P(None, "mp"),
            P("mp"),
            P(None, "mp"),
            P(None, "mp"),
            P("mp"),
            P("mp", None),
            P(),
            P(),
            P(),
            P(None, "mp"),
            P("mp"),
            P("mp", None),
            P(),
            P("dp", None, None),
        ),
        out_specs=(
            P("dp", None, None),
            P("dp", None, None),
            P(),
            P(),
            P("dp", "mp"),
            P("mp"),
            P("dp", "mp"),
            P("dp", "mp"),
            P("mp"),
            P("mp", "dp"),
            P(),
            P(),
            P(),
            P("dp", "mp"),
            P("mp"),
            P("mp", "dp"),
            P(),
        ),
        check_vma=False,
    )
```

profile of v0, /device:TPU:0, one launch (start us, length us, event | category | flops | bytes accessed | tf_op | source)
XLA Modules:
  0.0 1006.9 jit_solution(2403655448056727484)
XLA Ops:
  18.8 3.4 add_convert_fusion.4
  25.1 3.4 add_convert_fusion.3
  39.0 2.7 fusion.79
  42.0 3.4 fusion.75
  45.3 22.4 %all-reduce.6.cloned.1.call-done = f32[1024,768]{1,0:T(8,128)} async-done(((f32[1024,768]{1,0:T(8,128)}), f32[1024,768]{1,0:T(8,128)}) %all-reduce.6.cloned.1.call-update) | async-done | bytes 3145744 | tf_op jit(solution)/shard_map/psum | solution.py:102
  67.8 3.3 fusion.73
  73.9 2.8 fusion.70
  76.7 8.1 convert_reduce_fusion
  86.5 4.3 fusion.81
  90.9 6.2 fusion.80
  97.1 18.3 %all-reduce.8.cloned.1.call-done = f32[1024,768]{1,0:T(8,128)} async-done(((f32[1024,768]{1,0:T(8,128)}), f32[1024,768]{1,0:T(8,128)}) %all-reduce.8.cloned.1.call-update) | async-done | bytes 3145744 | tf_op jit(solution)/shard_map/psum | solution.py:119
  115.4 3.9 multiply_reduce_fusion.1
  120.1 3.1 fusion.72
  126.8 3.7 fusion.55
  130.5 4.0 convert_reduce_fusion.1
  134.5 11.8 %fusion.45 = bf16[4,256,6,64]{1,3,2,0:T(8,128)(2,1)} fusion(f32[4,6,256,256]{2,3,1,0:T(8,128)} %fusion.55, f32[4,6,256,256]{2,3,1,0:T(8,128)} %copy-done.8, f32[4,6,256]{2,1,0:T(8,128)S(1)} %log_add_fusion, bf16[4,256,6,64]{1,0,3,2:T(4,128)(2,1)S(1)} %copy-done.22), kind=kOutput, calls=%fused_computation.63 | convolution fusion | flops 212736256 | bytes 14180352 | tf_op jit(solution)/shard_map/rhqk,rqhe->rkhe/dot_general | solution.py:143
  146.4 11.7 %convert_reduce_fusion.2 = (f32[6,64]{1,0:T(8,128)S(1)}, bf16[4,256,6,64]{1,3,2,0:T(8,128)(2,1)}) fusion(f32[4,6,256,256]{2,3,1,0:T(8,128)} %fusion.55, f32[4,6,256,256]{2,3,1,0:T(8,128)} %copy-done.8, f32[4,6,256]{2,1,0:T(8,128)S(1)} %log_add_fusion, bf16[4,256,6,64]{1,0,3,2:T(4,128)(2,1)S(1)} %copy-done.21), kind=kOutput, calls=%fused_computation.52 | convolution fusion | flops 213522304 | bytes 14181888 | tf_op jit(solution)/shard_map/rhqk,rkhe->rqhe/dot_general | solution.py:140
  163.1 2.8 add_add_fusion
  166.0 3.9 fusion.51
  175.8 3.9 fusion.85
  179.7 3.5 fusion.84
  183.4 8.4 fusion.69
  193.2 6.5 fusion.87
  200.0 3.6 multiply_reduce_fusion.2
  203.5 77.8 %all-reduce = (f32[768]{0:T(1024)}, f32[768]{0:T(1024)}, f32[384]{0:T(512)}, f32[384]{0:T(512)}, f32[768]{0:T(1024)}, /*index=5*/f32[768]{0:T(1024)}, f32[768]{0:T(1024)}, f32[1536]{0:T(1024)}, f32[768]{0:T(1024)}) all-reduce(f32[768]{0:T(1024)S(1)} %get-tuple-element.19, ...), channel_id=1, replica_groups=mesh['dp'=16,'mp'=2] {'dp'}, use_global_device_ids=true, to_apply=%region_16.17 | all-reduce | flops 6912 | bytes 55296 | tf_op jit(solution)/shard_map/psum | solution.py:173
  281.4 5.1 add_add_fusion.1
  290.6 39.4 %reduce-scatter.13.cloned.1.call-done = f32[384,48]{0,1:T(8,128)} async-done(((f32[384,768]{0,1:T(8,128)}), f32[384,48]{0,1:T(8,128)}) %reduce-scatter.13.cloned.1.call-update) | async-done | bytes 73744 | tf_op jit(solution)/shard_map/reduce_scatter | solution.py:168
  330.0 128.5 %reduce-scatter.11.cloned.1.call-done = f32[48,384]{1,0:T(8,128)} async-done(((f32[768,384]{1,0:T(8,128)}), f32[48,384]{1,0:T(8,128)}) %reduce-scatter.11.cloned.1.call-update) | async-done | bytes 73744 | tf_op jit(solution)/shard_map/reduce_scatter | solution.py:167
  458.5 128.5 %reduce-scatter.9.cloned.1.call-done = f32[48,384]{1,0:T(8,128)} async-done(((f32[768,384]{1,0:T(8,128)}), f32[48,384]{1,0:T(8,128)}) %reduce-scatter.9.cloned.1.call-update) | async-done | bytes 73744 | tf_op jit(solution)/shard_map/reduce_scatter | solution.py:166
  587.0 128.6 %reduce-scatter.7.cloned.1.call-done = f32[48,384]{1,0:T(8,128)} async-done(((f32[768,384]{1,0:T(8,128)}), f32[48,384]{1,0:T(8,128)}) %reduce-scatter.7.cloned.1.call-update) | async-done | bytes 73744 | tf_op jit(solution)/shard_map/reduce_scatter | solution.py:165
  715.6 142.3 %reduce-scatter.15.cloned.1.call-done = f32[48,1536]{1,0:T(8,128)} async-done(((f32[768,1536]{1,0:T(8,128)}), f32[48,1536]{1,0:T(8,128)}) %reduce-scatter.15.cloned.1.call-update) | async-done | bytes 294928 | tf_op jit(solution)/shard_map/reduce_scatter | solution.py:169
  858.0 142.2 %reduce-scatter.17.cloned.1.call-done = f32[1536,48]{0,1:T(8,128)} async-done(((f32[1536,768]{0,1:T(8,128)}), f32[1536,48]{0,1:T(8,128)}) %reduce-scatter.17.cloned.1.call-update) | async-done | bytes 294928 | tf_op jit(solution)/shard_map/reduce_scatter | solution.py:170
  (144 shorter events, 50.7 us)
Async XLA Ops:
  7.2 69.5 %copy-start = (bf16[1536,768]{1,0:T(8,128)(2,1)S(1)}, bf16[1536,768]{1,0:T(8,128)(2,1)}, u32[]{:S(2)}) copy-start(bf16[1536,768]{1,0:T(8,128)(2,1)} %param.33) | copy-start | bytes 7077892
  7.2 4.9 copy-start.31
  7.2 5.1 copy-start.29
  7.2 5.1 copy-start.30
  7.2 60.5 %all-reduce.6.cloned.1.call-start = ((), (), s32[]{:S(2)}) async-start(), calls=%async_computation.6 | async-start | bytes 6291456 | tf_op jit(solution)/shard_map/psum | solution.py:102
  9.5 2.8 copy-start.2
  14.1 4.7 copy-start.38
  18.8 6.3 copy-start.39
  41.7 26.0 %copy-start.33 = (f32[768]{0:T(1024)S(1)}, f32[768]{0:T(1024)}, u32[]{:S(2)}) copy-start(f32[768]{0:T(1024)} %param.28) | copy-start | bytes 9220
  41.7 73.7 %all-reduce.8.cloned.1.call-start = ((), (), s32[]{:S(2)}) async-start(), calls=%async_computation.7 | async-start | bytes 6291456 | tf_op jit(solution)/shard_map/psum | solution.py:119
  71.0 5.6 copy-start.4
  73.9 2.8 copy-start.17
  73.9 2.8 copy-start.36
  90.9 109.1 %all-reduce.10.cloned.1.call-start = ((), (), s32[]{:S(2)}) async-start(), calls=%async_computation.14 | async-start | bytes 12582912 | tf_op jit(solution)/shard_map/psum | solution.py:109
  115.4 4.0 copy-start.5
  115.4 4.7 copy-start.9
  120.1 4.8 copy-start.16
  130.5 4.0 copy-start.22
  134.5 11.8 %copy-start.21 = (bf16[4,256,6,64]{1,0,3,2:T(4,128)(2,1)S(1)}, bf16[4,256,6,64]{1,0,3,2:T(4,128)(2,1)}, u32[]{:S(2)}) copy-start(bf16[4,256,6,64]{1,0,3,2:T(4,128)(2,1)} %reshape.219) | copy-start | bytes 2359300
  159.2 3.9 copy-start.13
  165.9 164.1 %reduce-scatter.13.cloned.1.call-start = ((), (), s32[]{:S(2)}) async-start(), calls=%async_computation.11 | async-start | bytes 1253376 | tf_op jit(solution)/shard_map/reduce_scatter | solution.py:168
  169.9 3.7 copy-start.14
  170.0 288.5 %reduce-scatter.11.cloned.1.call-start = ((), (), s32[]{:S(2)}) async-start(), calls=%async_computation.10 | async-start | bytes 1253376 | tf_op jit(solution)/shard_map/reduce_scatter | solution.py:167
  175.8 411.2 %reduce-scatter.9.cloned.1.call-start = ((), (), s32[]{:S(2)}) async-start(), calls=%async_computation.9 | async-start | bytes 1253376 | tf_op jit(solution)/shard_map/reduce_scatter | solution.py:166
  179.7 535.9 %reduce-scatter.7.cloned.1.call-start = ((), (), s32[]{:S(2)}) async-start(), calls=%async_computation.8 | async-start | bytes 1253376 | tf_op jit(solution)/shard_map/reduce_scatter | solution.py:165
  183.3 674.6 %reduce-scatter.15.cloned.1.call-start = ((), (), s32[]{:S(2)}) async-start(), calls=%async_computation.12 | async-start | bytes 5013504 | tf_op jit(solution)/shard_map/reduce_scatter | solution.py:169
  191.8 808.4 %reduce-scatter.17.cloned.1.call-start = ((), (), s32[]{:S(2)}) async-start(), calls=%async_computation.13 | async-start | bytes 5013504 | tf_op jit(solution)/shard_map/reduce_scatter | solution.py:170
  199.9 81.4 %copy-start.34 = (f32[768]{0:T(1024)S(1)}, f32[768]{0:T(1024)}, u32[]{:S(2)}) copy-start(f32[768]{0:T(1024)} %param.34) | copy-start | bytes 9220
  281.4 5.1 copy-start.3
  281.4 5.5 copy-start.7
  281.4 6.8 copy-start.10
  288.2 712.0 %copy-start.1 = (bf16[1536,768]{1,0:T(8,128)(2,1)S(1)}, bf16[1536,768]{1,0:T(8,128)(2,1)}, u32[]{:S(2)}) copy-start(bf16[1536,768]{1,0:T(8,128)(2,1)} %param.33) | copy-start | bytes 7077892
  (18 other events, 30.8 us)
Sparse Core Ops, SparseCore 0:
  41.8 25.8 all-reduce.5
  91.0 24.3 all-reduce.7
  166.1 33.3 all-reduce.9
  205.3 124.6 reduce-scatter.12
  335.9 122.5 reduce-scatter.10
  464.4 122.5 reduce-scatter.8
  593.0 122.5 reduce-scatter.6
  722.2 135.7 reduce-scatter.14
  863.7 136.4 reduce-scatter.16
where the time goes:
time: 1020 us; the launch traced here: 1010 us
  waiting for transfers between devices  750 us (74%)
  matrix products  102 us (10%)
  blocking collectives  77.8 us (8%)
  other arithmetic  34.4 us (3%)
  local copies, waits for them, and re-layouts  26.8 us (3%)
  between operations  14.6 us (1%)
    reduce_scatter x1, waiting for transfers between devices, on_device(): lax.psum_scatter(grad_w_up, 'dp', scatter_dimension=0, tiled=True)  142 us
    reduce_scatter x1, waiting for transfers between devices, on_device(): lax.psum_scatter(grad_w_down, 'dp', scatter_dimension=1, tiled=True)  142 us
    reduce_scatter x1, waiting for transfers between devices, on_device(): lax.psum_scatter(grad_w_query, 'dp', scatter_dimension=0, tiled=True)  129 us
    reduce_scatter x1, waiting for transfers between devices, on_device(): lax.psum_scatter(grad_w_key, 'dp', scatter_dimension=0, tiled=True)  128 us
    reduce_scatter x1, waiting for transfers between devices, on_device(): lax.psum_scatter(grad_w_value, 'dp', scatter_dimension=0, tiled=True)  128 us
    psum x1, blocking collectives, on_device(): lax.psum((grad_ln1_gain, grad_ln1_bias, grad_b_query, grad_b_value, grad_...  77.8 us
    reduce_scatter x1, waiting for transfers between devices, on_device(): lax.psum_scatter(grad_w_output, 'dp', scatter_dimension=1, tiled=True)  39.4 us
    dot_general x6, matrix products, left_product(): jnp.einsum('ta,tb->ab', left, right, preferred_element_type=jnp.float32)  28.3 us
  transfers between devices with their start and end apart: 9, of which 8 were waited for; matrix products, arithmetic and copies ran while one was open for 5% of the time, Pallas kernels for 0%

commit v1 on v0

--- a/solution.py
+++ b/solution.py
@@ -4,6 +4,8 @@
 import jax
 import jax.numpy as jnp
 from jax import lax
+from jax.experimental import pallas as pl
+from jax.experimental.pallas import tpu as pltpu
 from jax.sharding import PartitionSpec as P
 
 HD = 64
@@ -43,6 +45,144 @@
 
 def right_product(left, right):
     return jnp.einsum("tb,ab->ta", left, right, preferred_element_type=jnp.float32)
+
+
+def sum_over_mp(part):
+    size = lax.axis_size("mp")
+    if size != 2:
+        return lax.psum(part, "mp")
+    return part + lax.ppermute(part, "mp", [(0, 1), (1, 0)])
+
+
+def orders_for(kind, bits):
+    low, rest = [1 << b for b in range(min(bits, 2))], [1 << b for b in range(2, bits)]
+    if kind == "near":
+        return [low + rest, low[::-1] + rest]
+    return [rest[:1] + low + rest[1:], rest[:1] + low[::-1] + rest[1:]]
+
+
+def order_of_member(orders, member):
+    return orders[member % 2]
+
+
+def block_table(orders, bits):
+    me = lax.axis_index("dp")
+    count = 1 << bits
+    masks = []
+    for order in orders:
+        masks.append(
+            [
+                sum(order[k] for k in range(bits) if r >> (bits - 1 - k) & 1)
+                for r in range(count)
+            ]
+        )
+    masks = jnp.asarray(masks, jnp.int32)
+    return masks[lax.axis_index("mp") % 2] ^ me.astype(jnp.int32)
+
+
+def exchange(array, orders, stage):
+    dp, mp = lax.axis_size("dp"), lax.axis_size("mp")
+    pairs = []
+    for d in range(dp):
+        for m in range(mp):
+            pairs.append((d * mp + m, (d ^ order_of_member(orders, m)[stage]) * mp + m))
+    return lax.ppermute(array, ("dp", "mp"), pairs)
+
+
+def finish_scatter(send, keep, orders, bits):
+    received = []
+    for stage in range(bits):
+        received.append(exchange(send, orders, stage))
+        half = keep.shape[0] >> (stage + 1)
+        if stage + 1 < bits:
+            send = keep[half : 2 * half]
+            for got in received:
+                send = send + got[half : 2 * half]
+    total = keep[0]
+    for got in received:
+        total = total + got[0]
+    return total
+
+
+def all_sum(vector, bits):
+    orders = orders_for("near", bits)
+    for stage in range(bits):
+        vector = vector + exchange(vector, orders, stage)
+    return vector
+
+
+def grad_kernel(table, left_ref, right_ref, *refs):
+    outs, acc = refs[:-1], refs[-1]
+    acc[...] = lax.dot_general(
+        left_ref[...],
+        right_ref[...],
+        (((0,), (0,)), ((), ())),
+        preferred_element_type=jnp.float32,
+    )
+    send, keep = outs
+    half, size = keep.shape[0], keep.shape[1]
+    for r in range(half):
+        at = pl.multiple_of(table[r] * size, 8)
+        keep[r] = acc[pl.ds(at, size), :]
+        at = pl.multiple_of(table[half + r] * size, 8)
+        send[r] = acc[pl.ds(at, size), :]
+
+
+def blocked_grad(table, left, right, start, columns, tile):
+    tokens, width = left.shape
+    count = table.shape[0]
+    size = width // count
+    shape = jax.ShapeDtypeStruct((count // 2, size, columns), jnp.float32)
+    block = pl.BlockSpec((count // 2, size, tile), lambda i, t: (0, 0, i))
+    first = start // tile
+    return pl.pallas_call(
+        grad_kernel,
+        grid_spec=pltpu.PrefetchScalarGridSpec(
+            num_scalar_prefetch=1,
+            grid=(columns // tile,),
+            in_specs=[
+                pl.BlockSpec((tokens, width), lambda i, t: (0, 0)),
+                pl.BlockSpec((tokens, tile), lambda i, t: (0, i + first)),
+            ],
+            out_specs=[block, block],
+            scratch_shapes=[pltpu.VMEM((width, tile), jnp.float32)],
+        ),
+        out_shape=[shape, shape],
+        cost_estimate=pl.CostEstimate(
+            flops=2 * tokens * width * columns,
+            bytes_accessed=2 * tokens * (width + columns) + 4 * width * columns,
+            transcendentals=0,
+        ),
+        compiler_params=pltpu.CompilerParams(vmem_limit_bytes=40 << 20),
+    )(table, left, right)
+
+
+def scattered_grad(left, right, kind, start, columns, tile):
+    dp = lax.axis_size("dp")
+    bits = dp.bit_length() - 1
+    size = left.shape[1] // dp
+    if (1 << bits) != dp or size % 8 or bits < 3:
+        part = left_product(left, right[:, start : start + columns])
+        return lax.psum_scatter(part, "dp", scatter_dimension=0, tiled=True)
+    orders = orders_for(kind, bits)
+    table = block_table(orders, bits)
+    send, keep = blocked_grad(table, left, right, start, columns, tile)
+    return finish_scatter(send, keep, orders, bits)
+
+
+def sum_small(parts):
+    dp = lax.axis_size("dp")
+    bits = dp.bit_length() - 1
+    if (1 << bits) != dp:
+        return lax.psum(parts, "dp")
+    sizes = [part.shape[0] for part in parts]
+    flat = jnp.concatenate(parts).reshape(-1, 128)
+    flat = all_sum(flat, bits).reshape(-1)
+    out, at = [], 0
+    for size in sizes:
+        out.append(flat[at : at + size])
+        at += size
+    return out
 
 
 def on_device(
@@ -99,31 +239,35 @@
         preferred_element_type=jnp.float32,
     )
     context_b = context.reshape(tokens, local_cols).astype(jnp.bfloat16)
-    attn_out = lax.psum(matmul(context_b, w_output), "mp")
+    attn_out = sum_over_mp(matmul(context_b, w_output))
     middle = tokens_flat + attn_out + b_output
     normed_two, unit_two, inv_two = norm_parts(middle, ln2_gain, ln2_bias)
     normed_two_b = normed_two.astype(jnp.bfloat16)
     upper = matmul(normed_two_b, w_up) + b_up
     activated, gelu_pull = jax.vjp(partial(jax.nn.gelu, approximate=True), upper)
     activated_b = activated.astype(jnp.bfloat16)
-    down_out = lax.psum(matmul(activated_b, w_down), "mp")
+    down_out = sum_over_mp(matmul(activated_b, w_down))
     outcome = middle + down_out + b_down
     grad_top = cotangent.reshape(tokens, width)
     grad_top_b = grad_top.astype(jnp.bfloat16)
-    grad_w_down = left_product(activated_b, grad_top_b)
+    hidden = w_up.shape[1]
+    far = hidden // 3
+    down_near = scattered_grad(grad_top_b, activated_b, "near", 0, hidden - far, far)
+    down_far = scattered_grad(grad_top_b, activated_b, "far", hidden - far, far, far)
     grad_b_down = jnp.sum(grad_top, axis=0)
     grad_act = right_product(grad_top_b, w_down)
     grad_upper = gelu_pull(grad_act)[0].astype(jnp.bfloat16)
-    grad_w_up = left_product(normed_two_b, grad_upper)
+    up_near = scattered_grad(normed_two_b, grad_upper, "near", 0, hidden - far, far)
+    up_far = scattered_grad(normed_two_b, grad_upper, "far", hidden - far, far, far)
     grad_b_up = jnp.sum(grad_upper.astype(jnp.float32), axis=0)
-    grad_norm_two = lax.psum(right_product(grad_upper, w_up), "mp")
+    grad_norm_two = sum_over_mp(right_product(grad_upper, w_up))
     grad_mid_part, grad_ln2_gain, grad_ln2_bias = norm_back(
         grad_norm_two, unit_two, inv_two, ln2_gain
     )
     grad_middle = grad_top + grad_mid_part
     grad_middle_b = grad_middle.astype(jnp.bfloat16)
     grad_b_output = jnp.sum(grad_middle, axis=0)
-    grad_w_output = left_product(context_b, grad_middle_b)
+    out_part = scattered_grad(grad_middle_b, context_b, "far", 0, local_cols, local_cols)
     grad_context = right_product(grad_middle_b, w_output).astype(jnp.bfloat16).reshape(head_shape)
     again = jnp.exp(scores_of(query_four, key_four) - log_total)
     grad_probs = jnp.einsum(
@@ -146,9 +290,10 @@
     grad_queries = grad_queries.reshape(tokens, local_cols)
     grad_keys = grad_keys.reshape(tokens, local_cols)
     grad_values = grad_values.reshape(tokens, local_cols)
-    grad_w_query = left_product(normed_b, grad_queries)
-    grad_w_key = left_product(normed_b, grad_keys)
-    grad_w_value = left_product(normed_b, grad_values)
+    out_value = scattered_grad(normed_b, grad_values, "far", 0, local_cols, local_cols)
+    two = jnp.concatenate([grad_queries, grad_keys], axis=1)
+    pair = scattered_grad(normed_b, two, "near", 0, 2 * local_cols, local_cols)
+    out_query, out_key = pair[:, :local_cols], pair[:, local_cols:]
     grad_b_query = jnp.sum(grad_queries.astype(jnp.float32), axis=0)
     grad_b_value = jnp.sum(grad_values.astype(jnp.float32), axis=0)
     partial_norm = (
@@ -156,21 +301,15 @@
         + right_product(grad_keys, w_key)
         + right_product(grad_values, w_value)
     )
-    grad_norm_one = lax.psum(partial_norm, "mp")
+    grad_norm_one = sum_over_mp(partial_norm)
     grad_in_part, grad_ln1_gain, grad_ln1_bias = norm_back(
         grad_norm_one, unit_one, inv_one, ln1_gain
     )
     grad_inputs = grad_middle + grad_in_part
-    reduced = (
-        lax.psum_scatter(grad_w_query, "dp", scatter_dimension=0, tiled=True),
-        lax.psum_scatter(grad_w_key, "dp", scatter_dimension=0, tiled=True),
-        lax.psum_scatter(grad_w_value, "dp", scatter_dimension=0, tiled=True),
-        lax.psum_scatter(grad_w_output, "dp", scatter_dimension=1, tiled=True),
-        lax.psum_scatter(grad_w_up, "dp", scatter_dimension=0, tiled=True),
-        lax.psum_scatter(grad_w_down, "dp", scatter_dimension=1, tiled=True),
-    )
-    out_query, out_key, out_value, out_output, out_up, out_down = reduced
-    smalls = lax.psum(
+    out_up = jnp.concatenate([up_near, up_far], axis=1)
+    out_down = jnp.concatenate([down_near, down_far], axis=1).T
+    out_output = out_part.T
+    smalls = sum_small(
         (
             grad_ln1_gain,
             grad_ln1_bias,
@@ -181,8 +320,7 @@
             grad_ln2_bias,
             grad_b_up,
             grad_b_down,
-        ),
-        "dp",
+        )
     )
     return (
         outcome.reshape(rows, length, width),

time: 1020 us -> 330 us (0.32)
  waiting for transfers between devices: 750 us -> 91.1 us
  blocking collectives: 77.8 us -> 0 us
  starting transfers between devices: 0.59 us -> 38.3 us
  other arithmetic: 34.4 us -> 65.3 us
  matrix products: 102 us -> 77.9 us
  Pallas kernels: 0 us -> 18.5 us
  between operations: 14.6 us -> 1.85 us
    reduce_scatter x6 -> x0, waiting for transfers between devices: 710 us -> none  [the longest x1 142 us: on_device(): lax.psum_scatter(grad_w_up, 'dp', scatter_dimension=0, tiled=True)]
    ppermute x0 -> x36, waiting for transfers between devices: none -> 91.1 us  [the longest x32 91 us: exchange(): return lax.ppermute(array, ('dp', 'mp'), pairs)]
    psum x1 -> x0, blocking collectives: 77.8 us -> none  [on_device(): lax.psum((grad_ln1_gain, grad_ln1_bias, grad_b_query, grad_b_value, grad_...]
    psum x3 -> x0, waiting for transfers between devices: 40.7 us -> none  [the longest x1 22.4 us: on_device(): attn_out = lax.psum(matmul(context_b, w_output), 'mp')]
    ppermute x0 -> x36, starting transfers between devices: none -> 38.3 us  [the longest x32 37.3 us: exchange(): return lax.ppermute(array, ('dp', 'mp'), pairs)]
    dot_general x6 -> x0, matrix products: 28.3 us -> none  [left_product(): jnp.einsum('ta,tb->ab', left, right, preferred_element_type=jnp.float32)]
    pallas_call x0 -> x7, Pallas kernels: none -> 18.5 us  [blocked_grad(): pl.pallas_call(grad_kernel, grid_spec=pltpu.PrefetchScalarGridSpec(num_sc...]
    add x1 -> x31, other arithmetic: 5.09 us -> 21.3 us  [the longest x21 15.4 us: finish_scatter(): send = send + got[half:2 * half]]
  transfers between devices with their start and end apart: 9 -> 36, of which waited for: 8 -> 21; matrix products, arithmetic and copies ran while one was open for 5% -> 20% of each run, Pallas kernels for 0% -> 4%
where the time goes in v1:
time: 330 us; the launch traced here: 327 us
  waiting for transfers between devices  91.1 us (28%)
  matrix products  77.9 us (24%)
  other arithmetic  65.3 us (20%)
  starting transfers between devices  38.3 us (12%)
  local copies, waits for them, and re-layouts  33.8 us (10%)
  Pallas kernels  18.5 us (6%)
    ppermute x32, waiting for transfers between devices, exchange(): return lax.ppermute(array, ('dp', 'mp'), pairs)  91 us
    ppermute x32, starting transfers between devices, exchange(): return lax.ppermute(array, ('dp', 'mp'), pairs)  37.3 us
    dot_general x6, matrix products, matmul(): return jnp.dot(left, right, preferred_element_type=jnp.float32)  22.8 us
    pallas_call x7, Pallas kernels, blocked_grad(): pl.pallas_call(grad_kernel, grid_spec=pltpu.PrefetchScalarGridSpec(num_sc...  18.5 us
    dot_general x6, matrix products, right_product(): jnp.einsum('tb,ab->ta', left, right, preferred_element_type=jnp.float32)  16.6 us
    reduce_sum x1, other arithmetic, on_device(): grad_b_down = jnp.sum(grad_top, axis=0)  15.6 us
    add x21, other arithmetic, finish_scatter(): send = send + got[half:2 * half]  15.4 us
    dot_general x1, matrix products, on_device(): jnp.einsum('rhqk,rkhe->rqhe', grad_scores, key_four, preferred_element_ty...  12.3 us
  transfers between devices with their start and end apart: 36, of which 21 were waited for; matrix products, arithmetic and copies ran while one was open for 20% of the time, Pallas kernels for 4%

profile of v1, /device:TPU:0, one launch (start us, length us, event | category | flops | bytes accessed | tf_op | source)
XLA Modules:
  0.0 326.7 jit_solution(2459474922291981767)
XLA Ops:
  12.3 3.4 %convolution_convert_fusion.1 = bf16[1024,384]{1,0:T(8,128)(2,1)} fusion(bf16[1024,768]{1,0:T(8,128)(2,1)} %copy-done.2, bf16[768,384]{1,0:T(8,128)(2,1)} %param.31), kind=kOutput, calls=%fused_computation.56 | convolution fusion | flops 604372992 | bytes 2949120 | tf_op jit(solution)/shard_map/dot_general | solution.py:39
  18.8 3.4 %add_convert_fusion.3 = bf16[1024,384]{1,0:T(8,128)(2,1)} fusion(bf16[1024,768]{1,0:T(8,128)(2,1)} %copy-done.2, bf16[768,384]{1,0:T(8,128)(2,1)} %param.32, f32[384]{0:T(512)S(1)} %copy-done.50), kind=kOutput, calls=%fused_computation.54 | convolution fusion | flops 604766208 | bytes 2950656 | tf_op jit(solution)/shard_map/dot_general | solution.py:39
  38.1 15.6 %fusion.83 = (f32[768]{0:T(1024)}, bf16[1024,768]{1,0:T(8,128)(2,1)S(1)}) fusion(f32[4,256,768]{2,1,0:T(8,128)} %param.42), kind=kLoop, calls=%fused_computation.191 | loop fusion | flops 1572096 | bytes 4721664 | tf_op jit(solution)/shard_map/reduce_sum | solution.py:257
  56.3 3.4 %fusion.81 = (f32[1024]{0:T(1024)S(1)}, f32[1024,768]{1,0:T(8,128)S(1)}) fusion(f32[768]{0:T(1024)S(1)} %copy-done.41, f32[1024,768]{1,0:T(8,128)} %fusion.88, f32[1024,768]{1,0:T(8,128)} %collective-permute-done, f32[4,256,768]{2,1,0:T(8,128)S(1)} %copy-done.10), kind=kLoop, calls=%fused_computation.190 | loop fusion | flops 3144704 | bytes 12590080 | tf_op jit(solution)/shard_map/reduce_sum | solution.py:19
  61.0 8.9 %convert_reduce_fusion = (f32[1536]{0:T(1024)}, bf16[1024,1536]{1,0:T(8,128)(2,1)S(1)}, bf16[1024,1536]{1,0:T(8,128)(2,1)S(1)}) fusion(f32[1024,1536]{1,0:T(8,128)S(1)} %fusion.90, f32[1536]{0:T(1024)S(1)} %copy-done.48, bf16[1024,768]{1,0:T(8,128)(2,1)S(1)} %add_convert_fusion.left_ref, bf16[768,1536]{1,0:T(8,128)(2,1)S(1)} %copy-done), kind=kOutput, calls=%fused_computation.10 | convolution fusion | flops 2455239168 | bytes 16527360 | tf_op jit(solution)/shard_map/dot_general | solution.py:39
  69.9 3.2 shard_map.373
  78.9 3.2 shard_map.371
  87.0 10.8 %collective-permute-done.32 = f32[8,48,512]{2,1,0:T(8,128)} collective-permute-done((f32[8,48,512]{2,1,0:T(8,128)S(1)}, f32[8,48,512]{2,1,0:T(8,128)}, u32[]{:S(2)}, u32[]{:S(2)}) %collective-permute-start.32) | collective-permute-done | bytes 786464 | tf_op jit(solution)/shard_map/ppermute | solution.py:89
  98.9 15.0 %collective-permute-done.24 = f32[8,48,512]{2,1,0:T(8,128)S(1)} collective-permute-done((f32[8,48,512]{2,1,0:T(8,128)S(1)}, f32[8,48,512]{2,1,0:T(8,128)S(1)}, u32[]{:S(2)}, u32[]{:S(2)}) %collective-permute-start.24) | collective-permute-done | bytes 786464 | tf_op jit(solution)/shard_map/ppermute | solution.py:89
  118.3 3.5 %collective-permute-done.25 = f32[4,48,512]{2,1,0:T(8,128)S(1)} collective-permute-done((f32[4,48,512]{2,1,0:T(8,128)S(1)}, f32[4,48,512]{2,1,0:T(8,128)S(1)}, u32[]{:S(2)}, u32[]{:S(2)}) %collective-permute-start.25) | collective-permute-done | bytes 393248 | tf_op jit(solution)/shard_map/ppermute | solution.py:89
  132.2 2.9 collective-permute-done.35
  135.1 2.7 collective-permute-start.27
  139.8 3.8 %collective-permute-start.30 = (f32[2,48,1024]{2,1,0:T(8,128)S(1)}, f32[2,48,1024]{2,1,0:T(8,128)S(1)}, u32[]{:S(2)}, u32[]{:S(2)}) collective-permute-start(f32[2,48,1024]{2,1,0:T(8,128)S(1)} %slice_add_fusion.4), channel_id=1, source_target_pairs={{0,8},{1,9},{2,10},{3,11},{4,12},{5,13},{6,14},{7,15},{8,0},{9,1},... | collective-permute-start | bytes 1179656 | tf_op jit(solution)/shard_map/ppermute | solution.py:89
  143.6 2.8 collective-permute-done.21
  153.7 8.3 %collective-permute-done.22 = f32[2,48,1024]{2,1,0:T(8,128)S(1)} collective-permute-done((f32[2,48,1024]{2,1,0:T(8,128)S(1)}, f32[2,48,1024]{2,1,0:T(8,128)S(1)}, u32[]{:S(2)}, u32[]{:S(2)}) %collective-permute-start.22) | collective-permute-done | bytes 393248 | tf_op jit(solution)/shard_map/ppermute | solution.py:89
  166.2 7.1 %collective-permute-done.23 = f32[1,48,1024]{2,1,0:T(8,128)S(1)} collective-permute-done((f32[1,48,1024]{2,1,0:T(8,128)S(1)}, f32[1,48,1024]{2,1,0:T(8,128)S(1)}, u32[]{:S(2)}, u32[]{:S(2)}) %collective-permute-start.23) | collective-permute-done | bytes 196640 | tf_op jit(solution)/shard_map/ppermute | solution.py:89
  177.3 3.5 %fusion.80 = (f32[768]{0:T(1024)}, f32[1024,768]{1,0:T(8,128)S(1)}, f32[1024,768]{1,0:T(8,128)}) fusion(f32[1024]{0:T(1024)S(1)} %get-tuple-element.83, f32[1024,768]{1,0:T(8,128)S(1)} %get-tuple-element.60, f32[1024]{0:T(1024)S(1)} %broadcast_multiply_fusion.4, f32[1024]{0:T(1024)S(1)} %get-tuple-element.84, f32[1024,768]{1,0:T(8,128)S(1)} %get-tuple-element.58, ...), kind=kLoop, calls=%fused_computation.189 | loop fusion | flops 9436416 | bytes 22045696 | tf_op jit(solution)/shard_map/reduce_sum | solution.py:269
  187.2 4.8 %fusion.52 = f32[4,6,256,256]{2,3,1,0:T(8,128)} fusion(bf16[4,256,6,64]{1,0,3,2:T(4,128)(2,1)S(1)} %reshape.220, bf16[4,256,6,64]{1,0,3,2:T(4,128)(2,1)} %reshape.215), kind=kOutput, calls=%fused_computation.68 | convolution fusion | flops 201326592 | bytes 7864320 | tf_op jit(solution)/shard_map/rqhe,rkhe->rhqk/dot_general | solution.py:273
  192.0 5.4 %convert_reduce_fusion.1 = (f32[6,64]{1,0:T(8,128)}, bf16[4,256,6,64]{1,3,2,0:T(8,128)(2,1)}) fusion(f32[4,6,256,256]{2,3,1,0:T(8,128)} %copy-done.14, f32[4,6,256]{2,1,0:T(8,128)S(1)} %log_add_fusion, bf16[4,256,6,64]{1,0,3,2:T(4,128)(2,1)S(1)} %reshape.220), kind=kOutput, calls=%fused_computation.51 | convolution fusion | flops 205651584 | bytes 7890432 | tf_op jit(solution)/shard_map/rhqk,rqhe->rkhe/dot_general | solution.py:276
  197.4 12.1 %fusion.45 = bf16[4,256,6,64]{1,3,2,0:T(8,128)(2,1)} fusion(f32[4,6,256,256]{2,3,1,0:T(8,128)} %fusion.52, f32[4,6,256,256]{2,3,1,0:T(8,128)} %copy-done.14, f32[4,6,256]{2,1,0:T(8,128)S(1)} %log_add_fusion, bf16[4,256,6,64]{1,0,3,2:T(4,128)(2,1)} %reshape.216), kind=kOutput, calls=%fused_computation.63 | convolution fusion | flops 212736256 | bytes 14180352 | tf_op jit(solution)/shard_map/rhqk,rqhe->rkhe/dot_general | solution.py:287
  209.5 12.3 %convert_reduce_fusion.2 = (f32[6,64]{1,0:T(8,128)}, bf16[4,256,6,64]{1,3,2,0:T(8,128)(2,1)}) fusion(f32[4,6,256,256]{2,3,1,0:T(8,128)} %fusion.52, f32[4,6,256,256]{2,3,1,0:T(8,128)} %copy-done.14, f32[4,6,256]{2,1,0:T(8,128)S(1)} %log_add_fusion, bf16[4,256,6,64]{1,0,3,2:T(4,128)(2,1)S(1)} %copy-done.22), kind=kOutput, calls=%fused_computation.52 | convolution fusion | flops 213522304 | bytes 14181888 | tf_op jit(solution)/shard_map/rhqk,rkhe->rqhe/dot_general | solution.py:284
  225.0 3.8 %fusion.93 = f32[1024,768]{1,0:T(8,128)} fusion(bf16[1024,384]{0,1:T(8,128)(2,1)S(1)} %bitcast.135, bf16[768,384]{1,0:T(8,128)(2,1)} %param.31), kind=kOutput, calls=%fused_computation.199 | convolution fusion | flops 603979776 | bytes 4521984 | tf_op jit(solution)/shard_map/tb,ab->ta/dot_general | solution.py:47
  230.8 3.8 %fusion.92 = f32[1024,768]{1,0:T(8,128)} fusion(bf16[1024,384]{0,1:T(8,128)(2,1)S(1)} %bitcast.137, bf16[768,384]{1,0:T(8,128)(2,1)} %param.29), kind=kOutput, calls=%fused_computation.198 | convolution fusion | flops 603979776 | bytes 4521984 | tf_op jit(solution)/shard_map/tb,ab->ta/dot_general | solution.py:47
  246.7 3.8 %shard_map.368 = (f32[8,48,768]{2,1,0:T(8,128)}, f32[8,48,768]{2,1,0:T(8,128)S(1)}) custom-call(s32[16]{0:T(128)S(1)} %get-tuple-element.86.table, bf16[1024,768]{1,0:T(8,128)(2,1)S(1)} %copy-done.4, bf16[1024,768]{1,0:T(8,128)(2,1)S(1)} %pad_maximum_fusion.right_ref), custom_call_target="tpu_custom_call" | custom-call | flops 1207959552 | bytes 5505024 | tf_op jit(solution)/shard_map/pallas_call | solution.py:138
  259.8 5.0 %collective-permute-done.12 = f32[8,48,384]{2,1,0:T(8,128)} collective-permute-done((f32[8,48,384]{2,1,0:T(8,128)}, f32[8,48,384]{2,1,0:T(8,128)}, u32[]{:S(2)}, u32[]{:S(2)}) %collective-permute-start.12) | collective-permute-done | bytes 589856 | tf_op jit(solution)/shard_map/ppermute | solution.py:89
  268.2 3.7 %collective-permute-done.17 = f32[4,48,384]{2,1,0:T(8,128)S(1)} collective-permute-done((f32[4,48,384]{2,1,0:T(8,128)S(1)}, f32[4,48,384]{2,1,0:T(8,128)S(1)}, u32[]{:S(2)}, u32[]{:S(2)}) %collective-permute-start.17) | collective-permute-done | bytes 294944 | tf_op jit(solution)/shard_map/ppermute | solution.py:89
  274.2 4.1 %collective-permute-done.13 = f32[4,48,384]{2,1,0:T(8,128)S(1)} collective-permute-done((f32[4,48,384]{2,1,0:T(8,128)S(1)}, f32[4,48,384]{2,1,0:T(8,128)S(1)}, u32[]{:S(2)}, u32[]{:S(2)}) %collective-permute-start.13) | collective-permute-done | bytes 294944 | tf_op jit(solution)/shard_map/ppermute | solution.py:89
  289.7 5.1 %collective-permute-done.10 = f32[2,48,768]{2,1,0:T(8,128)S(1)} collective-permute-done((f32[2,48,768]{2,1,0:T(8,128)S(1)}, f32[2,48,768]{2,1,0:T(8,128)S(1)}, u32[]{:S(2)}, u32[]{:S(2)}) %collective-permute-start.10) | collective-permute-done | bytes 294944 | tf_op jit(solution)/shard_map/ppermute | solution.py:89
  296.5 7.2 %collective-permute-done.11 = f32[1,48,768]{2,1,0:T(8,128)S(1)} collective-permute-done((f32[1,48,768]{2,1,0:T(8,128)S(1)}, f32[1,48,768]{2,1,0:T(8,128)S(1)}, u32[]{:S(2)}, u32[]{:S(2)}) %collective-permute-start.11) | collective-permute-done | bytes 147488 | tf_op jit(solution)/shard_map/ppermute | solution.py:89
  303.9 4.0 %multiply_reduce_fusion.2 = (f32[768]{0:T(1024)S(1)}, f32[1024]{0:T(1024)S(1)}, f32[1024]{0:T(1024)S(1)}, f32[768]{0:T(1024)S(1)}, f32[1024,768]{1,0:T(8,128)S(1)}) fusion(f32[4,256,768]{2,1,0:T(8,128)S(1)} %copy-done.11, f32[1024]{0:T(1024)S(1)} %bitcast.148, f32[1024]{0:T(1024)S(1)} %bitcast.151, f32[768]{0:T(1024)S(1)} %copy-done.32, ...), kind=kLoop, calls=%fused_computation.31 | loop fusion | flops 7860736 | bytes 12608512 | tf_op jit(solution)/shard_map/reduce_sum | solution.py:27
  313.0 3.0 collective-permute-done.5
  316.0 3.8 %collective-permute-done.6 = f32[54,128]{1,0:T(8,128)S(1)} collective-permute-done((f32[54,128]{1,0:T(8,128)S(1)}, f32[54,128]{1,0:T(8,128)S(1)}, u32[]{:S(2)}, u32[]{:S(2)}) %collective-permute-start.6) | collective-permute-done | bytes 27680 | tf_op jit(solution)/shard_map/ppermute | solution.py:89
  (263 shorter events, 141.5 us)
Async XLA Ops:
  36.0 20.3 %collective-permute-start = (f32[1024,768]{1,0:T(8,128)}, f32[1024,768]{1,0:T(8,128)}, u32[]{:S(2)}, u32[]{:S(2)}) collective-permute-start(f32[1024,768]{1,0:T(8,128)} %fusion.88), channel_id=1, source_target_pairs={{0,1},{1,0},{2,3},{3,2},{4,5},{5,4},{6,7},{7,6},{8,9},{9,8},{10,11... | collective-permute-start | bytes 9437192 | tf_op jit(solution)/shard_map/ppermute | solution.py:54
  73.0 49.1 %collective-permute-start.28 = (f32[8,48,1024]{2,1,0:T(8,128)S(1)}, f32[8,48,1024]{2,1,0:T(8,128)}, u32[]{:S(2)}, u32[]{:S(2)}) collective-permute-start(f32[8,48,1024]{2,1,0:T(8,128)S(1)} %get-tuple-element.42), channel_id=1, source_target_pairs={{0,2},{1,5},{2,0},{3,7},{4,6},{5,1},{6,4},{7,3},{8,10},{9,13},{10,... | collective-permute-start | bytes 4718600 | tf_op jit(solution)/shard_map/ppermute | solution.py:89
  77.2 20.5 %collective-permute-start.32 = (f32[8,48,512]{2,1,0:T(8,128)S(1)}, f32[8,48,512]{2,1,0:T(8,128)}, u32[]{:S(2)}, u32[]{:S(2)}) collective-permute-start(f32[8,48,512]{2,1,0:T(8,128)S(1)} %get-tuple-element.44), channel_id=1, source_target_pairs={{0,8},{1,9},{2,10},{3,11},{4,12},{5,13},{6,14},{7,15},{8,0},{9,1},... | collective-permute-start | bytes 2359304 | tf_op jit(solution)/shard_map/ppermute | solution.py:89
  82.0 43.1 %collective-permute-start.20 = (f32[8,48,1024]{2,1,0:T(8,128)S(1)}, f32[8,48,1024]{2,1,0:T(8,128)}, u32[]{:S(2)}, u32[]{:S(2)}) collective-permute-start(f32[8,48,1024]{2,1,0:T(8,128)S(1)} %get-tuple-element.38), channel_id=1, source_target_pairs={{0,2},{1,5},{2,0},{3,7},{4,6},{5,1},{6,4},{7,3},{8,10},{9,13},{10,... | collective-permute-start | bytes 4718600 | tf_op jit(solution)/shard_map/ppermute | solution.py:89
  84.3 29.5 %collective-permute-start.24 = (f32[8,48,512]{2,1,0:T(8,128)S(1)}, f32[8,48,512]{2,1,0:T(8,128)S(1)}, u32[]{:S(2)}, u32[]{:S(2)}) collective-permute-start(f32[8,48,512]{2,1,0:T(8,128)S(1)} %get-tuple-element.40), channel_id=1, source_target_pairs={{0,8},{1,9},{2,10},{3,11},{4,12},{5,13},{6,14},{7,15},{8,0},{9,1},... | collective-permute-start | bytes 2359304 | tf_op jit(solution)/shard_map/ppermute | solution.py:89
  98.8 18.0 %collective-permute-start.33 = (f32[4,48,512]{2,1,0:T(8,128)S(1)}, f32[4,48,512]{2,1,0:T(8,128)S(1)}, u32[]{:S(2)}, u32[]{:S(2)}) collective-permute-start(f32[4,48,512]{2,1,0:T(8,128)S(1)} %slice_add_fusion.3), channel_id=1, source_target_pairs={{0,2},{1,5},{2,0},{3,7},{4,6},{5,1},{6,4},{7,3},{8,10},{9,13},{10,... | collective-permute-start | bytes 1179656 | tf_op jit(solution)/shard_map/ppermute | solution.py:89
  113.9 7.8 %collective-permute-start.25 = (f32[4,48,512]{2,1,0:T(8,128)S(1)}, f32[4,48,512]{2,1,0:T(8,128)S(1)}, u32[]{:S(2)}, u32[]{:S(2)}) collective-permute-start(f32[4,48,512]{2,1,0:T(8,128)S(1)} %slice_add_fusion.6), channel_id=1, source_target_pairs={{0,2},{1,5},{2,0},{3,7},{4,6},{5,1},{6,4},{7,3},{8,10},{9,13},{10,... | collective-permute-start | bytes 1179656 | tf_op jit(solution)/shard_map/ppermute | solution.py:89
  116.7 58.1 %collective-permute-start.2 = (f32[1024,768]{1,0:T(8,128)S(1)}, f32[1024,768]{1,0:T(8,128)S(1)}, u32[]{:S(2)}, u32[]{:S(2)}) collective-permute-start(f32[1024,768]{1,0:T(8,128)S(1)} %fusion.91), channel_id=1, source_target_pairs={{0,1},{1,0},{2,3},{3,2},{4,5},{5,4},{6,7},{7,6},{8,9},{9,8},{10,11... | collective-permute-start | bytes 9437192 | tf_op jit(solution)/shard_map/ppermute | solution.py:54
  116.8 60.5 %collective-permute-start.1 = (f32[1024,768]{1,0:T(8,128)S(1)}, f32[1024,768]{1,0:T(8,128)S(1)}, u32[]{:S(2)}, u32[]{:S(2)}) collective-permute-start(f32[1024,768]{1,0:T(8,128)S(1)} %fusion.89), channel_id=1, source_target_pairs={{0,1},{1,0},{2,3},{3,2},{4,5},{5,4},{6,7},{7,6},{8,9},{9,8},{10,11... | collective-permute-start | bytes 9437192 | tf_op jit(solution)/shard_map/ppermute | solution.py:54
  121.8 5.7 %collective-permute-start.34 = (f32[2,48,512]{2,1,0:T(8,128)S(1)}, f32[2,48,512]{2,1,0:T(8,128)S(1)}, u32[]{:S(2)}, u32[]{:S(2)}) collective-permute-start(f32[2,48,512]{2,1,0:T(8,128)S(1)} %slice_add_fusion.13), channel_id=1, source_target_pairs={{0,4},{1,3},{2,6},{3,1},{4,0},{5,7},{6,2},{7,5},{8,12},{9,11},{10,... | collective-permute-start | bytes 589832 | tf_op jit(solution)/shard_map/ppermute | solution.py:89
  122.2 7.4 %collective-permute-start.26 = (f32[2,48,512]{2,1,0:T(8,128)S(1)}, f32[2,48,512]{2,1,0:T(8,128)S(1)}, u32[]{:S(2)}, u32[]{:S(2)}) collective-permute-start(f32[2,48,512]{2,1,0:T(8,128)S(1)} %slice_add_fusion.21), channel_id=1, source_target_pairs={{0,4},{1,3},{2,6},{3,1},{4,0},{5,7},{6,2},{7,5},{8,12},{9,11},{10,... | collective-permute-start | bytes 589832 | tf_op jit(solution)/shard_map/ppermute | solution.py:89
  125.2 13.6 %collective-permute-start.29 = (f32[4,48,1024]{2,1,0:T(8,128)S(1)}, f32[4,48,1024]{2,1,0:T(8,128)S(1)}, u32[]{:S(2)}, u32[]{:S(2)}) collective-permute-start(f32[4,48,1024]{2,1,0:T(8,128)S(1)} %slice_add_fusion), channel_id=1, source_target_pairs={{0,4},{1,3},{2,6},{3,1},{4,0},{5,7},{6,2},{7,5},{8,12},{9,11},{10,... | collective-permute-start | bytes 2359304 | tf_op jit(solution)/shard_map/ppermute | solution.py:89
  127.4 19.0 %collective-permute-start.21 = (f32[4,48,1024]{2,1,0:T(8,128)S(1)}, f32[4,48,1024]{2,1,0:T(8,128)S(1)}, u32[]{:S(2)}, u32[]{:S(2)}) collective-permute-start(f32[4,48,1024]{2,1,0:T(8,128)S(1)} %slice_add_fusion.1), channel_id=1, source_target_pairs={{0,4},{1,3},{2,6},{3,1},{4,0},{5,7},{6,2},{7,5},{8,12},{9,11},{10,... | collective-permute-start | bytes 2359304 | tf_op jit(solution)/shard_map/ppermute | solution.py:89
  129.5 5.6 %collective-permute-start.35 = (f32[1,48,512]{2,1,0:T(8,128)S(1)}, f32[1,48,512]{2,1,0:T(8,128)S(1)}, u32[]{:S(2)}, u32[]{:S(2)}) collective-permute-start(f32[1,48,512]{2,1,0:T(8,128)S(1)} %slice_add_fusion.39), channel_id=1, source_target_pairs={{0,16},{1,17},{2,18},{3,19},{4,20},{5,21},{6,22},{7,23},{8,24},{9,... | collective-permute-start | bytes 294920 | tf_op jit(solution)/shard_map/ppermute | solution.py:89
  135.1 14.0 %collective-permute-start.27 = (f32[1,48,512]{2,1,0:T(8,128)S(1)}, f32[1,48,512]{2,1,0:T(8,128)S(1)}, u32[]{:S(2)}, u32[]{:S(2)}) collective-permute-start(f32[1,48,512]{2,1,0:T(8,128)S(1)} %slice_add_fusion.45), channel_id=1, source_target_pairs={{0,16},{1,17},{2,18},{3,19},{4,20},{5,21},{6,22},{7,23},{8,24},{9,... | collective-permute-start | bytes 294920 | tf_op jit(solution)/shard_map/ppermute | solution.py:89
  139.8 10.9 %collective-permute-start.30 = (f32[2,48,1024]{2,1,0:T(8,128)S(1)}, f32[2,48,1024]{2,1,0:T(8,128)S(1)}, u32[]{:S(2)}, u32[]{:S(2)}) collective-permute-start(f32[2,48,1024]{2,1,0:T(8,128)S(1)} %slice_add_fusion.4), channel_id=1, source_target_pairs={{0,8},{1,9},{2,10},{3,11},{4,12},{5,13},{6,14},{7,15},{8,0},{9,1},... | collective-permute-start | bytes 1179656 | tf_op jit(solution)/shard_map/ppermute | solution.py:89
  147.5 14.5 %collective-permute-start.22 = (f32[2,48,1024]{2,1,0:T(8,128)S(1)}, f32[2,48,1024]{2,1,0:T(8,128)S(1)}, u32[]{:S(2)}, u32[]{:S(2)}) collective-permute-start(f32[2,48,1024]{2,1,0:T(8,128)S(1)} %slice_add_fusion.7), channel_id=1, source_target_pairs={{0,8},{1,9},{2,10},{3,11},{4,12},{5,13},{6,14},{7,15},{8,0},{9,1},... | collective-permute-start | bytes 1179656 | tf_op jit(solution)/shard_map/ppermute | solution.py:89
  151.7 12.7 %collective-permute-start.31 = (f32[1,48,1024]{2,1,0:T(8,128)S(1)}, f32[1,48,1024]{2,1,0:T(8,128)S(1)}, u32[]{:S(2)}, u32[]{:S(2)}) collective-permute-start(f32[1,48,1024]{2,1,0:T(8,128)S(1)} %slice_add_fusion.15), channel_id=1, source_target_pairs={{0,16},{1,17},{2,18},{3,19},{4,20},{5,21},{6,22},{7,23},{8,24},{9,... | collective-permute-start | bytes 589832 | tf_op jit(solution)/shard_map/ppermute | solution.py:89
  162.9 10.3 %collective-permute-start.23 = (f32[1,48,1024]{2,1,0:T(8,128)S(1)}, f32[1,48,1024]{2,1,0:T(8,128)S(1)}, u32[]{:S(2)}, u32[]{:S(2)}) collective-permute-start(f32[1,48,1024]{2,1,0:T(8,128)S(1)} %slice_add_fusion.23), channel_id=1, source_target_pairs={{0,16},{1,17},{2,18},{3,19},{4,20},{5,21},{6,22},{7,23},{8,24},{9,... | collective-permute-start | bytes 589832 | tf_op jit(solution)/shard_map/ppermute | solution.py:89
  237.2 20.7 %collective-permute-start.16 = (f32[8,48,384]{2,1,0:T(8,128)}, f32[8,48,384]{2,1,0:T(8,128)}, u32[]{:S(2)}, u32[]{:S(2)}) collective-permute-start(f32[8,48,384]{2,1,0:T(8,128)} %get-tuple-element.36), channel_id=1, source_target_pairs={{0,8},{1,9},{2,10},{3,11},{4,12},{5,13},{6,14},{7,15},{8,0},{9,1},... | collective-permute-start | bytes 1769480 | tf_op jit(solution)/shard_map/ppermute | solution.py:89
  242.9 21.9 %collective-permute-start.12 = (f32[8,48,384]{2,1,0:T(8,128)}, f32[8,48,384]{2,1,0:T(8,128)}, u32[]{:S(2)}, u32[]{:S(2)}) collective-permute-start(f32[8,48,384]{2,1,0:T(8,128)} %get-tuple-element.34), channel_id=1, source_target_pairs={{0,8},{1,9},{2,10},{3,11},{4,12},{5,13},{6,14},{7,15},{8,0},{9,1},... | collective-permute-start | bytes 1769480 | tf_op jit(solution)/shard_map/ppermute | solution.py:89
  250.6 16.5 %collective-permute-start.8 = (f32[8,48,768]{2,1,0:T(8,128)}, f32[8,48,768]{2,1,0:T(8,128)S(1)}, u32[]{:S(2)}, u32[]{:S(2)}) collective-permute-start(f32[8,48,768]{2,1,0:T(8,128)} %get-tuple-element.32), channel_id=1, source_target_pairs={{0,2},{1,5},{2,0},{3,7},{4,6},{5,1},{6,4},{7,3},{8,10},{9,13},{10,... | collective-permute-start | bytes 3538952 | tf_op jit(solution)/shard_map/ppermute | solution.py:89
  254.4 49.5 %collective-permute-start.3 = (f32[1024,768]{1,0:T(8,128)}, f32[1024,768]{1,0:T(8,128)}, u32[]{:S(2)}, u32[]{:S(2)}) collective-permute-start(f32[1024,768]{1,0:T(8,128)} %add_add_fusion), channel_id=1, source_target_pairs={{0,1},{1,0},{2,3},{3,2},{4,5},{5,4},{6,7},{7,6},{8,9},{9,8},{10,11... | collective-permute-start | bytes 9437192 | tf_op jit(solution)/shard_map/ppermute | solution.py:54
  258.9 13.1 %collective-permute-start.17 = (f32[4,48,384]{2,1,0:T(8,128)S(1)}, f32[4,48,384]{2,1,0:T(8,128)S(1)}, u32[]{:S(2)}, u32[]{:S(2)}) collective-permute-start(f32[4,48,384]{2,1,0:T(8,128)S(1)} %slice_add_fusion.9), channel_id=1, source_target_pairs={{0,2},{1,5},{2,0},{3,7},{4,6},{5,1},{6,4},{7,3},{8,10},{9,13},{10,... | collective-permute-start | bytes 884744 | tf_op jit(solution)/shard_map/ppermute | solution.py:89
  265.9 12.4 %collective-permute-start.13 = (f32[4,48,384]{2,1,0:T(8,128)S(1)}, f32[4,48,384]{2,1,0:T(8,128)S(1)}, u32[]{:S(2)}, u32[]{:S(2)}) collective-permute-start(f32[4,48,384]{2,1,0:T(8,128)S(1)} %slice_add_fusion.10), channel_id=1, source_target_pairs={{0,2},{1,5},{2,0},{3,7},{4,6},{5,1},{6,4},{7,3},{8,10},{9,13},{10,... | collective-permute-start | bytes 884744 | tf_op jit(solution)/shard_map/ppermute | solution.py:89
  267.1 14.8 %collective-permute-start.9 = (f32[4,48,768]{2,1,0:T(8,128)S(1)}, f32[4,48,768]{2,1,0:T(8,128)S(1)}, u32[]{:S(2)}, u32[]{:S(2)}) collective-permute-start(f32[4,48,768]{2,1,0:T(8,128)S(1)} %slice_add_fusion.2), channel_id=1, source_target_pairs={{0,4},{1,3},{2,6},{3,1},{4,0},{5,7},{6,2},{7,5},{8,12},{9,11},{10,... | collective-permute-start | bytes 1769480 | tf_op jit(solution)/shard_map/ppermute | solution.py:89
  272.9 7.6 %collective-permute-start.18 = (f32[2,48,384]{2,1,0:T(8,128)S(1)}, f32[2,48,384]{2,1,0:T(8,128)S(1)}, u32[]{:S(2)}, u32[]{:S(2)}) collective-permute-start(f32[2,48,384]{2,1,0:T(8,128)S(1)} %slice_add_fusion.29), channel_id=1, source_target_pairs={{0,4},{1,3},{2,6},{3,1},{4,0},{5,7},{6,2},{7,5},{8,12},{9,11},{10,... | collective-permute-start | bytes 442376 | tf_op jit(solution)/shard_map/ppermute | solution.py:89
  279.2 5.2 %collective-permute-start.14 = (f32[2,48,384]{2,1,0:T(8,128)S(1)}, f32[2,48,384]{2,1,0:T(8,128)S(1)}, u32[]{:S(2)}, u32[]{:S(2)}) collective-permute-start(f32[2,48,384]{2,1,0:T(8,128)S(1)} %slice_add_fusion.31), channel_id=1, source_target_pairs={{0,4},{1,3},{2,6},{3,1},{4,0},{5,7},{6,2},{7,5},{8,12},{9,11},{10,... | collective-permute-start | bytes 442376 | tf_op jit(solution)/shard_map/ppermute | solution.py:89
  281.4 6.8 %collective-permute-start.19 = (f32[1,48,384]{2,1,0:T(8,128)S(1)}, f32[1,48,384]{2,1,0:T(8,128)S(1)}, u32[]{:S(2)}, u32[]{:S(2)}) collective-permute-start(f32[1,48,384]{2,1,0:T(8,128)S(1)} %slice_add_fusion.51), channel_id=1, source_target_pairs={{0,16},{1,17},{2,18},{3,19},{4,20},{5,21},{6,22},{7,23},{8,24},{9,... | collective-permute-start | bytes 221192 | tf_op jit(solution)/shard_map/ppermute | solution.py:89
  282.0 12.9 %collective-permute-start.10 = (f32[2,48,768]{2,1,0:T(8,128)S(1)}, f32[2,48,768]{2,1,0:T(8,128)S(1)}, u32[]{:S(2)}, u32[]{:S(2)}) collective-permute-start(f32[2,48,768]{2,1,0:T(8,128)S(1)} %slice_add_fusion.11), channel_id=1, source_target_pairs={{0,8},{1,9},{2,10},{3,11},{4,12},{5,13},{6,14},{7,15},{8,0},{9,1},... | collective-permute-start | bytes 884744 | tf_op jit(solution)/shard_map/ppermute | solution.py:89
  285.3 9.7 %collective-permute-start.15 = (f32[1,48,384]{2,1,0:T(8,128)S(1)}, f32[1,48,384]{2,1,0:T(8,128)S(1)}, u32[]{:S(2)}, u32[]{:S(2)}) collective-permute-start(f32[1,48,384]{2,1,0:T(8,128)S(1)} %slice_add_fusion.57), channel_id=1, source_target_pairs={{0,16},{1,17},{2,18},{3,19},{4,20},{5,21},{6,22},{7,23},{8,24},{9,... | collective-permute-start | bytes 221192 | tf_op jit(solution)/shard_map/ppermute | solution.py:89
  294.9 8.9 %collective-permute-start.11 = (f32[1,48,768]{2,1,0:T(8,128)S(1)}, f32[1,48,768]{2,1,0:T(8,128)S(1)}, u32[]{:S(2)}, u32[]{:S(2)}) collective-permute-start(f32[1,48,768]{2,1,0:T(8,128)S(1)} %slice_add_fusion.33), channel_id=1, source_target_pairs={{0,16},{1,17},{2,18},{3,19},{4,20},{5,21},{6,22},{7,23},{8,24},{9,... | collective-permute-start | bytes 442376 | tf_op jit(solution)/shard_map/ppermute | solution.py:89
  (55 other events, 384.8 us)

commit v2 on v1

v2 whole, which is shorter than its diff:
```python
import math

import jax
import jax.numpy as jnp
from jax import lax
from jax.experimental import pallas as pl
from jax.experimental.pallas import tpu as pltpu
from jax.sharding import PartitionSpec as P

HD = 64
PAIR = 2 * HD
EPSILON = 1e-06
MASKED = -1000000000.0
SCALE = 1.0 / math.sqrt(HD)
CURVE = math.sqrt(2.0 / math.pi)
CUBIC = 0.044715
F32 = jnp.float32
BF16 = jnp.bfloat16


def product(left, right, over):
    return lax.dot_general(
        left, right, ((over[:1], over[1:]), ((), ())), preferred_element_type=F32
    )


def left_product(left, right):
    return product(left, right, (0, 0))


def unit_rows(values):
    centered = values - jnp.mean(values, axis=-1, keepdims=True)
    inv_std = lax.rsqrt(jnp.mean(centered * centered, axis=-1, keepdims=True) + EPSILON)
    return centered * inv_std, inv_std


def norm_back(grad_out, unit, inv_std, gain):
    grad_unit = grad_out * gain
    return inv_std * (
        grad_unit
        - jnp.mean(grad_unit, axis=-1, keepdims=True)
        - unit * jnp.mean(grad_unit * unit, axis=-1, keepdims=True)
    )


def column_sum(values):
    return jnp.sum(values, axis=0, keepdims=True)


def add_up(ref, value):
    @pl.when(pl.program_id(0) == 0)
    def _():
        ref[...] = jnp.zeros_like(ref)

    ref[...] += value


def lane_halves(width):
    lane = lax.broadcasted_iota(jnp.int32, (1, width), 1)
    low = (lane % PAIR < HD).astype(F32)
    return low, 1.0 - low


def attend_kernel(
    x_ref, seg_col, seg_row, gain, shift, wq, bq, wk, wv, bv, wo,
    normed_ref, qkv_ref, probs_ref, context_ref, out_ref,
):
    cols = wq.shape[1]
    unit, _ = unit_rows(x_ref[...])
    normed = (unit * gain[...] + shift[...]).astype(BF16)
    normed_ref[...] = normed
    low, high = lane_halves(cols)
    queries = (product(normed, wq[...], (1, 0)) + bq[...]) * SCALE
    keys = product(normed, wk[...], (1, 0)).astype(BF16)
    values = (product(normed, wv[...], (1, 0)) + bv[...]).astype(BF16)
    qkv_ref[:, :cols] = queries.astype(BF16)
    qkv_ref[:, cols : 2 * cols] = keys
    qkv_ref[:, 2 * cols :] = values
    split = ((queries * low).astype(BF16), (queries * high).astype(BF16))
    same = seg_col[0] == seg_row[0]
    first = lax.broadcasted_iota(jnp.int32, (1, PAIR), 1) < HD
    for pair in range(cols // PAIR):
        part = slice(pair * PAIR, (pair + 1) * PAIR)
        made = []
        for half in range(2):
            scores = product(keys[:, part], split[half][:, part], (1, 1))
            scores = jnp.where(same, scores, MASKED)
            expo = jnp.exp(scores - jnp.max(scores, axis=0, keepdims=True))
            probs = (expo * (1.0 / column_sum(expo))).astype(BF16)
            probs_ref[0, 2 * pair + half] = probs
            made.append(product(probs, values[:, part], (0, 0)))
        context_ref[:, part] = jnp.where(first, made[0], made[1]).astype(BF16)
    out_ref[...] = product(context_ref[...], wo[...], (1, 0))


def whole(array):
    zeros = (0,) * array.ndim
    return pl.BlockSpec(array.shape, lambda i: zeros, pipeline_mode=pl.Buffered(1))


def rows_of(length, width):
    return pl.BlockSpec((length, width), lambda i: (i, 0))


def cost(flops, moved, special=0):
    return pl.CostEstimate(flops=flops, bytes_accessed=moved, transcendentals=special)


def params():
    return pltpu.CompilerParams(vmem_limit_bytes=48 << 20)


def attend(x, segments, gain, shift, wq, bq, wk, wv, bv, wo):
    rows, length = segments.shape
    tokens, width = x.shape
    cols = wq.shape[1]
    heads = cols // HD
    made = lambda w, kind: jax.ShapeDtypeStruct((tokens, w), kind)
    return pl.pallas_call(
        attend_kernel,
        grid=(rows,),
        in_specs=[
            rows_of(length, width),
            pl.BlockSpec((1, length, 1), lambda i: (i, 0, 0)),
            pl.BlockSpec((1, 1, length), lambda i: (i, 0, 0)),
        ]
        + [whole(w) for w in (gain, shift, wq, bq, wk, wv, bv, wo)],
        out_specs=[
            rows_of(length, width),
            rows_of(length, 3 * cols),
            pl.BlockSpec((1, heads, length, length), lambda i: (i, 0, 0, 0)),
            rows_of(length, cols),
            rows_of(length, width),
        ],
        out_shape=[
            made(width, BF16),
            made(3 * cols, BF16),
            jax.ShapeDtypeStruct((rows, heads, length, length), BF16),
            made(cols, BF16),
            made(width, F32),
        ],
        cost_estimate=cost(
            8 * tokens * width * cols + 4 * tokens * length * cols,
            tokens * (10 * width + 8 * cols + 2 * heads * length) + 8 * width * cols,
            tokens * heads * length,
        ),
        compiler_params=params(),
    )(x, segments[:, :, None], segments[:, None, :], gain, shift, wq, bq, wk, wv, bv, wo)


def upper_kernel(
    x_ref, mine, other, bias, gain, shift, w_up, b_up,
    middle_ref, normed_ref, act_ref, slope_ref, *, step,
):
    middle = x_ref[...] + (mine[...] + other[...]) + bias[...]
    middle_ref[...] = middle
    unit, _ = unit_rows(middle)
    normed = (unit * gain[...] + shift[...]).astype(BF16)
    normed_ref[...] = normed
    for at in range(0, w_up.shape[1], step):
        part = slice(at, at + step)
        u = product(normed, w_up[:, part], (1, 0)) + b_up[:, part]
        square = u * u
        bend = jnp.tanh(u * (CURVE + (CURVE * CUBIC) * square))
        half = 0.5 + 0.5 * bend
        act = u * half
        act_ref[:, part] = act.astype(BF16)
        slope = half + act * (1.0 - bend) * (CURVE + (3.0 * CURVE * CUBIC) * square)
        slope_ref[:, part] = slope.astype(BF16)


def upper(x, mine, other, bias, gain, shift, w_up, b_up, length):
    tokens, width = x.shape
    hidden = w_up.shape[1]
    made = lambda w, kind: jax.ShapeDtypeStruct((tokens, w), kind)
    return pl.pallas_call(
        lambda *refs: upper_kernel(*refs, step=hidden // 6),
        grid=(tokens // length,),
        in_specs=[rows_of(length, width)] * 3
        + [whole(w) for w in (bias, gain, shift, w_up, b_up)],
        out_specs=[
            rows_of(length, width),
            rows_of(length, width),
            rows_of(length, hidden),
            rows_of(length, hidden),
        ],
        out_shape=[made(width, F32), made(width, BF16), made(hidden, BF16), made(hidden, BF16)],
        cost_estimate=cost(
            2 * tokens * width * hidden,
            tokens * (18 * width + 4 * hidden) + 2 * width * hidden,
            tokens * hidden,
        ),
        compiler_params=params(),
    )(x, mine, other, bias, gain, shift, w_up, b_up)


def hidden_kernel(
    top_ref, act_ref, slope_ref, w_down, w_up,
    grad_ref, down_ref, back_ref, bias_ref, *, step,
):
    sums = []
    for at in range(0, w_up.shape[1], step):
        part = slice(at, at + step)
        grad = product(top_ref[...], w_down[part, :], (1, 1)) * slope_ref[:, part].astype(F32)
        grad = grad.astype(BF16)
        grad_ref[:, part] = grad
        sums.append(column_sum(grad.astype(F32)))
    add_up(bias_ref, jnp.concatenate(sums, axis=1))
    back_ref[...] = product(grad_ref[...], w_up[...], (1, 1))
    down_ref[...] = product(act_ref[...], w_down[...], (1, 0))


def hidden_back(top, act, slope, w_down, w_up, length):
    tokens, width = top.shape
    hidden = w_up.shape[1]
    made = lambda w, kind: jax.ShapeDtypeStruct((tokens, w), kind)
    return pl.pallas_call(
        lambda *refs: hidden_kernel(*refs, step=hidden // 6),
        grid=(tokens // length,),
        in_specs=[rows_of(length, width), rows_of(length, hidden), rows_of(length, hidden)]
        + [whole(w) for w in (w_down, w_up)],
        out_specs=[
            rows_of(length, hidden),
            rows_of(length, width),
            rows_of(length, width),
            pl.BlockSpec((1, hidden), lambda i: (0, 0)),
        ],
        out_shape=[
            made(hidden, BF16),
            made(width, F32),
            made(width, F32),
            jax.ShapeDtypeStruct((1, hidden), F32),
        ],
        cost_estimate=cost(
            6 * tokens * width * hidden,
            tokens * (10 * width + 6 * hidden) + 4 * width * hidden,
        ),
        compiler_params=params(),
    )(top, act, slope, w_down, w_up)


def attend_back_kernel(
    top_ref, mine, other, middle_ref, gain, wo, qkv_ref, probs_ref, wq, wk, wv,
    grad_middle_ref, rounded_ref, grad_qkv_ref, back_ref,
    sum_gain, sum_shift, sum_out, sum_qkv,
):
    cols = wq.shape[1]
    unit, inv_std = unit_rows(middle_ref[...])
    grad_normed = mine[...] + other[...]
    add_up(sum_gain, column_sum(grad_normed * unit))
    add_up(sum_shift, column_sum(grad_normed))
    grad_middle = top_ref[...] + norm_back(grad_normed, unit, inv_std, gain[...])
    grad_middle_ref[...] = grad_middle
    add_up(sum_out, column_sum(grad_middle))
    rounded = grad_middle.astype(BF16)
    rounded_ref[...] = rounded
    grad_context = product(rounded, wo[...], (1, 1)).astype(BF16).astype(F32)
    low, high = lane_halves(cols)
    split = ((grad_context * low).astype(BF16), (grad_context * high).astype(BF16))
    first = lax.broadcasted_iota(jnp.int32, (1, PAIR), 1) < HD
    for pair in range(cols // PAIR):
        at = pair * PAIR
        query = qkv_ref[:, at : at + PAIR]
        key = qkv_ref[:, cols + at : cols + at + PAIR]
        value = qkv_ref[:, 2 * cols + at : 2 * cols + at + PAIR]
        to_query, to_key, to_value = [], [], []
        for half in range(2):
            grad_out = split[half][:, at : at + PAIR]
            probs = probs_ref[0, 2 * pair + half]
            wide = probs.astype(F32)
            grad_probs = product(value, grad_out, (1, 1))
            delta = column_sum(wide * grad_probs)
            grad_scores = (wide * (grad_probs - delta)).astype(BF16)
            to_value.append(product(probs, grad_out, (1, 0)))
            to_key.append(product(grad_scores, query, (1, 0)))
            to_query.append(product(grad_scores, key, (0, 0)))
        grad_query = jnp.where(first, to_query[0], to_query[1]) * SCALE
        grad_key = jnp.where(first, to_key[0], to_key[1])
        grad_value = to_value[0] + to_value[1]
        grad_qkv_ref[:, at : at + PAIR] = grad_query.astype(BF16)
        grad_qkv_ref[:, cols + at : cols + at + PAIR] = grad_key.astype(BF16)
        grad_qkv_ref[:, 2 * cols + at : 2 * cols + at + PAIR] = grad_value.astype(BF16)
    grads = grad_qkv_ref[...]
    add_up(sum_qkv, column_sum(grads.astype(F32)))
    back_ref[...] = (
        product(grads[:, :cols], wq[...], (1, 1))
        + product(grads[:, cols : 2 * cols], wk[...], (1, 1))
        + product(grads[:, 2 * cols :], wv[...], (1, 1))
    )


def attend_back(top, mine, other, middle, gain, wo, qkv, probs, wq, wk, wv):
    tokens, width = top.shape
    rows, heads, length, _ = probs.shape
    cols = wq.shape[1]
    made = lambda w, kind: jax.ShapeDtypeStruct((tokens, w), kind)
    line = lambda w: jax.ShapeDtypeStruct((1, w), F32)
    fixed = lambda w: pl.BlockSpec((1, w), lambda i: (0, 0))
    return pl.pallas_call(
        attend_back_kernel,
        grid=(rows,),
        in_specs=[rows_of(length, width)] * 4
        + [whole(gain), whole(wo), rows_of(length, 3 * cols)]
        + [pl.BlockSpec((1, heads, length, length), lambda i: (i, 0, 0, 0))]
        + [whole(w) for w in (wq, wk, wv)],
        out_specs=[
            rows_of(length, width),
            rows_of(length, width),
            rows_of(length, 3 * cols),
            rows_of(length, width),
            fixed(width),
            fixed(width),
            fixed(width),
            fixed(3 * cols),
        ],
        out_shape=[
            made(width, F32),
            made(width, BF16),
            made(3 * cols, BF16),
            made(width, F32),
            line(width),
            line(width),
            line(width),
            line(3 * cols),
        ],
        cost_estimate=cost(
            8 * tokens * width * cols + 8 * tokens * length * cols,
            tokens * (26 * width + 12 * cols + 2 * heads * length) + 8 * width * cols,
        ),
        compiler_params=params(),
    )(top, mine, other, middle, gain, wo, qkv, probs, wq, wk, wv)


def first_back_kernel(x_ref, mine, other, above, gain, out_ref, sum_gain, sum_shift):
    unit, inv_std = unit_rows(x_ref[...])
    grad_normed = mine[...] + other[...]
    add_up(sum_gain, column_sum(grad_normed * unit))
    add_up(sum_shift, column_sum(grad_normed))
    out_ref[...] = above[...] + norm_back(grad_normed, unit, inv_std, gain[...])


def first_back(x, mine, other, above, gain, length):
    tokens, width = x.shape
    line = jax.ShapeDtypeStruct((1, width), F32)
    fixed = pl.BlockSpec((1, width), lambda i: (0, 0))
    return pl.pallas_call(
        first_back_kernel,
        grid=(tokens // length,),
        in_specs=[rows_of(length, width)] * 4 + [whole(gain)],
        out_specs=[rows_of(length, width), fixed, fixed],
        out_shape=[jax.ShapeDtypeStruct((tokens, width), F32), line, line],
        cost_estimate=cost(20 * tokens * width, 20 * tokens * width),
        compiler_params=params(),
    )(x, mine, other, above, gain)


def from_partner(part):
    return lax.ppermute(part, "mp", [(0, 1), (1, 0)])


def orders_for(kind, bits):
    low, rest = [1 << b for b in range(min(bits, 2))], [1 << b for b in range(2, bits)]
    if kind == "near":
        return [low + rest, low[::-1] + rest]
    return [rest[:1] + low + rest[1:], rest[:1] + low[::-1] + rest[1:]]


def order_of_member(orders, member):
    return orders[member % 2]


def block_table(orders, bits):
    me = lax.axis_index("dp")
    count = 1 << bits
    masks = []
    for order in orders:
        masks.append(
            [
                sum(order[k] for k in range(bits) if r >> (bits - 1 - k) & 1)
                for r in range(count)
            ]
        )
    masks = jnp.asarray(masks, jnp.int32)
    return masks[lax.axis_index("mp") % 2] ^ me.astype(jnp.int32)


def exchange(array, orders, stage):
    dp, mp = lax.axis_size("dp"), lax.axis_size("mp")
    pairs = []
    for d in range(dp):
        for m in range(mp):
            pairs.append((d * mp + m, (d ^ order_of_member(orders, m)[stage]) * mp + m))
    return lax.ppermute(array, ("dp", "mp"), pairs)


def finish_scatter(send, keep, orders, bits):
    received = []
    for stage in range(bits):
        received.append(exchange(send, orders, stage))
        half = keep.shape[0] >> (stage + 1)
        if stage + 1 < bits:
            send = keep[half : 2 * half]
            for got in received:
                send = send + got[half : 2 * half]
    total = keep[0]
    for got in received:
        total = total + got[0]
    return total


def all_sum(vector, bits):
    orders = orders_for("near", bits)
    for stage in range(bits):
        vector = vector + exchange(vector, orders, stage)
    return vector


def grad_kernel(table, left_ref, right_ref, *refs):
    outs, acc = refs[:-1], refs[-1]
    acc[...] = lax.dot_general(
        left_ref[...],
        right_ref[...],
        (((0,), (0,)), ((), ())),
        preferred_element_type=jnp.float32,
    )
    send, keep = outs
    half, size = keep.shape[0], keep.shape[1]
    for r in range(half):
        at = pl.multiple_of(table[r] * size, 8)
        keep[r] = acc[pl.ds(at, size), :]
        at = pl.multiple_of(table[half + r] * size, 8)
        send[r] = acc[pl.ds(at, size), :]


def blocked_grad(table, left, right, start, columns, tile):
    tokens, width = left.shape
    count = table.shape[0]
    size = width // count
    shape = jax.ShapeDtypeStruct((count // 2, size, columns), jnp.float32)
    block = pl.BlockSpec((count // 2, size, tile), lambda i, t: (0, 0, i))
    first = start // tile
    return pl.pallas_call(
        grad_kernel,
        grid_spec=pltpu.PrefetchScalarGridSpec(
            num_scalar_prefetch=1,
            grid=(columns // tile,),
            in_specs=[
                pl.BlockSpec((tokens, width), lambda i, t: (0, 0)),
                pl.BlockSpec((tokens, tile), lambda i, t: (0, i + first)),
            ],
            out_specs=[block, block],
            scratch_shapes=[pltpu.VMEM((width, tile), jnp.float32)],
        ),
        out_shape=[shape, shape],
        cost_estimate=pl.CostEstimate(
            flops=2 * tokens * width * columns,
            bytes_accessed=2 * tokens * (width + columns) + 4 * width * columns,
            transcendentals=0,
        ),
        compiler_params=pltpu.CompilerParams(vmem_limit_bytes=40 << 20),
    )(table, left, right)


def scattered_grad(left, right, kind, start, columns, tile):
    dp = lax.axis_size("dp")
    bits = dp.bit_length() - 1
    size = left.shape[1] // dp
    if (1 << bits) != dp or size % 8 or bits < 3:
        part = left_product(left, right[:, start : start + columns])
        return lax.psum_scatter(part, "dp", scatter_dimension=0, tiled=True)
    orders = orders_for(kind, bits)
    table = block_table(orders, bits)
    send, keep = blocked_grad(table, left, right, start, columns, tile)
    return finish_scatter(send, keep, orders, bits)


def sum_small(parts):
    dp = lax.axis_size("dp")
    bits = dp.bit_length() - 1
    if (1 << bits) != dp:
        return lax.psum(parts, "dp")
    sizes = [part.shape[0] for part in parts]
    flat = jnp.concatenate(parts).reshape(-1, 128)
    flat = all_sum(flat, bits).reshape(-1)
    out, at = [], 0
    for size in sizes:
        out.append(flat[at : at + size])
        at += size
    return out


def on_device(
    inputs,
    segment_ids,
    ln1_gain,
    ln1_bias,
    w_query,
    b_query,
    w_key,
    w_value,
    b_value,
    w_output,
    b_output,
    ln2_gain,
    ln2_bias,
    w_up,
    b_up,
    w_down,
    b_down,
    cotangent,
):
    rows, length, width = inputs.shape
    cols = w_query.shape[1]
    tokens = rows * length
    hidden = w_up.shape[1]
    far = hidden // 3
    row = lambda vector: vector.reshape(1, -1)
    x = inputs.reshape(tokens, width)
    top = cotangent.reshape(tokens, width)
    normed, qkv, probs, context, out_mine = attend(
        x, segment_ids, row(ln1_gain), row(ln1_bias), w_query, row(b_query),
        w_key, w_value, row(b_value), w_output,
    )
    out_other = from_partner(out_mine)
    top_b = top.astype(BF16)
    middle, normed_two, act, slope = upper(
        x, out_mine, out_other, row(b_output), row(ln2_gain), row(ln2_bias), w_up, row(b_up), length
    )
    down_far = scattered_grad(top_b, act, "far", hidden - far, far, far)
    down_near = scattered_grad(top_b, act, "near", 0, hidden - far, far)
    grad_upper, down_mine, back_mine, sum_up = hidden_back(top_b, act, slope, w_down, w_up, length)
    back_other = from_partner(back_mine)
    down_other = from_partner(down_mine)
    up_far = scattered_grad(normed_two, grad_upper, "far", hidden - far, far, far)
    up_near = scattered_grad(normed_two, grad_upper, "near", 0, hidden - far, far)
    outcome = middle + (down_mine + down_other) + b_down
    (
        grad_middle, grad_middle_b, grad_qkv, first_mine,
        sum_gain_two, sum_shift_two, sum_out, sum_qkv,
    ) = attend_back(
        top, back_mine, back_other, middle, row(ln2_gain), w_output, qkv, probs,
        w_query, w_key, w_value,
    )
    first_other = from_partner(first_mine)
    out_value = scattered_grad(normed, grad_qkv, "far", 2 * cols, cols, cols)
    pair = scattered_grad(normed, grad_qkv, "near", 0, 2 * cols, cols)
    out_part = scattered_grad(grad_middle_b, context, "far", 0, cols, cols)
    grad_x, sum_gain_one, sum_shift_one = first_back(
        x, first_mine, first_other, grad_middle, row(ln1_gain), length
    )
    smalls = sum_small(
        (
            sum_gain_one[0],
            sum_shift_one[0],
            sum_qkv[0, :cols],
            sum_qkv[0, 2 * cols :],
            sum_out[0],
            sum_gain_two[0],
            sum_shift_two[0],
            sum_up[0],
            jnp.sum(top, axis=0),
        )
    )
    shape = inputs.shape
    return (
        outcome.reshape(shape),
        grad_x.reshape(shape),
        smalls[0],
        smalls[1],
        pair[:, :cols],
        smalls[2],
        pair[:, cols:],
        out_value,
        smalls[3],
        out_part.T,
        smalls[4],
        smalls[5],
        smalls[6],
        jnp.concatenate([up_near, up_far], axis=1),
        smalls[7],
        jnp.concatenate([down_near, down_far], axis=1).T,
        smalls[8],
    )


def solution(mesh):
    return jax.shard_map(
        on_device,
        mesh=mesh,
        in_specs=(
            P("dp", None, None),
            P("dp", None),
            P(),
            P(),
            P(None, "mp"),
            P("mp"),
            P(None, "mp"),
            P(None, "mp"),
            P("mp"),
            P("mp", None),
            P(),
            P(),
            P(),
            P(None, "mp"),
            P("mp"),
            P("mp", None),
            P(),
            P("dp", None, None),
        ),
        out_specs=(
            P("dp", None, None),
            P("dp", None, None),
            P(),
            P(),
            P("dp", "mp"),
            P("mp"),
            P("dp", "mp"),
            P("dp", "mp"),
            P("mp"),
            P("mp", "dp"),
            P(),
            P(),
            P(),
            P("dp", "mp"),
            P("mp"),
            P("mp", "dp"),
            P(),
        ),
        check_vma=False,
    )
```

time: 330 us -> 270 us (0.82)
  matrix products: 77.9 us -> 0 us
  Pallas kernels: 18.5 us -> 78.8 us
  other arithmetic: 65.3 us -> 35.4 us
  local copies, waits for them, and re-layouts: 33.8 us -> 16.2 us
  starting transfers between devices: 38.3 us -> 47.3 us
    dot_general x18 -> x0, matrix products: 77.9 us -> none  [the longest x6 22.8 us: matmul(): return jnp.dot(left, right, preferred_element_type=jnp.float32)]
    pallas_call x0 -> x5, Pallas kernels: none -> 60.7 us  [the longest x1 20 us: attend_back(): pl.pallas_call(attend_back_kernel, grid=(rows,), in_specs=[rows_of(length...]
    reduce_sum x9 -> x1, other arithmetic: 35.2 us -> 2.38 us  [on_device(): jnp.sum(top, axis=0)]
    convert_element_type x9 -> x0, local copies, waits for them, and re-layouts: 10.4 us -> none  [the longest x2 2.1 us: on_device(): context_b = context.reshape(tokens, local_cols).astype(jnp.bfloat16)]
    ppermute x32, starting transfers between devices: 37.3 us -> 46.8 us  [exchange(): return lax.ppermute(array, ('dp', 'mp'), pairs)]
    reshape x7 -> x8, local copies, waits for them, and re-layouts: 10.7 us -> 2.77 us  [on_device(): row = lambda vector: vector.reshape(1, -1)]
    add x21, other arithmetic: 15.4 us -> 20.6 us  [finish_scatter(): send = send + got[half:2 * half]]
    ppermute x32, waiting for transfers between devices: 91 us -> 86.2 us  [exchange(): return lax.ppermute(array, ('dp', 'mp'), pairs)]
  transfers between devices with their start and end apart: 36 -> 36, of which waited for: 21 -> 18; matrix products, arithmetic and copies ran while one was open for 20% -> 13% of each run, Pallas kernels for 4% -> 21%
where the time goes in v2:
time: 270 us; the launch traced here: 268 us
  waiting for transfers between devices  89.3 us (33%)
  Pallas kernels  78.8 us (29%)
  starting transfers between devices  47.3 us (18%)
  other arithmetic  35.4 us (13%)
  local copies, waits for them, and re-layouts  16.2 us (6%)
    ppermute x32, waiting for transfers between devices, exchange(): return lax.ppermute(array, ('dp', 'mp'), pairs)  86.2 us
    ppermute x32, starting transfers between devices, exchange(): return lax.ppermute(array, ('dp', 'mp'), pairs)  46.8 us
    add x21, other arithmetic, finish_scatter(): send = send + got[half:2 * half]  20.6 us
    pallas_call x1, Pallas kernels, attend_back(): pl.pallas_call(attend_back_kernel, grid=(rows,), in_specs=[rows_of(length...  20 us
    pallas_call x7, Pallas kernels, blocked_grad(): pl.pallas_call(grad_kernel, grid_spec=pltpu.PrefetchScalarGridSpec(num_sc...  18.1 us
    pallas_call x1, Pallas kernels, hidden_back(): pl.pallas_call(lambda *refs: hidden_kernel(*refs, step=hidden // 6), grid...  12.6 us
    pallas_call x1, Pallas kernels, attend(): pl.pallas_call(attend_kernel, grid=(rows,), in_specs=[rows_of(length, wid...  11 us
    pallas_call x1, Pallas kernels, upper(): pl.pallas_call(lambda *refs: upper_kernel(*refs, step=hidden // 6), grid=...  10.2 us
  transfers between devices with their start and end apart: 36, of which 18 were waited for; matrix products, arithmetic and copies ran while one was open for 13% of the time, Pallas kernels for 21%

profile of v2, /device:TPU:0, one launch (start us, length us, event | category | flops | bytes accessed | tf_op | source)
XLA Modules:
  0.0 268.3 jit_solution(15278621086546262433)
XLA Ops:
  9.3 11.0 %shard_map.368 = (bf16[1024,768]{1,0:T(8,128)(2,1)S(1)}, bf16[1024,1152]{1,0:T(8,128)(2,1)}, bf16[4,6,256,256]{3,2,1,0:T(8,128)(2,1)}, bf16[1024,384]{1,0:T(8,128)(2,1)S(1)}, f32[1024,768]{1,0:T(8,128)}) custom-call(f32[1024,768]{1,0:T(8,128)} %bitcast.50, s32[4,256,1]{2,1,0:T(8,128)S(1)} %copy.42.seg_col, s32[4,1,256]{2,1,0:T(1,128)S(1)} %broadcast_in_dim.8.seg_row, ...), custom_call_target="tpu_custom_call" | custom-call | flops 2818572288 | bytes 16515072 | tf_op jit(solution)/shard_map/pallas_call | solution.py:119
  21.8 2.4 fusion.14
  24.2 3.1 %collective-permute-done.refs_2_ = f32[1024,768]{1,0:T(8,128)} collective-permute-done((f32[1024,768]{1,0:T(8,128)}, f32[1024,768]{1,0:T(8,128)}, u32[]{:S(2)}, u32[]{:S(2)}) %collective-permute-start) | collective-permute-done | bytes 3145760 | tf_op jit(solution)/shard_map/ppermute | solution.py:358
  27.3 10.2 %shard_map.369 = (f32[1024,768]{1,0:T(8,128)}, bf16[1024,768]{1,0:T(8,128)(2,1)S(1)}, bf16[1024,1536]{1,0:T(8,128)(2,1)}, bf16[1024,1536]{1,0:T(8,128)(2,1)}) custom-call(f32[1024,768]{1,0:T(8,128)} %bitcast.51, f32[1024,768]{1,0:T(8,128)} %get-tuple-element.55.refs_1_, f32[1024,768]{1,0:T(8,128)} %collective-permute-done.refs_2_, ...), custom_call_target="tpu_custom_call" | custom-call | flops 2415919104 | bytes 22806528 | tf_op jit(solution)/shard_map/pallas_call | solution.py:176
  37.5 1.9 copy-done.1
  41.1 3.0 %collective-permute-start.32 = (f32[8,48,512]{2,1,0:T(8,128)S(1)}, f32[8,48,512]{2,1,0:T(8,128)S(1)}, u32[]{:S(2)}, u32[]{:S(2)}) collective-permute-start(f32[8,48,512]{2,1,0:T(8,128)S(1)} %get-tuple-element.92), channel_id=1, source_target_pairs={{0,8},{1,9},{2,10},{3,11},{4,12},{5,13},{6,14},{7,15},{8,0},{9,1},... | collective-permute-start | bytes 2359304 | tf_op jit(solution)/shard_map/ppermute | solution.py:393
  44.1 12.6 %shard_map.370 = (bf16[1024,1536]{1,0:T(8,128)(2,1)}, f32[1024,768]{1,0:T(8,128)}, f32[1024,768]{1,0:T(8,128)}, f32[1,1536]{1,0:T(1,128)S(1)}) custom-call(bf16[1024,768]{1,0:T(8,128)(2,1)S(1)} %get-tuple-element.96.refs_0_.left_ref, bf16[1024,1536]{1,0:T(8,128)(2,1)} %get-tuple-element.57.refs_1_.right_ref, bf16[1024,1536]{1,0:T(8,128)(2,1)} %get-tuple-element.58.refs_2_, ...), custom_call_target="tpu_custom_call" | custom-call | flops 7247757312 | bytes 22020096 | tf_op jit(solution)/shard_map/pallas_call | solution.py:217
  56.7 1.9 copy-done.3
  60.5 3.9 %shard_map.378 = (f32[8,48,1024]{2,1,0:T(8,128)}, f32[8,48,1024]{2,1,0:T(8,128)S(1)}) custom-call(s32[16]{0:T(128)S(1)} %get-tuple-element.108.table, bf16[1024,768]{1,0:T(8,128)(2,1)S(1)} %get-tuple-element.96.refs_0_.left_ref, bf16[1024,1536]{1,0:T(8,128)(2,1)S(1)} %copy-done.2), custom_call_target="tpu_custom_call" | custom-call | flops 1610612736 | bytes 6815744 | tf_op jit(solution)/shard_map/pallas_call | solution.py:442
  66.1 3.9 %shard_map.376 = (f32[8,48,1024]{2,1,0:T(8,128)}, f32[8,48,1024]{2,1,0:T(8,128)S(1)}) custom-call(s32[16]{0:T(128)S(1)} %get-tuple-element.108.table, bf16[1024,768]{1,0:T(8,128)(2,1)S(1)} %get-tuple-element.83.left_ref, bf16[1024,1536]{1,0:T(8,128)(2,1)S(1)} %copy-done.3), custom_call_target="tpu_custom_call" | custom-call | flops 1610612736 | bytes 6815744 | tf_op jit(solution)/shard_map/pallas_call | solution.py:442
  72.9 6.7 %collective-permute-done.24 = f32[8,48,512]{2,1,0:T(8,128)S(1)} collective-permute-done((f32[8,48,512]{2,1,0:T(8,128)S(1)}, f32[8,48,512]{2,1,0:T(8,128)S(1)}, u32[]{:S(2)}, u32[]{:S(2)}) %collective-permute-start.24) | collective-permute-done | bytes 786464 | tf_op jit(solution)/shard_map/ppermute | solution.py:393
  82.2 23.9 %collective-permute-done.33 = f32[4,48,512]{2,1,0:T(8,128)} collective-permute-done((f32[4,48,512]{2,1,0:T(8,128)}, f32[4,48,512]{2,1,0:T(8,128)}, u32[]{:S(2)}, u32[]{:S(2)}) %collective-permute-start.33) | collective-permute-done | bytes 393248 | tf_op jit(solution)/shard_map/ppermute | solution.py:393
  107.3 3.1 %collective-permute-done.25 = f32[4,48,512]{2,1,0:T(8,128)} collective-permute-done((f32[4,48,512]{2,1,0:T(8,128)}, f32[4,48,512]{2,1,0:T(8,128)}, u32[]{:S(2)}, u32[]{:S(2)}) %collective-permute-start.25) | collective-permute-done | bytes 393248 | tf_op jit(solution)/shard_map/ppermute | solution.py:393
  114.9 1.8 collective-permute-start.29
  119.3 2.9 %collective-permute-start.35 = (f32[1,48,512]{2,1,0:T(8,128)S(1)}, f32[1,48,512]{2,1,0:T(8,128)S(1)}, u32[]{:S(2)}, u32[]{:S(2)}) collective-permute-start(f32[1,48,512]{2,1,0:T(8,128)S(1)} %slice_add_fusion.39), channel_id=1, source_target_pairs={{0,16},{1,17},{2,18},{3,19},{4,20},{5,21},{6,22},{7,23},{8,24},{9,... | collective-permute-start | bytes 294920 | tf_op jit(solution)/shard_map/ppermute | solution.py:393
  124.9 2.9 %collective-permute-start.27 = (f32[1,48,512]{2,1,0:T(8,128)S(1)}, f32[1,48,512]{2,1,0:T(8,128)S(1)}, u32[]{:S(2)}, u32[]{:S(2)}) collective-permute-start(f32[1,48,512]{2,1,0:T(8,128)S(1)} %slice_add_fusion.45), channel_id=1, source_target_pairs={{0,16},{1,17},{2,18},{3,19},{4,20},{5,21},{6,22},{7,23},{8,24},{9,... | collective-permute-start | bytes 294920 | tf_op jit(solution)/shard_map/ppermute | solution.py:393
  130.0 4.5 %collective-permute-start.30 = (f32[2,48,1024]{2,1,0:T(8,128)S(1)}, f32[2,48,1024]{2,1,0:T(8,128)S(1)}, u32[]{:S(2)}, u32[]{:S(2)}) collective-permute-start(f32[2,48,1024]{2,1,0:T(8,128)S(1)} %slice_add_fusion.4), channel_id=1, source_target_pairs={{0,8},{1,9},{2,10},{3,11},{4,12},{5,13},{6,14},{7,15},{8,0},{9,1},... | collective-permute-start | bytes 1179656 | tf_op jit(solution)/shard_map/ppermute | solution.py:393
  139.7 5.6 %collective-permute-done.30 = f32[2,48,1024]{2,1,0:T(8,128)S(1)} collective-permute-done((f32[2,48,1024]{2,1,0:T(8,128)S(1)}, f32[2,48,1024]{2,1,0:T(8,128)S(1)}, u32[]{:S(2)}, u32[]{:S(2)}) %collective-permute-start.30) | collective-permute-done | bytes 393248 | tf_op jit(solution)/shard_map/ppermute | solution.py:393
  146.4 4.6 %collective-permute-done.22 = f32[2,48,1024]{2,1,0:T(8,128)S(1)} collective-permute-done((f32[2,48,1024]{2,1,0:T(8,128)S(1)}, f32[2,48,1024]{2,1,0:T(8,128)S(1)}, u32[]{:S(2)}, u32[]{:S(2)}) %collective-permute-start.22) | collective-permute-done | bytes 393248 | tf_op jit(solution)/shard_map/ppermute | solution.py:393
  153.7 7.5 %collective-permute-done.31 = f32[1,48,1024]{2,1,0:T(8,128)S(1)} collective-permute-done((f32[1,48,1024]{2,1,0:T(8,128)S(1)}, f32[1,48,1024]{2,1,0:T(8,128)S(1)}, u32[]{:S(2)}, u32[]{:S(2)}) %collective-permute-start.31) | collective-permute-done | bytes 196640 | tf_op jit(solution)/shard_map/ppermute | solution.py:393
  164.5 20.0 %shard_map.371 = (f32[1024,768]{1,0:T(8,128)}, bf16[1024,768]{1,0:T(8,128)(2,1)S(1)}, bf16[1024,1152]{1,0:T(8,128)(2,1)}, f32[1024,768]{1,0:T(8,128)}, f32[1,768...) custom-call(f32[1024,768]{1,0:T(8,128)} %bitcast.53, ...), custom_call_target="tpu_custom_call" | custom-call | flops 3221225472 | bytes 30670848 | tf_op jit(solution)/shard_map/pallas_call | solution.py:299
  187.1 3.8 %shard_map.373 = (f32[8,48,768]{2,1,0:T(8,128)}, f32[8,48,768]{2,1,0:T(8,128)S(1)}) custom-call(s32[16]{0:T(128)S(1)} %get-tuple-element.108.table, bf16[1024,768]{1,0:T(8,128)(2,1)S(1)} %get-tuple-element.73.left_ref, bf16[1024,1152]{1,0:T(8,128)(2,1)S(1)} %copy-done.4), custom_call_target="tpu_custom_call" | custom-call | flops 1207959552 | bytes 5505024 | tf_op jit(solution)/shard_map/pallas_call | solution.py:442
  192.6 2.1 collective-permute-start.12
  196.4 2.5 add_add_fusion
  198.9 4.3 %collective-permute-done.16 = f32[8,48,384]{2,1,0:T(8,128)S(1)} collective-permute-done((f32[8,48,384]{2,1,0:T(8,128)S(1)}, f32[8,48,384]{2,1,0:T(8,128)S(1)}, u32[]{:S(2)}, u32[]{:S(2)}) %collective-permute-start.16) | collective-permute-done | bytes 589856 | tf_op jit(solution)/shard_map/ppermute | solution.py:393
  205.1 10.4 %collective-permute-done.12 = f32[8,48,384]{2,1,0:T(8,128)S(1)} collective-permute-done((f32[8,48,384]{2,1,0:T(8,128)S(1)}, f32[8,48,384]{2,1,0:T(8,128)S(1)}, u32[]{:S(2)}, u32[]{:S(2)}) %collective-permute-start.12) | collective-permute-done | bytes 589856 | tf_op jit(solution)/shard_map/ppermute | solution.py:393
  220.8 4.1 %collective-permute-done.13 = f32[4,48,384]{2,1,0:T(8,128)} collective-permute-done((f32[4,48,384]{2,1,0:T(8,128)}, f32[4,48,384]{2,1,0:T(8,128)}, u32[]{:S(2)}, u32[]{:S(2)}) %collective-permute-start.13) | collective-permute-done | bytes 294944 | tf_op jit(solution)/shard_map/ppermute | solution.py:393
  234.0 2.2 collective-permute-done.19
  238.7 6.8 %shard_map.372 = (f32[1024,768]{1,0:T(8,128)}, f32[1,768]{1,0:T(1,128)S(1)}, f32[1,768]{1,0:T(1,128)S(1)}) custom-call(f32[1024,768]{1,0:T(8,128)S(1)} %bitcast.52, f32[1024,768]{1,0:T(8,128)} %get-tuple-element.63.mine, f32[1024,768]{1,0:T(8,128)} %collective-permute-done.3.other, f32[1024,768]{1,0:T(8,128)} %get-tuple-element.64.above, ...), custom_call_target="tpu_custom_call" | custom-call | flops 15728640 | bytes 15728640 | tf_op jit(solution)/shard_map/pallas_call | solution.py:346
  252.3 2.3 collective-permute-start.11
  255.6 4.6 %collective-permute-done.11 = f32[1,48,768]{2,1,0:T(8,128)S(1)} collective-permute-done((f32[1,48,768]{2,1,0:T(8,128)S(1)}, f32[1,48,768]{2,1,0:T(8,128)S(1)}, u32[]{:S(2)}, u32[]{:S(2)}) %collective-permute-start.11) | collective-permute-done | bytes 147488 | tf_op jit(solution)/shard_map/ppermute | solution.py:393
  262.8 3.7 %collective-permute-done.7 = f32[54,128]{1,0:T(8,128)S(1)} collective-permute-done((f32[54,128]{1,0:T(8,128)S(1)}, f32[54,128]{1,0:T(8,128)S(1)}, u32[]{:S(2)}, u32[]{:S(2)}) %collective-permute-start.7) | collective-permute-done | bytes 27680 | tf_op jit(solution)/shard_map/ppermute | solution.py:393
  (194 shorter events, 82.8 us)
Async XLA Ops:
  21.2 6.1 %collective-permute-start = (f32[1024,768]{1,0:T(8,128)}, f32[1024,768]{1,0:T(8,128)}, u32[]{:S(2)}, u32[]{:S(2)}) collective-permute-start(f32[1024,768]{1,0:T(8,128)} %get-tuple-element.55.refs_1_), channel_id=1, source_target_pairs={{0,1},{1,0},{2,3},{3,2},{4,5},{5,4},{6,7},{7,6},{8,9},{9,8},{10,11... | collective-permute-start | bytes 9437192 | tf_op jit(solution)/shard_map/ppermute | solution.py:358
  41.1 29.2 %collective-permute-start.32 = (f32[8,48,512]{2,1,0:T(8,128)S(1)}, f32[8,48,512]{2,1,0:T(8,128)S(1)}, u32[]{:S(2)}, u32[]{:S(2)}) collective-permute-start(f32[8,48,512]{2,1,0:T(8,128)S(1)} %get-tuple-element.92), channel_id=1, source_target_pairs={{0,8},{1,9},{2,10},{3,11},{4,12},{5,13},{6,14},{7,15},{8,0},{9,1},... | collective-permute-start | bytes 2359304 | tf_op jit(solution)/shard_map/ppermute | solution.py:393
  60.2 19.4 %collective-permute-start.24 = (f32[8,48,512]{2,1,0:T(8,128)S(1)}, f32[8,48,512]{2,1,0:T(8,128)S(1)}, u32[]{:S(2)}, u32[]{:S(2)}) collective-permute-start(f32[8,48,512]{2,1,0:T(8,128)S(1)} %get-tuple-element.88), channel_id=1, source_target_pairs={{0,8},{1,9},{2,10},{3,11},{4,12},{5,13},{6,14},{7,15},{8,0},{9,1},... | collective-permute-start | bytes 2359304 | tf_op jit(solution)/shard_map/ppermute | solution.py:393
  64.4 49.0 %collective-permute-start.28 = (f32[8,48,1024]{2,1,0:T(8,128)}, f32[8,48,1024]{2,1,0:T(8,128)}, u32[]{:S(2)}, u32[]{:S(2)}) collective-permute-start(f32[8,48,1024]{2,1,0:T(8,128)} %get-tuple-element.90), channel_id=1, source_target_pairs={{0,2},{1,5},{2,0},{3,7},{4,6},{5,1},{6,4},{7,3},{8,10},{9,13},{10,... | collective-permute-start | bytes 4718600 | tf_op jit(solution)/shard_map/ppermute | solution.py:393
  70.0 44.9 %collective-permute-start.20 = (f32[8,48,1024]{2,1,0:T(8,128)}, f32[8,48,1024]{2,1,0:T(8,128)}, u32[]{:S(2)}, u32[]{:S(2)}) collective-permute-start(f32[8,48,1024]{2,1,0:T(8,128)} %get-tuple-element.86), channel_id=1, source_target_pairs={{0,2},{1,5},{2,0},{3,7},{4,6},{5,1},{6,4},{7,3},{8,10},{9,13},{10,... | collective-permute-start | bytes 4718600 | tf_op jit(solution)/shard_map/ppermute | solution.py:393
  71.2 35.0 %collective-permute-start.33 = (f32[4,48,512]{2,1,0:T(8,128)}, f32[4,48,512]{2,1,0:T(8,128)}, u32[]{:S(2)}, u32[]{:S(2)}) collective-permute-start(f32[4,48,512]{2,1,0:T(8,128)} %slice_add_fusion.3), channel_id=1, source_target_pairs={{0,2},{1,5},{2,0},{3,7},{4,6},{5,1},{6,4},{7,3},{8,10},{9,13},{10,... | collective-permute-start | bytes 1179656 | tf_op jit(solution)/shard_map/ppermute | solution.py:393
  80.7 29.7 %collective-permute-start.25 = (f32[4,48,512]{2,1,0:T(8,128)}, f32[4,48,512]{2,1,0:T(8,128)}, u32[]{:S(2)}, u32[]{:S(2)}) collective-permute-start(f32[4,48,512]{2,1,0:T(8,128)} %slice_add_fusion.6), channel_id=1, source_target_pairs={{0,2},{1,5},{2,0},{3,7},{4,6},{5,1},{6,4},{7,3},{8,10},{9,13},{10,... | collective-permute-start | bytes 1179656 | tf_op jit(solution)/shard_map/ppermute | solution.py:393
  82.2 82.3 %collective-permute-start.2 = (f32[1024,768]{1,0:T(8,128)}, f32[1024,768]{1,0:T(8,128)}, u32[]{:S(2)}, u32[]{:S(2)}) collective-permute-start(f32[1024,768]{1,0:T(8,128)} %get-tuple-element.60.mine), channel_id=1, source_target_pairs={{0,1},{1,0},{2,3},{3,2},{4,5},{5,4},{6,7},{7,6},{8,9},{9,8},{10,11... | collective-permute-start | bytes 9437192 | tf_op jit(solution)/shard_map/ppermute | solution.py:358
  106.2 90.2 %collective-permute-start.1 = (f32[1024,768]{1,0:T(8,128)}, f32[1024,768]{1,0:T(8,128)S(1)}, u32[]{:S(2)}, u32[]{:S(2)}) collective-permute-start(f32[1024,768]{1,0:T(8,128)} %get-tuple-element.59), channel_id=1, source_target_pairs={{0,1},{1,0},{2,3},{3,2},{4,5},{5,4},{6,7},{7,6},{8,9},{9,8},{10,11... | collective-permute-start | bytes 9437192 | tf_op jit(solution)/shard_map/ppermute | solution.py:358
  110.4 7.6 %collective-permute-start.34 = (f32[2,48,512]{2,1,0:T(8,128)S(1)}, f32[2,48,512]{2,1,0:T(8,128)S(1)}, u32[]{:S(2)}, u32[]{:S(2)}) collective-permute-start(f32[2,48,512]{2,1,0:T(8,128)S(1)} %slice_add_fusion.13), channel_id=1, source_target_pairs={{0,4},{1,3},{2,6},{3,1},{4,0},{5,7},{6,2},{7,5},{8,12},{9,11},{10,... | collective-permute-start | bytes 589832 | tf_op jit(solution)/shard_map/ppermute | solution.py:393
  113.3 6.0 %collective-permute-start.26 = (f32[2,48,512]{2,1,0:T(8,128)S(1)}, f32[2,48,512]{2,1,0:T(8,128)S(1)}, u32[]{:S(2)}, u32[]{:S(2)}) collective-permute-start(f32[2,48,512]{2,1,0:T(8,128)S(1)} %slice_add_fusion.21), channel_id=1, source_target_pairs={{0,4},{1,3},{2,6},{3,1},{4,0},{5,7},{6,2},{7,5},{8,12},{9,11},{10,... | collective-permute-start | bytes 589832 | tf_op jit(solution)/shard_map/ppermute | solution.py:393
  114.9 14.0 %collective-permute-start.29 = (f32[4,48,1024]{2,1,0:T(8,128)S(1)}, f32[4,48,1024]{2,1,0:T(8,128)S(1)}, u32[]{:S(2)}, u32[]{:S(2)}) collective-permute-start(f32[4,48,1024]{2,1,0:T(8,128)S(1)} %slice_add_fusion), channel_id=1, source_target_pairs={{0,4},{1,3},{2,6},{3,1},{4,0},{5,7},{6,2},{7,5},{8,12},{9,11},{10,... | collective-permute-start | bytes 2359304 | tf_op jit(solution)/shard_map/ppermute | solution.py:393
  118.0 17.9 %collective-permute-start.21 = (f32[4,48,1024]{2,1,0:T(8,128)S(1)}, f32[4,48,1024]{2,1,0:T(8,128)S(1)}, u32[]{:S(2)}, u32[]{:S(2)}) collective-permute-start(f32[4,48,1024]{2,1,0:T(8,128)S(1)} %slice_add_fusion.1), channel_id=1, source_target_pairs={{0,4},{1,3},{2,6},{3,1},{4,0},{5,7},{6,2},{7,5},{8,12},{9,11},{10,... | collective-permute-start | bytes 2359304 | tf_op jit(solution)/shard_map/ppermute | solution.py:393
  119.3 5.6 %collective-permute-start.35 = (f32[1,48,512]{2,1,0:T(8,128)S(1)}, f32[1,48,512]{2,1,0:T(8,128)S(1)}, u32[]{:S(2)}, u32[]{:S(2)}) collective-permute-start(f32[1,48,512]{2,1,0:T(8,128)S(1)} %slice_add_fusion.39), channel_id=1, source_target_pairs={{0,16},{1,17},{2,18},{3,19},{4,20},{5,21},{6,22},{7,23},{8,24},{9,... | collective-permute-start | bytes 294920 | tf_op jit(solution)/shard_map/ppermute | solution.py:393
  124.9 13.7 %collective-permute-start.27 = (f32[1,48,512]{2,1,0:T(8,128)S(1)}, f32[1,48,512]{2,1,0:T(8,128)S(1)}, u32[]{:S(2)}, u32[]{:S(2)}) collective-permute-start(f32[1,48,512]{2,1,0:T(8,128)S(1)} %slice_add_fusion.45), channel_id=1, source_target_pairs={{0,16},{1,17},{2,18},{3,19},{4,20},{5,21},{6,22},{7,23},{8,24},{9,... | collective-permute-start | bytes 294920 | tf_op jit(solution)/shard_map/ppermute | solution.py:393
  130.0 15.3 %collective-permute-start.30 = (f32[2,48,1024]{2,1,0:T(8,128)S(1)}, f32[2,48,1024]{2,1,0:T(8,128)S(1)}, u32[]{:S(2)}, u32[]{:S(2)}) collective-permute-start(f32[2,48,1024]{2,1,0:T(8,128)S(1)} %slice_add_fusion.4), channel_id=1, source_target_pairs={{0,8},{1,9},{2,10},{3,11},{4,12},{5,13},{6,14},{7,15},{8,0},{9,1},... | collective-permute-start | bytes 1179656 | tf_op jit(solution)/shard_map/ppermute | solution.py:393
  137.0 14.0 %collective-permute-start.22 = (f32[2,48,1024]{2,1,0:T(8,128)S(1)}, f32[2,48,1024]{2,1,0:T(8,128)S(1)}, u32[]{:S(2)}, u32[]{:S(2)}) collective-permute-start(f32[2,48,1024]{2,1,0:T(8,128)S(1)} %slice_add_fusion.7), channel_id=1, source_target_pairs={{0,8},{1,9},{2,10},{3,11},{4,12},{5,13},{6,14},{7,15},{8,0},{9,1},... | collective-permute-start | bytes 1179656 | tf_op jit(solution)/shard_map/ppermute | solution.py:393
  146.3 14.9 %collective-permute-start.31 = (f32[1,48,1024]{2,1,0:T(8,128)S(1)}, f32[1,48,1024]{2,1,0:T(8,128)S(1)}, u32[]{:S(2)}, u32[]{:S(2)}) collective-permute-start(f32[1,48,1024]{2,1,0:T(8,128)S(1)} %slice_add_fusion.15), channel_id=1, source_target_pairs={{0,16},{1,17},{2,18},{3,19},{4,20},{5,21},{6,22},{7,23},{8,24},{9,... | collective-permute-start | bytes 589832 | tf_op jit(solution)/shard_map/ppermute | solution.py:393
  152.0 11.4 %collective-permute-start.23 = (f32[1,48,1024]{2,1,0:T(8,128)S(1)}, f32[1,48,1024]{2,1,0:T(8,128)S(1)}, u32[]{:S(2)}, u32[]{:S(2)}) collective-permute-start(f32[1,48,1024]{2,1,0:T(8,128)S(1)} %slice_add_fusion.23), channel_id=1, source_target_pairs={{0,16},{1,17},{2,18},{3,19},{4,20},{5,21},{6,22},{7,23},{8,24},{9,... | collective-permute-start | bytes 589832 | tf_op jit(solution)/shard_map/ppermute | solution.py:393
  184.6 54.2 %collective-permute-start.3 = (f32[1024,768]{1,0:T(8,128)}, f32[1024,768]{1,0:T(8,128)}, u32[]{:S(2)}, u32[]{:S(2)}) collective-permute-start(f32[1024,768]{1,0:T(8,128)} %get-tuple-element.63.mine), channel_id=1, source_target_pairs={{0,1},{1,0},{2,3},{3,2},{4,5},{5,4},{6,7},{7,6},{8,9},{9,8},{10,11... | collective-permute-start | bytes 9437192 | tf_op jit(solution)/shard_map/ppermute | solution.py:358
  187.0 16.2 %collective-permute-start.16 = (f32[8,48,384]{2,1,0:T(8,128)S(1)}, f32[8,48,384]{2,1,0:T(8,128)S(1)}, u32[]{:S(2)}, u32[]{:S(2)}) collective-permute-start(f32[8,48,384]{2,1,0:T(8,128)S(1)} %get-tuple-element.82), channel_id=1, source_target_pairs={{0,8},{1,9},{2,10},{3,11},{4,12},{5,13},{6,14},{7,15},{8,0},{9,1},... | collective-permute-start | bytes 1769480 | tf_op jit(solution)/shard_map/ppermute | solution.py:393
  192.6 22.9 %collective-permute-start.12 = (f32[8,48,384]{2,1,0:T(8,128)S(1)}, f32[8,48,384]{2,1,0:T(8,128)S(1)}, u32[]{:S(2)}, u32[]{:S(2)}) collective-permute-start(f32[8,48,384]{2,1,0:T(8,128)S(1)} %get-tuple-element.78), channel_id=1, source_target_pairs={{0,8},{1,9},{2,10},{3,11},{4,12},{5,13},{6,14},{7,15},{8,0},{9,1},... | collective-permute-start | bytes 1769480 | tf_op jit(solution)/shard_map/ppermute | solution.py:393
  194.6 32.9 %collective-permute-start.8 = (f32[8,48,768]{2,1,0:T(8,128)}, f32[8,48,768]{2,1,0:T(8,128)S(1)}, u32[]{:S(2)}, u32[]{:S(2)}) collective-permute-start(f32[8,48,768]{2,1,0:T(8,128)} %get-tuple-element.76), channel_id=1, source_target_pairs={{0,2},{1,5},{2,0},{3,7},{4,6},{5,1},{6,4},{7,3},{8,10},{9,13},{10,... | collective-permute-start | bytes 3538952 | tf_op jit(solution)/shard_map/ppermute | solution.py:393
  203.3 14.9 %collective-permute-start.17 = (f32[4,48,384]{2,1,0:T(8,128)S(1)}, f32[4,48,384]{2,1,0:T(8,128)}, u32[]{:S(2)}, u32[]{:S(2)}) collective-permute-start(f32[4,48,384]{2,1,0:T(8,128)S(1)} %slice_add_fusion.9), channel_id=1, source_target_pairs={{0,2},{1,5},{2,0},{3,7},{4,6},{5,1},{6,4},{7,3},{8,10},{9,13},{10,... | collective-permute-start | bytes 884744 | tf_op jit(solution)/shard_map/ppermute | solution.py:393
  216.3 8.6 %collective-permute-start.13 = (f32[4,48,384]{2,1,0:T(8,128)}, f32[4,48,384]{2,1,0:T(8,128)}, u32[]{:S(2)}, u32[]{:S(2)}) collective-permute-start(f32[4,48,384]{2,1,0:T(8,128)} %slice_add_fusion.10), channel_id=1, source_target_pairs={{0,2},{1,5},{2,0},{3,7},{4,6},{5,1},{6,4},{7,3},{8,10},{9,13},{10,... | collective-permute-start | bytes 884744 | tf_op jit(solution)/shard_map/ppermute | solution.py:393
  219.2 9.0 %collective-permute-start.18 = (f32[2,48,384]{2,1,0:T(8,128)S(1)}, f32[2,48,384]{2,1,0:T(8,128)S(1)}, u32[]{:S(2)}, u32[]{:S(2)}) collective-permute-start(f32[2,48,384]{2,1,0:T(8,128)S(1)} %slice_add_fusion.29), channel_id=1, source_target_pairs={{0,4},{1,3},{2,6},{3,1},{4,0},{5,7},{6,2},{7,5},{8,12},{9,11},{10,... | collective-permute-start | bytes 442376 | tf_op jit(solution)/shard_map/ppermute | solution.py:393
  227.6 10.2 %collective-permute-start.9 = (f32[4,48,768]{2,1,0:T(8,128)S(1)}, f32[4,48,768]{2,1,0:T(8,128)S(1)}, u32[]{:S(2)}, u32[]{:S(2)}) collective-permute-start(f32[4,48,768]{2,1,0:T(8,128)S(1)} %slice_add_fusion.2), channel_id=1, source_target_pairs={{0,4},{1,3},{2,6},{3,1},{4,0},{5,7},{6,2},{7,5},{8,12},{9,11},{10,... | collective-permute-start | bytes 1769480 | tf_op jit(solution)/shard_map/ppermute | solution.py:393
  229.5 6.8 %collective-permute-start.19 = (f32[1,48,384]{2,1,0:T(8,128)S(1)}, f32[1,48,384]{2,1,0:T(8,128)S(1)}, u32[]{:S(2)}, u32[]{:S(2)}) collective-permute-start(f32[1,48,384]{2,1,0:T(8,128)S(1)} %slice_add_fusion.51), channel_id=1, source_target_pairs={{0,16},{1,17},{2,18},{3,19},{4,20},{5,21},{6,22},{7,23},{8,24},{9,... | collective-permute-start | bytes 221192 | tf_op jit(solution)/shard_map/ppermute | solution.py:393
  232.7 14.8 %collective-permute-start.15 = (f32[1,48,384]{2,1,0:T(8,128)}, f32[1,48,384]{2,1,0:T(8,128)}, u32[]{:S(2)}, u32[]{:S(2)}) collective-permute-start(f32[1,48,384]{2,1,0:T(8,128)} %slice_add_fusion.57), channel_id=1, source_target_pairs={{0,16},{1,17},{2,18},{3,19},{4,20},{5,21},{6,22},{7,23},{8,24},{9,... | collective-permute-start | bytes 221192 | tf_op jit(solution)/shard_map/ppermute | solution.py:393
  238.7 12.5 %collective-permute-start.10 = (f32[2,48,768]{2,1,0:T(8,128)}, f32[2,48,768]{2,1,0:T(8,128)S(1)}, u32[]{:S(2)}, u32[]{:S(2)}) collective-permute-start(f32[2,48,768]{2,1,0:T(8,128)} %slice_add_fusion.11), channel_id=1, source_target_pairs={{0,8},{1,9},{2,10},{3,11},{4,12},{5,13},{6,14},{7,15},{8,0},{9,1},... | collective-permute-start | bytes 884744 | tf_op jit(solution)/shard_map/ppermute | solution.py:393
  252.3 8.0 %collective-permute-start.11 = (f32[1,48,768]{2,1,0:T(8,128)S(1)}, f32[1,48,768]{2,1,0:T(8,128)S(1)}, u32[]{:S(2)}, u32[]{:S(2)}) collective-permute-start(f32[1,48,768]{2,1,0:T(8,128)S(1)} %slice_add_fusion.33), channel_id=1, source_target_pairs={{0,16},{1,17},{2,18},{3,19},{4,20},{5,21},{6,22},{7,23},{8,24},{9,... | collective-permute-start | bytes 442376 | tf_op jit(solution)/shard_map/ppermute | solution.py:393
  254.5 6.8 %collective-permute-start.6 = (f32[54,128]{1,0:T(8,128)S(1)}, f32[54,128]{1,0:T(8,128)S(1)}, u32[]{:S(2)}, u32[]{:S(2)}) collective-permute-start(f32[54,128]{1,0:T(8,128)S(1)} %fusion.16), channel_id=1, source_target_pairs={{0,8},{1,9},{2,10},{3,11},{4,12},{5,13},{6,14},{7,15},{8,0},{9,1},... | collective-permute-start | bytes 82952 | tf_op jit(solution)/shard_map/ppermute | solution.py:393
  (41 other events, 362.7 us)

commit v3 on v2

--- a/solution.py
+++ b/solution.py
@@ -14,6 +14,7 @@
 SCALE = 1.0 / math.sqrt(HD)
 CURVE = math.sqrt(2.0 / math.pi)
 CUBIC = 0.044715
+WEIGHT = 60
 F32 = jnp.float32
 BF16 = jnp.bfloat16
 
@@ -47,6 +48,10 @@
     return jnp.sum(values, axis=0, keepdims=True)
 
 
+def line(ref):
+    return jnp.concatenate([ref[r : r + 1, :] for r in range(ref.shape[0])], axis=1)
+
+
 def add_up(ref, value):
     @pl.when(pl.program_id(0) == 0)
     def _():
@@ -62,22 +67,25 @@
 
 
 def attend_kernel(
-    x_ref, seg_col, seg_row, gain, shift, wq, bq, wk, wv, bv, wo,
-    normed_ref, qkv_ref, probs_ref, context_ref, out_ref,
+    seg_ref, gain, shift, wq, bq, wk, wv, bv, wo, x_ref, *refs, first_row
 ):
+    normed_ref, qkv_ref, probs_ref, context_ref, out_ref = refs[-5:]
     cols = wq.shape[1]
     unit, _ = unit_rows(x_ref[...])
-    normed = (unit * gain[...] + shift[...]).astype(BF16)
+    normed = (unit * line(gain) + line(shift)).astype(BF16)
     normed_ref[...] = normed
     low, high = lane_halves(cols)
-    queries = (product(normed, wq[...], (1, 0)) + bq[...]) * SCALE
+    queries = (product(normed, wq[...], (1, 0)) + line(bq)) * SCALE
     keys = product(normed, wk[...], (1, 0)).astype(BF16)
-    values = (product(normed, wv[...], (1, 0)) + bv[...]).astype(BF16)
+    values = (product(normed, wv[...], (1, 0)) + line(bv)).astype(BF16)
     qkv_ref[:, :cols] = queries.astype(BF16)
     qkv_ref[:, cols : 2 * cols] = keys
     qkv_ref[:, 2 * cols :] = values
     split = ((queries * low).astype(BF16), (queries * high).astype(BF16))
-    same = seg_col[0] == seg_row[0]
+    seg_row = seg_ref[pl.ds(pl.program_id(0) + first_row, 1), :].astype(F32)
+    length = seg_row.shape[1]
+    seg_col = jnp.broadcast_to(seg_row, (128, length)).T
+    same = jnp.concatenate([seg_col] * (length // 128), axis=1) == seg_row
     first = lax.broadcasted_iota(jnp.int32, (1, PAIR), 1) < HD
     for pair in range(cols // PAIR):
         part = slice(pair * PAIR, (pair + 1) * PAIR)
@@ -103,63 +111,67 @@
 
 
 def cost(flops, moved, special=0):
-    return pl.CostEstimate(flops=flops, bytes_accessed=moved, transcendentals=special)
-
-
-def params():
-    return pltpu.CompilerParams(vmem_limit_bytes=48 << 20)
-
-
-def attend(x, segments, gain, shift, wq, bq, wk, wv, bv, wo):
+    return pl.CostEstimate(
+        flops=WEIGHT * flops, bytes_accessed=WEIGHT * moved, transcendentals=special
+    )
+
+
+def params(limit=26 << 20):
+    return pltpu.CompilerParams(vmem_limit_bytes=limit)
+
+
+def attend(x, segments, gain, shift, wq, bq, wk, wv, bv, wo, first_row, count, made):
     rows, length = segments.shape
     tokens, width = x.shape
     cols = wq.shape[1]
     heads = cols // HD
-    made = lambda w, kind: jax.ShapeDtypeStruct((tokens, w), kind)
+    at = lambda w: pl.BlockSpec((length, w), lambda i: (i + first_row, 0))
+    shape = lambda w, kind: jax.ShapeDtypeStruct((tokens, w), kind)
+    fixed = (segments, gain, shift, wq, bq, wk, wv, bv, wo)
+    done = tokens * count // rows
     return pl.pallas_call(
-        attend_kernel,
-        grid=(rows,),
-        in_specs=[
-            rows_of(length, width),
-            pl.BlockSpec((1, length, 1), lambda i: (i, 0, 0)),
-            pl.BlockSpec((1, 1, length), lambda i: (i, 0, 0)),
-        ]
-        + [whole(w) for w in (gain, shift, wq, bq, wk, wv, bv, wo)],
+        lambda *refs: attend_kernel(*refs, first_row=first_row),
+        grid=(count,),
+        in_specs=[whole(w) for w in fixed]
+        + [at(width)]
+        + [pl.BlockSpec(memory_space=pl.ANY)] * len(made),
         out_specs=[
-            rows_of(length, width),
-            rows_of(length, 3 * cols),
-            pl.BlockSpec((1, heads, length, length), lambda i: (i, 0, 0, 0)),
-            rows_of(length, cols),
+            at(width),
+            at(3 * cols),
+            pl.BlockSpec((1, heads, length, length), lambda i: (i + first_row, 0, 0, 0)),
+            at(cols),
             rows_of(length, width),
         ],
         out_shape=[
-            made(width, BF16),
-            made(3 * cols, BF16),
+            shape(width, BF16),
+            shape(3 * cols, BF16),
             jax.ShapeDtypeStruct((rows, heads, length, length), BF16),
-            made(cols, BF16),
-            made(width, F32),
+            shape(cols, BF16),
+            jax.ShapeDtypeStruct((count * length, width), F32),
         ],
+        input_output_aliases={len(fixed) + 1 + i: i for i in range(len(made))},
         cost_estimate=cost(
-            8 * tokens * width * cols + 4 * tokens * length * cols,
-            tokens * (10 * width + 8 * cols + 2 * heads * length) + 8 * width * cols,
-            tokens * heads * length,
-        ),
-        compiler_params=params(),
-    )(x, segments[:, :, None], segments[:, None, :], gain, shift, wq, bq, wk, wv, bv, wo)
+            8 * done * width * cols + 4 * done * length * cols,
+            done * (10 * width + 8 * cols + 2 * heads * length) + 8 * width * cols,
+            done * heads * length,
+        ),
+        compiler_params=params(63 << 20),
+    )(*fixed, x, *made)
 
 
 def upper_kernel(
-    x_ref, mine, other, bias, gain, shift, w_up, b_up,
-    middle_ref, normed_ref, act_ref, slope_ref, *, step,
+    x_ref, mine, other, bias, gain, shift, w_up, b_up, *refs, step
 ):
-    middle = x_ref[...] + (mine[...] + other[...]) + bias[...]
+    middle_ref, normed_ref, act_ref, slope_ref = refs[-4:]
+    bias_up = line(b_up)
+    middle = x_ref[...] + (mine[...] + other[...]) + line(bias)
     middle_ref[...] = middle
     unit, _ = unit_rows(middle)
-    normed = (unit * gain[...] + shift[...]).astype(BF16)
+    normed = (unit * line(gain) + line(shift)).astype(BF16)
     normed_ref[...] = normed
     for at in range(0, w_up.shape[1], step):
         part = slice(at, at + step)
-        u = product(normed, w_up[:, part], (1, 0)) + b_up[:, part]
+        u = product(normed, w_up[:, part], (1, 0)) + bias_up[:, part]
         square = u * u
         bend = jnp.tanh(u * (CURVE + (CURVE * CUBIC) * square))
         half = 0.5 + 0.5 * bend
@@ -169,29 +181,29 @@
         slope_ref[:, part] = slope.astype(BF16)
 
 
-def upper(x, mine, other, bias, gain, shift, w_up, b_up, length):
+def upper(x, mine, other, bias, gain, shift, w_up, b_up, length, first_row, made):
     tokens, width = x.shape
     hidden = w_up.shape[1]
-    made = lambda w, kind: jax.ShapeDtypeStruct((tokens, w), kind)
+    count = mine.shape[0] // length
+    at = lambda w: pl.BlockSpec((length, w), lambda i: (i + first_row, 0))
+    shape = lambda w, kind: jax.ShapeDtypeStruct((tokens, w), kind)
+    fixed = (bias, gain, shift, w_up, b_up)
     return pl.pallas_call(
         lambda *refs: upper_kernel(*refs, step=hidden // 6),
-        grid=(tokens // length,),
-        in_specs=[rows_of(length, width)] * 3
-        + [whole(w) for w in (bias, gain, shift, w_up, b_up)],
-        out_specs=[
-            rows_of(length, width),
-            rows_of(length, width),
-            rows_of(length, hidden),
-            rows_of(length, hidden),
-        ],
-        out_shape=[made(width, F32), made(width, BF16), made(hidden, BF16), made(hidden, BF16)],
+        grid=(count,),
+        in_specs=[at(width), rows_of(length, width), rows_of(length, width)]
+        + [whole(w) for w in fixed]
+        + [pl.BlockSpec(memory_space=pl.ANY)] * len(made),
+        out_specs=[at(width), at(width), at(hidden), at(hidden)],
+        out_shape=[shape(width, F32), shape(width, BF16), shape(hidden, BF16), shape(hidden, BF16)],
+        input_output_aliases={3 + len(fixed) + i: i for i in range(len(made))},
         cost_estimate=cost(
-            2 * tokens * width * hidden,
-            tokens * (18 * width + 4 * hidden) + 2 * width * hidden,
-            tokens * hidden,
+            2 * count * length * width * hidden,
+            count * length * (18 * width + 4 * hidden) + 2 * width * hidden,
+            count * length * hidden,
         ),
         compiler_params=params(),
-    )(x, mine, other, bias, gain, shift, w_up, b_up)
+    )(x, mine, other, *fixed, *made)
 
 
 def hidden_kernel(
@@ -249,7 +261,7 @@
     grad_normed = mine[...] + other[...]
     add_up(sum_gain, column_sum(grad_normed * unit))
     add_up(sum_shift, column_sum(grad_normed))
-    grad_middle = top_ref[...] + norm_back(grad_normed, unit, inv_std, gain[...])
+    grad_middle = top_ref[...] + norm_back(grad_normed, unit, inv_std, line(gain))
     grad_middle_ref[...] = grad_middle
     add_up(sum_out, column_sum(grad_middle))
     rounded = grad_middle.astype(BF16)
@@ -331,27 +343,61 @@
     )(top, mine, other, middle, gain, wo, qkv, probs, wq, wk, wv)
 
 
-def first_back_kernel(x_ref, mine, other, above, gain, out_ref, sum_gain, sum_shift):
+def first_back_kernel(
+    x_ref, mine, other, above, gain, qkv_sum, out_sum, gain_two, shift_two, up_sum, top_sum,
+    out_ref, smalls_ref, sum_gain, sum_shift,
+):
     unit, inv_std = unit_rows(x_ref[...])
     grad_normed = mine[...] + other[...]
     add_up(sum_gain, column_sum(grad_normed * unit))
     add_up(sum_shift, column_sum(grad_normed))
-    out_ref[...] = above[...] + norm_back(grad_normed, unit, inv_std, gain[...])
-
-
-def first_back(x, mine, other, above, gain, length):
+    out_ref[...] = above[...] + norm_back(grad_normed, unit, inv_std, line(gain))
+
+    @pl.when(pl.program_id(0) == pl.num_programs(0) - 1)
+    def _():
+        smalls_ref[...] = jnp.zeros_like(smalls_ref)
+        cols = qkv_sum.shape[1] // 3
+        to = 0
+        for ref, start, size in (
+            (sum_gain, 0, sum_gain.shape[1]),
+            (sum_shift, 0, sum_shift.shape[1]),
+            (qkv_sum, 0, cols),
+            (qkv_sum, 2 * cols, cols),
+            (out_sum, 0, out_sum.shape[1]),
+            (gain_two, 0, gain_two.shape[1]),
+            (shift_two, 0, shift_two.shape[1]),
+            (up_sum, 0, up_sum.shape[1]),
+            (top_sum, 0, top_sum.shape[1]),
+        ):
+            for r in range(size // 128):
+                at = start + 128 * r
+                smalls_ref[to + r : to + r + 1, :] = ref[:, at : at + 128]
+            to += padded_rows(size)
+
+
+def padded_rows(size):
+    return -(-size // 1024) * 8
+
+
+def first_back(x, mine, other, above, gain, sums, length):
     tokens, width = x.shape
-    line = jax.ShapeDtypeStruct((1, width), F32)
-    fixed = pl.BlockSpec((1, width), lambda i: (0, 0))
-    return pl.pallas_call(
+    cols = sums[0].shape[1] // 3
+    sizes = [width, width, cols, cols] + [array.shape[1] for array in sums[1:]]
+    shape = (sum(padded_rows(size) for size in sizes), 128)
+    grad_x, smalls = pl.pallas_call(
         first_back_kernel,
         grid=(tokens // length,),
-        in_specs=[rows_of(length, width)] * 4 + [whole(gain)],
-        out_specs=[rows_of(length, width), fixed, fixed],
-        out_shape=[jax.ShapeDtypeStruct((tokens, width), F32), line, line],
+        in_specs=[rows_of(length, width)] * 4 + [whole(w) for w in (gain, *sums)],
+        out_specs=[rows_of(length, width), pl.BlockSpec(shape, lambda i: (0, 0))],
+        out_shape=[
+            jax.ShapeDtypeStruct((tokens, width), F32),
+            jax.ShapeDtypeStruct(shape, F32),
+        ],
+        scratch_shapes=[pltpu.VMEM((1, width), F32)] * 2,
         cost_estimate=cost(20 * tokens * width, 20 * tokens * width),
         compiler_params=params(),
-    )(x, mine, other, above, gain)
+    )(x, mine, other, above, gain, *sums)
+    return grad_x, smalls, sizes
 
 
 def from_partner(part):
@@ -393,25 +439,52 @@
     return lax.ppermute(array, ("dp", "mp"), pairs)
 
 
-def finish_scatter(send, keep, orders, bits):
-    received = []
+def add_kernel(*refs):
+    total = refs[0][...]
+    for ref in refs[1:-1]:
+        total = total + ref[...]
+    refs[-1][...] = total
+
+
+def add_blocks(arrays, first, count):
+    shape = (count, *arrays[0].shape[1:])
+    step = min(count, 2)
+    spec = pl.BlockSpec((step, *shape[1:]), lambda i: (i + first // step, 0, 0))
+    size = math.prod(shape)
+    return pl.pallas_call(
+        add_kernel,
+        grid=(count // step,),
+        in_specs=[spec] * len(arrays),
+        out_specs=pl.BlockSpec((step, *shape[1:]), lambda i: (i, 0, 0)),
+        out_shape=jax.ShapeDtypeStruct(shape, F32),
+        cost_estimate=cost(size * len(arrays), 4 * size * (1 + len(arrays))),
+        compiler_params=params(),
+    )(*arrays)
+
+
+class Scatter:
+    def __init__(self, send, keep, orders):
+        self.keep, self.orders = keep, orders
+        self.got = [exchange(send, orders, 0)]
+
+    def take(self, after):
+        self.got[-1] = lax.optimization_barrier((self.got[-1], after))[0]
+        return [self.keep, *self.got]
+
+    def step(self, after):
+        half = self.keep.shape[0] >> len(self.got)
+        send = add_blocks(self.take(after), half, half)
+        self.got.append(exchange(send, self.orders, len(self.got)))
+        return send
+
+    def result(self, after):
+        return add_blocks(self.take(after), 0, 1)[0]
+
+
+def all_sum(vector, bits):
+    order = [1 << b for b in range(bits)]
     for stage in range(bits):
-        received.append(exchange(send, orders, stage))
-        half = keep.shape[0] >> (stage + 1)
-        if stage + 1 < bits:
-            send = keep[half : 2 * half]
-            for got in received:
-                send = send + got[half : 2 * half]
-    total = keep[0]
-    for got in received:
-        total = total + got[0]
-    return total
-
-
-def all_sum(vector, bits):
-    orders = orders_for("near", bits)
-    for stage in range(bits):
-        vector = vector + exchange(vector, orders, stage)
+        vector = vector + exchange(vector, [order, order], stage)
     return vector
 
 
@@ -452,40 +525,68 @@
             scratch_shapes=[pltpu.VMEM((width, tile), jnp.float32)],
         ),
         out_shape=[shape, shape],
-        cost_estimate=pl.CostEstimate(
-            flops=2 * tokens * width * columns,
-            bytes_accessed=2 * tokens * (width + columns) + 4 * width * columns,
-            transcendentals=0,
-        ),
-        compiler_params=pltpu.CompilerParams(vmem_limit_bytes=40 << 20),
+        cost_estimate=cost(
+            2 * tokens * width * columns, 2 * tokens * (width + columns) + 4 * width * columns
+        ),
+        compiler_params=params(),
     )(table, left, right)
 
 
-def scattered_grad(left, right, kind, start, columns, tile):
+def pieces_kernel(table, *refs, pieces, sources):
+    lefts, rights = refs[:sources], refs[sources : 2 * sources]
+    send, keep, acc = refs[2 * sources :]
+    half, size = keep.shape[0], keep.shape[1]
+    to = 0
+    for source, start, columns in pieces:
+        acc[:, :columns] = product(
+            lefts[source][...], rights[source][:, start : start + columns], (0, 0)
+        )
+        for r in range(half):
+            at = pl.multiple_of(table[r] * size, 8)
+            keep[r, :, to : to + columns] = acc[pl.ds(at, size), :columns]
+            at = pl.multiple_of(table[half + r] * size, 8)
+            send[r, :, to : to + columns] = acc[pl.ds(at, size), :columns]
+        to += columns
+
+
+def blocked_pieces(table, lefts, rights, pieces):
+    tokens, width = lefts[0].shape
+    count = table.shape[0]
+    columns = sum(piece[2] for piece in pieces)
+    shape = jax.ShapeDtypeStruct((count // 2, width // count, columns), F32)
+    spec = lambda array: pl.BlockSpec(array.shape, lambda i, t: (0, 0), pipeline_mode=pl.Buffered(1))
+    block = pl.BlockSpec(shape.shape, lambda i, t: (0, 0, 0))
+    return pl.pallas_call(
+        lambda *refs: pieces_kernel(*refs, pieces=pieces, sources=len(lefts)),
+        grid_spec=pltpu.PrefetchScalarGridSpec(
+            num_scalar_prefetch=1,
+            grid=(1,),
+            in_specs=[spec(array) for array in (*lefts, *rights)],
+            out_specs=[block, block],
+            scratch_shapes=[pltpu.VMEM((width, max(p[2] for p in pieces)), F32)],
+        ),
+        out_shape=[shape, shape],
+        cost_estimate=cost(
+            2 * tokens * width * columns, 2 * tokens * (width + columns) + 4 * width * columns
+        ),
+        compiler_params=params(),
+    )(table, *lefts, *rights)
+
+
+def butterfly_bits(width):
     dp = lax.axis_size("dp")
     bits = dp.bit_length() - 1
-    size = left.shape[1] // dp
-    if (1 << bits) != dp or size % 8 or bits < 3:
-        part = left_product(left, right[:, start : start + columns])
-        return lax.psum_scatter(part, "dp", scatter_dimension=0, tiled=True)
-    orders = orders_for(kind, bits)
-    table = block_table(orders, bits)
-    send, keep = blocked_grad(table, left, right, start, columns, tile)
-    return finish_scatter(send, keep, orders, bits)
-
-
-def sum_small(parts):
+    return bits if (1 << bits) == dp and bits >= 3 and width // dp % 8 == 0 else 0
+
+
+def sum_small(rows, sizes):
     dp = lax.axis_size("dp")
     bits = dp.bit_length() - 1
-    if (1 << bits) != dp:
-        return lax.psum(parts, "dp")
-    sizes = [part.shape[0] for part in parts]
-    flat = jnp.concatenate(parts).reshape(-1, 128)
-    flat = all_sum(flat, bits).reshape(-1)
+    rows = all_sum(rows, bits) if (1 << bits) == dp else lax.psum(rows, "dp")
     out, at = [], 0
     for size in sizes:
-        out.append(flat[at : at + size])
-        at += size
+        out.append(rows[at : at + size // 128].reshape(size))
+        at += padded_rows(size)
     return out
 
 
@@ -514,71 +615,138 @@
     tokens = rows * length
     hidden = w_up.shape[1]
     far = hidden // 3
-    row = lambda vector: vector.reshape(1, -1)
+    near = hidden - far
+    row = lambda vector: vector.reshape(-1, 128)
+    pin = lambda values, after: lax.optimization_barrier((values, after))[0]
     x = inputs.reshape(tokens, width)
     top = cotangent.reshape(tokens, width)
-    normed, qkv, probs, context, out_mine = attend(
-        x, segment_ids, row(ln1_gain), row(ln1_bias), w_query, row(b_query),
-        w_key, w_value, row(b_value), w_output,
-    )
-    out_other = from_partner(out_mine)
-    top_b = top.astype(BF16)
-    middle, normed_two, act, slope = upper(
-        x, out_mine, out_other, row(b_output), row(ln2_gain), row(ln2_bias), w_up, row(b_up), length
-    )
-    down_far = scattered_grad(top_b, act, "far", hidden - far, far, far)
-    down_near = scattered_grad(top_b, act, "near", 0, hidden - far, far)
-    grad_upper, down_mine, back_mine, sum_up = hidden_back(top_b, act, slope, w_down, w_up, length)
+    bits = butterfly_bits(width)
+
+    half = rows // 2
+    ln1 = (row(ln1_gain), row(ln1_bias))
+    firsts = (*ln1, w_query, row(b_query), w_key, w_value, row(b_value), w_output)
+    *made, out_low = attend(x, segment_ids, *firsts, 0, half, ())
+    low_other = from_partner(out_low)
+    *made, out_high = attend(x, segment_ids, *firsts, half, rows - half, made)
+    high_other = from_partner(out_high)
+    normed, qkv, probs, context = made
+    seconds = (row(b_output), row(ln2_gain), row(ln2_bias), w_up, row(b_up), length)
+    made = upper(x, pin(out_low, out_high), low_other, *seconds, 0, ())
+    top_pinned = pin(top, made[1])
+    top_b, sum_top = top_pinned.astype(BF16), jnp.sum(top_pinned, axis=0, keepdims=True)
+    made = upper(x, pin(out_high, top_b), high_other, *seconds, half, made)
+    middle, normed_two, act, slope = made
+
+    if bits:
+        near_orders, far_orders = orders_for("near", bits), orders_for("far", bits)
+        near_table, far_table = block_table(near_orders, bits), block_table(far_orders, bits)
+        down_far = blocked_grad(far_table, top_b, act, near, far, far)
+        after = down_far[0]
+        down_far = Scatter(*down_far, far_orders)
+        down_near = blocked_grad(near_table, pin(top_b, after), act, 0, near, far)
+        after = down_near[0]
+        down_near = Scatter(*down_near, near_orders)
+    else:
+        after = middle
+    grad_upper, down_mine, back_mine, sum_up = hidden_back(
+        pin(top_b, after), act, slope, w_down, w_up, length
+    )
     back_other = from_partner(back_mine)
     down_other = from_partner(down_mine)
-    up_far = scattered_grad(normed_two, grad_upper, "far", hidden - far, far, far)
-    up_near = scattered_grad(normed_two, grad_upper, "near", 0, hidden - far, far)
-    outcome = middle + (down_mine + down_other) + b_down
+    after = sum_up
+    if bits:
+        after = down_far.step(after)
+        after = down_near.step(after)
+        up_far = blocked_grad(far_table, normed_two, pin(grad_upper, after), near, far, far)
+        after = up_far[0]
+        up_far = Scatter(*up_far, far_orders)
+        up_near = blocked_grad(near_table, normed_two, pin(grad_upper, after), 0, near, far)
+        after = up_near[0]
+        up_near = Scatter(*up_near, near_orders)
     (
         grad_middle, grad_middle_b, grad_qkv, first_mine,
         sum_gain_two, sum_shift_two, sum_out, sum_qkv,
     ) = attend_back(
-        top, back_mine, back_other, middle, row(ln2_gain), w_output, qkv, probs,
+        top, pin(back_mine, after), back_other, middle, row(ln2_gain), w_output, qkv, probs,
         w_query, w_key, w_value,
     )
     first_other = from_partner(first_mine)
-    out_value = scattered_grad(normed, grad_qkv, "far", 2 * cols, cols, cols)
-    pair = scattered_grad(normed, grad_qkv, "near", 0, 2 * cols, cols)
-    out_part = scattered_grad(grad_middle_b, context, "far", 0, cols, cols)
-    grad_x, sum_gain_one, sum_shift_one = first_back(
-        x, first_mine, first_other, grad_middle, row(ln1_gain), length
-    )
-    smalls = sum_small(
-        (
-            sum_gain_one[0],
-            sum_shift_one[0],
-            sum_qkv[0, :cols],
-            sum_qkv[0, 2 * cols :],
-            sum_out[0],
-            sum_gain_two[0],
-            sum_shift_two[0],
-            sum_up[0],
-            jnp.sum(top, axis=0),
+    after = sum_qkv
+    if bits:
+        lefts, rights = (normed, grad_middle_b), (grad_qkv, context)
+        split = cols // 3 * 2
+        pieces = ((0, cols, cols), (0, 2 * cols, cols), (1, 0, split))
+        last_near = blocked_pieces(near_table, lefts, rights, pieces)
+        after = last_near[0]
+        last_near = Scatter(*last_near, near_orders)
+        pieces = ((0, 0, cols), (1, split, cols - split))
+        last_far = blocked_pieces(far_table, lefts, pin(rights, after), pieces)
+        after = last_far[0]
+        last_far = Scatter(*last_far, far_orders)
+        after = up_far.step(after)
+        after = up_near.step(after)
+        after = down_far.step(after)
+        after = down_near.step(after)
+    grad_x, smalls, sizes = first_back(
+        x, pin(first_mine, after), first_other, grad_middle, row(ln1_gain),
+        (sum_qkv, sum_out, sum_gain_two, sum_shift_two, sum_up, sum_top), length,
+    )
+    after = smalls
+    smalls = sum_small(smalls, sizes)
+    if bits:
+        after = last_near.step(after)
+        after = last_far.step(after)
+        after = up_far.step(after)
+        after = up_near.step(after)
+        after = down_far.step(after)
+        after = down_near.step(after)
+    outcome = pin(middle, after) + (down_mine + down_other) + b_down
+    after = outcome
+    if bits:
+        after = last_near.step(after)
+        after = last_far.step(after)
+        after = up_far.step(after)
+        after = up_near.step(after)
+        out_down = jnp.concatenate([down_near.result(after), down_far.result(after)], axis=1).T
+        after = out_down
+        after = last_near.step(after)
+        after = last_far.step(after)
+        out_up = jnp.concatenate([up_near.result(after), up_far.result(after)], axis=1)
+        after = out_up
+        last_near, last_far = last_near.result(after), last_far.result(after)
+        out_query, out_key, out_value = (
+            last_far[:, :cols],
+            last_near[:, :cols],
+            last_near[:, cols : 2 * cols],
         )
-    )
+        out_output = jnp.concatenate([last_near[:, 2 * cols :], last_far[:, cols:]], axis=1).T
+    else:
+        scatter = lambda left, right: lax.psum_scatter(
+            left_product(left, right), "dp", scatter_dimension=0, tiled=True
+        )
+        out_down, out_up = scatter(top_b, act).T, scatter(normed_two, grad_upper)
+        out_query, out_key, out_value = (
+            scatter(normed, grad_qkv[:, at : at + cols]) for at in (0, cols, 2 * cols)
+        )
+        out_output = scatter(grad_middle_b, context).T
     shape = inputs.shape
     return (
         outcome.reshape(shape),
         grad_x.reshape(shape),
         smalls[0],
         smalls[1],
-        pair[:, :cols],
+        out_query,
         smalls[2],
-        pair[:, cols:],
+        out_key,
         out_value,
         smalls[3],
-        out_part.T,
+        out_output,
         smalls[4],
         smalls[5],
         smalls[6],
-        jnp.concatenate([up_near, up_far], axis=1),
+        out_up,
         smalls[7],
-        jnp.concatenate([down_near, down_far], axis=1).T,
+        out_down,
         smalls[8],
     )
 

time: 270 us -> 201 us (0.74)
  waiting for transfers between devices: 89.3 us -> 51.5 us
  other arithmetic: 35.4 us -> 8.42 us
  Pallas kernels: 78.8 us -> 92.5 us
  starting transfers between devices: 47.3 us -> 35.7 us
  local copies, waits for them, and re-layouts: 16.2 us -> 11 us
    ppermute x32 -> x28, waiting for transfers between devices: 86.2 us -> 51.5 us  [exchange(): return lax.ppermute(array, ('dp', 'mp'), pairs)]
    pallas_call x1 -> x28, Pallas kernels: 11 us -> 39 us  [the longest x24 19 us: add_blocks(): pl.pallas_call(add_kernel, grid=(count // step,), in_specs=[spec] * len(a...]
    add x32 -> x5, other arithmetic: 29.8 us -> 5.36 us  [the longest x1 5.33 us: on_device(): outcome = pin(middle, after) + (down_mine + down_other) + b_down]
    ppermute x32 -> x28, starting transfers between devices: 46.8 us -> 34.6 us  [exchange(): return lax.ppermute(array, ('dp', 'mp'), pairs)]
    pallas_call x7 -> x4, Pallas kernels: 18.1 us -> 12.9 us  [blocked_grad(): pl.pallas_call(grad_kernel, grid_spec=pltpu.PrefetchScalarGridSpec(num_sc...]
    ppermute x4 -> x5, waiting for transfers between devices: 3.13 us -> 0.01 us  [from_partner(): return lax.ppermute(part, 'mp', [(0, 1), (1, 0)])]
    pallas_call x1, Pallas kernels: 6.84 us -> 4.08 us  [first_back(): pl.pallas_call(first_back_kernel, grid=(tokens // length,), in_specs=[row...]
    pallas_call x1 -> x2, Pallas kernels: 10.2 us -> 7.75 us  [upper(): pl.pallas_call(lambda *refs: upper_kernel(*refs, step=hidden // 6), grid=...]
  transfers between devices with their start and end apart: 36 -> 33, of which waited for: 18 -> 11; matrix products, arithmetic and copies ran while one was open for 13% -> 5% of each run, Pallas kernels for 21% -> 40%
where the time goes in v3:
time: 201 us; the launch traced here: 200 us
  Pallas kernels  92.5 us (46%)
  waiting for transfers between devices  51.5 us (26%)
  starting transfers between devices  35.7 us (18%)
  local copies, waits for them, and re-layouts  11 us (5%)
  other arithmetic  8.42 us (4%)
    ppermute x28, waiting for transfers between devices, exchange(): return lax.ppermute(array, ('dp', 'mp'), pairs)  51.5 us
    ppermute x28, starting transfers between devices, exchange(): return lax.ppermute(array, ('dp', 'mp'), pairs)  34.6 us
    pallas_call x24, Pallas kernels, add_blocks(): pl.pallas_call(add_kernel, grid=(count // step,), in_specs=[spec] * len(a...  19 us
    pallas_call x1, Pallas kernels, attend_back(): pl.pallas_call(attend_back_kernel, grid=(rows,), in_specs=[rows_of(length...  18.5 us
    pallas_call x2, Pallas kernels, attend(): pl.pallas_call(lambda *refs: attend_kernel(*refs, first_row=first_row), g...  14.9 us
    pallas_call x4, Pallas kernels, blocked_grad(): pl.pallas_call(grad_kernel, grid_spec=pltpu.PrefetchScalarGridSpec(num_sc...  12.9 us
    pallas_call x1, Pallas kernels, hidden_back(): pl.pallas_call(lambda *refs: hidden_kernel(*refs, step=hidden // 6), grid...  10.2 us
    unnamed x82, local copies, waits for them, and re-layouts  7.93 us
  transfers between devices with their start and end apart: 33, of which 11 were waited for; matrix products, arithmetic and copies ran while one was open for 5% of the time, Pallas kernels for 40%

profile of v3, /device:TPU:0, one launch (start us, length us, event | category | flops | bytes accessed | tf_op | source)
XLA Modules:
  0.0 200.4 jit_solution(8122769866526974630)
XLA Ops:
  0.7 7.4 %shard_map.323 = (bf16[1024,768]{1,0:T(8,128)(2,1)}, bf16[1024,1152]{1,0:T(8,128)(2,1)}, bf16[4,6,256,256]{3,2,1,0:T(8,128)(2,1)}, bf16[1024,384]{1,0:T(8,128)(2,1)}, f32[512,768]{1,0:T(8,128)}) custom-call(s32[4,256]{1,0:T(4,128)} %refs_0_.3, f32[6,128]{1,0:T(8,128)} %bitcast.59, f32[6,128]{1,0:T(8,128)} %bitcast.73, bf16[768,384]{1,0:T(8,128)(2,1)} %wq.1, ...), custom_call_target="tpu_custom_call" | custom-call | flops 84557168640 | bytes 566231040 | tf_op jit(solution)/shard_map/pallas_call | solution.py:132
  8.5 7.5 %shard_map.324 = (bf16[1024,768]{1,0:T(8,128)(2,1)}, bf16[1024,1152]{1,0:T(8,128)(2,1)}, bf16[4,6,256,256]{3,2,1,0:T(8,128)(2,1)}, bf16[1024,384]{1,0:T(8,128)(2,1)}, f32[512,768]{1,0:T(8,128)}) custom-call(s32[4,256]{1,0:T(4,128)} %refs_0_.3, f32[6,128]{1,0:T(8,128)} %bitcast.60, ...), custom_call_target="tpu_custom_call", output_to_operand_aliasing={{0}: (10, {}), {1}: (11, {}), {2}: (12, {}), {3}: (13, {})} | custom-call | flops 84557168640 | bytes 566231040 | tf_op jit(solution)/shard_map/pallas_call | solution.py:132
  16.2 1.9 copy-done.6
  18.1 1.7 copy-done.16
  21.1 4.5 %shard_map.325 = (f32[1024,768]{1,0:T(8,128)S(1)}, bf16[1024,768]{1,0:T(8,128)(2,1)S(1)}, bf16[1024,1536]{1,0:T(8,128)(2,1)S(1)}, bf16[1024,1536]{1,0:T(8,128)(2,1)S(1)}) custom-call(f32[1024,768]{1,0:T(8,128)S(1)} %bitcast.48, f32[512,768]{1,0:T(8,128)S(1)} %copy-done.21, f32[512,768]{1,0:T(8,128)} %collective-permute-done.refs_2_, f32[6,128]{1,0:T(8,128)S(1)} %bitcast.64, ...), custom_call_target="tpu_custom_call" | custom-call | flops 72477573120 | bytes 754974720 | tf_op jit(solution)/shard_map/pallas_call | solution.py:191
  27.8 3.2 %shard_map.326 = (f32[1024,768]{1,0:T(8,128)S(1)}, bf16[1024,768]{1,0:T(8,128)(2,1)S(1)}, bf16[1024,1536]{1,0:T(8,128)(2,1)S(1)}, bf16[1024,1536]{1,0:T(8,128)(2,1)S(1)}) custom-call(f32[1024,768]{1,0:T(8,128)S(1)} %bitcast.49, f32[512,768]{1,0:T(8,128)S(1)} %copy-done.20, ...), custom_call_target="tpu_custom_call", output_to_operand_aliasing={{0}: (8, {}), {1}: (9, {}), {2}: (10, {}), {3}: (11, {})} | custom-call | flops 72477573120 | bytes 754974720 | tf_op jit(solution)/shard_map/pallas_call | solution.py:191
  32.7 2.6 %shard_map.327 = (f32[8,48,512]{2,1,0:T(8,128)}, f32[8,48,512]{2,1,0:T(8,128)S(1)}) custom-call(s32[16]{0:T(128)S(1)} %get-tuple-element.189.table.refs_0_, bf16[1024,768]{1,0:T(8,128)(2,1)S(1)} %get-tuple-element.117.left_ref.refs_0_, bf16[1024,1536]{1,0:T(8,128)(2,1)S(1)} %get-tuple-element.111.right_ref.refs_1_), custom_call_target="tpu_custom_call" | custom-call | flops 48318382080 | bytes 251658240 | tf_op jit(solution)/shard_map/pallas_call | solution.py:515
  35.3 3.0 %collective-permute-start.3 = (f32[8,48,512]{2,1,0:T(8,128)}, f32[8,48,512]{2,1,0:T(8,128)}, u32[]{:S(2)}, u32[]{:S(2)}) collective-permute-start(f32[8,48,512]{2,1,0:T(8,128)} %get-tuple-element.112), channel_id=1, source_target_pairs={{0,8},{1,9},{2,10},{3,11},{4,12},{5,13},{6,14},{7,15},{8,0},{9,1},... | collective-permute-start | bytes 2359304 | tf_op jit(solution)/shard_map/ppermute | solution.py:439
  38.3 3.9 %shard_map.328 = (f32[8,48,1024]{2,1,0:T(8,128)}, f32[8,48,1024]{2,1,0:T(8,128)S(1)}) custom-call(s32[16]{0:T(128)S(1)} %get-tuple-element.190.table.refs_0_, bf16[1024,768]{1,0:T(8,128)(2,1)S(1)} %get-tuple-element.117.left_ref.refs_0_, bf16[1024,1536]{1,0:T(8,128)(2,1)S(1)} %get-tuple-element.111.right_ref.refs_1_), custom_call_target="tpu_custom_call" | custom-call | flops 96636764160 | bytes 408944640 | tf_op jit(solution)/shard_map/pallas_call | solution.py:515
  43.7 10.2 %shard_map.329 = (bf16[1024,1536]{1,0:T(8,128)(2,1)S(1)}, f32[1024,768]{1,0:T(8,128)}, f32[1024,768]{1,0:T(8,128)}, f32[1,1536]{1,0:T(1,128)S(1)}) custom-call(bf16[1024,768]{1,0:T(8,128)(2,1)S(1)} %get-tuple-element.117.left_ref.refs_0_, bf16[1024,1536]{1,0:T(8,128)(2,1)S(1)} %get-tuple-element.111.right_ref.refs_1_, bf16[1024,1536]{1,0:T(8,128)(2,1)S(1)} %copy-done.34, ...), custom_call_target="tpu_custom_call" | custom-call | flops 434865438720 | bytes 1321205760 | tf_op jit(solution)/shard_map/pallas_call | solution.py:229
  54.5 1.9 collective-permute-done.3.refs_1_
  56.4 1.7 shard_map.330
  59.8 3.2 %collective-permute-done.2.refs_1_ = f32[8,48,1024]{2,1,0:T(8,128)} collective-permute-done((f32[8,48,1024]{2,1,0:T(8,128)}, f32[8,48,1024]{2,1,0:T(8,128)}, u32[]{:S(2)}, u32[]{:S(2)}) %collective-permute-start.2) | collective-permute-done | bytes 1572896 | tf_op jit(solution)/shard_map/ppermute | solution.py:439
  63.0 1.9 shard_map.331
  66.4 2.5 %shard_map.332 = (f32[8,48,512]{2,1,0:T(8,128)}, f32[8,48,512]{2,1,0:T(8,128)S(1)}) custom-call(s32[16]{0:T(128)S(1)} %get-tuple-element.189.table.refs_0_, bf16[1024,768]{1,0:T(8,128)(2,1)S(1)} %copy-done.32, bf16[1024,1536]{1,0:T(8,128)(2,1)S(1)} %get-tuple-element.126.right_ref), custom_call_target="tpu_custom_call" | custom-call | flops 48318382080 | bytes 251658240 | tf_op jit(solution)/shard_map/pallas_call | solution.py:515
  69.5 3.9 %shard_map.333 = (f32[8,48,1024]{2,1,0:T(8,128)}, f32[8,48,1024]{2,1,0:T(8,128)S(1)}) custom-call(s32[16]{0:T(128)S(1)} %get-tuple-element.190.table.refs_0_, bf16[1024,768]{1,0:T(8,128)(2,1)S(1)} %copy-done.32, bf16[1024,1536]{1,0:T(8,128)(2,1)S(1)} %get-tuple-element.126.right_ref), custom_call_target="tpu_custom_call" | custom-call | flops 96636764160 | bytes 408944640 | tf_op jit(solution)/shard_map/pallas_call | solution.py:515
  75.0 18.5 %shard_map.334 = (f32[1024,768]{1,0:T(8,128)S(1)}, bf16[1024,768]{1,0:T(8,128)(2,1)S(1)}, bf16[1024,1152]{1,0:T(8,128)(2,1)S(1)}, f32[1024,768]{1,0:T(8,128)S(1)...) custom-call(f32[1024,768]{1,0:T(8,128)S(1)} %bitcast.45, ...), custom_call_target="tpu_custom_call" | custom-call | flops 193273528320 | bytes 1840250880 | tf_op jit(solution)/shard_map/pallas_call | solution.py:311
  93.6 3.0 %shard_map.335 = (f32[8,48,1024]{2,1,0:T(8,128)S(1)}, f32[8,48,1024]{2,1,0:T(8,128)S(1)}) custom-call(s32[16]{0:T(128)S(1)} %copy-done.15, bf16[1024,768]{1,0:T(8,128)(2,1)S(1)} %copy-done.30, bf16[1024,768]{1,0:T(8,128)(2,1)S(1)} %get-tuple-element.135.refs_2_, bf16[1024,1152]{1,0:T(8,128)(2,1)S(1)} %get-tuple-element.139.refs_3_, ...), custom_call_target="tpu_custom_call" | custom-call | flops 96636764160 | bytes 408944640 | tf_op jit(solution)/shard_map/pallas_call | solution.py:559
  97.2 2.1 %shard_map.336 = (f32[8,48,512]{2,1,0:T(8,128)S(1)}, f32[8,48,512]{2,1,0:T(8,128)S(1)}) custom-call(s32[16]{0:T(128)S(1)} %copy-done.13, bf16[1024,768]{1,0:T(8,128)(2,1)S(1)} %copy-done.30, bf16[1024,768]{1,0:T(8,128)(2,1)S(1)} %get-tuple-element.135.refs_2_, bf16[1024,1152]{1,0:T(8,128)(2,1)S(1)} %get-tuple-element.139.refs_3_, ...), custom_call_target="tpu_custom_call" | custom-call | flops 48318382080 | bytes 251658240 | tf_op jit(solution)/shard_map/pallas_call | solution.py:559
  107.9 4.1 %shard_map.341 = (f32[1024,768]{1,0:T(8,128)}, f32[80,128]{1,0:T(8,128)S(1)}) custom-call(f32[1024,768]{1,0:T(8,128)S(1)} %bitcast.50, f32[1024,768]{1,0:T(8,128)S(1)} %get-tuple-element.149.mine, f32[1024,768]{1,0:T(8,128)S(1)} %collective-permute-done.15.other, f32[1024,768]{1,0:T(8,128)S(1)} %get-tuple-element.150.above, f32[6,128]{1,0:T(8,128)S(1)} %bitcast.61, ...), custom_call_target="tpu_custom_call" | custom-call | flops 943718400 | bytes 943718400 | tf_op jit(solution)/shard_map/pallas_call | solution.py:387
  112.0 17.9 %collective-permute-done.12.refs_2_ = f32[4,48,512]{2,1,0:T(8,128)S(1)} collective-permute-done((f32[4,48,512]{2,1,0:T(8,128)S(1)}, f32[4,48,512]{2,1,0:T(8,128)S(1)}, u32[]{:S(2)}, u32[]{:S(2)}) %collective-permute-start.12) | collective-permute-done | bytes 393248 | tf_op jit(solution)/shard_map/ppermute | solution.py:439
  130.4 3.5 %collective-permute-done.17 = f32[80,128]{1,0:T(8,128)S(1)} collective-permute-done((f32[80,128]{1,0:T(8,128)S(1)}, f32[80,128]{1,0:T(8,128)S(1)}, u32[]{:S(2)}, u32[]{:S(2)}) %collective-permute-start.17) | collective-permute-done | bytes 40992 | tf_op jit(solution)/shard_map/ppermute | solution.py:439
  136.0 3.5 %collective-permute-done.18 = f32[80,128]{1,0:T(8,128)S(1)} collective-permute-done((f32[80,128]{1,0:T(8,128)S(1)}, f32[80,128]{1,0:T(8,128)S(1)}, u32[]{:S(2)}, u32[]{:S(2)}) %collective-permute-start.18) | collective-permute-done | bytes 40992 | tf_op jit(solution)/shard_map/ppermute | solution.py:439
  141.8 1.7 collective-permute-start.27
  147.3 2.7 %collective-permute-start.28 = (f32[1,48,512]{2,1,0:T(8,128)S(1)}, f32[1,48,512]{2,1,0:T(8,128)S(1)}, u32[]{:S(2)}, u32[]{:S(2)}) collective-permute-start(f32[1,48,512]{2,1,0:T(8,128)S(1)} %shard_map.346), channel_id=1, source_target_pairs={{0,16},{1,17},{2,18},{3,19},{4,20},{5,21},{6,22},{7,23},{8,24},{9,... | collective-permute-start | bytes 294920 | tf_op jit(solution)/shard_map/ppermute | solution.py:439
  152.0 5.3 %add_add_fusion = f32[1024,768]{1,0:T(8,128)} fusion(f32[1024,768]{1,0:T(8,128)S(1)} %copy-done.10, f32[1024,768]{1,0:T(8,128)} %get-tuple-element.163, f32[1024,768]{1,0:T(8,128)} %collective-permute-done.16, f32[768]{0:T(1024)S(1)} %copy-done.38), kind=kLoop, calls=%fused_computation | loop fusion | flops 2359296 | bytes 12585984 | tf_op jit(solution)/shard_map/add | solution.py:703
  159.1 6.3 %collective-permute-done.22.refs_2_ = f32[4,48,1024]{2,1,0:T(8,128)S(1)} collective-permute-done((f32[4,48,1024]{2,1,0:T(8,128)S(1)}, f32[4,48,1024]{2,1,0:T(8,128)S(1)}, u32[]{:S(2)}, u32[]{:S(2)}) %collective-permute-start.22) | collective-permute-done | bytes 786464 | tf_op jit(solution)/shard_map/ppermute | solution.py:439
  165.4 2.3 %collective-permute-start.25 = (f32[1,48,1024]{2,1,0:T(8,128)S(1)}, f32[1,48,1024]{2,1,0:T(8,128)S(1)}, u32[]{:S(2)}, u32[]{:S(2)}) collective-permute-start(f32[1,48,1024]{2,1,0:T(8,128)S(1)} %shard_map.347), channel_id=1, source_target_pairs={{0,16},{1,17},{2,18},{3,19},{4,20},{5,21},{6,22},{7,23},{8,24},{9,... | collective-permute-start | bytes 589832 | tf_op jit(solution)/shard_map/ppermute | solution.py:439
  175.1 6.1 %collective-permute-done.25.refs_4_ = f32[1,48,1024]{2,1,0:T(8,128)S(1)} collective-permute-done((f32[1,48,1024]{2,1,0:T(8,128)S(1)}, f32[1,48,1024]{2,1,0:T(8,128)S(1)}, u32[]{:S(2)}, u32[]{:S(2)}) %collective-permute-start.25) | collective-permute-done | bytes 196640 | tf_op jit(solution)/shard_map/ppermute | solution.py:439
  184.2 3.0 %collective-permute-start.29 = (f32[1,48,512]{2,1,0:T(8,128)S(1)}, f32[1,48,512]{2,1,0:T(8,128)S(1)}, u32[]{:S(2)}, u32[]{:S(2)}) collective-permute-start(f32[1,48,512]{2,1,0:T(8,128)S(1)} %shard_map.355), channel_id=1, source_target_pairs={{0,16},{1,17},{2,18},{3,19},{4,20},{5,21},{6,22},{7,23},{8,24},{9,... | collective-permute-start | bytes 294920 | tf_op jit(solution)/shard_map/ppermute | solution.py:439
  188.2 6.4 %collective-permute-done.30.refs_4_ = f32[1,48,1024]{2,1,0:T(8,128)S(1)} collective-permute-done((f32[1,48,1024]{2,1,0:T(8,128)S(1)}, f32[1,48,1024]{2,1,0:T(8,128)S(1)}, u32[]{:S(2)}, u32[]{:S(2)}) %collective-permute-start.30) | collective-permute-done | bytes 196640 | tf_op jit(solution)/shard_map/ppermute | solution.py:439
  196.4 1.9 collective-permute-done.29.refs_4_
  (171 shorter events, 49.7 us)
Async XLA Ops:
  8.1 8.1 %collective-permute-start = (f32[512,768]{1,0:T(8,128)}, f32[512,768]{1,0:T(8,128)}, u32[]{:S(2)}, u32[]{:S(2)}) collective-permute-start(f32[512,768]{1,0:T(8,128)} %get-tuple-element.103.refs_1_), channel_id=1, source_target_pairs={{0,1},{1,0},{2,3},{3,2},{4,5},{5,4},{6,7},{7,6},{8,9},{9,8},{10,11... | collective-permute-start | bytes 4718600 | tf_op jit(solution)/shard_map/ppermute | solution.py:404
  16.0 10.6 %collective-permute-start.1 = (f32[512,768]{1,0:T(8,128)}, f32[512,768]{1,0:T(8,128)S(1)}, u32[]{:S(2)}, u32[]{:S(2)}) collective-permute-start(f32[512,768]{1,0:T(8,128)} %get-tuple-element.106.refs_1_), channel_id=1, source_target_pairs={{0,1},{1,0},{2,3},{3,2},{4,5},{5,4},{6,7},{7,6},{8,9},{9,8},{10,11... | collective-permute-start | bytes 4718600 | tf_op jit(solution)/shard_map/ppermute | solution.py:404
  35.3 21.1 %collective-permute-start.3 = (f32[8,48,512]{2,1,0:T(8,128)}, f32[8,48,512]{2,1,0:T(8,128)}, u32[]{:S(2)}, u32[]{:S(2)}) collective-permute-start(f32[8,48,512]{2,1,0:T(8,128)} %get-tuple-element.112), channel_id=1, source_target_pairs={{0,8},{1,9},{2,10},{3,11},{4,12},{5,13},{6,14},{7,15},{8,0},{9,1},... | collective-permute-start | bytes 2359304 | tf_op jit(solution)/shard_map/ppermute | solution.py:439
  42.2 20.7 %collective-permute-start.2 = (f32[8,48,1024]{2,1,0:T(8,128)}, f32[8,48,1024]{2,1,0:T(8,128)}, u32[]{:S(2)}, u32[]{:S(2)}) collective-permute-start(f32[8,48,1024]{2,1,0:T(8,128)} %get-tuple-element.115), channel_id=1, source_target_pairs={{0,2},{1,5},{2,0},{3,7},{4,6},{5,1},{6,4},{7,3},{8,10},{9,13},{10,... | collective-permute-start | bytes 4718600 | tf_op jit(solution)/shard_map/ppermute | solution.py:439
  54.0 19.4 %collective-permute-start.8 = (f32[1024,768]{1,0:T(8,128)}, f32[1024,768]{1,0:T(8,128)}, u32[]{:S(2)}, u32[]{:S(2)}) collective-permute-start(f32[1024,768]{1,0:T(8,128)} %get-tuple-element.132.mine), channel_id=1, source_target_pairs={{0,1},{1,0},{2,3},{3,2},{4,5},{5,4},{6,7},{7,6},{8,9},{9,8},{10,11... | collective-permute-start | bytes 9437192 | tf_op jit(solution)/shard_map/ppermute | solution.py:404
  54.0 97.6 %collective-permute-start.16 = (f32[1024,768]{1,0:T(8,128)}, f32[1024,768]{1,0:T(8,128)}, u32[]{:S(2)}, u32[]{:S(2)}) collective-permute-start(f32[1024,768]{1,0:T(8,128)} %get-tuple-element.163), channel_id=1, source_target_pairs={{0,1},{1,0},{2,3},{3,2},{4,5},{5,4},{6,7},{7,6},{8,9},{9,8},{10,11... | collective-permute-start | bytes 9437192 | tf_op jit(solution)/shard_map/ppermute | solution.py:404
  58.1 38.5 %collective-permute-start.5 = (f32[4,48,512]{2,1,0:T(8,128)}, f32[4,48,512]{2,1,0:T(8,128)}, u32[]{:S(2)}, u32[]{:S(2)}) collective-permute-start(f32[4,48,512]{2,1,0:T(8,128)} %shard_map.330), channel_id=1, source_target_pairs={{0,2},{1,5},{2,0},{3,7},{4,6},{5,1},{6,4},{7,3},{8,10},{9,13},{10,... | collective-permute-start | bytes 1179656 | tf_op jit(solution)/shard_map/ppermute | solution.py:439
  64.9 32.3 %collective-permute-start.4 = (f32[4,48,1024]{2,1,0:T(8,128)}, f32[4,48,1024]{2,1,0:T(8,128)}, u32[]{:S(2)}, u32[]{:S(2)}) collective-permute-start(f32[4,48,1024]{2,1,0:T(8,128)} %shard_map.331), channel_id=1, source_target_pairs={{0,4},{1,3},{2,6},{3,1},{4,0},{5,7},{6,2},{7,5},{8,12},{9,11},{10,... | collective-permute-start | bytes 2359304 | tf_op jit(solution)/shard_map/ppermute | solution.py:439
  69.0 30.3 %collective-permute-start.7 = (f32[8,48,512]{2,1,0:T(8,128)}, f32[8,48,512]{2,1,0:T(8,128)}, u32[]{:S(2)}, u32[]{:S(2)}) collective-permute-start(f32[8,48,512]{2,1,0:T(8,128)} %get-tuple-element.125), channel_id=1, source_target_pairs={{0,8},{1,9},{2,10},{3,11},{4,12},{5,13},{6,14},{7,15},{8,0},{9,1},... | collective-permute-start | bytes 2359304 | tf_op jit(solution)/shard_map/ppermute | solution.py:439
  73.4 28.6 %collective-permute-start.6 = (f32[8,48,1024]{2,1,0:T(8,128)}, f32[8,48,1024]{2,1,0:T(8,128)}, u32[]{:S(2)}, u32[]{:S(2)}) collective-permute-start(f32[8,48,1024]{2,1,0:T(8,128)} %get-tuple-element.128), channel_id=1, source_target_pairs={{0,2},{1,5},{2,0},{3,7},{4,6},{5,1},{6,4},{7,3},{8,10},{9,13},{10,... | collective-permute-start | bytes 4718600 | tf_op jit(solution)/shard_map/ppermute | solution.py:439
  96.6 43.4 %collective-permute-start.14 = (f32[8,48,1024]{2,1,0:T(8,128)S(1)}, f32[8,48,1024]{2,1,0:T(8,128)S(1)}, u32[]{:S(2)}, u32[]{:S(2)}) collective-permute-start(f32[8,48,1024]{2,1,0:T(8,128)S(1)} %get-tuple-element.138), channel_id=1, source_target_pairs={{0,2},{1,5},{2,0},{3,7},{4,6},{5,1},{6,4},{7,3},{8,10},{9,13},{10,... | collective-permute-start | bytes 4718600 | tf_op jit(solution)/shard_map/ppermute | solution.py:439
  97.2 7.6 %collective-permute-start.15 = (f32[1024,768]{1,0:T(8,128)S(1)}, f32[1024,768]{1,0:T(8,128)S(1)}, u32[]{:S(2)}, u32[]{:S(2)}) collective-permute-start(f32[1024,768]{1,0:T(8,128)S(1)} %get-tuple-element.149.mine), channel_id=1, source_target_pairs={{0,1},{1,0},{2,3},{3,2},{4,5},{5,4},{6,7},{7,6},{8,9},{9,8},{10,11... | collective-permute-start | bytes 9437192 | tf_op jit(solution)/shard_map/ppermute | solution.py:404
  99.3 36.1 %collective-permute-start.13 = (f32[8,48,512]{2,1,0:T(8,128)S(1)}, f32[8,48,512]{2,1,0:T(8,128)S(1)}, u32[]{:S(2)}, u32[]{:S(2)}) collective-permute-start(f32[8,48,512]{2,1,0:T(8,128)S(1)} %get-tuple-element.141), channel_id=1, source_target_pairs={{0,8},{1,9},{2,10},{3,11},{4,12},{5,13},{6,14},{7,15},{8,0},{9,1},... | collective-permute-start | bytes 2359304 | tf_op jit(solution)/shard_map/ppermute | solution.py:439
  102.1 27.8 %collective-permute-start.12 = (f32[4,48,512]{2,1,0:T(8,128)S(1)}, f32[4,48,512]{2,1,0:T(8,128)S(1)}, u32[]{:S(2)}, u32[]{:S(2)}) collective-permute-start(f32[4,48,512]{2,1,0:T(8,128)S(1)} %shard_map.337), channel_id=1, source_target_pairs={{0,2},{1,5},{2,0},{3,7},{4,6},{5,1},{6,4},{7,3},{8,10},{9,13},{10,... | collective-permute-start | bytes 1179656 | tf_op jit(solution)/shard_map/ppermute | solution.py:439
  104.8 37.0 %collective-permute-start.11 = (f32[4,48,1024]{2,1,0:T(8,128)S(1)}, f32[4,48,1024]{2,1,0:T(8,128)S(1)}, u32[]{:S(2)}, u32[]{:S(2)}) collective-permute-start(f32[4,48,1024]{2,1,0:T(8,128)S(1)} %shard_map.338), channel_id=1, source_target_pairs={{0,4},{1,3},{2,6},{3,1},{4,0},{5,7},{6,2},{7,5},{8,12},{9,11},{10,... | collective-permute-start | bytes 2359304 | tf_op jit(solution)/shard_map/ppermute | solution.py:439
  133.9 13.4 %collective-permute-start.9 = (f32[2,48,1024]{2,1,0:T(8,128)S(1)}, f32[2,48,1024]{2,1,0:T(8,128)S(1)}, u32[]{:S(2)}, u32[]{:S(2)}) collective-permute-start(f32[2,48,1024]{2,1,0:T(8,128)S(1)} %shard_map.340), channel_id=1, source_target_pairs={{0,8},{1,9},{2,10},{3,11},{4,12},{5,13},{6,14},{7,15},{8,0},{9,1},... | collective-permute-start | bytes 1179656 | tf_op jit(solution)/shard_map/ppermute | solution.py:439
  135.4 4.1 %collective-permute-start.18 = (f32[80,128]{1,0:T(8,128)S(1)}, f32[80,128]{1,0:T(8,128)S(1)}, u32[]{:S(2)}, u32[]{:S(2)}) collective-permute-start(f32[80,128]{1,0:T(8,128)S(1)} %add.41), channel_id=1, source_target_pairs={{0,4},{1,5},{2,6},{3,7},{4,0},{5,1},{6,2},{7,3},{8,12},{9,13},{10,... | collective-permute-start | bytes 122888 | tf_op jit(solution)/shard_map/ppermute | solution.py:439
  139.5 5.7 %collective-permute-start.10 = (f32[2,48,512]{2,1,0:T(8,128)S(1)}, f32[2,48,512]{2,1,0:T(8,128)S(1)}, u32[]{:S(2)}, u32[]{:S(2)}) collective-permute-start(f32[2,48,512]{2,1,0:T(8,128)S(1)} %shard_map.339), channel_id=1, source_target_pairs={{0,4},{1,3},{2,6},{3,1},{4,0},{5,7},{6,2},{7,5},{8,12},{9,11},{10,... | collective-permute-start | bytes 589832 | tf_op jit(solution)/shard_map/ppermute | solution.py:439
  140.0 11.0 %collective-permute-start.19 = (f32[80,128]{1,0:T(8,128)S(1)}, f32[80,128]{1,0:T(8,128)S(1)}, u32[]{:S(2)}, u32[]{:S(2)}) collective-permute-start(f32[80,128]{1,0:T(8,128)S(1)} %add.42), channel_id=1, source_target_pairs={{0,8},{1,9},{2,10},{3,11},{4,12},{5,13},{6,14},{7,15},{8,0},{9,1},... | collective-permute-start | bytes 122888 | tf_op jit(solution)/shard_map/ppermute | solution.py:439
  141.8 27.5 %collective-permute-start.27 = (f32[2,48,512]{2,1,0:T(8,128)S(1)}, f32[2,48,512]{2,1,0:T(8,128)S(1)}, u32[]{:S(2)}, u32[]{:S(2)}) collective-permute-start(f32[2,48,512]{2,1,0:T(8,128)S(1)} %shard_map.344), channel_id=1, source_target_pairs={{0,4},{1,3},{2,6},{3,1},{4,0},{5,7},{6,2},{7,5},{8,12},{9,11},{10,... | collective-permute-start | bytes 589832 | tf_op jit(solution)/shard_map/ppermute | solution.py:439
  145.2 25.9 %collective-permute-start.26 = (f32[2,48,1024]{2,1,0:T(8,128)S(1)}, f32[2,48,1024]{2,1,0:T(8,128)S(1)}, u32[]{:S(2)}, u32[]{:S(2)}) collective-permute-start(f32[2,48,1024]{2,1,0:T(8,128)S(1)} %shard_map.345), channel_id=1, source_target_pairs={{0,8},{1,9},{2,10},{3,11},{4,12},{5,13},{6,14},{7,15},{8,0},{9,1},... | collective-permute-start | bytes 1179656 | tf_op jit(solution)/shard_map/ppermute | solution.py:439
  147.3 26.3 %collective-permute-start.28 = (f32[1,48,512]{2,1,0:T(8,128)S(1)}, f32[1,48,512]{2,1,0:T(8,128)S(1)}, u32[]{:S(2)}, u32[]{:S(2)}) collective-permute-start(f32[1,48,512]{2,1,0:T(8,128)S(1)} %shard_map.346), channel_id=1, source_target_pairs={{0,16},{1,17},{2,18},{3,19},{4,20},{5,21},{6,22},{7,23},{8,24},{9,... | collective-permute-start | bytes 294920 | tf_op jit(solution)/shard_map/ppermute | solution.py:439
  151.0 14.3 %collective-permute-start.22 = (f32[4,48,1024]{2,1,0:T(8,128)S(1)}, f32[4,48,1024]{2,1,0:T(8,128)S(1)}, u32[]{:S(2)}, u32[]{:S(2)}) collective-permute-start(f32[4,48,1024]{2,1,0:T(8,128)S(1)} %shard_map.342), channel_id=1, source_target_pairs={{0,4},{1,3},{2,6},{3,1},{4,0},{5,7},{6,2},{7,5},{8,12},{9,11},{10,... | collective-permute-start | bytes 2359304 | tf_op jit(solution)/shard_map/ppermute | solution.py:439
  151.6 5.8 %collective-permute-start.20 = (f32[80,128]{1,0:T(8,128)S(1)}, f32[80,128]{1,0:T(8,128)S(1)}, u32[]{:S(2)}, u32[]{:S(2)}) collective-permute-start(f32[80,128]{1,0:T(8,128)S(1)} %add.43), channel_id=1, source_target_pairs={{0,16},{1,17},{2,18},{3,19},{4,20},{5,21},{6,22},{7,23},{8,24},{9,... | collective-permute-start | bytes 122888 | tf_op jit(solution)/shard_map/ppermute | solution.py:439
  157.3 10.4 %collective-permute-start.21 = (f32[4,48,512]{2,1,0:T(8,128)S(1)}, f32[4,48,512]{2,1,0:T(8,128)S(1)}, u32[]{:S(2)}, u32[]{:S(2)}) collective-permute-start(f32[4,48,512]{2,1,0:T(8,128)S(1)} %shard_map.343), channel_id=1, source_target_pairs={{0,2},{1,5},{2,0},{3,7},{4,6},{5,1},{6,4},{7,3},{8,10},{9,13},{10,... | collective-permute-start | bytes 1179656 | tf_op jit(solution)/shard_map/ppermute | solution.py:439
  165.4 15.8 %collective-permute-start.25 = (f32[1,48,1024]{2,1,0:T(8,128)S(1)}, f32[1,48,1024]{2,1,0:T(8,128)S(1)}, u32[]{:S(2)}, u32[]{:S(2)}) collective-permute-start(f32[1,48,1024]{2,1,0:T(8,128)S(1)} %shard_map.347), channel_id=1, source_target_pairs={{0,16},{1,17},{2,18},{3,19},{4,20},{5,21},{6,22},{7,23},{8,24},{9,... | collective-permute-start | bytes 589832 | tf_op jit(solution)/shard_map/ppermute | solution.py:439
  167.7 16.3 %collective-permute-start.24 = (f32[2,48,1024]{2,1,0:T(8,128)S(1)}, f32[2,48,1024]{2,1,0:T(8,128)S(1)}, u32[]{:S(2)}, u32[]{:S(2)}) collective-permute-start(f32[2,48,1024]{2,1,0:T(8,128)S(1)} %shard_map.348), channel_id=1, source_target_pairs={{0,8},{1,9},{2,10},{3,11},{4,12},{5,13},{6,14},{7,15},{8,0},{9,1},... | collective-permute-start | bytes 1179656 | tf_op jit(solution)/shard_map/ppermute | solution.py:439
  169.3 14.8 %collective-permute-start.23 = (f32[2,48,512]{2,1,0:T(8,128)S(1)}, f32[2,48,512]{2,1,0:T(8,128)S(1)}, u32[]{:S(2)}, u32[]{:S(2)}) collective-permute-start(f32[2,48,512]{2,1,0:T(8,128)S(1)} %shard_map.349), channel_id=1, source_target_pairs={{0,4},{1,3},{2,6},{3,1},{4,0},{5,7},{6,2},{7,5},{8,12},{9,11},{10,... | collective-permute-start | bytes 589832 | tf_op jit(solution)/shard_map/ppermute | solution.py:439
  171.1 16.2 %collective-permute-start.31 = (f32[1,48,512]{2,1,0:T(8,128)S(1)}, f32[1,48,512]{2,1,0:T(8,128)S(1)}, u32[]{:S(2)}, u32[]{:S(2)}) collective-permute-start(f32[1,48,512]{2,1,0:T(8,128)S(1)} %shard_map.350), channel_id=1, source_target_pairs={{0,16},{1,17},{2,18},{3,19},{4,20},{5,21},{6,22},{7,23},{8,24},{9,... | collective-permute-start | bytes 294920 | tf_op jit(solution)/shard_map/ppermute | solution.py:439
  173.6 21.0 %collective-permute-start.30 = (f32[1,48,1024]{2,1,0:T(8,128)S(1)}, f32[1,48,1024]{2,1,0:T(8,128)S(1)}, u32[]{:S(2)}, u32[]{:S(2)}) collective-permute-start(f32[1,48,1024]{2,1,0:T(8,128)S(1)} %shard_map.351), channel_id=1, source_target_pairs={{0,16},{1,17},{2,18},{3,19},{4,20},{5,21},{6,22},{7,23},{8,24},{9,... | collective-permute-start | bytes 589832 | tf_op jit(solution)/shard_map/ppermute | solution.py:439
  184.1 14.9 %collective-permute-start.32 = (f32[1,48,1024]{2,1,0:T(8,128)S(1)}, f32[1,48,1024]{2,1,0:T(8,128)S(1)}, u32[]{:S(2)}, u32[]{:S(2)}) collective-permute-start(f32[1,48,1024]{2,1,0:T(8,128)S(1)} %shard_map.354), channel_id=1, source_target_pairs={{0,16},{1,17},{2,18},{3,19},{4,20},{5,21},{6,22},{7,23},{8,24},{9,... | collective-permute-start | bytes 589832 | tf_op jit(solution)/shard_map/ppermute | solution.py:439
  184.2 14.1 %collective-permute-start.29 = (f32[1,48,512]{2,1,0:T(8,128)S(1)}, f32[1,48,512]{2,1,0:T(8,128)S(1)}, u32[]{:S(2)}, u32[]{:S(2)}) collective-permute-start(f32[1,48,512]{2,1,0:T(8,128)S(1)} %shard_map.355), channel_id=1, source_target_pairs={{0,16},{1,17},{2,18},{3,19},{4,20},{5,21},{6,22},{7,23},{8,24},{9,... | collective-permute-start | bytes 294920 | tf_op jit(solution)/shard_map/ppermute | solution.py:439
  (42 other events, 381.6 us)

commit v4 on v0

v4 whole, which is shorter than its diff:
```python
import math

import jax
import jax.numpy as jnp
from jax import lax
from jax.experimental import pallas as pl
from jax.experimental.pallas import tpu as pltpu
from jax.sharding import PartitionSpec as P

HD = 64
PAIR = 2 * HD
EPSILON = 1e-06
MASKED = -1000000000.0
SCALE = 1.0 / math.sqrt(HD)
CURVE = math.sqrt(2.0 / math.pi)
CUBIC = 0.044715
COSTS = {"attend": 0.01, "forward": 0.01, "back": 0.01, "first": 0.01, "add": 0.01}
BIG = 63 << 20
STEP = 512
SLAB = 64
F32 = jnp.float32
BF16 = jnp.bfloat16


def product(left, right, over):
    return lax.dot_general(
        left, right, ((over[:1], over[1:]), ((), ())), preferred_element_type=F32
    )


def left_product(left, right):
    return product(left, right, (0, 0))


def unit_rows(values):
    centered = values - jnp.mean(values, axis=-1, keepdims=True)
    inv_std = lax.rsqrt(jnp.mean(centered * centered, axis=-1, keepdims=True) + EPSILON)
    return centered * inv_std, inv_std


def norm_back(grad_out, unit, inv_std, gain):
    grad_unit = grad_out * gain
    return inv_std * (
        grad_unit
        - jnp.mean(grad_unit, axis=-1, keepdims=True)
        - unit * jnp.mean(grad_unit * unit, axis=-1, keepdims=True)
    )


def column_sum(values):
    return jnp.sum(values, axis=0, keepdims=True)


def line(ref):
    return jnp.concatenate([ref[r : r + 1, :] for r in range(ref.shape[0])], axis=1)


def add_up(ref, value):
    @pl.when(pl.program_id(0) == 0)
    def _():
        ref[...] = jnp.zeros_like(ref)

    ref[...] += value


def in_rows(far, near, sems, first, chunks):
    size = far.shape[0] // chunks
    rows = [pl.ds(c * size, size) for c in range(chunks)]
    return [
        pltpu.make_async_copy(far.at[part], near.at[part], sems.at[first + c])
        for c, part in enumerate(rows)
    ]


def started(copies):
    return lambda: [copy.start() for copy in copies] and None


def arrived(copies):
    return lambda: [copy.wait() for copy in copies] and None


def when_first(action):
    pl.when(pl.program_id(0) == 0)(action)


def either(low, high, rows_low, slab):
    return jnp.where(pl.program_id(0) < rows_low, low[slab, :], high[slab, :])


def last_step():
    return pl.program_id(0) == pl.num_programs(0) - 1


def leaving(tables, outs, pieces, widths, total, sems, make):
    copies, start = [], 0
    for turned, right, at, columns, index, to in pieces:
        if make:
            total[:, start : start + columns] = product(
                turned[...], right[:, at : at + columns], (1, 0)
            )
        fresh = []
        if tables:
            table, send, keep = tables[index], outs[2 * index], outs[2 * index + 1]
            half, size, _ = send.shape
            for r in range(2 * half):
                row = pl.multiple_of(table[r] * size, 8)
                far = send.at[r - half] if r >= half else keep.at[r]
                fresh.append(
                    pltpu.make_async_copy(
                        total.at[pl.ds(row, size), pl.ds(start, columns)],
                        far.at[:, pl.ds(to, columns)],
                        sems.at[len(copies) + r],
                    )
                )
        else:
            fresh.append(
                pltpu.make_async_copy(
                    total.at[:, pl.ds(start, columns)],
                    outs[0].at[:, pl.ds(sum(widths[:index]) + to, columns)],
                    sems.at[len(copies)],
                )
            )
        if make:
            started(fresh)()
        copies += fresh
        start += columns
    return copies


def leave(*args):
    arrived(leaving(*args, True))()


def pieces_of(sources, first, widths):
    pieces = []
    for turned, right, at, columns in sources:
        end = at + columns
        while at < end:
            index, to, left = place_of(first, widths)
            size = min(512, end - at, left)
            pieces.append((turned, right, at, size, index, to))
            at, first = at + size, first + size
    return pieces


def place_of(column, widths):
    for index, width in enumerate(widths):
        if column < width:
            return index, column, width - column
        column -= width


def step_rows(length):
    return pl.ds(pl.multiple_of(pl.program_id(0) * length, length), length)


def gradient_outs(tables, widths, width):
    if not tables:
        return [jax.ShapeDtypeStruct((width, sum(widths)), F32)], 8
    blocks = tables[0].shape[0]
    shapes = [
        jax.ShapeDtypeStruct((blocks // 2, width // blocks, columns), F32)
        for columns in widths
        for _ in range(2)
    ]
    return shapes, blocks * 6


def table_spec():
    return pl.BlockSpec(memory_space=pltpu.SMEM)


def in_turn(stages, count):
    for turn in range(count + len(stages) - 1):
        for late, stage in enumerate(stages):
            if 0 <= turn - late < count:
                stage(turn - late)


def lane_halves(width):
    lane = lax.broadcasted_iota(jnp.int32, (1, width), 1)
    low = (lane % PAIR < HD).astype(F32)
    return low, 1.0 - low


def attend_kernel(
    seg_ref, gain, shift, bq, bv, bo, wq_far, wk_far, wv_far, wo_far, x_ref, *refs, first_row
):
    normed_ref, qkv_ref, probs_ref, context_ref, out_ref = refs[-10:-5]
    wq, wk, wv, wo, sems = refs[-5:]
    fetches = []
    for i, (far, near) in enumerate(((wq_far, wq), (wk_far, wk), (wv_far, wv), (wo_far, wo))):
        fetches += in_rows(far, near, sems, 2 * i, 2)
    when_first(started(fetches))

    cols = wq.shape[1]
    gain_row, shift_row = line(gain), line(shift)
    for at in range(0, x_ref.shape[0], SLAB):
        slab = slice(at, at + SLAB)
        unit, _ = unit_rows(x_ref[slab, :])
        normed_ref[slab, :] = (unit * gain_row + shift_row).astype(BF16)
    normed = normed_ref[...]
    low, high = lane_halves(cols)
    when_first(arrived(fetches))
    queries = (product(normed, wq[...], (1, 0)) + line(bq)) * SCALE
    keys = product(normed, wk[...], (1, 0)).astype(BF16)
    values = (product(normed, wv[...], (1, 0)) + line(bv)).astype(BF16)
    qkv_ref[:, :cols] = queries.astype(BF16)
    qkv_ref[:, cols : 2 * cols] = keys
    qkv_ref[:, 2 * cols :] = values
    split = ((queries * low).astype(BF16), (queries * high).astype(BF16))
    seg_row = seg_ref[pl.ds(pl.program_id(0) + first_row, 1), :].astype(F32)
    length = seg_row.shape[1]
    seg_col = jnp.broadcast_to(seg_row, (128, length)).T
    same = jnp.concatenate([seg_col] * (length // 128), axis=1) == seg_row
    first = lax.broadcasted_iota(jnp.int32, (1, PAIR), 1) < HD
    scores, probs, made = {}, {}, {}

    def score(head):
        part = slice(head // 2 * PAIR, head // 2 * PAIR + PAIR)
        scores[head] = product(keys[:, part], split[head % 2][:, part], (1, 1))

    def soften(head):
        masked = jnp.where(same, scores.pop(head), MASKED)
        expo = jnp.exp(masked - jnp.max(masked, axis=0, keepdims=True))
        probs[head] = (expo * (1.0 / column_sum(expo))).astype(BF16)
        probs_ref[0, head] = probs[head]

    def gather(head):
        part = slice(head // 2 * PAIR, head // 2 * PAIR + PAIR)
        made[head] = product(probs.pop(head), values[:, part], (0, 0))
        if head % 2:
            context_ref[:, part] = jnp.where(first, made.pop(head - 1), made.pop(head)).astype(BF16)

    in_turn((score, soften, gather), cols // HD)
    out_ref[...] = product(context_ref[...], wo[...], (1, 0)) + 0.5 * (x_ref[...] + line(bo))


def whole(array):
    zeros = (0,) * array.ndim
    return pl.BlockSpec(array.shape, lambda i: zeros, pipeline_mode=pl.Buffered(1))


def rows_of(length, width):
    return pl.BlockSpec((length, width), lambda i: (i, 0))


def cost(name, flops, moved):
    weight = COSTS[name]
    return pl.CostEstimate(
        flops=int(weight * flops), bytes_accessed=int(weight * moved), transcendentals=0
    )


def params(limit=26 << 20):
    return pltpu.CompilerParams(vmem_limit_bytes=limit)


def attend(x, segments, gain, shift, wq, bq, wk, wv, bv, wo, bo, first_row, count, made):
    rows, length = segments.shape
    tokens, width = x.shape
    cols = wq.shape[1]
    heads = cols // HD
    at = lambda w: pl.BlockSpec((length, w), lambda i: (i + first_row, 0))
    shape = lambda w, kind: jax.ShapeDtypeStruct((tokens, w), kind)
    fixed = (segments, gain, shift, bq, bv, bo)
    weights = (wq, wk, wv, wo)
    done = tokens * count // rows
    return pl.pallas_call(
        lambda *refs: attend_kernel(*refs, first_row=first_row),
        grid=(count,),
        in_specs=[whole(w) for w in fixed]
        + [pl.BlockSpec(memory_space=pl.ANY)] * len(weights)
        + [at(width)]
        + [pl.BlockSpec(memory_space=pl.ANY)] * len(made),
        out_specs=[
            at(width),
            at(3 * cols),
            pl.BlockSpec((1, heads, length, length), lambda i: (i + first_row, 0, 0, 0)),
            at(cols),
            rows_of(length, width),
        ],
        out_shape=[
            shape(width, BF16),
            shape(3 * cols, BF16),
            jax.ShapeDtypeStruct((rows, heads, length, length), BF16),
            shape(cols, BF16),
            jax.ShapeDtypeStruct((count * length, width), F32),
        ],
        input_output_aliases={len(fixed) + len(weights) + 1 + i: i for i in range(len(made))},
        scratch_shapes=[pltpu.VMEM(w.shape, w.dtype) for w in weights]
        + [pltpu.SemaphoreType.DMA((2 * len(weights),))],
        name="attend",
        cost_estimate=cost("attend",
            8 * done * width * cols + 4 * done * length * cols,
            done * (10 * width + 8 * cols + 2 * heads * length) + 8 * width * cols,
        ),
        compiler_params=params(BIG),
    )(*fixed, *weights, x, *made)


def forward_kernel(*refs, count, rows, rows_low, widths):
    tables, refs = refs[:count], refs[count:]
    mine_low, mine_high, other_low, other_high, top_ref, gain, shift, b_up, w_up, w_down = refs[:10]
    middle_ref, down_ref, back_ref, by_top, by_up = refs[10:15]
    outs, refs = refs[15:-14], refs[-14:]
    up_near, down_near, tops, turned_top, turned, acts, slopes, down_total, up_total = refs[:9]
    normed, up_sems, down_sems, down_outs, up_outs = refs[9:]
    step, length = pl.program_id(0), top_ref.shape[0]
    here = pl.ds(pl.multiple_of(step % rows * length, length), length)
    ups, downs = in_rows(w_up, up_near, up_sems, 0, 4), in_rows(w_down, down_near, down_sems, 0, 4)
    hidden = up_near.shape[1]
    of_down = pieces_of([(turned_top, acts, 0, hidden)], 0, widths)
    of_up = pieces_of([(turned, slopes, 0, hidden)], hidden, widths)
    down_args = (tables, outs, of_down, widths, down_total, down_outs)
    up_args = (tables, outs, of_up, widths, up_total, up_outs)
    when_first(started(ups + downs))

    @pl.when(step < rows)
    def _():
        bias_up, gain_row, shift_row, top_sum = line(b_up), line(gain), line(shift), 0.0
        for at in range(0, length, SLAB):
            slab = slice(at, at + SLAB)
            middle = either(mine_low, mine_high, rows_low, slab) + either(
                other_low, other_high, rows_low, slab
            )
            middle_ref[slab, :] = middle
            unit, _ = unit_rows(middle)
            normed[slab, :] = (unit * gain_row + shift_row).astype(BF16)
            top_sum += column_sum(top_ref[slab, :])
        add_up(by_top, top_sum)
        tops[here, :] = top_ref[...].astype(BF16)
        turned_top[:, here] = tops[here, :].T
        turned[:, here] = normed[...].T
        when_first(arrived(ups))
        for at in range(0, hidden, STEP):
            units = slice(at, at + STEP)
            u = product(normed[...], up_near[:, units], (1, 0)) + bias_up[:, units]
            square = u * u
            bend = jnp.tanh(u * (CURVE + (CURVE * CUBIC) * square))
            above = 0.5 + 0.5 * bend
            act = u * above
            acts[here, units] = act.astype(BF16)
            slope = above + act * (1.0 - bend) * (CURVE + (3.0 * CURVE * CUBIC) * square)
            slopes[here, units] = slope.astype(BF16)

    @pl.when(step == rows - 1)
    def _():
        leaving(*down_args, True)

    @pl.when(step == rows)
    def _():
        arrived(downs)()
        by_up[...] = jnp.zeros_like(by_up)

    @pl.when(step >= rows)
    def _():
        for at in range(0, hidden, STEP):
            units = slice(at, at + STEP)
            grad = product(tops[here, :], down_near[units, :], (1, 1))
            grad = (grad * slopes[here, units].astype(F32)).astype(BF16)
            slopes[here, units] = grad
            by_up[:, units] += column_sum(grad.astype(F32))
        back_ref[...] = product(slopes[here, :], up_near[...], (1, 1))
        down_ref[...] = product(acts[here, :], down_near[...], (1, 0))

    @pl.when(step == 2 * rows - 1)
    def _():
        leave(*up_args)
        arrived(leaving(*down_args, False))()


def forward(mines, others, top, gain, shift, w_up, b_up, w_down, length, tables, widths):
    tokens, width = top.shape
    hidden = w_up.shape[1]
    rows, low = tokens // length, mines[0].shape[0] // length
    first = lambda i: jnp.minimum(i, rows - 1)
    low_spec = pl.BlockSpec((length, width), lambda i: (jnp.minimum(i, low - 1), 0))
    high_spec = pl.BlockSpec((length, width), lambda i: (jnp.clip(i - low, 0, rows - low - 1), 0))
    up_spec = pl.BlockSpec((length, width), lambda i: (first(i), 0))
    back_spec = pl.BlockSpec((length, width), lambda i: (jnp.maximum(i - rows, 0), 0))
    sum_spec = lambda w: pl.BlockSpec((1, w), lambda i: (0, 0))
    shape = lambda *dims: jax.ShapeDtypeStruct(dims, F32)
    anywhere = pl.BlockSpec(memory_space=pl.ANY)
    outs, copies = gradient_outs(tables, widths, width)
    fixed = (gain, shift, b_up)
    made = pl.pallas_call(
        lambda *refs: forward_kernel(
            *refs, count=len(tables), rows=rows, rows_low=low, widths=widths
        ),
        grid=(2 * rows,),
        in_specs=[table_spec()] * len(tables)
        + [low_spec, high_spec] * 2
        + [up_spec]
        + [whole(w) for w in fixed]
        + [anywhere] * 2,
        out_specs=[up_spec, back_spec, back_spec, sum_spec(width), sum_spec(hidden)]
        + [anywhere] * len(outs),
        out_shape=[shape(tokens, width)] * 3 + [shape(1, width), shape(1, hidden)] + outs,
        scratch_shapes=[
            pltpu.VMEM(w_up.shape, BF16),
            pltpu.VMEM(w_down.shape, BF16),
            pltpu.VMEM((tokens, width), BF16),
            pltpu.VMEM((width, tokens), BF16),
            pltpu.VMEM((width, tokens), BF16),
            pltpu.VMEM((tokens, hidden), BF16),
            pltpu.VMEM((tokens, hidden), BF16),
            pltpu.VMEM((width, hidden), F32),
            pltpu.VMEM((width, hidden), F32),
            pltpu.VMEM((length, width), BF16),
            pltpu.SemaphoreType.DMA((4,)),
            pltpu.SemaphoreType.DMA((4,)),
            pltpu.SemaphoreType.DMA((copies,)),
            pltpu.SemaphoreType.DMA((copies,)),
        ],
        name="forward",
        cost_estimate=cost(
            "forward",
            12 * tokens * width * hidden,
            tokens * 24 * width + 12 * width * hidden,
        ),
        compiler_params=params(BIG),
    )(*tables, *mines, *others, top, *fixed, w_up, w_down)
    return made[:5], made[5:]


def attend_back_kernel(*refs, count, widths):
    tables, refs = refs[:count], refs[count:]
    mine, other, refs = refs[0], refs[1], refs[2:]
    top_ref, middle_ref, gain, qkv_ref, probs_ref, normed_ref, context_ref = refs[:7]
    wo_far, wq_far, wk_far, wv_far = refs[7:11]
    grad_middle_ref, back_ref, sum_gain, sum_shift, sum_out, sum_qkv = refs[11:17]
    outs, refs = refs[17:-12], refs[-12:]
    rounded, grad_qkv_ref, contexts, turned, turned_two, total, wo, wq, wk, wv = refs[:10]
    sems, out_sems = refs[10:]
    cols, length = wq.shape[1], top_ref.shape[0]
    here = step_rows(length)
    fetches = []
    for i, (far, near) in enumerate(((wo_far, wo), (wq_far, wq), (wk_far, wk), (wv_far, wv))):
        fetches += in_rows(far, near, sems, 2 * i, 2)
    when_first(started(fetches))
    gain_row, by_gain, by_shift, by_out = line(gain), 0.0, 0.0, 0.0
    for at in range(0, length, SLAB):
        slab = slice(at, at + SLAB)
        unit, inv_std = unit_rows(middle_ref[slab, :])
        grad_normed = mine[slab, :] + other[slab, :]
        by_gain += column_sum(grad_normed * unit)
        by_shift += column_sum(grad_normed)
        grad_middle = top_ref[slab, :] + norm_back(grad_normed, unit, inv_std, gain_row)
        grad_middle_ref[slab, :] = grad_middle
        by_out += column_sum(grad_middle)
        rounded[slab, :] = grad_middle.astype(BF16)
    add_up(sum_gain, by_gain)
    add_up(sum_shift, by_shift)
    add_up(sum_out, by_out)
    turned[:, here] = normed_ref[...].T
    turned_two[:, here] = rounded[...].T
    contexts[here, :] = context_ref[...]
    when_first(arrived(fetches))
    grad_context = product(rounded[...], wo[...], (1, 1)).astype(BF16).astype(F32)
    low, high = lane_halves(cols)
    split = ((grad_context * low).astype(BF16), (grad_context * high).astype(BF16))
    first = lax.broadcasted_iota(jnp.int32, (1, PAIR), 1) < HD
    grad_probs, grad_scores, made = {}, {}, {}

    def at(head, which):
        start = which * cols + head // 2 * PAIR
        return slice(start, start + PAIR)

    def spread(head):
        grad_probs[head] = product(
            qkv_ref[:, at(head, 2)], split[head % 2][:, at(head, 0)], (1, 1)
        )

    def soften(head):
        wide = probs_ref[0, head].astype(F32)
        moved = wide * grad_probs.pop(head)
        grad_scores[head] = (moved - wide * column_sum(moved)).astype(BF16)

    def gather(head):
        grads = grad_scores.pop(head)
        made[head] = (
            product(grads, qkv_ref[:, at(head, 1)], (0, 0)),
            product(grads, qkv_ref[:, at(head, 0)], (1, 0)),
            product(probs_ref[0, head], split[head % 2][:, at(head, 0)], (1, 0)),
        )
        if head % 2:
            even, odd = made.pop(head - 1), made.pop(head)
            grad_query = jnp.where(first, even[0], odd[0]) * SCALE
            grad_qkv_ref[here, at(head, 0)] = grad_query.astype(BF16)
            grad_qkv_ref[here, at(head, 1)] = jnp.where(first, even[1], odd[1]).astype(BF16)
            grad_qkv_ref[here, at(head, 2)] = (even[2] + odd[2]).astype(BF16)

    in_turn((spread, soften, gather), cols // HD)
    grads = grad_qkv_ref[here, :]
    add_up(sum_qkv, column_sum(grads.astype(F32)))
    back_ref[...] = (
        product(grads[:, :cols], wq[...], (1, 1))
        + product(grads[:, cols : 2 * cols], wk[...], (1, 1))
        + product(grads[:, 2 * cols :], wv[...], (1, 1))
    )
    pieces = pieces_of(
        [(turned, grad_qkv_ref, 0, 3 * cols), (turned_two, contexts, 0, cols)], 0, widths
    )
    pl.when(last_step())(lambda: leave(tables, outs, pieces, widths, total, out_sems))


def attend_back(
    top, mine, other, middle, gain, wo, qkv, probs, normed, context, wq, wk, wv, tables, widths
):
    tokens, width = top.shape
    rows, heads, length, _ = probs.shape
    cols = wq.shape[1]
    line = lambda w: jax.ShapeDtypeStruct((1, w), F32)
    fixed = lambda w: pl.BlockSpec((1, w), lambda i: (0, 0))
    weights = (wo, wq, wk, wv)
    outs, copies = gradient_outs(tables, widths, width)
    anywhere = pl.BlockSpec(memory_space=pl.ANY)
    made = pl.pallas_call(
        lambda *refs: attend_back_kernel(*refs, count=len(tables), widths=widths),
        grid=(rows,),
        in_specs=[table_spec()] * len(tables)
        + [rows_of(length, width)] * 4
        + [whole(gain), rows_of(length, 3 * cols)]
        + [pl.BlockSpec((1, heads, length, length), lambda i: (i, 0, 0, 0))]
        + [rows_of(length, width), rows_of(length, cols)]
        + [anywhere] * len(weights),
        out_specs=[rows_of(length, width)] * 2
        + [fixed(width), fixed(width), fixed(width), fixed(3 * cols)]
        + [anywhere] * len(outs),
        out_shape=[jax.ShapeDtypeStruct((tokens, width), F32)] * 2
        + [line(width), line(width), line(width), line(3 * cols)]
        + outs,
        scratch_shapes=[
            pltpu.VMEM((length, width), BF16),
            pltpu.VMEM((tokens, 3 * cols), BF16),
            pltpu.VMEM((tokens, cols), BF16),
            pltpu.VMEM((width, tokens), BF16),
            pltpu.VMEM((width, tokens), BF16),
            pltpu.VMEM((width, 4 * cols), F32),
        ]
        + [pltpu.VMEM(w.shape, w.dtype) for w in weights]
        + [
            pltpu.SemaphoreType.DMA((2 * len(weights),)),
            pltpu.SemaphoreType.DMA((copies,)),
        ],
        name="back",
        cost_estimate=cost(
            "back",
            16 * tokens * width * cols + 8 * tokens * length * cols,
            tokens * (26 * width + 8 * cols + 2 * heads * length) + 24 * width * cols,
        ),
        compiler_params=params(BIG),
    )(*tables, mine, other, top, middle, gain, qkv, probs, normed, context, *weights)
    return made[:6], made[6:]


def first_back_kernel(*refs):
    mine, other, refs = refs[0], refs[1], refs[2:]
    x_ref, above, gain, qkv_sum, out_sum, gain_two, shift_two, up_sum, top_sum = refs[:9]
    out_ref, smalls_ref, sum_gain, sum_shift = refs[9:]
    gain_row, by_gain, by_shift = line(gain), 0.0, 0.0
    for at in range(0, x_ref.shape[0], SLAB):
        slab = slice(at, at + SLAB)
        unit, inv_std = unit_rows(x_ref[slab, :])
        grad_normed = mine[slab, :] + other[slab, :]
        by_gain += column_sum(grad_normed * unit)
        by_shift += column_sum(grad_normed)
        out_ref[slab, :] = above[slab, :] + norm_back(grad_normed, unit, inv_std, gain_row)
    add_up(sum_gain, by_gain)
    add_up(sum_shift, by_shift)

    @pl.when(pl.program_id(0) == pl.num_programs(0) - 1)
    def _():
        smalls_ref[...] = jnp.zeros_like(smalls_ref)
        cols = qkv_sum.shape[1] // 3
        to = 0
        for ref, start, size in (
            (sum_gain, 0, sum_gain.shape[1]),
            (sum_shift, 0, sum_shift.shape[1]),
            (qkv_sum, 0, cols),
            (qkv_sum, 2 * cols, cols),
            (out_sum, 0, out_sum.shape[1]),
            (gain_two, 0, gain_two.shape[1]),
            (shift_two, 0, shift_two.shape[1]),
            (up_sum, 0, up_sum.shape[1]),
            (top_sum, 0, top_sum.shape[1]),
        ):
            wide = smalls_ref.shape[2]
            for at in range(0, size, wide):
                count = min(wide, size - at)
                smalls_ref[0, to : to + 1, :count] = ref[:, start + at : start + at + count]
                to += 1
            to += to % 2


def first_back(x, mine, other, above, gain, sums, length, shape):
    tokens, width = x.shape
    cols = sums[0].shape[1] // 3
    sizes = [width, width, cols, cols] + [array.shape[1] for array in sums[1:]]
    grad_x, smalls = pl.pallas_call(
        first_back_kernel,
        grid=(tokens // length,),
        in_specs=[rows_of(length, width)] * 4
        + [whole(w) for w in (gain, *sums)],
        out_specs=[rows_of(length, width), pl.BlockSpec(shape, lambda i: (0, 0, 0))],
        out_shape=[
            jax.ShapeDtypeStruct((tokens, width), F32),
            jax.ShapeDtypeStruct(shape, F32),
        ],
        scratch_shapes=[pltpu.VMEM((1, width), F32)] * 2,
        name="first",
        cost_estimate=cost("first", 20 * tokens * width, 20 * tokens * width),
        compiler_params=params(),
    )(mine, other, x, above, gain, *sums)
    return grad_x, smalls, sizes


def from_partner(part):
    return lax.ppermute(part, "mp", [(0, 1), (1, 0)])


ORDERS = {"a": ("xynf", "yfxn"), "b": ("fnxy", "nyfx"), "q": ("xfyn", "xyfn"), "r": ("nyxf", "yxnf")}
SIXTHS = {"a": 4, "b": 2, "q": 3, "r": 3}


def orders_for(kind, bits):
    orders = []
    for names in kind:
        order = ["xynf".index(name) for name in names]
        order = [b for b in order if b < bits] + list(range(4, bits))
        orders.append([1 << b for b in order])
    return orders


def order_of_member(orders, member):
    return orders[member % 2]


def block_table(orders, bits):
    me = lax.axis_index("dp")
    count = 1 << bits
    masks = []
    for order in orders:
        masks.append(
            [
                sum(order[k] for k in range(bits) if r >> (bits - 1 - k) & 1)
                for r in range(count)
            ]
        )
    masks = jnp.asarray(masks, jnp.int32)
    return masks[lax.axis_index("mp") % 2] ^ me.astype(jnp.int32)


def exchange(array, orders, stage):
    dp, mp = lax.axis_size("dp"), lax.axis_size("mp")
    pairs = []
    for d in range(dp):
        for m in range(mp):
            pairs.append((d * mp + m, (d ^ order_of_member(orders, m)[stage]) * mp + m))
    return lax.ppermute(array, ("dp", "mp"), pairs)


def last_block(array):
    last = array.shape[0] - 1
    return pl.BlockSpec((1, *array.shape[1:]), lambda i: (last, 0, 0))


def add_kernel(*refs, counts, riders):
    outs, at = refs[sum(counts) + riders :], riders
    for k, count in enumerate(counts):
        total = refs[at][...]
        for ref in refs[at + 1 : at + count]:
            total = total + ref[...]
        if riders and not k:
            blocks = outs[k].shape[0] - 1
            outs[k][:blocks] = total
            outs[k][blocks:] = refs[0][...] + refs[1][...]
        else:
            outs[k][...] = total
        at += count


class Scatter:
    def __init__(self, send, keep, orders):
        self.keep, self.orders = keep, orders
        self.got, self.riders = [exchange(send, orders, 0)], ()

    def board(self, block):
        self.riders = (block, exchange(block, self.orders, 0))

    def take(self, after):
        self.got[-1] = lax.optimization_barrier((self.got[-1], after))[0]
        return [self.keep, *self.got]


def advance(scatters, after, passing=()):
    arrays = [scatter.take(after) for scatter in scatters]
    riders = list(scatters[0].riders)
    stage = len(scatters[0].got)
    half = scatters[0].keep.shape[0] >> stage
    step = half if riders or half == 1 else half // 2
    shapes, in_specs, out_specs = [], [last_block(array) for array in riders], []
    for k, group in enumerate(arrays):
        kept = group[0].shape[1:]
        more = 1 if riders and not k else 0
        spec = pl.BlockSpec((step, *kept), lambda i: (i + half // step, 0, 0))
        in_specs += [spec] * len(group)
        out_specs.append(pl.BlockSpec((step + more, *kept), lambda i: (i, 0, 0)))
        shapes.append(jax.ShapeDtypeStruct((half + more, *kept), F32))
    flat = riders + [array for group in arrays for array in group]
    anywhere = [pl.BlockSpec(memory_space=pl.ANY)] * len(passing)
    counts = [len(group) for group in arrays]
    made = pl.pallas_call(
        lambda *refs: add_kernel(
            *refs[: len(flat)],
            *refs[len(flat) + len(passing) : len(flat) + len(passing) + len(counts)],
            counts=counts,
            riders=len(riders),
        ),
        grid=(half // step,),
        in_specs=in_specs + anywhere,
        out_specs=out_specs + anywhere,
        out_shape=shapes + [jax.ShapeDtypeStruct(array.shape, array.dtype) for array in passing],
        input_output_aliases={len(flat) + i: len(shapes) + i for i in range(len(passing))},
        name="add",
        cost_estimate=cost("add", 0, 4 * sum(math.prod(shape.shape) for shape in shapes)),
        compiler_params=params(),
    )(*flat, *passing)
    for scatter, send in zip(scatters, made):
        scatter.got.append(exchange(send, scatter.orders, stage))
        if scatter.riders:
            scatter.riders = (send, scatter.got[-1])
    return made[0], made[len(scatters) :]


def finish_kernel(*refs, counts, outs, riders):
    values, at = [], riders
    for count in counts:
        total = refs[at][0]
        for ref in refs[at + 1 : at + count]:
            total = total + ref[0]
        values.append(total)
        at += count
    for out_ref, pieces in zip(refs[at:], outs):
        to = 0
        for part, start, columns in pieces:
            out_ref[:, to : to + columns] = values[part][:, start : start + columns]
            to += columns
    if riders:
        refs[-1][...] = refs[0][0] + refs[1][0]


def finish(scatters, after, widths):
    arrays = [scatter.take(after) for scatter in scatters]
    riders = [array for scatter in scatters for array in scatter.riders]
    flat = [array for group in arrays for array in group]
    size, parts = flat[0].shape[1], [group[0].shape[2] for group in arrays]
    outs, first = [], 0
    for width in widths:
        pieces, end = [], first + width
        while first < end:
            index, start, left = place_of(first, parts)
            pieces.append((index, start, min(end - first, left)))
            first += min(end - first, left)
        outs.append(pieces)
    shapes = [(size, width) for width in widths] + [(size, parts[0])] * (len(riders) // 2)
    block = lambda array: pl.BlockSpec((1, *array.shape[1:]), lambda i: (0, 0, 0))
    return pl.pallas_call(
        lambda *refs: finish_kernel(
            *refs, counts=[len(group) for group in arrays], outs=outs, riders=len(riders)
        ),
        grid=(1,),
        in_specs=[last_block(array) for array in riders] + [block(array) for array in flat],
        out_specs=[pl.BlockSpec(shape, lambda i: (0, 0)) for shape in shapes],
        out_shape=[jax.ShapeDtypeStruct(shape, F32) for shape in shapes],
        name="finish",
        cost_estimate=cost("add", 0, 4 * len(flat) * size * max(parts)),
        compiler_params=params(),
    )(*riders, *flat)


def butterfly_bits(width):
    dp = lax.axis_size("dp")
    bits = dp.bit_length() - 1
    return bits if (1 << bits) == dp and bits >= 3 and width // dp % 8 == 0 else 0


def parted(block, sizes):
    out, at, wide = [], 0, block.shape[1]
    for size in sizes:
        rows = -(-size // wide)
        out.append(block[at : at + rows].reshape(-1)[:size])
        at += rows + rows % 2
    return out


def on_device(
    inputs,
    segment_ids,
    ln1_gain,
    ln1_bias,
    w_query,
    b_query,
    w_key,
    w_value,
    b_value,
    w_output,
    b_output,
    ln2_gain,
    ln2_bias,
    w_up,
    b_up,
    w_down,
    b_down,
    cotangent,
):
    rows, length, width = inputs.shape
    cols = w_query.shape[1]
    tokens = rows * length
    hidden = w_up.shape[1]
    row = lambda vector: vector.reshape(-1, 128)
    pin = lambda values, after: lax.optimization_barrier((values, after))[0]
    x = inputs.reshape(tokens, width)
    top = cotangent.reshape(tokens, width)
    bits = butterfly_bits(width)

    orders = {key: orders_for(ORDERS[key], bits) for key in ORDERS}
    widths = [2 * hidden * SIXTHS[key] // 6 for key in "ab"] + [4 * cols * SIXTHS[key] // 6 for key in "qr"]
    tables = {key: block_table(orders[key], bits) for key in ORDERS} if bits else {}

    most = rows - 1
    firsts = (
        row(ln1_gain), row(ln1_bias), w_query, row(b_query), w_key, w_value, row(b_value),
        w_output, row(b_output),
    )
    *made, out_low = attend(x, segment_ids, *firsts, 0, most, ())
    low_other = from_partner(out_low)
    *made, out_high = attend(x, segment_ids, *firsts, most, rows - most, made)
    high_other = from_partner(out_high)
    normed, qkv, probs, context = made
    (middle, down_mine, back_mine, sum_top, sum_up), grad_hidden = forward(
        (out_low, out_high), (low_other, high_other), top, row(ln2_gain), row(ln2_bias),
        w_up, row(b_up), w_down, length, [tables[key] for key in "ab" if bits], widths[:2],
    )
    back_other, down_other = from_partner(back_mine), from_partner(down_mine)
    if bits:
        hiddens = [
            Scatter(*grad_hidden[:2], orders["a"]), Scatter(*grad_hidden[2:], orders["b"])
        ]
    (
        grad_middle, first_mine, sum_gain_two, sum_shift_two, sum_out, sum_qkv,
    ), grad_heads = attend_back(
        top, back_mine, back_other, middle, row(ln2_gain), w_output, qkv, probs, normed, context,
        w_query, w_key, w_value, [tables[key] for key in "qr" if bits], widths[2:],
    )
    outcome = pin(middle, sum_qkv) + (down_mine + down_other) + b_down

    if bits:
        after, passed = advance(hiddens, outcome, (first_mine, grad_heads[0], grad_heads[2]))
        first_mine = passed[0]
        heads = [
            Scatter(passed[1], grad_heads[1], orders["q"]),
            Scatter(passed[2], grad_heads[3], orders["r"]),
        ]
    first_other = from_partner(first_mine)
    grad_x, smalls, sizes = first_back(
        x, first_mine, first_other, grad_middle, row(ln1_gain),
        (sum_qkv, sum_out, sum_gain_two, sum_shift_two, sum_up, sum_top), length,
        (1, width // (1 << bits) if bits else 48, widths[2]),
    )
    if bits:
        heads[0].board(smalls)
        after, _ = advance(heads, smalls)
        for _ in range(2, bits):
            after, _ = advance(hiddens, after)
            after, _ = advance(heads, after)
        out_down, out_up = finish(hiddens, after, (hidden,) * 2)
        out_query, out_key, out_value, out_output, smalls = finish(heads, out_up, (cols,) * 4)
    else:
        scatter = lambda whole: lax.psum_scatter(whole, "dp", scatter_dimension=0, tiled=True)
        out_down, out_up = scatter(grad_hidden[0][:, :hidden]), scatter(grad_hidden[0][:, hidden:])
        out_query, out_key, out_value, out_output = (
            scatter(grad_heads[0][:, at : at + cols]) for at in range(0, 4 * cols, cols)
        )
        smalls = lax.psum(smalls[0], "dp")
    out_down, out_output = out_down.T, out_output.T
    smalls = parted(smalls, sizes)
    shape = inputs.shape
    return (
        outcome.reshape(shape),
        grad_x.reshape(shape),
        smalls[0],
        smalls[1],
        out_query,
        smalls[2],
        out_key,
        out_value,
        smalls[3],
        out_output,
        smalls[4],
        smalls[5],
        smalls[6],
        out_up,
        smalls[7],
        out_down,
        smalls[8],
    )


def solution(mesh):
    return jax.shard_map(
        on_device,
        mesh=mesh,
        in_specs=(
            P("dp", None, None),
            P("dp", None),
            P(),
            P(),
            P(None, "mp"),
            P("mp"),
            P(None, "mp"),
            P(None, "mp"),
            P("mp"),
            P("mp", None),
            P(),
            P(),
            P(),
            P(None, "mp"),
            P("mp"),
            P("mp", None),
            P(),
            P("dp", None, None),
        ),
        out_specs=(
            P("dp", None, None),
            P("dp", None, None),
            P(),
            P(),
            P("dp", "mp"),
            P("mp"),
            P("dp", "mp"),
            P("dp", "mp"),
            P("mp"),
            P("mp", "dp"),
            P(),
            P(),
            P(),
            P("dp", "mp"),
            P("mp"),
            P("mp", "dp"),
            P(),
        ),
        check_vma=False,
    )
```

time: 1020 us -> 193 us (0.19); the launches traced: 1010 us -> 192 us
  waiting for transfers between devices: 750 us -> 71.2 us
  matrix products: 102 us -> 0 us
  Pallas kernels: 0 us -> 83.3 us
  blocking collectives: 77.8 us -> 0 us
  other arithmetic: 34.4 us -> 7.22 us
  starting transfers between devices: 0.59 us -> 26.9 us
  local copies, waits for them, and re-layouts: 26.8 us -> 2.84 us
  between operations: 14.6 us -> 0.99 us
    reduce_scatter x6 -> x0, waiting for transfers between devices: 710 us -> none  [the longest x1 142 us: on_device(): lax.psum_scatter(grad_w_up, 'dp', scatter_dimension=0, tiled=True)]
    dot_general x24 -> x0, matrix products: 102 us -> none  [the longest x6 28.3 us: left_product(): jnp.einsum('ta,tb->ab', left, right, preferred_element_type=jnp.float32)]
    pallas_call x0 -> x13, Pallas kernels: none -> 83.3 us  [the longest x1 30.4 us: forward(): pl.pallas_call(lambda *refs: forward_kernel(*refs, count=len(tables), row...]
    psum x1 -> x0, blocking collectives: 77.8 us -> none  [on_device(): lax.psum((grad_ln1_gain, grad_ln1_bias, grad_b_query, grad_b_value, grad_...]
    ppermute x0 -> x22, waiting for transfers between devices: none -> 71.2 us  [the longest x17 68.7 us: exchange(): return lax.ppermute(array, ('dp', 'mp'), pairs)]
    psum x3 -> x0, waiting for transfers between devices: 40.7 us -> none  [the longest x1 22.4 us: on_device(): attn_out = lax.psum(matmul(context_b, w_output), 'mp')]
    ppermute x0 -> x22, starting transfers between devices: none -> 26.9 us  [the longest x17 25.6 us: exchange(): return lax.ppermute(array, ('dp', 'mp'), pairs)]
    reduce_sum x9 -> x0, other arithmetic: 23.6 us -> none  [the longest x2 7.51 us: norm_back(): grad_gain = jnp.sum(grad_out * unit_rows, axis=0)]
  transfers between devices with their start and end apart: 9 -> 22, of which waited for: 8 -> 13; matrix products, arithmetic and copies ran while one was open for 5% -> 4% of each run, Pallas kernels for 0% -> 21%
where the time goes in v4:
time: 193 us; the launch traced here: 192 us
  Pallas kernels  83.3 us (43%)
  waiting for transfers between devices  71.2 us (37%)
  starting transfers between devices  26.9 us (14%)
  other arithmetic  7.22 us (4%)
  local copies, waits for them, and re-layouts  2.84 us (1%)
    ppermute x17, waiting for transfers between devices, exchange(): return lax.ppermute(array, ('dp', 'mp'), pairs)  68.7 us
    pallas_call x1, Pallas kernels, forward(): pl.pallas_call(lambda *refs: forward_kernel(*refs, count=len(tables), row...  30.4 us
    ppermute x17, starting transfers between devices, exchange(): return lax.ppermute(array, ('dp', 'mp'), pairs)  25.6 us
    pallas_call x1, Pallas kernels, attend_back(): pl.pallas_call(lambda *refs: attend_back_kernel(*refs, count=len(tables),...  25.4 us
    pallas_call x2, Pallas kernels, attend(): pl.pallas_call(lambda *refs: attend_kernel(*refs, first_row=first_row), g...  15.9 us
    add x1, other arithmetic, on_device(): outcome = pin(middle, sum_qkv) + (down_mine + down_other) + b_down  6.18 us
    pallas_call x6, Pallas kernels, advance(): pl.pallas_call(lambda *refs: add_kernel(*refs[:len(flat)], *refs[len(flat...  4.93 us
  transfers between devices with their start and end apart: 22, of which 13 were waited for; matrix products, arithmetic and copies ran while one was open for 4% of the time, Pallas kernels for 21%

profile of v4, /device:TPU:0, one launch (start us, length us, event | category | flops | bytes accessed | tf_op | source)
XLA Modules:
  0.0 192.5 jit_solution(7579991236605567615)
XLA Ops:
  0.7 10.3 %attend.2 = (bf16[1024,768]{1,0:T(8,128)(2,1)}, bf16[1024,1152]{1,0:T(8,128)(2,1)}, bf16[4,6,256,256]{3,2,1,0:T(8,128)(2,1)}, bf16[1024,384]{1,0:T(8,128)(2,1)}, f32[768,768]{1,0:T(8,128)}) custom-call(s32[4,256]{1,0:T(4,128)} %refs_0_.3, f32[6,128]{1,0:T(8,128)} %bitcast.25, f32[6,128]{1,0:T(8,128)} %bitcast.31, f32[3,128]{1,0:T(4,128)} %bitcast.38, ...), custom_call_target="tpu_custom_call" | custom-call | flops 21139292 | bytes 129761 | tf_op jit(solution)/shard_map/attend/pallas_call | solution.py:270
  11.5 5.6 %attend.3 = (bf16[1024,768]{1,0:T(8,128)(2,1)}, bf16[1024,1152]{1,0:T(8,128)(2,1)}, bf16[4,6,256,256]{3,2,1,0:T(8,128)(2,1)}, bf16[1024,384]{1,0:T(8,128)(2,1)}, f32[256,768]{1,0:T(8,128)}) custom-call(s32[4,256]{1,0:T(4,128)} %refs_0_.3, f32[6,128]{1,0:T(8,128)} %bitcast.26, ...), custom_call_target="tpu_custom_call", output_to_operand_aliasing={{0}: (11, {}), {1}: (12, {}), {2}: (13, {}), {3}: (14, {})} | custom-call | flops 7046430 | bytes 58982 | tf_op jit(solution)/shard_map/attend/pallas_call | solution.py:270
  17.7 1.9 collective-permute-done.1.refs_5_
  19.6 0.9 copy-done.16
  20.5 30.4 %forward.1 = (f32[1024,768]{1,0:T(8,128)}, f32[1024,768]{1,0:T(8,128)}, f32[1024,768]{1,0:T(8,128)}, f32[1,768]{1,0:T(1,128)}, f32[1,1536]{1,0:T(1,128)}, /*inde...) custom-call(s32[16]{0:T(128)} %get-tuple-element.165.refs_0_, ...), custom_call_target="tpu_custom_call" | custom-call | flops 144955152 | bytes 330301 | tf_op jit(solution)/shard_map/forward/pallas_call | solution.py:388
  51.5 2.6 %collective-permute-start.4 = (f32[8,48,2048]{2,1,0:T(8,128)}, f32[8,48,2048]{2,1,0:T(8,128)}, u32[]{:S(2)}, u32[]{:S(2)}) collective-permute-start(f32[8,48,2048]{2,1,0:T(8,128)} %get-tuple-element.103), channel_id=1, source_target_pairs={{0,2},{1,5},{2,0},{3,7},{4,6},{5,1},{6,4},{7,3},{8,10},{9,13},{10,... | collective-permute-start | bytes 9437192 | tf_op jit(solution)/shard_map/ppermute | solution.py:662
  54.1 2.6 %collective-permute-start.5 = (f32[8,48,1024]{2,1,0:T(8,128)}, f32[8,48,1024]{2,1,0:T(8,128)}, u32[]{:S(2)}, u32[]{:S(2)}) collective-permute-start(f32[8,48,1024]{2,1,0:T(8,128)} %get-tuple-element.106), channel_id=1, source_target_pairs={{0,16},{1,9},{2,18},{3,11},{4,20},{5,13},{6,22},{7,15},{8,24},{9,1... | collective-permute-start | bytes 4718600 | tf_op jit(solution)/shard_map/ppermute | solution.py:662
  57.2 25.4 %back.1 = (f32[1024,768]{1,0:T(8,128)}, f32[1024,768]{1,0:T(8,128)}, f32[1,768]{1,0:T(1,128)}, f32[1,768]{1,0:T(1,128)}, f32[1,768]{1,0:T(1,128)}, /*index=5*/f3...) custom-call(s32[16]{0:T(128)} %get-tuple-element.167.refs_0_, ...), custom_call_target="tpu_custom_call" | custom-call | flops 56371444 | bytes 338165 | tf_op jit(solution)/shard_map/back/pallas_call | solution.py:520
  82.7 6.2 %add_add_fusion = f32[1024,768]{1,0:T(8,128)} fusion(f32[1024,768]{1,0:T(8,128)} %get-tuple-element.100.refs_5_, f32[1024,768]{1,0:T(8,128)} %get-tuple-element.101, f32[1024,768]{1,0:T(8,128)} %collective-permute-done.3, f32[768]{0:T(1024)S(1)} %copy-done.17), kind=kLoop, calls=%fused_computation | loop fusion | flops 2359296 | bytes 12585984 | tf_op jit(solution)/shard_map/add | solution.py:858
  88.9 2.8 %collective-permute-done.5.refs_3_.refs_4_.refs_5_.refs_6_ = f32[8,48,1024]{2,1,0:T(8,128)} collective-permute-done((f32[8,48,1024]{2,1,0:T(8,128)}, f32[8,48,1024]{2,1,0:T(8,128)}, u32[]{:S(2)}, u32[]{:S(2)}) %collective-permute-start.5) | collective-permute-done | bytes 1572896 | tf_op jit(solution)/shard_map/ppermute | solution.py:662
  91.9 1.9 add.51
  93.9 2.5 %collective-permute-start.11 = (f32[4,48,2048]{2,1,0:T(8,128)S(1)}, f32[4,48,2048]{2,1,0:T(8,128)S(1)}, u32[]{:S(2)}, u32[]{:S(2)}) collective-permute-start(f32[4,48,2048]{2,1,0:T(8,128)S(1)} %get-tuple-element.127), channel_id=1, source_target_pairs={{0,4},{1,17},{2,6},{3,19},{4,0},{5,21},{6,2},{7,23},{8,12},{9,25},... | collective-permute-start | bytes 4718600 | tf_op jit(solution)/shard_map/ppermute | solution.py:662
  97.1 1.3 collective-permute-start.8
  99.6 3.8 %first.1 = (f32[1024,768]{1,0:T(8,128)}, f32[1,48,768]{2,1,0:T(8,128)S(1)}) custom-call(f32[1024,768]{1,0:T(8,128)S(1)} %get-tuple-element.111.refs_0_, f32[1024,768]{1,0:T(8,128)S(1)} %collective-permute-done.6.refs_1_, f32[1024,768]{1,0:T(8,128)S(1)} %bitcast.24, f32[1024,768]{1,0:T(8,128)S(1)} %copy-done.6, f32[6,128]{1,0:T(8,128)S(1)} %bitcast.27, ...), custom_call_target="tpu_custom_call" | custom-call | flops 157286 | bytes 157286 | tf_op jit(solution)/shard_map/first/pallas_call | solution.py:602
  103.4 1.1 collective-permute-start.7
  104.5 19.0 %collective-permute-done.9.refs_5_.refs_6_.refs_7_.refs_8_ = f32[8,48,768]{2,1,0:T(8,128)S(1)} collective-permute-done((f32[8,48,768]{2,1,0:T(8,128)S(1)}, f32[8,48,768]{2,1,0:T(8,128)S(1)}, u32[]{:S(2)}, u32[]{:S(2)}) %collective-permute-start.9) | collective-permute-done | bytes 1179680 | tf_op jit(solution)/shard_map/ppermute | solution.py:662
  123.5 2.4 %collective-permute-done.8.refs_3_ = f32[8,48,768]{2,1,0:T(8,128)S(1)} collective-permute-done((f32[8,48,768]{2,1,0:T(8,128)S(1)}, f32[8,48,768]{2,1,0:T(8,128)S(1)}, u32[]{:S(2)}, u32[]{:S(2)}) %collective-permute-start.8) | collective-permute-done | bytes 1179680 | tf_op jit(solution)/shard_map/ppermute | solution.py:662
  125.9 2.6 %collective-permute-done.7.refs_1_ = f32[1,48,768]{2,1,0:T(8,128)S(1)} collective-permute-done((f32[1,48,768]{2,1,0:T(8,128)S(1)}, f32[1,48,768]{2,1,0:T(8,128)S(1)}, u32[]{:S(2)}, u32[]{:S(2)}) %collective-permute-start.7) | collective-permute-done | bytes 147488 | tf_op jit(solution)/shard_map/ppermute | solution.py:662
  128.7 1.8 collective-permute-start.10
  130.7 9.7 %collective-permute-done.12.refs_5_.refs_6_.refs_7_ = f32[4,48,1024]{2,1,0:T(8,128)S(1)} collective-permute-done((f32[4,48,1024]{2,1,0:T(8,128)S(1)}, f32[4,48,1024]{2,1,0:T(8,128)S(1)}, u32[]{:S(2)}, u32[]{:S(2)}) %collective-permute-start.12) | collective-permute-done | bytes 786464 | tf_op jit(solution)/shard_map/ppermute | solution.py:662
  140.4 1.4 add.53
  142.0 4.7 %collective-permute-done.13.refs_7_.refs_8_.refs_9_ = f32[4,48,768]{2,1,0:T(8,128)S(1)} collective-permute-done((f32[4,48,768]{2,1,0:T(8,128)S(1)}, f32[4,48,768]{2,1,0:T(8,128)S(1)}, u32[]{:S(2)}, u32[]{:S(2)}) %collective-permute-start.13) | collective-permute-done | bytes 589856 | tf_op jit(solution)/shard_map/ppermute | solution.py:662
  146.7 11.8 %collective-permute-done.10.refs_1_.refs_4_ = f32[5,48,768]{2,1,0:T(8,128)S(1)} collective-permute-done((f32[5,48,768]{2,1,0:T(8,128)S(1)}, f32[5,48,768]{2,1,0:T(8,128)S(1)}, u32[]{:S(2)}, u32[]{:S(2)}) %collective-permute-start.10) | collective-permute-done | bytes 737312 | tf_op jit(solution)/shard_map/ppermute | solution.py:662
  158.7 4.0 %collective-permute-start.17 = (f32[2,48,768]{2,1,0:T(8,128)S(1)}, f32[2,48,768]{2,1,0:T(8,128)S(1)}, u32[]{:S(2)}, u32[]{:S(2)}) collective-permute-start(f32[2,48,768]{2,1,0:T(8,128)S(1)} %get-tuple-element.141), channel_id=1, source_target_pairs={{0,2},{1,9},{2,0},{3,11},{4,6},{5,13},{6,4},{7,15},{8,10},{9,1},{1... | collective-permute-start | bytes 884744 | tf_op jit(solution)/shard_map/ppermute | solution.py:662
  162.7 7.4 %collective-permute-done.15.refs_3_ = f32[2,48,2048]{2,1,0:T(8,128)S(1)} collective-permute-done((f32[2,48,2048]{2,1,0:T(8,128)S(1)}, f32[2,48,2048]{2,1,0:T(8,128)S(1)}, u32[]{:S(2)}, u32[]{:S(2)}) %collective-permute-start.15) | collective-permute-done | bytes 786464 | tf_op jit(solution)/shard_map/ppermute | solution.py:662
  170.1 1.2 add.55
  171.3 5.3 %collective-permute-start.19 = (f32[1,48,2048]{2,1,0:T(8,128)S(1)}, f32[1,48,2048]{2,1,0:T(8,128)S(1)}, u32[]{:S(2)}, u32[]{:S(2)}) collective-permute-start(f32[1,48,2048]{2,1,0:T(8,128)S(1)} %get-tuple-element.139), channel_id=1, source_target_pairs={{0,16},{1,9},{2,18},{3,11},{4,20},{5,13},{6,22},{7,15},{8,24},{9,1... | collective-permute-start | bytes 1179656 | tf_op jit(solution)/shard_map/ppermute | solution.py:662
  176.8 2.7 %collective-permute-start.18 = (f32[2,48,768]{2,1,0:T(8,128)S(1)}, f32[2,48,768]{2,1,0:T(8,128)S(1)}, u32[]{:S(2)}, u32[]{:S(2)}) collective-permute-start(f32[2,48,768]{2,1,0:T(8,128)S(1)} %get-tuple-element.143.refs_0_), channel_id=1, source_target_pairs={{0,8},{1,9},{2,10},{3,11},{4,12},{5,13},{6,14},{7,15},{8,0},{9,1},... | collective-permute-start | bytes 884744 | tf_op jit(solution)/shard_map/ppermute | solution.py:662
  179.5 5.6 %collective-permute-done.20.refs_9_ = f32[1,48,1024]{2,1,0:T(8,128)S(1)} collective-permute-done((f32[1,48,1024]{2,1,0:T(8,128)S(1)}, f32[1,48,1024]{2,1,0:T(8,128)S(1)}, u32[]{:S(2)}, u32[]{:S(2)}) %collective-permute-start.20) | collective-permute-done | bytes 196640 | tf_op jit(solution)/shard_map/ppermute | solution.py:662
  185.1 1.5 collective-permute-done.19.refs_4_
  186.7 2.1 %finish.2 = (f32[48,1536]{1,0:T(8,128)}, f32[48,1536]{1,0:T(8,128)}) custom-call(f32[8,48,2048]{2,1,0:T(8,128)S(1)} %copy-done, f32[8,48,2048]{2,1,0:T(8,128)} %collective-permute-done.4.refs_1_, f32[4,48,2048]{2,1,0:T(8,128)S(1)} %collective-permute-done.11.refs_2_, f32[2,48,2048]{2,1,0:T(8,128)S(1)} %collective-permute-done.15.refs_3_, ...), custom_call_target="tpu_custom_call" | custom-call | bytes 39321 | tf_op jit(solution)/shard_map/finish/pallas_call | solution.py:770
  188.7 1.1 collective-permute-done.21.refs_11_
  (76 shorter events, 7.8 us)
Async XLA Ops:
  10.9 8.7 %collective-permute-start = (f32[768,768]{1,0:T(8,128)}, f32[768,768]{1,0:T(8,128)}, u32[]{:S(2)}, u32[]{:S(2)}) collective-permute-start(f32[768,768]{1,0:T(8,128)} %get-tuple-element.87.refs_2_), channel_id=1, source_target_pairs={{0,1},{1,0},{2,3},{3,2},{4,5},{5,4},{6,7},{7,6},{8,9},{9,8},{10,11... | collective-permute-start | bytes 7077896 | tf_op jit(solution)/shard_map/ppermute | solution.py:621
  17.1 2.6 %collective-permute-start.1 = (f32[256,768]{1,0:T(8,128)}, f32[256,768]{1,0:T(8,128)S(1)}, u32[]{:S(2)}, u32[]{:S(2)}) collective-permute-start(f32[256,768]{1,0:T(8,128)} %get-tuple-element.92.refs_3_), channel_id=1, source_target_pairs={{0,1},{1,0},{2,3},{3,2},{4,5},{5,4},{6,7},{7,6},{8,9},{9,8},{10,11... | collective-permute-start | bytes 2359304 | tf_op jit(solution)/shard_map/ppermute | solution.py:621
  20.5 36.2 %copy-start.18 = (s32[2,16]{1,0:T(2,128)S(1)}, s32[2,16]{1,0:T(2,128)}, u32[]{:S(2)}) copy-start(s32[2,16]{1,0:T(2,128)} %constant.39.clone) | copy-start | bytes 388
  20.5 36.2 %copy-start.19 = (s32[2,16]{1,0:T(2,128)S(1)}, s32[2,16]{1,0:T(2,128)}, u32[]{:S(2)}) copy-start(s32[2,16]{1,0:T(2,128)} %constant.38.clone) | copy-start | bytes 388
  50.9 6.3 %collective-permute-start.2 = (f32[1024,768]{1,0:T(8,128)}, f32[1024,768]{1,0:T(8,128)}, u32[]{:S(2)}, u32[]{:S(2)}) collective-permute-start(f32[1024,768]{1,0:T(8,128)} %get-tuple-element.94.refs_2_), channel_id=1, source_target_pairs={{0,1},{1,0},{2,3},{3,2},{4,5},{5,4},{6,7},{7,6},{8,9},{9,8},{10,11... | collective-permute-start | bytes 9437192 | tf_op jit(solution)/shard_map/ppermute | solution.py:621
  51.1 31.6 %collective-permute-start.3 = (f32[1024,768]{1,0:T(8,128)}, f32[1024,768]{1,0:T(8,128)}, u32[]{:S(2)}, u32[]{:S(2)}) collective-permute-start(f32[1024,768]{1,0:T(8,128)} %get-tuple-element.101), channel_id=1, source_target_pairs={{0,1},{1,0},{2,3},{3,2},{4,5},{5,4},{6,7},{7,6},{8,9},{9,8},{10,11... | collective-permute-start | bytes 9437192 | tf_op jit(solution)/shard_map/ppermute | solution.py:621
  51.5 40.2 %collective-permute-start.4 = (f32[8,48,2048]{2,1,0:T(8,128)}, f32[8,48,2048]{2,1,0:T(8,128)}, u32[]{:S(2)}, u32[]{:S(2)}) collective-permute-start(f32[8,48,2048]{2,1,0:T(8,128)} %get-tuple-element.103), channel_id=1, source_target_pairs={{0,2},{1,5},{2,0},{3,7},{4,6},{5,1},{6,4},{7,3},{8,10},{9,13},{10,... | collective-permute-start | bytes 9437192 | tf_op jit(solution)/shard_map/ppermute | solution.py:662
  54.1 37.6 %collective-permute-start.5 = (f32[8,48,1024]{2,1,0:T(8,128)}, f32[8,48,1024]{2,1,0:T(8,128)}, u32[]{:S(2)}, u32[]{:S(2)}) collective-permute-start(f32[8,48,1024]{2,1,0:T(8,128)} %get-tuple-element.106), channel_id=1, source_target_pairs={{0,16},{1,9},{2,18},{3,11},{4,20},{5,13},{6,22},{7,15},{8,24},{9,1... | collective-permute-start | bytes 4718600 | tf_op jit(solution)/shard_map/ppermute | solution.py:662
  57.2 25.5 %copy-start.17 = (f32[768]{0:T(1024)S(1)}, f32[768]{0:T(1024)}, u32[]{:S(2)}) copy-start(f32[768]{0:T(1024)} %param.38) | copy-start | bytes 9220
  82.7 9.0 %copy-start = (f32[8,48,2048]{2,1,0:T(8,128)S(1)}, f32[8,48,2048]{2,1,0:T(8,128)}, u32[]{:S(2)}) copy-start(f32[8,48,2048]{2,1,0:T(8,128)} %get-tuple-element.102.refs_0_) | copy-start | bytes 9437188
  82.7 9.0 %copy-start.2 = (f32[8,48,1024]{2,1,0:T(8,128)S(1)}, f32[8,48,1024]{2,1,0:T(8,128)}, u32[]{:S(2)}) copy-start(f32[8,48,1024]{2,1,0:T(8,128)} %get-tuple-element.105.refs_2_.refs_3_.refs_4_.refs_5_) | copy-start | bytes 4718596
  82.7 9.0 %copy-start.5 = (f32[1024,768]{1,0:T(8,128)S(1)}, f32[1024,768]{1,0:T(8,128)}, u32[]{:S(2)}) copy-start(f32[1024,768]{1,0:T(8,128)} %get-tuple-element.108.refs_4_) | copy-start | bytes 9437188
  82.7 9.0 %copy-start.7 = (f32[8,48,768]{2,1,0:T(8,128)S(1)}, f32[8,48,768]{2,1,0:T(8,128)}, u32[]{:S(2)}) copy-start(f32[8,48,768]{2,1,0:T(8,128)} %get-tuple-element.109.refs_5_) | copy-start | bytes 3538948
  82.7 9.0 %copy-start.8 = (f32[8,48,768]{2,1,0:T(8,128)S(1)}, f32[8,48,768]{2,1,0:T(8,128)}, u32[]{:S(2)}) copy-start(f32[8,48,768]{2,1,0:T(8,128)} %get-tuple-element.110.refs_6_) | copy-start | bytes 3538948
  93.8 5.7 %collective-permute-start.6 = (f32[1024,768]{1,0:T(8,128)S(1)}, f32[1024,768]{1,0:T(8,128)S(1)}, u32[]{:S(2)}, u32[]{:S(2)}) collective-permute-start(f32[1024,768]{1,0:T(8,128)S(1)} %get-tuple-element.111.refs_0_), channel_id=1, source_target_pairs={{0,1},{1,0},{2,3},{3,2},{4,5},{5,4},{6,7},{7,6},{8,9},{9,8},{10,11... | collective-permute-start | bytes 9437192 | tf_op jit(solution)/shard_map/ppermute | solution.py:621
  93.9 46.6 %collective-permute-start.11 = (f32[4,48,2048]{2,1,0:T(8,128)S(1)}, f32[4,48,2048]{2,1,0:T(8,128)S(1)}, u32[]{:S(2)}, u32[]{:S(2)}) collective-permute-start(f32[4,48,2048]{2,1,0:T(8,128)S(1)} %get-tuple-element.127), channel_id=1, source_target_pairs={{0,4},{1,17},{2,6},{3,19},{4,0},{5,21},{6,2},{7,23},{8,12},{9,25},... | collective-permute-start | bytes 4718600 | tf_op jit(solution)/shard_map/ppermute | solution.py:662
  96.4 27.1 %collective-permute-start.9 = (f32[8,48,768]{2,1,0:T(8,128)S(1)}, f32[8,48,768]{2,1,0:T(8,128)S(1)}, u32[]{:S(2)}, u32[]{:S(2)}) collective-permute-start(f32[8,48,768]{2,1,0:T(8,128)S(1)} %get-tuple-element.124), channel_id=1, source_target_pairs={{0,8},{1,5},{2,10},{3,7},{4,12},{5,1},{6,14},{7,3},{8,0},{9,13},{1... | collective-permute-start | bytes 3538952 | tf_op jit(solution)/shard_map/ppermute | solution.py:662
  97.1 28.8 %collective-permute-start.8 = (f32[8,48,768]{2,1,0:T(8,128)S(1)}, f32[8,48,768]{2,1,0:T(8,128)S(1)}, u32[]{:S(2)}, u32[]{:S(2)}) collective-permute-start(f32[8,48,768]{2,1,0:T(8,128)S(1)} %get-tuple-element.121), channel_id=1, source_target_pairs={{0,2},{1,3},{2,0},{3,1},{4,6},{5,7},{6,4},{7,5},{8,10},{9,11},{10,... | collective-permute-start | bytes 3538952 | tf_op jit(solution)/shard_map/ppermute | solution.py:662
  98.4 42.0 %collective-permute-start.12 = (f32[4,48,1024]{2,1,0:T(8,128)S(1)}, f32[4,48,1024]{2,1,0:T(8,128)S(1)}, u32[]{:S(2)}, u32[]{:S(2)}) collective-permute-start(f32[4,48,1024]{2,1,0:T(8,128)S(1)} %get-tuple-element.129), channel_id=1, source_target_pairs={{0,8},{1,5},{2,10},{3,7},{4,12},{5,1},{6,14},{7,3},{8,0},{9,13},{1... | collective-permute-start | bytes 2359304 | tf_op jit(solution)/shard_map/ppermute | solution.py:662
  99.6 28.9 %copy-start.3 = (f32[8,48,768]{2,1,0:T(8,128)S(1)}, f32[8,48,768]{2,1,0:T(8,128)}, u32[]{:S(2)}) copy-start(f32[8,48,768]{2,1,0:T(8,128)} %get-tuple-element.120.refs_2_) | copy-start | bytes 3538948
  99.6 28.9 %copy-start.4 = (f32[8,48,768]{2,1,0:T(8,128)S(1)}, f32[8,48,768]{2,1,0:T(8,128)}, u32[]{:S(2)}) copy-start(f32[8,48,768]{2,1,0:T(8,128)} %get-tuple-element.123.refs_4_.refs_5_.refs_6_.refs_7_) | copy-start | bytes 3538948
  103.4 25.1 %collective-permute-start.7 = (f32[1,48,768]{2,1,0:T(8,128)S(1)}, f32[1,48,768]{2,1,0:T(8,128)S(1)}, u32[]{:S(2)}, u32[]{:S(2)}) collective-permute-start(f32[1,48,768]{2,1,0:T(8,128)S(1)} %get-tuple-element.119.refs_0_), channel_id=1, source_target_pairs={{0,2},{1,3},{2,0},{3,1},{4,6},{5,7},{6,4},{7,5},{8,10},{9,11},{10,... | collective-permute-start | bytes 442376 | tf_op jit(solution)/shard_map/ppermute | solution.py:662
  128.7 29.8 %collective-permute-start.10 = (f32[5,48,768]{2,1,0:T(8,128)S(1)}, f32[5,48,768]{2,1,0:T(8,128)S(1)}, u32[]{:S(2)}, u32[]{:S(2)}) collective-permute-start(f32[5,48,768]{2,1,0:T(8,128)S(1)} %get-tuple-element.126.refs_0_), channel_id=1, source_target_pairs={{0,16},{1,5},{2,18},{3,7},{4,20},{5,1},{6,22},{7,3},{8,24},{9,13},... | collective-permute-start | bytes 2211848 | tf_op jit(solution)/shard_map/ppermute | solution.py:662
  130.4 16.3 %collective-permute-start.13 = (f32[4,48,768]{2,1,0:T(8,128)S(1)}, f32[4,48,768]{2,1,0:T(8,128)S(1)}, u32[]{:S(2)}, u32[]{:S(2)}) collective-permute-start(f32[4,48,768]{2,1,0:T(8,128)S(1)} %get-tuple-element.133), channel_id=1, source_target_pairs={{0,4},{1,3},{2,6},{3,1},{4,0},{5,7},{6,2},{7,5},{8,12},{9,11},{10,... | collective-permute-start | bytes 1769480 | tf_op jit(solution)/shard_map/ppermute | solution.py:662
  141.9 28.3 %collective-permute-start.15 = (f32[2,48,2048]{2,1,0:T(8,128)S(1)}, f32[2,48,2048]{2,1,0:T(8,128)S(1)}, u32[]{:S(2)}, u32[]{:S(2)}) collective-permute-start(f32[2,48,2048]{2,1,0:T(8,128)S(1)} %get-tuple-element.131), channel_id=1, source_target_pairs={{0,8},{1,3},{2,10},{3,1},{4,12},{5,7},{6,14},{7,5},{8,0},{9,11},{1... | collective-permute-start | bytes 2359304 | tf_op jit(solution)/shard_map/ppermute | solution.py:662
  141.9 20.8 %collective-permute-start.16 = (f32[2,48,1024]{2,1,0:T(8,128)S(1)}, f32[2,48,1024]{2,1,0:T(8,128)S(1)}, u32[]{:S(2)}, u32[]{:S(2)}) collective-permute-start(f32[2,48,1024]{2,1,0:T(8,128)S(1)} %get-tuple-element.137), channel_id=1, source_target_pairs={{0,2},{1,17},{2,0},{3,19},{4,6},{5,21},{6,4},{7,23},{8,10},{9,25},... | collective-permute-start | bytes 1179656 | tf_op jit(solution)/shard_map/ppermute | solution.py:662
  158.6 18.0 %collective-permute-start.14 = (f32[3,48,768]{2,1,0:T(8,128)S(1)}, f32[3,48,768]{2,1,0:T(8,128)S(1)}, u32[]{:S(2)}, u32[]{:S(2)}) collective-permute-start(f32[3,48,768]{2,1,0:T(8,128)S(1)} %get-tuple-element.135.refs_0_), channel_id=1, source_target_pairs={{0,4},{1,17},{2,6},{3,19},{4,0},{5,21},{6,2},{7,23},{8,12},{9,25},... | collective-permute-start | bytes 1327112 | tf_op jit(solution)/shard_map/ppermute | solution.py:662
  158.7 18.0 %collective-permute-start.17 = (f32[2,48,768]{2,1,0:T(8,128)S(1)}, f32[2,48,768]{2,1,0:T(8,128)S(1)}, u32[]{:S(2)}, u32[]{:S(2)}) collective-permute-start(f32[2,48,768]{2,1,0:T(8,128)S(1)} %get-tuple-element.141), channel_id=1, source_target_pairs={{0,2},{1,9},{2,0},{3,11},{4,6},{5,13},{6,4},{7,15},{8,10},{9,1},{1... | collective-permute-start | bytes 884744 | tf_op jit(solution)/shard_map/ppermute | solution.py:662
  171.3 15.3 %collective-permute-start.19 = (f32[1,48,2048]{2,1,0:T(8,128)S(1)}, f32[1,48,2048]{2,1,0:T(8,128)S(1)}, u32[]{:S(2)}, u32[]{:S(2)}) collective-permute-start(f32[1,48,2048]{2,1,0:T(8,128)S(1)} %get-tuple-element.139), channel_id=1, source_target_pairs={{0,16},{1,9},{2,18},{3,11},{4,20},{5,13},{6,22},{7,15},{8,24},{9,1... | collective-permute-start | bytes 1179656 | tf_op jit(solution)/shard_map/ppermute | solution.py:662
  176.8 13.1 %collective-permute-start.18 = (f32[2,48,768]{2,1,0:T(8,128)S(1)}, f32[2,48,768]{2,1,0:T(8,128)S(1)}, u32[]{:S(2)}, u32[]{:S(2)}) collective-permute-start(f32[2,48,768]{2,1,0:T(8,128)S(1)} %get-tuple-element.143.refs_0_), channel_id=1, source_target_pairs={{0,8},{1,9},{2,10},{3,11},{4,12},{5,13},{6,14},{7,15},{8,0},{9,1},... | collective-permute-start | bytes 884744 | tf_op jit(solution)/shard_map/ppermute | solution.py:662
  179.4 5.7 %collective-permute-start.20 = (f32[1,48,1024]{2,1,0:T(8,128)S(1)}, f32[1,48,1024]{2,1,0:T(8,128)S(1)}, u32[]{:S(2)}, u32[]{:S(2)}) collective-permute-start(f32[1,48,1024]{2,1,0:T(8,128)S(1)} %get-tuple-element.145), channel_id=1, source_target_pairs={{0,4},{1,3},{2,6},{3,1},{4,0},{5,7},{6,2},{7,5},{8,12},{9,11},{10,... | collective-permute-start | bytes 589832 | tf_op jit(solution)/shard_map/ppermute | solution.py:662
  179.4 10.4 %collective-permute-start.21 = (f32[1,48,768]{2,1,0:T(8,128)S(1)}, f32[1,48,768]{2,1,0:T(8,128)S(1)}, u32[]{:S(2)}, u32[]{:S(2)}) collective-permute-start(f32[1,48,768]{2,1,0:T(8,128)S(1)} %get-tuple-element.149), channel_id=1, source_target_pairs={{0,16},{1,17},{2,18},{3,19},{4,20},{5,21},{6,22},{7,23},{8,24},{9,... | collective-permute-start | bytes 442376 | tf_op jit(solution)/shard_map/ppermute | solution.py:662
  (12 other events, 82.0 us)

commit v5 on v4

--- a/solution.py
+++ b/solution.py
@@ -15,7 +15,7 @@
 CURVE = math.sqrt(2.0 / math.pi)
 CUBIC = 0.044715
 COSTS = {"attend": 0.01, "forward": 0.01, "back": 0.01, "first": 0.01, "add": 0.01}
-BIG = 63 << 20
+BIG = 67043328
 STEP = 512
 SLAB = 64
 F32 = jnp.float32
@@ -94,6 +94,7 @@
 
 def leaving(tables, outs, pieces, widths, total, sems, make):
     copies, start = [], 0
+    me, even = lax.axis_index("dp"), lax.axis_index("mp") % 2 == 0
     for turned, right, at, columns, index, to in pieces:
         if make:
             total[:, start : start + columns] = product(
@@ -104,7 +105,8 @@
             table, send, keep = tables[index], outs[2 * index], outs[2 * index + 1]
             half, size, _ = send.shape
             for r in range(2 * half):
-                row = pl.multiple_of(table[r] * size, 8)
+                owner = jnp.where(even, table[0][r], table[1][r]) ^ me
+                row = pl.multiple_of(owner * size, 8)
                 far = send.at[r - half] if r >= half else keep.at[r]
                 fresh.append(
                     pltpu.make_async_copy(
@@ -158,17 +160,13 @@
 def gradient_outs(tables, widths, width):
     if not tables:
         return [jax.ShapeDtypeStruct((width, sum(widths)), F32)], 8
-    blocks = tables[0].shape[0]
+    blocks = len(tables[0][0])
     shapes = [
         jax.ShapeDtypeStruct((blocks // 2, width // blocks, columns), F32)
         for columns in widths
         for _ in range(2)
     ]
     return shapes, blocks * 6
-
-
-def table_spec():
-    return pl.BlockSpec(memory_space=pltpu.SMEM)
 
 
 def in_turn(stages, count):
@@ -300,8 +298,7 @@
     )(*fixed, *weights, x, *made)
 
 
-def forward_kernel(*refs, count, rows, rows_low, widths):
-    tables, refs = refs[:count], refs[count:]
+def forward_kernel(*refs, tables, rows, rows_low, widths):
     mine_low, mine_high, other_low, other_high, top_ref, gain, shift, b_up, w_up, w_down = refs[:10]
     middle_ref, down_ref, back_ref, by_top, by_up = refs[10:15]
     outs, refs = refs[15:-14], refs[-14:]
@@ -315,7 +312,8 @@
     of_up = pieces_of([(turned, slopes, 0, hidden)], hidden, widths)
     down_args = (tables, outs, of_down, widths, down_total, down_outs)
     up_args = (tables, outs, of_up, widths, up_total, up_outs)
-    when_first(started(ups + downs))
+    when_first(started(ups))
+    pl.when(step == 1)(started(downs))
 
     @pl.when(step < rows)
     def _():
@@ -387,11 +385,10 @@
     fixed = (gain, shift, b_up)
     made = pl.pallas_call(
         lambda *refs: forward_kernel(
-            *refs, count=len(tables), rows=rows, rows_low=low, widths=widths
+            *refs, tables=tables, rows=rows, rows_low=low, widths=widths
         ),
         grid=(2 * rows,),
-        in_specs=[table_spec()] * len(tables)
-        + [low_spec, high_spec] * 2
+        in_specs=[low_spec, high_spec] * 2
         + [up_spec]
         + [whole(w) for w in fixed]
         + [anywhere] * 2,
@@ -421,12 +418,11 @@
             tokens * 24 * width + 12 * width * hidden,
         ),
         compiler_params=params(BIG),
-    )(*tables, *mines, *others, top, *fixed, w_up, w_down)
+    )(*mines, *others, top, *fixed, w_up, w_down)
     return made[:5], made[5:]
 
 
-def attend_back_kernel(*refs, count, widths):
-    tables, refs = refs[:count], refs[count:]
+def attend_back_kernel(*refs, tables, widths):
     mine, other, refs = refs[0], refs[1], refs[2:]
     top_ref, middle_ref, gain, qkv_ref, probs_ref, normed_ref, context_ref = refs[:7]
     wo_far, wq_far, wk_far, wv_far = refs[7:11]
@@ -518,10 +514,9 @@
     outs, copies = gradient_outs(tables, widths, width)
     anywhere = pl.BlockSpec(memory_space=pl.ANY)
     made = pl.pallas_call(
-        lambda *refs: attend_back_kernel(*refs, count=len(tables), widths=widths),
+        lambda *refs: attend_back_kernel(*refs, tables=tables, widths=widths),
         grid=(rows,),
-        in_specs=[table_spec()] * len(tables)
-        + [rows_of(length, width)] * 4
+        in_specs=[rows_of(length, width)] * 4
         + [whole(gain), rows_of(length, 3 * cols)]
         + [pl.BlockSpec((1, heads, length, length), lambda i: (i, 0, 0, 0))]
         + [rows_of(length, width), rows_of(length, cols)]
@@ -552,7 +547,7 @@
             tokens * (26 * width + 8 * cols + 2 * heads * length) + 24 * width * cols,
         ),
         compiler_params=params(BIG),
-    )(*tables, mine, other, top, middle, gain, qkv, probs, normed, context, *weights)
+    )(mine, other, top, middle, gain, qkv, probs, normed, context, *weights)
     return made[:6], made[6:]
 
 
@@ -638,19 +633,14 @@
     return orders[member % 2]
 
 
-def block_table(orders, bits):
-    me = lax.axis_index("dp")
-    count = 1 << bits
-    masks = []
-    for order in orders:
-        masks.append(
-            [
-                sum(order[k] for k in range(bits) if r >> (bits - 1 - k) & 1)
-                for r in range(count)
-            ]
-        )
-    masks = jnp.asarray(masks, jnp.int32)
-    return masks[lax.axis_index("mp") % 2] ^ me.astype(jnp.int32)
+def block_masks(orders, bits):
+    return [
+        [
+            sum(order[k] for k in range(bits) if r >> (bits - 1 - k) & 1)
+            for r in range(1 << bits)
+        ]
+        for order in orders
+    ]
 
 
 def exchange(array, orders, stage):
@@ -749,10 +739,17 @@
             out_ref[:, to : to + columns] = values[part][:, start : start + columns]
             to += columns
     if riders:
-        refs[-1][...] = refs[0][0] + refs[1][0]
-
-
-def finish(scatters, after, widths):
+        block, row = refs[0][0] + refs[1][0], 0
+        for out_ref in refs[at + len(outs) :]:
+            count, wide = out_ref.shape[0], block.shape[1] // 128
+            for r in range(count):
+                start = r % wide * 128
+                out_ref[r : r + 1, :] = block[row + r // wide : row + r // wide + 1, start : start + 128]
+            rows = -(-count // wide)
+            row += rows + rows % 2
+
+
+def finish(scatters, after, widths, sizes=()):
     arrays = [scatter.take(after) for scatter in scatters]
     riders = [array for scatter in scatters for array in scatter.riders]
     flat = [array for group in arrays for array in group]
@@ -765,7 +762,7 @@
             pieces.append((index, start, min(end - first, left)))
             first += min(end - first, left)
         outs.append(pieces)
-    shapes = [(size, width) for width in widths] + [(size, parts[0])] * (len(riders) // 2)
+    shapes = [(size, width) for width in widths] + [(count // 128, 128) for count in sizes]
     block = lambda array: pl.BlockSpec((1, *array.shape[1:]), lambda i: (0, 0, 0))
     return pl.pallas_call(
         lambda *refs: finish_kernel(
@@ -828,7 +825,7 @@
 
     orders = {key: orders_for(ORDERS[key], bits) for key in ORDERS}
     widths = [2 * hidden * SIXTHS[key] // 6 for key in "ab"] + [4 * cols * SIXTHS[key] // 6 for key in "qr"]
-    tables = {key: block_table(orders[key], bits) for key in ORDERS} if bits else {}
+    tables = {key: block_masks(orders[key], bits) for key in ORDERS} if bits else {}
 
     most = rows - 1
     firsts = (
@@ -877,16 +874,18 @@
             after, _ = advance(hiddens, after)
             after, _ = advance(heads, after)
         out_down, out_up = finish(hiddens, after, (hidden,) * 2)
-        out_query, out_key, out_value, out_output, smalls = finish(heads, out_up, (cols,) * 4)
+        out_query, out_key, out_value, out_output, *smalls = finish(
+            heads, out_up, (cols,) * 4, sizes
+        )
+        smalls = [vector.reshape(-1) for vector in smalls]
     else:
         scatter = lambda whole: lax.psum_scatter(whole, "dp", scatter_dimension=0, tiled=True)
         out_down, out_up = scatter(grad_hidden[0][:, :hidden]), scatter(grad_hidden[0][:, hidden:])
         out_query, out_key, out_value, out_output = (
             scatter(grad_heads[0][:, at : at + cols]) for at in range(0, 4 * cols, cols)
         )
-        smalls = lax.psum(smalls[0], "dp")
+        smalls = parted(lax.psum(smalls[0], "dp"), sizes)
     out_down, out_output = out_down.T, out_output.T
-    smalls = parted(smalls, sizes)
     shape = inputs.shape
     return (
         outcome.reshape(shape),

time: 193 us -> 188 us (0.974)
  local copies, waits for them, and re-layouts: 2.84 us -> 0.08 us
  transfers between devices with their start and end apart: 22 -> 22, of which waited for: 13 -> 13; matrix products, arithmetic and copies ran while one was open for 4% -> 3% of each run, Pallas kernels for 21% -> 21%
where the time goes in v5:
time: 188 us
  Pallas kernels  82.9 us (44%)
  waiting for transfers between devices  70.4 us (37%)
  starting transfers between devices  26.9 us (14%)
  other arithmetic  6.18 us (3%)
    ppermute x17, waiting for transfers between devices, exchange(): return lax.ppermute(array, ('dp', 'mp'), pairs)  66.9 us
    pallas_call x1, Pallas kernels, forward(): pl.pallas_call(lambda *refs: forward_kernel(*refs, tables=tables, rows=ro...  29.9 us
    ppermute x17, starting transfers between devices, exchange(): return lax.ppermute(array, ('dp', 'mp'), pairs)  25.6 us
    pallas_call x1, Pallas kernels, attend_back(): pl.pallas_call(lambda *refs: attend_back_kernel(*refs, tables=tables, wid...  25.4 us
    pallas_call x2, Pallas kernels, attend(): pl.pallas_call(lambda *refs: attend_kernel(*refs, first_row=first_row), g...  15.9 us
    add x1, other arithmetic, on_device(): outcome = pin(middle, sum_qkv) + (down_mine + down_other) + b_down  6.18 us
    pallas_call x6, Pallas kernels, advance(): pl.pallas_call(lambda *refs: add_kernel(*refs[:len(flat)], *refs[len(flat...  4.93 us
    pallas_call x1, Pallas kernels, first_back(): pl.pallas_call(first_back_kernel, grid=(tokens // length,), in_specs=[row...  3.84 us
  transfers between devices with their start and end apart: 22, of which 13 were waited for; matrix products, arithmetic and copies ran while one was open for 3% of the time, Pallas kernels for 21%

profile of v5, /device:TPU:0, one launch (start us, length us, event | category | flops | bytes accessed | tf_op | source)
XLA Modules:
  0.0 187.5 jit_solution(7504555050050952637)
XLA Ops:
  0.7 10.3 %attend.2 = (bf16[1024,768]{1,0:T(8,128)(2,1)}, bf16[1024,1152]{1,0:T(8,128)(2,1)}, bf16[4,6,256,256]{3,2,1,0:T(8,128)(2,1)}, bf16[1024,384]{1,0:T(8,128)(2,1)}, f32[768,768]{1,0:T(8,128)}) custom-call(s32[4,256]{1,0:T(4,128)} %refs_0_.3, f32[6,128]{1,0:T(8,128)} %bitcast.26, f32[6,128]{1,0:T(8,128)} %bitcast.32, f32[3,128]{1,0:T(4,128)} %bitcast.39, ...), custom_call_target="tpu_custom_call" | custom-call | flops 21139292 | bytes 129761 | tf_op jit(solution)/shard_map/attend/pallas_call | solution.py:268
  11.5 5.6 %attend.3 = (bf16[1024,768]{1,0:T(8,128)(2,1)}, bf16[1024,1152]{1,0:T(8,128)(2,1)}, bf16[4,6,256,256]{3,2,1,0:T(8,128)(2,1)}, bf16[1024,384]{1,0:T(8,128)(2,1)}, f32[256,768]{1,0:T(8,128)}) custom-call(s32[4,256]{1,0:T(4,128)} %refs_0_.3, f32[6,128]{1,0:T(8,128)} %bitcast.27, ...), custom_call_target="tpu_custom_call", output_to_operand_aliasing={{0}: (11, {}), {1}: (12, {}), {2}: (13, {}), {3}: (14, {})} | custom-call | flops 7046430 | bytes 58982 | tf_op jit(solution)/shard_map/attend/pallas_call | solution.py:268
  17.2 2.6 %collective-permute-done.1.refs_3_ = f32[256,768]{1,0:T(8,128)} collective-permute-done((f32[256,768]{1,0:T(8,128)}, f32[256,768]{1,0:T(8,128)}, u32[]{:S(2)}, u32[]{:S(2)}) %collective-permute-start.1) | collective-permute-done | bytes 786464 | tf_op jit(solution)/shard_map/ppermute | solution.py:616
  19.8 29.9 %forward.1 = (f32[1024,768]{1,0:T(8,128)}, f32[1024,768]{1,0:T(8,128)}, f32[1024,768]{1,0:T(8,128)}, f32[1,768]{1,0:T(1,128)}, f32[1,1536]{1,0:T(1,128)}, /*inde...) custom-call(f32[768,768]{1,0:T(8,128)} %get-tuple-element.95.refs_0_, ...), custom_call_target="tpu_custom_call" | custom-call | flops 144955152 | bytes 330301 | tf_op jit(solution)/shard_map/forward/pallas_call | solution.py:386
  50.3 2.6 %collective-permute-start.4 = (f32[8,48,2048]{2,1,0:T(8,128)}, f32[8,48,2048]{2,1,0:T(8,128)}, u32[]{:S(2)}, u32[]{:S(2)}) collective-permute-start(f32[8,48,2048]{2,1,0:T(8,128)} %get-tuple-element.111), channel_id=1, source_target_pairs={{0,2},{1,5},{2,0},{3,7},{4,6},{5,1},{6,4},{7,3},{8,10},{9,13},{10,... | collective-permute-start | bytes 9437192 | tf_op jit(solution)/shard_map/ppermute | solution.py:652
  52.9 2.6 %collective-permute-start.5 = (f32[8,48,1024]{2,1,0:T(8,128)}, f32[8,48,1024]{2,1,0:T(8,128)}, u32[]{:S(2)}, u32[]{:S(2)}) collective-permute-start(f32[8,48,1024]{2,1,0:T(8,128)} %get-tuple-element.114), channel_id=1, source_target_pairs={{0,16},{1,9},{2,18},{3,11},{4,20},{5,13},{6,22},{7,15},{8,24},{9,1... | collective-permute-start | bytes 4718600 | tf_op jit(solution)/shard_map/ppermute | solution.py:652
  55.7 25.4 %back.1 = (f32[1024,768]{1,0:T(8,128)}, f32[1024,768]{1,0:T(8,128)}, f32[1,768]{1,0:T(1,128)}, f32[1,768]{1,0:T(1,128)}, f32[1,768]{1,0:T(1,128)}, /*index=5*/f3...) custom-call(f32[1024,768]{1,0:T(8,128)} %get-tuple-element.102.refs_, ...), custom_call_target="tpu_custom_call" | custom-call | flops 56371444 | bytes 338165 | tf_op jit(solution)/shard_map/back/pallas_call | solution.py:516
  81.3 6.2 %add_add_fusion = f32[1024,768]{1,0:T(8,128)} fusion(f32[1024,768]{1,0:T(8,128)} %get-tuple-element.108.refs_3_, f32[1024,768]{1,0:T(8,128)} %get-tuple-element.109, f32[1024,768]{1,0:T(8,128)} %collective-permute-done.3, f32[768]{0:T(1024)} %param.34), kind=kLoop, calls=%fused_computation | loop fusion | flops 2359296 | bytes 12585984 | tf_op jit(solution)/shard_map/add | solution.py:855
  87.4 3.0 %collective-permute-done.5.refs_3_.refs_4_.refs_5_.refs_6_ = f32[8,48,1024]{2,1,0:T(8,128)} collective-permute-done((f32[8,48,1024]{2,1,0:T(8,128)}, f32[8,48,1024]{2,1,0:T(8,128)}, u32[]{:S(2)}, u32[]{:S(2)}) %collective-permute-start.5) | collective-permute-done | bytes 1572896 | tf_op jit(solution)/shard_map/ppermute | solution.py:652
  90.6 1.9 %add.28 = (f32[4,48,2048]{2,1,0:T(8,128)S(1)}, f32[4,48,1024]{2,1,0:T(8,128)S(1)}, f32[1024,768]{1,0:T(8,128)S(1)}, f32[8,48,768]{2,1,0:T(8,128)S(1)}, f32[8,48,768]{2,1,0:T(8,128)S(1)}) custom-call(f32[8,48,2048]{2,1,0:T(8,128)S(1)} %copy-done, ...), custom_call_target="tpu_custom_call", output_to_operand_aliasing={{2}: (4, {}), {3}: (5, {}), {4}: (6, {})} | custom-call | bytes 23592 | tf_op jit(solution)/shard_map/add/pallas_call | solution.py:705
  92.6 2.5 %collective-permute-start.11 = (f32[4,48,2048]{2,1,0:T(8,128)S(1)}, f32[4,48,2048]{2,1,0:T(8,128)S(1)}, u32[]{:S(2)}, u32[]{:S(2)}) collective-permute-start(f32[4,48,2048]{2,1,0:T(8,128)S(1)} %get-tuple-element.135), channel_id=1, source_target_pairs={{0,4},{1,17},{2,6},{3,19},{4,0},{5,21},{6,2},{7,23},{8,12},{9,25},... | collective-permute-start | bytes 4718600 | tf_op jit(solution)/shard_map/ppermute | solution.py:652
  95.1 0.7 collective-permute-start.9
  95.9 1.3 collective-permute-start.8
  98.4 3.8 %first.1 = (f32[1024,768]{1,0:T(8,128)}, f32[1,48,768]{2,1,0:T(8,128)S(1)}) custom-call(f32[1024,768]{1,0:T(8,128)S(1)} %get-tuple-element.119.refs_0_, f32[1024,768]{1,0:T(8,128)S(1)} %collective-permute-done.6.refs_1_, f32[1024,768]{1,0:T(8,128)S(1)} %bitcast.25, f32[1024,768]{1,0:T(8,128)S(1)} %copy-done.6, f32[6,128]{1,0:T(8,128)S(1)} %bitcast.28, ...), custom_call_target="tpu_custom_call" | custom-call | flops 157286 | bytes 157286 | tf_op jit(solution)/shard_map/first/pallas_call | solution.py:597
  102.2 1.1 collective-permute-start.7
  103.3 19.0 %collective-permute-done.9.refs_5_.refs_6_.refs_7_.refs_8_ = f32[8,48,768]{2,1,0:T(8,128)S(1)} collective-permute-done((f32[8,48,768]{2,1,0:T(8,128)S(1)}, f32[8,48,768]{2,1,0:T(8,128)S(1)}, u32[]{:S(2)}, u32[]{:S(2)}) %collective-permute-start.9) | collective-permute-done | bytes 1179680 | tf_op jit(solution)/shard_map/ppermute | solution.py:652
  122.3 2.3 %collective-permute-done.8.refs_3_ = f32[8,48,768]{2,1,0:T(8,128)S(1)} collective-permute-done((f32[8,48,768]{2,1,0:T(8,128)S(1)}, f32[8,48,768]{2,1,0:T(8,128)S(1)}, u32[]{:S(2)}, u32[]{:S(2)}) %collective-permute-start.8) | collective-permute-done | bytes 1179680 | tf_op jit(solution)/shard_map/ppermute | solution.py:652
  124.6 2.7 %collective-permute-done.7.refs_1_ = f32[1,48,768]{2,1,0:T(8,128)S(1)} collective-permute-done((f32[1,48,768]{2,1,0:T(8,128)S(1)}, f32[1,48,768]{2,1,0:T(8,128)S(1)}, u32[]{:S(2)}, u32[]{:S(2)}) %collective-permute-start.7) | collective-permute-done | bytes 147488 | tf_op jit(solution)/shard_map/ppermute | solution.py:652
  127.5 1.7 collective-permute-start.10
  129.5 9.7 %collective-permute-done.12.refs_5_.refs_6_.refs_7_ = f32[4,48,1024]{2,1,0:T(8,128)S(1)} collective-permute-done((f32[4,48,1024]{2,1,0:T(8,128)S(1)}, f32[4,48,1024]{2,1,0:T(8,128)S(1)}, u32[]{:S(2)}, u32[]{:S(2)}) %collective-permute-start.12) | collective-permute-done | bytes 786464 | tf_op jit(solution)/shard_map/ppermute | solution.py:652
  139.2 1.4 add.30
  140.8 4.6 %collective-permute-done.13.refs_7_.refs_8_.refs_9_ = f32[4,48,768]{2,1,0:T(8,128)S(1)} collective-permute-done((f32[4,48,768]{2,1,0:T(8,128)S(1)}, f32[4,48,768]{2,1,0:T(8,128)S(1)}, u32[]{:S(2)}, u32[]{:S(2)}) %collective-permute-start.13) | collective-permute-done | bytes 589856 | tf_op jit(solution)/shard_map/ppermute | solution.py:652
  145.5 12.0 %collective-permute-done.10.refs_1_.refs_4_ = f32[5,48,768]{2,1,0:T(8,128)S(1)} collective-permute-done((f32[5,48,768]{2,1,0:T(8,128)S(1)}, f32[5,48,768]{2,1,0:T(8,128)S(1)}, u32[]{:S(2)}, u32[]{:S(2)}) %collective-permute-start.10) | collective-permute-done | bytes 737312 | tf_op jit(solution)/shard_map/ppermute | solution.py:652
  157.6 4.0 %collective-permute-start.17 = (f32[2,48,768]{2,1,0:T(8,128)S(1)}, f32[2,48,768]{2,1,0:T(8,128)S(1)}, u32[]{:S(2)}, u32[]{:S(2)}) collective-permute-start(f32[2,48,768]{2,1,0:T(8,128)S(1)} %get-tuple-element.149), channel_id=1, source_target_pairs={{0,2},{1,9},{2,0},{3,11},{4,6},{5,13},{6,4},{7,15},{8,10},{9,1},{1... | collective-permute-start | bytes 884744 | tf_op jit(solution)/shard_map/ppermute | solution.py:652
  161.6 7.2 %collective-permute-done.15.refs_3_ = f32[2,48,2048]{2,1,0:T(8,128)S(1)} collective-permute-done((f32[2,48,2048]{2,1,0:T(8,128)S(1)}, f32[2,48,2048]{2,1,0:T(8,128)S(1)}, u32[]{:S(2)}, u32[]{:S(2)}) %collective-permute-start.15) | collective-permute-done | bytes 786464 | tf_op jit(solution)/shard_map/ppermute | solution.py:652
  168.8 1.2 add.32
  170.0 3.7 %collective-permute-start.19 = (f32[1,48,2048]{2,1,0:T(8,128)S(1)}, f32[1,48,2048]{2,1,0:T(8,128)S(1)}, u32[]{:S(2)}, u32[]{:S(2)}) collective-permute-start(f32[1,48,2048]{2,1,0:T(8,128)S(1)} %get-tuple-element.147), channel_id=1, source_target_pairs={{0,16},{1,9},{2,18},{3,11},{4,20},{5,13},{6,22},{7,15},{8,24},{9,1... | collective-permute-start | bytes 1179656 | tf_op jit(solution)/shard_map/ppermute | solution.py:652
  173.8 4.3 %collective-permute-start.18 = (f32[2,48,768]{2,1,0:T(8,128)S(1)}, f32[2,48,768]{2,1,0:T(8,128)S(1)}, u32[]{:S(2)}, u32[]{:S(2)}) collective-permute-start(f32[2,48,768]{2,1,0:T(8,128)S(1)} %get-tuple-element.151.refs_0_), channel_id=1, source_target_pairs={{0,8},{1,9},{2,10},{3,11},{4,12},{5,13},{6,14},{7,15},{8,0},{9,1},... | collective-permute-start | bytes 884744 | tf_op jit(solution)/shard_map/ppermute | solution.py:652
  178.1 5.6 %collective-permute-done.20.refs_9_ = f32[1,48,1024]{2,1,0:T(8,128)S(1)} collective-permute-done((f32[1,48,1024]{2,1,0:T(8,128)S(1)}, f32[1,48,1024]{2,1,0:T(8,128)S(1)}, u32[]{:S(2)}, u32[]{:S(2)}) %collective-permute-start.20) | collective-permute-done | bytes 196640 | tf_op jit(solution)/shard_map/ppermute | solution.py:652
  183.8 0.7 collective-permute-done.19.refs_4_
  184.5 2.1 %finish.2 = (f32[48,1536]{1,0:T(8,128)}, f32[48,1536]{1,0:T(8,128)}) custom-call(f32[8,48,2048]{2,1,0:T(8,128)S(1)} %copy-done, f32[8,48,2048]{2,1,0:T(8,128)} %collective-permute-done.4.refs_1_, f32[4,48,2048]{2,1,0:T(8,128)S(1)} %collective-permute-done.11.refs_2_, f32[2,48,2048]{2,1,0:T(8,128)S(1)} %collective-permute-done.15.refs_3_, ...), custom_call_target="tpu_custom_call" | custom-call | bytes 39321 | tf_op jit(solution)/shard_map/finish/pallas_call | solution.py:767
  186.5 0.8 finish.3
  (58 shorter events, 3.7 us)
Async XLA Ops:
  11.0 8.8 %collective-permute-start = (f32[768,768]{1,0:T(8,128)}, f32[768,768]{1,0:T(8,128)}, u32[]{:S(2)}, u32[]{:S(2)}) collective-permute-start(f32[768,768]{1,0:T(8,128)} %get-tuple-element.95.refs_0_), channel_id=1, source_target_pairs={{0,1},{1,0},{2,3},{3,2},{4,5},{5,4},{6,7},{7,6},{8,9},{9,8},{10,11... | collective-permute-start | bytes 7077896 | tf_op jit(solution)/shard_map/ppermute | solution.py:616
  17.1 2.7 %collective-permute-start.1 = (f32[256,768]{1,0:T(8,128)}, f32[256,768]{1,0:T(8,128)}, u32[]{:S(2)}, u32[]{:S(2)}) collective-permute-start(f32[256,768]{1,0:T(8,128)} %get-tuple-element.100.refs_1_), channel_id=1, source_target_pairs={{0,1},{1,0},{2,3},{3,2},{4,5},{5,4},{6,7},{7,6},{8,9},{9,8},{10,11... | collective-permute-start | bytes 2359304 | tf_op jit(solution)/shard_map/ppermute | solution.py:616
  49.7 6.1 %collective-permute-start.2 = (f32[1024,768]{1,0:T(8,128)}, f32[1024,768]{1,0:T(8,128)}, u32[]{:S(2)}, u32[]{:S(2)}) collective-permute-start(f32[1024,768]{1,0:T(8,128)} %get-tuple-element.102.refs_0_), channel_id=1, source_target_pairs={{0,1},{1,0},{2,3},{3,2},{4,5},{5,4},{6,7},{7,6},{8,9},{9,8},{10,11... | collective-permute-start | bytes 9437192 | tf_op jit(solution)/shard_map/ppermute | solution.py:616
  49.9 31.4 %collective-permute-start.3 = (f32[1024,768]{1,0:T(8,128)}, f32[1024,768]{1,0:T(8,128)}, u32[]{:S(2)}, u32[]{:S(2)}) collective-permute-start(f32[1024,768]{1,0:T(8,128)} %get-tuple-element.109), channel_id=1, source_target_pairs={{0,1},{1,0},{2,3},{3,2},{4,5},{5,4},{6,7},{7,6},{8,9},{9,8},{10,11... | collective-permute-start | bytes 9437192 | tf_op jit(solution)/shard_map/ppermute | solution.py:616
  50.3 40.2 %collective-permute-start.4 = (f32[8,48,2048]{2,1,0:T(8,128)}, f32[8,48,2048]{2,1,0:T(8,128)}, u32[]{:S(2)}, u32[]{:S(2)}) collective-permute-start(f32[8,48,2048]{2,1,0:T(8,128)} %get-tuple-element.111), channel_id=1, source_target_pairs={{0,2},{1,5},{2,0},{3,7},{4,6},{5,1},{6,4},{7,3},{8,10},{9,13},{10,... | collective-permute-start | bytes 9437192 | tf_op jit(solution)/shard_map/ppermute | solution.py:652
  52.9 37.6 %collective-permute-start.5 = (f32[8,48,1024]{2,1,0:T(8,128)}, f32[8,48,1024]{2,1,0:T(8,128)}, u32[]{:S(2)}, u32[]{:S(2)}) collective-permute-start(f32[8,48,1024]{2,1,0:T(8,128)} %get-tuple-element.114), channel_id=1, source_target_pairs={{0,16},{1,9},{2,18},{3,11},{4,20},{5,13},{6,22},{7,15},{8,24},{9,1... | collective-permute-start | bytes 4718600 | tf_op jit(solution)/shard_map/ppermute | solution.py:652
  81.2 9.3 %copy-start = (f32[8,48,2048]{2,1,0:T(8,128)S(1)}, f32[8,48,2048]{2,1,0:T(8,128)}, u32[]{:S(2)}) copy-start(f32[8,48,2048]{2,1,0:T(8,128)} %get-tuple-element.110.refs_0_) | copy-start | bytes 9437188
  81.2 9.3 %copy-start.2 = (f32[8,48,1024]{2,1,0:T(8,128)S(1)}, f32[8,48,1024]{2,1,0:T(8,128)}, u32[]{:S(2)}) copy-start(f32[8,48,1024]{2,1,0:T(8,128)} %get-tuple-element.113.refs_2_.refs_3_.refs_4_.refs_5_) | copy-start | bytes 4718596
  81.2 9.3 %copy-start.5 = (f32[1024,768]{1,0:T(8,128)S(1)}, f32[1024,768]{1,0:T(8,128)}, u32[]{:S(2)}) copy-start(f32[1024,768]{1,0:T(8,128)} %get-tuple-element.116.refs_4_) | copy-start | bytes 9437188
  81.2 9.3 %copy-start.7 = (f32[8,48,768]{2,1,0:T(8,128)S(1)}, f32[8,48,768]{2,1,0:T(8,128)}, u32[]{:S(2)}) copy-start(f32[8,48,768]{2,1,0:T(8,128)} %get-tuple-element.117.refs_5_) | copy-start | bytes 3538948
  81.2 9.3 %copy-start.8 = (f32[8,48,768]{2,1,0:T(8,128)S(1)}, f32[8,48,768]{2,1,0:T(8,128)}, u32[]{:S(2)}) copy-start(f32[8,48,768]{2,1,0:T(8,128)} %get-tuple-element.118.refs_6_) | copy-start | bytes 3538948
  90.5 7.8 %copy-start.1 = (f32[4,256,768]{2,1,0:T(8,128)S(1)}, f32[4,256,768]{2,1,0:T(8,128)}, u32[]{:S(2)}) copy-start(f32[4,256,768]{2,1,0:T(8,128)} %param.18) | copy-start | bytes 9437188
  90.5 7.8 %copy-start.6 = (f32[1024,768]{1,0:T(8,128)S(1)}, f32[1024,768]{1,0:T(8,128)}, u32[]{:S(2)}) copy-start(f32[1024,768]{1,0:T(8,128)} %get-tuple-element.120.refs_3_) | copy-start | bytes 9437188
  90.5 7.7 %copy-start.9 = (f32[768]{0:T(1024)S(1)}, f32[768]{0:T(1024)}, u32[]{:S(2)}) copy-start(f32[768]{0:T(1024)} %param.20) | copy-start | bytes 9220
  92.5 5.7 %collective-permute-start.6 = (f32[1024,768]{1,0:T(8,128)S(1)}, f32[1024,768]{1,0:T(8,128)S(1)}, u32[]{:S(2)}, u32[]{:S(2)}) collective-permute-start(f32[1024,768]{1,0:T(8,128)S(1)} %get-tuple-element.119.refs_0_), channel_id=1, source_target_pairs={{0,1},{1,0},{2,3},{3,2},{4,5},{5,4},{6,7},{7,6},{8,9},{9,8},{10,11... | collective-permute-start | bytes 9437192 | tf_op jit(solution)/shard_map/ppermute | solution.py:616
  92.6 46.5 %collective-permute-start.11 = (f32[4,48,2048]{2,1,0:T(8,128)S(1)}, f32[4,48,2048]{2,1,0:T(8,128)S(1)}, u32[]{:S(2)}, u32[]{:S(2)}) collective-permute-start(f32[4,48,2048]{2,1,0:T(8,128)S(1)} %get-tuple-element.135), channel_id=1, source_target_pairs={{0,4},{1,17},{2,6},{3,19},{4,0},{5,21},{6,2},{7,23},{8,12},{9,25},... | collective-permute-start | bytes 4718600 | tf_op jit(solution)/shard_map/ppermute | solution.py:652
  95.1 27.1 %collective-permute-start.9 = (f32[8,48,768]{2,1,0:T(8,128)S(1)}, f32[8,48,768]{2,1,0:T(8,128)S(1)}, u32[]{:S(2)}, u32[]{:S(2)}) collective-permute-start(f32[8,48,768]{2,1,0:T(8,128)S(1)} %get-tuple-element.132), channel_id=1, source_target_pairs={{0,8},{1,5},{2,10},{3,7},{4,12},{5,1},{6,14},{7,3},{8,0},{9,13},{1... | collective-permute-start | bytes 3538952 | tf_op jit(solution)/shard_map/ppermute | solution.py:652
  95.9 28.8 %collective-permute-start.8 = (f32[8,48,768]{2,1,0:T(8,128)S(1)}, f32[8,48,768]{2,1,0:T(8,128)S(1)}, u32[]{:S(2)}, u32[]{:S(2)}) collective-permute-start(f32[8,48,768]{2,1,0:T(8,128)S(1)} %get-tuple-element.129), channel_id=1, source_target_pairs={{0,2},{1,3},{2,0},{3,1},{4,6},{5,7},{6,4},{7,5},{8,10},{9,11},{10,... | collective-permute-start | bytes 3538952 | tf_op jit(solution)/shard_map/ppermute | solution.py:652
  97.2 42.0 %collective-permute-start.12 = (f32[4,48,1024]{2,1,0:T(8,128)S(1)}, f32[4,48,1024]{2,1,0:T(8,128)S(1)}, u32[]{:S(2)}, u32[]{:S(2)}) collective-permute-start(f32[4,48,1024]{2,1,0:T(8,128)S(1)} %get-tuple-element.137), channel_id=1, source_target_pairs={{0,8},{1,5},{2,10},{3,7},{4,12},{5,1},{6,14},{7,3},{8,0},{9,13},{1... | collective-permute-start | bytes 2359304 | tf_op jit(solution)/shard_map/ppermute | solution.py:652
  98.3 29.0 %copy-start.3 = (f32[8,48,768]{2,1,0:T(8,128)S(1)}, f32[8,48,768]{2,1,0:T(8,128)}, u32[]{:S(2)}) copy-start(f32[8,48,768]{2,1,0:T(8,128)} %get-tuple-element.128.refs_2_) | copy-start | bytes 3538948
  98.3 29.0 %copy-start.4 = (f32[8,48,768]{2,1,0:T(8,128)S(1)}, f32[8,48,768]{2,1,0:T(8,128)}, u32[]{:S(2)}) copy-start(f32[8,48,768]{2,1,0:T(8,128)} %get-tuple-element.131.refs_4_.refs_5_.refs_6_.refs_7_) | copy-start | bytes 3538948
  102.2 25.1 %collective-permute-start.7 = (f32[1,48,768]{2,1,0:T(8,128)S(1)}, f32[1,48,768]{2,1,0:T(8,128)S(1)}, u32[]{:S(2)}, u32[]{:S(2)}) collective-permute-start(f32[1,48,768]{2,1,0:T(8,128)S(1)} %get-tuple-element.127.refs_0_), channel_id=1, source_target_pairs={{0,2},{1,3},{2,0},{3,1},{4,6},{5,7},{6,4},{7,5},{8,10},{9,11},{10,... | collective-permute-start | bytes 442376 | tf_op jit(solution)/shard_map/ppermute | solution.py:652
  127.5 29.9 %collective-permute-start.10 = (f32[5,48,768]{2,1,0:T(8,128)S(1)}, f32[5,48,768]{2,1,0:T(8,128)S(1)}, u32[]{:S(2)}, u32[]{:S(2)}) collective-permute-start(f32[5,48,768]{2,1,0:T(8,128)S(1)} %get-tuple-element.134.refs_0_), channel_id=1, source_target_pairs={{0,16},{1,5},{2,18},{3,7},{4,20},{5,1},{6,22},{7,3},{8,24},{9,13},... | collective-permute-start | bytes 2211848 | tf_op jit(solution)/shard_map/ppermute | solution.py:652
  129.2 16.3 %collective-permute-start.13 = (f32[4,48,768]{2,1,0:T(8,128)S(1)}, f32[4,48,768]{2,1,0:T(8,128)S(1)}, u32[]{:S(2)}, u32[]{:S(2)}) collective-permute-start(f32[4,48,768]{2,1,0:T(8,128)S(1)} %get-tuple-element.141), channel_id=1, source_target_pairs={{0,4},{1,3},{2,6},{3,1},{4,0},{5,7},{6,2},{7,5},{8,12},{9,11},{10,... | collective-permute-start | bytes 1769480 | tf_op jit(solution)/shard_map/ppermute | solution.py:652
  140.6 28.2 %collective-permute-start.15 = (f32[2,48,2048]{2,1,0:T(8,128)S(1)}, f32[2,48,2048]{2,1,0:T(8,128)S(1)}, u32[]{:S(2)}, u32[]{:S(2)}) collective-permute-start(f32[2,48,2048]{2,1,0:T(8,128)S(1)} %get-tuple-element.139), channel_id=1, source_target_pairs={{0,8},{1,3},{2,10},{3,1},{4,12},{5,7},{6,14},{7,5},{8,0},{9,11},{1... | collective-permute-start | bytes 2359304 | tf_op jit(solution)/shard_map/ppermute | solution.py:652
  140.7 21.0 %collective-permute-start.16 = (f32[2,48,1024]{2,1,0:T(8,128)S(1)}, f32[2,48,1024]{2,1,0:T(8,128)S(1)}, u32[]{:S(2)}, u32[]{:S(2)}) collective-permute-start(f32[2,48,1024]{2,1,0:T(8,128)S(1)} %get-tuple-element.145), channel_id=1, source_target_pairs={{0,2},{1,17},{2,0},{3,19},{4,6},{5,21},{6,4},{7,23},{8,10},{9,25},... | collective-permute-start | bytes 1179656 | tf_op jit(solution)/shard_map/ppermute | solution.py:652
  157.6 16.2 %collective-permute-start.14 = (f32[3,48,768]{2,1,0:T(8,128)S(1)}, f32[3,48,768]{2,1,0:T(8,128)S(1)}, u32[]{:S(2)}, u32[]{:S(2)}) collective-permute-start(f32[3,48,768]{2,1,0:T(8,128)S(1)} %get-tuple-element.143.refs_0_), channel_id=1, source_target_pairs={{0,4},{1,17},{2,6},{3,19},{4,0},{5,21},{6,2},{7,23},{8,12},{9,25},... | collective-permute-start | bytes 1327112 | tf_op jit(solution)/shard_map/ppermute | solution.py:652
  157.6 16.1 %collective-permute-start.17 = (f32[2,48,768]{2,1,0:T(8,128)S(1)}, f32[2,48,768]{2,1,0:T(8,128)S(1)}, u32[]{:S(2)}, u32[]{:S(2)}) collective-permute-start(f32[2,48,768]{2,1,0:T(8,128)S(1)} %get-tuple-element.149), channel_id=1, source_target_pairs={{0,2},{1,9},{2,0},{3,11},{4,6},{5,13},{6,4},{7,15},{8,10},{9,1},{1... | collective-permute-start | bytes 884744 | tf_op jit(solution)/shard_map/ppermute | solution.py:652
  170.0 14.4 %collective-permute-start.19 = (f32[1,48,2048]{2,1,0:T(8,128)S(1)}, f32[1,48,2048]{2,1,0:T(8,128)S(1)}, u32[]{:S(2)}, u32[]{:S(2)}) collective-permute-start(f32[1,48,2048]{2,1,0:T(8,128)S(1)} %get-tuple-element.147), channel_id=1, source_target_pairs={{0,16},{1,9},{2,18},{3,11},{4,20},{5,13},{6,22},{7,15},{8,24},{9,1... | collective-permute-start | bytes 1179656 | tf_op jit(solution)/shard_map/ppermute | solution.py:652
  173.8 12.7 %collective-permute-start.18 = (f32[2,48,768]{2,1,0:T(8,128)S(1)}, f32[2,48,768]{2,1,0:T(8,128)S(1)}, u32[]{:S(2)}, u32[]{:S(2)}) collective-permute-start(f32[2,48,768]{2,1,0:T(8,128)S(1)} %get-tuple-element.151.refs_0_), channel_id=1, source_target_pairs={{0,8},{1,9},{2,10},{3,11},{4,12},{5,13},{6,14},{7,15},{8,0},{9,1},... | collective-permute-start | bytes 884744 | tf_op jit(solution)/shard_map/ppermute | solution.py:652
  178.1 5.7 %collective-permute-start.20 = (f32[1,48,1024]{2,1,0:T(8,128)S(1)}, f32[1,48,1024]{2,1,0:T(8,128)S(1)}, u32[]{:S(2)}, u32[]{:S(2)}) collective-permute-start(f32[1,48,1024]{2,1,0:T(8,128)S(1)} %get-tuple-element.153), channel_id=1, source_target_pairs={{0,4},{1,3},{2,6},{3,1},{4,0},{5,7},{6,2},{7,5},{8,12},{9,11},{10,... | collective-permute-start | bytes 589832 | tf_op jit(solution)/shard_map/ppermute | solution.py:652
  178.1 8.4 %collective-permute-start.21 = (f32[1,48,768]{2,1,0:T(8,128)S(1)}, f32[1,48,768]{2,1,0:T(8,128)S(1)}, u32[]{:S(2)}, u32[]{:S(2)}) collective-permute-start(f32[1,48,768]{2,1,0:T(8,128)S(1)} %get-tuple-element.157), channel_id=1, source_target_pairs={{0,16},{1,17},{2,18},{3,19},{4,20},{5,21},{6,22},{7,23},{8,24},{9,... | collective-permute-start | bytes 442376 | tf_op jit(solution)/shard_map/ppermute | solution.py:652
  (6 other events, 46.4 us)

commit v6 on v5

--- a/solution.py
+++ b/solution.py
@@ -70,6 +70,22 @@
         pltpu.make_async_copy(far.at[part], near.at[part], sems.at[first + c])
         for c, part in enumerate(rows)
     ]
+
+
+def fetch_heads(fars, near, out_far, out_near, sems):
+    copies = in_rows(out_far, out_near, sems, 0, 2)
+    cols = fars[0].shape[1]
+    for i, far in enumerate(fars):
+        size = far.shape[0] // 2
+        for c in range(2):
+            copies.append(
+                pltpu.make_async_copy(
+                    far.at[pl.ds(c * size, size)],
+                    near.at[pl.ds(c * size, size), pl.ds(i * cols, cols)],
+                    sems.at[2 + 2 * i + c],
+                )
+            )
+    return copies
 
 
 def started(copies):
@@ -185,14 +201,12 @@
 def attend_kernel(
     seg_ref, gain, shift, bq, bv, bo, wq_far, wk_far, wv_far, wo_far, x_ref, *refs, first_row
 ):
-    normed_ref, qkv_ref, probs_ref, context_ref, out_ref = refs[-10:-5]
-    wq, wk, wv, wo, sems = refs[-5:]
-    fetches = []
-    for i, (far, near) in enumerate(((wq_far, wq), (wk_far, wk), (wv_far, wv), (wo_far, wo))):
-        fetches += in_rows(far, near, sems, 2 * i, 2)
+    normed_ref, qkv_ref, probs_ref, context_ref, out_ref = refs[-8:-3]
+    w_all, wo, sems = refs[-3:]
+    fetches = fetch_heads((wq_far, wk_far, wv_far), w_all, wo_far, wo, sems)
     when_first(started(fetches))
 
-    cols = wq.shape[1]
+    cols = wo.shape[0]
     gain_row, shift_row = line(gain), line(shift)
     for at in range(0, x_ref.shape[0], SLAB):
         slab = slice(at, at + SLAB)
@@ -201,9 +215,10 @@
     normed = normed_ref[...]
     low, high = lane_halves(cols)
     when_first(arrived(fetches))
-    queries = (product(normed, wq[...], (1, 0)) + line(bq)) * SCALE
-    keys = product(normed, wk[...], (1, 0)).astype(BF16)
-    values = (product(normed, wv[...], (1, 0)) + line(bv)).astype(BF16)
+    made_all = product(normed, w_all[...], (1, 0))
+    queries = (made_all[:, :cols] + line(bq)) * SCALE
+    keys = made_all[:, cols : 2 * cols].astype(BF16)
+    values = (made_all[:, 2 * cols :] + line(bv)).astype(BF16)
     qkv_ref[:, :cols] = queries.astype(BF16)
     qkv_ref[:, cols : 2 * cols] = keys
     qkv_ref[:, 2 * cols :] = values
@@ -287,8 +302,11 @@
             jax.ShapeDtypeStruct((count * length, width), F32),
         ],
         input_output_aliases={len(fixed) + len(weights) + 1 + i: i for i in range(len(made))},
-        scratch_shapes=[pltpu.VMEM(w.shape, w.dtype) for w in weights]
-        + [pltpu.SemaphoreType.DMA((2 * len(weights),))],
+        scratch_shapes=[
+            pltpu.VMEM((width, 3 * cols), BF16),
+            pltpu.VMEM(wo.shape, BF16),
+            pltpu.SemaphoreType.DMA((2 * len(weights),)),
+        ],
         name="attend",
         cost_estimate=cost("attend",
             8 * done * width * cols + 4 * done * length * cols,
@@ -360,8 +378,8 @@
             grad = (grad * slopes[here, units].astype(F32)).astype(BF16)
             slopes[here, units] = grad
             by_up[:, units] += column_sum(grad.astype(F32))
+        down_ref[...] = product(acts[here, :], down_near[...], (1, 0))
         back_ref[...] = product(slopes[here, :], up_near[...], (1, 1))
-        down_ref[...] = product(acts[here, :], down_near[...], (1, 0))
 
     @pl.when(step == 2 * rows - 1)
     def _():
@@ -427,14 +445,12 @@
     top_ref, middle_ref, gain, qkv_ref, probs_ref, normed_ref, context_ref = refs[:7]
     wo_far, wq_far, wk_far, wv_far = refs[7:11]
     grad_middle_ref, back_ref, sum_gain, sum_shift, sum_out, sum_qkv = refs[11:17]
-    outs, refs = refs[17:-12], refs[-12:]
-    rounded, grad_qkv_ref, contexts, turned, turned_two, total, wo, wq, wk, wv = refs[:10]
-    sems, out_sems = refs[10:]
-    cols, length = wq.shape[1], top_ref.shape[0]
+    outs, refs = refs[17:-10], refs[-10:]
+    rounded, grad_qkv_ref, contexts, turned, turned_two, total, wo, w_all = refs[:8]
+    sems, out_sems = refs[8:]
+    cols, length = wo.shape[0], top_ref.shape[0]
     here = step_rows(length)
-    fetches = []
-    for i, (far, near) in enumerate(((wo_far, wo), (wq_far, wq), (wk_far, wk), (wv_far, wv))):
-        fetches += in_rows(far, near, sems, 2 * i, 2)
+    fetches = fetch_heads((wq_far, wk_far, wv_far), w_all, wo_far, wo, sems)
     when_first(started(fetches))
     gain_row, by_gain, by_shift, by_out = line(gain), 0.0, 0.0, 0.0
     for at in range(0, length, SLAB):
@@ -491,11 +507,7 @@
     in_turn((spread, soften, gather), cols // HD)
     grads = grad_qkv_ref[here, :]
     add_up(sum_qkv, column_sum(grads.astype(F32)))
-    back_ref[...] = (
-        product(grads[:, :cols], wq[...], (1, 1))
-        + product(grads[:, cols : 2 * cols], wk[...], (1, 1))
-        + product(grads[:, 2 * cols :], wv[...], (1, 1))
-    )
+    back_ref[...] = product(grads, w_all[...], (1, 1))
     pieces = pieces_of(
         [(turned, grad_qkv_ref, 0, 3 * cols), (turned_two, contexts, 0, cols)], 0, widths
     )
@@ -535,8 +547,9 @@
             pltpu.VMEM((width, tokens), BF16),
             pltpu.VMEM((width, 4 * cols), F32),
         ]
-        + [pltpu.VMEM(w.shape, w.dtype) for w in weights]
         + [
+            pltpu.VMEM(wo.shape, BF16),
+            pltpu.VMEM((width, 3 * cols), BF16),
             pltpu.SemaphoreType.DMA((2 * len(weights),)),
             pltpu.SemaphoreType.DMA((copies,)),
         ],
@@ -616,7 +629,7 @@
     return lax.ppermute(part, "mp", [(0, 1), (1, 0)])
 
 
-ORDERS = {"a": ("xynf", "yfxn"), "b": ("fnxy", "nyfx"), "q": ("xfyn", "xyfn"), "r": ("nyxf", "yxnf")}
+ORDERS = {"a": ("ynxf", "xfyn"), "b": ("nxfy", "fxny"), "q": ("yfxn", "yxfn"), "r": ("xnyf", "xynf")}
 SIXTHS = {"a": 4, "b": 2, "q": 3, "r": 3}
 
 

time: 188 us -> 184 us (0.979)
  starting transfers between devices: 26.9 us -> 25 us
    ppermute x17, waiting for transfers between devices: 66.9 us -> 64 us  [exchange(): return lax.ppermute(array, ('dp', 'mp'), pairs)]
    ppermute x17, starting transfers between devices: 25.6 us -> 23.7 us  [exchange(): return lax.ppermute(array, ('dp', 'mp'), pairs)]
where the time goes in v6:
time: 184 us; the launch traced here: 183 us
  Pallas kernels  82.3 us (45%)
  waiting for transfers between devices  68.6 us (37%)
  starting transfers between devices  25 us (14%)
  other arithmetic  6.18 us (3%)
    ppermute x17, waiting for transfers between devices, exchange(): return lax.ppermute(array, ('dp', 'mp'), pairs)  64 us
    pallas_call x1, Pallas kernels, forward(): pl.pallas_call(lambda *refs: forward_kernel(*refs, tables=tables, rows=ro...  29.9 us
    pallas_call x1, Pallas kernels, attend_back(): pl.pallas_call(lambda *refs: attend_back_kernel(*refs, tables=tables, wid...  24.8 us
    ppermute x17, starting transfers between devices, exchange(): return lax.ppermute(array, ('dp', 'mp'), pairs)  23.7 us
    pallas_call x2, Pallas kernels, attend(): pl.pallas_call(lambda *refs: attend_kernel(*refs, first_row=first_row), g...  16 us
    add x1, other arithmetic, on_device(): outcome = pin(middle, sum_qkv) + (down_mine + down_other) + b_down  6.18 us
    pallas_call x6, Pallas kernels, advance(): pl.pallas_call(lambda *refs: add_kernel(*refs[:len(flat)], *refs[len(flat...  4.94 us
    ppermute x5, waiting for transfers between devices, from_partner(): return lax.ppermute(part, 'mp', [(0, 1), (1, 0)])  4.57 us
  transfers between devices with their start and end apart: 22, of which 13 were waited for; matrix products, arithmetic and copies ran while one was open for 3% of the time, Pallas kernels for 21%

profile of v6, /device:TPU:0, one launch (start us, length us, event | category | flops | bytes accessed | tf_op | source)
XLA Modules:
  0.0 183.3 jit_solution(14586436230812581450)
XLA Ops:
  0.7 10.3 %attend.2 = (bf16[1024,768]{1,0:T(8,128)(2,1)}, bf16[1024,1152]{1,0:T(8,128)(2,1)}, bf16[4,6,256,256]{3,2,1,0:T(8,128)(2,1)}, bf16[1024,384]{1,0:T(8,128)(2,1)}, f32[768,768]{1,0:T(8,128)}) custom-call(s32[4,256]{1,0:T(4,128)} %refs_0_.3, f32[6,128]{1,0:T(8,128)} %bitcast.26, f32[6,128]{1,0:T(8,128)} %bitcast.32, f32[3,128]{1,0:T(4,128)} %bitcast.39, ...), custom_call_target="tpu_custom_call" | custom-call | flops 21139292 | bytes 129761 | tf_op jit(solution)/shard_map/attend/pallas_call | solution.py:283
  11.5 5.6 %attend.3 = (bf16[1024,768]{1,0:T(8,128)(2,1)}, bf16[1024,1152]{1,0:T(8,128)(2,1)}, bf16[4,6,256,256]{3,2,1,0:T(8,128)(2,1)}, bf16[1024,384]{1,0:T(8,128)(2,1)}, f32[256,768]{1,0:T(8,128)}) custom-call(s32[4,256]{1,0:T(4,128)} %refs_0_.3, f32[6,128]{1,0:T(8,128)} %bitcast.27, ...), custom_call_target="tpu_custom_call", output_to_operand_aliasing={{0}: (11, {}), {1}: (12, {}), {2}: (13, {}), {3}: (14, {})} | custom-call | flops 7046430 | bytes 58982 | tf_op jit(solution)/shard_map/attend/pallas_call | solution.py:283
  17.3 2.6 %collective-permute-done.1.refs_3_ = f32[256,768]{1,0:T(8,128)} collective-permute-done((f32[256,768]{1,0:T(8,128)}, f32[256,768]{1,0:T(8,128)}, u32[]{:S(2)}, u32[]{:S(2)}) %collective-permute-start.1) | collective-permute-done | bytes 786464 | tf_op jit(solution)/shard_map/ppermute | solution.py:629
  19.9 29.9 %forward.1 = (f32[1024,768]{1,0:T(8,128)}, f32[1024,768]{1,0:T(8,128)}, f32[1024,768]{1,0:T(8,128)}, f32[1,768]{1,0:T(1,128)}, f32[1,1536]{1,0:T(1,128)}, /*inde...) custom-call(f32[768,768]{1,0:T(8,128)} %get-tuple-element.95.refs_0_, ...), custom_call_target="tpu_custom_call" | custom-call | flops 144955152 | bytes 330301 | tf_op jit(solution)/shard_map/forward/pallas_call | solution.py:404
  50.3 2.6 %collective-permute-start.4 = (f32[8,48,2048]{2,1,0:T(8,128)}, f32[8,48,2048]{2,1,0:T(8,128)}, u32[]{:S(2)}, u32[]{:S(2)}) collective-permute-start(f32[8,48,2048]{2,1,0:T(8,128)} %get-tuple-element.111), channel_id=1, source_target_pairs={{0,4},{1,3},{2,6},{3,1},{4,0},{5,7},{6,2},{7,5},{8,12},{9,11},{10,... | collective-permute-start | bytes 9437192 | tf_op jit(solution)/shard_map/ppermute | solution.py:665
  53.0 1.6 collective-permute-start.5
  54.6 1.3 collective-permute-done.2.refs_1_
  55.8 24.8 %back.1 = (f32[1024,768]{1,0:T(8,128)}, f32[1024,768]{1,0:T(8,128)}, f32[1,768]{1,0:T(1,128)}, f32[1,768]{1,0:T(1,128)}, f32[1,768]{1,0:T(1,128)}, /*index=5*/f3...) custom-call(f32[1024,768]{1,0:T(8,128)} %get-tuple-element.102.refs_, ...), custom_call_target="tpu_custom_call" | custom-call | flops 56371444 | bytes 338165 | tf_op jit(solution)/shard_map/back/pallas_call | solution.py:528
  80.7 6.2 %add_add_fusion = f32[1024,768]{1,0:T(8,128)} fusion(f32[1024,768]{1,0:T(8,128)} %get-tuple-element.108.refs_3_, f32[1024,768]{1,0:T(8,128)} %get-tuple-element.109, f32[1024,768]{1,0:T(8,128)} %collective-permute-done.3, f32[768]{0:T(1024)} %param.34), kind=kLoop, calls=%fused_computation | loop fusion | flops 2359296 | bytes 12585984 | tf_op jit(solution)/shard_map/add | solution.py:868
  86.9 3.7 %collective-permute-done.5.refs_3_.refs_4_.refs_5_.refs_6_ = f32[8,48,1024]{2,1,0:T(8,128)} collective-permute-done((f32[8,48,1024]{2,1,0:T(8,128)}, f32[8,48,1024]{2,1,0:T(8,128)}, u32[]{:S(2)}, u32[]{:S(2)}) %collective-permute-start.5) | collective-permute-done | bytes 1572896 | tf_op jit(solution)/shard_map/ppermute | solution.py:665
  90.7 1.9 %add.28 = (f32[4,48,2048]{2,1,0:T(8,128)S(1)}, f32[4,48,1024]{2,1,0:T(8,128)S(1)}, f32[1024,768]{1,0:T(8,128)S(1)}, f32[8,48,768]{2,1,0:T(8,128)S(1)}, f32[8,48,768]{2,1,0:T(8,128)S(1)}) custom-call(f32[8,48,2048]{2,1,0:T(8,128)S(1)} %copy-done, ...), custom_call_target="tpu_custom_call", output_to_operand_aliasing={{2}: (4, {}), {3}: (5, {}), {4}: (6, {})} | custom-call | bytes 23592 | tf_op jit(solution)/shard_map/add/pallas_call | solution.py:718
  92.7 1.5 collective-permute-start.11
  95.1 1.5 collective-permute-start.8
  96.6 1.0 collective-permute-start.12
  98.4 3.8 %first.1 = (f32[1024,768]{1,0:T(8,128)}, f32[1,48,768]{2,1,0:T(8,128)S(1)}) custom-call(f32[1024,768]{1,0:T(8,128)S(1)} %get-tuple-element.119.refs_0_, f32[1024,768]{1,0:T(8,128)S(1)} %collective-permute-done.6.refs_1_, f32[1024,768]{1,0:T(8,128)S(1)} %bitcast.25, f32[1024,768]{1,0:T(8,128)S(1)} %copy-done.6, f32[6,128]{1,0:T(8,128)S(1)} %bitcast.28, ...), custom_call_target="tpu_custom_call" | custom-call | flops 157286 | bytes 157286 | tf_op jit(solution)/shard_map/first/pallas_call | solution.py:610
  102.8 20.3 %collective-permute-done.9.refs_5_.refs_6_.refs_7_.refs_8_ = f32[8,48,768]{2,1,0:T(8,128)S(1)} collective-permute-done((f32[8,48,768]{2,1,0:T(8,128)S(1)}, f32[8,48,768]{2,1,0:T(8,128)S(1)}, u32[]{:S(2)}, u32[]{:S(2)}) %collective-permute-start.9) | collective-permute-done | bytes 1179680 | tf_op jit(solution)/shard_map/ppermute | solution.py:665
  123.8 2.9 %collective-permute-done.7.refs_1_ = f32[1,48,768]{2,1,0:T(8,128)S(1)} collective-permute-done((f32[1,48,768]{2,1,0:T(8,128)S(1)}, f32[1,48,768]{2,1,0:T(8,128)S(1)}, u32[]{:S(2)}, u32[]{:S(2)}) %collective-permute-start.7) | collective-permute-done | bytes 147488 | tf_op jit(solution)/shard_map/ppermute | solution.py:665
  127.3 2.4 %collective-permute-start.13 = (f32[4,48,768]{2,1,0:T(8,128)S(1)}, f32[4,48,768]{2,1,0:T(8,128)S(1)}, u32[]{:S(2)}, u32[]{:S(2)}) collective-permute-start(f32[4,48,768]{2,1,0:T(8,128)S(1)} %get-tuple-element.141), channel_id=1, source_target_pairs={{0,8},{1,5},{2,10},{3,7},{4,12},{5,1},{6,14},{7,3},{8,0},{9,13},{1... | collective-permute-start | bytes 1769480 | tf_op jit(solution)/shard_map/ppermute | solution.py:665
  129.7 10.2 %collective-permute-done.12.refs_5_.refs_6_.refs_7_ = f32[4,48,1024]{2,1,0:T(8,128)S(1)} collective-permute-done((f32[4,48,1024]{2,1,0:T(8,128)S(1)}, f32[4,48,1024]{2,1,0:T(8,128)S(1)}, u32[]{:S(2)}, u32[]{:S(2)}) %collective-permute-start.12) | collective-permute-done | bytes 786464 | tf_op jit(solution)/shard_map/ppermute | solution.py:665
  139.9 1.4 add.30
  142.3 3.3 %collective-permute-start.16 = (f32[2,48,1024]{2,1,0:T(8,128)S(1)}, f32[2,48,1024]{2,1,0:T(8,128)S(1)}, u32[]{:S(2)}, u32[]{:S(2)}) collective-permute-start(f32[2,48,1024]{2,1,0:T(8,128)S(1)} %get-tuple-element.145), channel_id=1, source_target_pairs={{0,16},{1,9},{2,18},{3,11},{4,20},{5,13},{6,22},{7,15},{8,24},{9,1... | collective-permute-start | bytes 1179656 | tf_op jit(solution)/shard_map/ppermute | solution.py:665
  145.6 2.3 %collective-permute-done.10.refs_1_.refs_4_ = f32[5,48,768]{2,1,0:T(8,128)S(1)} collective-permute-done((f32[5,48,768]{2,1,0:T(8,128)S(1)}, f32[5,48,768]{2,1,0:T(8,128)S(1)}, u32[]{:S(2)}, u32[]{:S(2)}) %collective-permute-start.10) | collective-permute-done | bytes 737312 | tf_op jit(solution)/shard_map/ppermute | solution.py:665
  148.0 1.1 collective-permute-start.14
  149.1 1.2 collective-permute-start.17
  150.3 11.6 %collective-permute-done.16.refs_7_.refs_8_ = f32[2,48,1024]{2,1,0:T(8,128)S(1)} collective-permute-done((f32[2,48,1024]{2,1,0:T(8,128)S(1)}, f32[2,48,1024]{2,1,0:T(8,128)S(1)}, u32[]{:S(2)}, u32[]{:S(2)}) %collective-permute-start.16) | collective-permute-done | bytes 393248 | tf_op jit(solution)/shard_map/ppermute | solution.py:665
  162.0 1.2 add.32
  163.4 3.1 %collective-permute-start.18 = (f32[2,48,768]{2,1,0:T(8,128)S(1)}, f32[2,48,768]{2,1,0:T(8,128)S(1)}, u32[]{:S(2)}, u32[]{:S(2)}) collective-permute-start(f32[2,48,768]{2,1,0:T(8,128)S(1)} %get-tuple-element.151.refs_0_), channel_id=1, source_target_pairs={{0,8},{1,9},{2,10},{3,11},{4,12},{5,13},{6,14},{7,15},{8,0},{9,1},... | collective-permute-start | bytes 884744 | tf_op jit(solution)/shard_map/ppermute | solution.py:665
  166.5 1.5 collective-permute-start.20
  168.0 4.2 %collective-permute-done.20.refs_9_ = f32[1,48,1024]{2,1,0:T(8,128)S(1)} collective-permute-done((f32[1,48,1024]{2,1,0:T(8,128)S(1)}, f32[1,48,1024]{2,1,0:T(8,128)S(1)}, u32[]{:S(2)}, u32[]{:S(2)}) %collective-permute-start.20) | collective-permute-done | bytes 196640 | tf_op jit(solution)/shard_map/ppermute | solution.py:665
  172.2 7.1 %collective-permute-done.19.refs_4_ = f32[1,48,2048]{2,1,0:T(8,128)S(1)} collective-permute-done((f32[1,48,2048]{2,1,0:T(8,128)S(1)}, f32[1,48,2048]{2,1,0:T(8,128)S(1)}, u32[]{:S(2)}, u32[]{:S(2)}) %collective-permute-start.19) | collective-permute-done | bytes 393248 | tf_op jit(solution)/shard_map/ppermute | solution.py:665
  179.2 2.1 %finish.2 = (f32[48,1536]{1,0:T(8,128)}, f32[48,1536]{1,0:T(8,128)}) custom-call(f32[8,48,2048]{2,1,0:T(8,128)S(1)} %copy-done, f32[8,48,2048]{2,1,0:T(8,128)} %collective-permute-done.4.refs_1_, f32[4,48,2048]{2,1,0:T(8,128)S(1)} %collective-permute-done.11.refs_2_, f32[2,48,2048]{2,1,0:T(8,128)S(1)} %collective-permute-done.15.refs_3_, ...), custom_call_target="tpu_custom_call" | custom-call | bytes 39321 | tf_op jit(solution)/shard_map/finish/pallas_call | solution.py:780
  181.3 1.1 collective-permute-done.21.refs_11_
  (58 shorter events, 6.8 us)
Async XLA Ops:
  11.0 8.9 %collective-permute-start = (f32[768,768]{1,0:T(8,128)}, f32[768,768]{1,0:T(8,128)}, u32[]{:S(2)}, u32[]{:S(2)}) collective-permute-start(f32[768,768]{1,0:T(8,128)} %get-tuple-element.95.refs_0_), channel_id=1, source_target_pairs={{0,1},{1,0},{2,3},{3,2},{4,5},{5,4},{6,7},{7,6},{8,9},{9,8},{10,11... | collective-permute-start | bytes 7077896 | tf_op jit(solution)/shard_map/ppermute | solution.py:629
  17.2 2.7 %collective-permute-start.1 = (f32[256,768]{1,0:T(8,128)}, f32[256,768]{1,0:T(8,128)}, u32[]{:S(2)}, u32[]{:S(2)}) collective-permute-start(f32[256,768]{1,0:T(8,128)} %get-tuple-element.100.refs_1_), channel_id=1, source_target_pairs={{0,1},{1,0},{2,3},{3,2},{4,5},{5,4},{6,7},{7,6},{8,9},{9,8},{10,11... | collective-permute-start | bytes 2359304 | tf_op jit(solution)/shard_map/ppermute | solution.py:629
  49.8 6.1 %collective-permute-start.2 = (f32[1024,768]{1,0:T(8,128)}, f32[1024,768]{1,0:T(8,128)}, u32[]{:S(2)}, u32[]{:S(2)}) collective-permute-start(f32[1024,768]{1,0:T(8,128)} %get-tuple-element.102.refs_0_), channel_id=1, source_target_pairs={{0,1},{1,0},{2,3},{3,2},{4,5},{5,4},{6,7},{7,6},{8,9},{9,8},{10,11... | collective-permute-start | bytes 9437192 | tf_op jit(solution)/shard_map/ppermute | solution.py:629
  49.9 30.7 %collective-permute-start.3 = (f32[1024,768]{1,0:T(8,128)}, f32[1024,768]{1,0:T(8,128)}, u32[]{:S(2)}, u32[]{:S(2)}) collective-permute-start(f32[1024,768]{1,0:T(8,128)} %get-tuple-element.109), channel_id=1, source_target_pairs={{0,1},{1,0},{2,3},{3,2},{4,5},{5,4},{6,7},{7,6},{8,9},{9,8},{10,11... | collective-permute-start | bytes 9437192 | tf_op jit(solution)/shard_map/ppermute | solution.py:629
  50.3 40.2 %collective-permute-start.4 = (f32[8,48,2048]{2,1,0:T(8,128)}, f32[8,48,2048]{2,1,0:T(8,128)}, u32[]{:S(2)}, u32[]{:S(2)}) collective-permute-start(f32[8,48,2048]{2,1,0:T(8,128)} %get-tuple-element.111), channel_id=1, source_target_pairs={{0,4},{1,3},{2,6},{3,1},{4,0},{5,7},{6,2},{7,5},{8,12},{9,11},{10,... | collective-permute-start | bytes 9437192 | tf_op jit(solution)/shard_map/ppermute | solution.py:665
  53.0 37.6 %collective-permute-start.5 = (f32[8,48,1024]{2,1,0:T(8,128)}, f32[8,48,1024]{2,1,0:T(8,128)}, u32[]{:S(2)}, u32[]{:S(2)}) collective-permute-start(f32[8,48,1024]{2,1,0:T(8,128)} %get-tuple-element.114), channel_id=1, source_target_pairs={{0,8},{1,17},{2,10},{3,19},{4,12},{5,21},{6,14},{7,23},{8,0},{9,25... | collective-permute-start | bytes 4718600 | tf_op jit(solution)/shard_map/ppermute | solution.py:665
  80.6 9.9 %copy-start = (f32[8,48,2048]{2,1,0:T(8,128)S(1)}, f32[8,48,2048]{2,1,0:T(8,128)}, u32[]{:S(2)}) copy-start(f32[8,48,2048]{2,1,0:T(8,128)} %get-tuple-element.110.refs_0_) | copy-start | bytes 9437188
  80.7 9.9 %copy-start.2 = (f32[8,48,1024]{2,1,0:T(8,128)S(1)}, f32[8,48,1024]{2,1,0:T(8,128)}, u32[]{:S(2)}) copy-start(f32[8,48,1024]{2,1,0:T(8,128)} %get-tuple-element.113.refs_2_.refs_3_.refs_4_.refs_5_) | copy-start | bytes 4718596
  80.7 9.9 %copy-start.5 = (f32[1024,768]{1,0:T(8,128)S(1)}, f32[1024,768]{1,0:T(8,128)}, u32[]{:S(2)}) copy-start(f32[1024,768]{1,0:T(8,128)} %get-tuple-element.116.refs_4_) | copy-start | bytes 9437188
  80.7 9.9 %copy-start.7 = (f32[8,48,768]{2,1,0:T(8,128)S(1)}, f32[8,48,768]{2,1,0:T(8,128)}, u32[]{:S(2)}) copy-start(f32[8,48,768]{2,1,0:T(8,128)} %get-tuple-element.117.refs_5_) | copy-start | bytes 3538948
  80.7 9.9 %copy-start.8 = (f32[8,48,768]{2,1,0:T(8,128)S(1)}, f32[8,48,768]{2,1,0:T(8,128)}, u32[]{:S(2)}) copy-start(f32[8,48,768]{2,1,0:T(8,128)} %get-tuple-element.118.refs_6_) | copy-start | bytes 3538948
  90.6 7.8 %copy-start.1 = (f32[4,256,768]{2,1,0:T(8,128)S(1)}, f32[4,256,768]{2,1,0:T(8,128)}, u32[]{:S(2)}) copy-start(f32[4,256,768]{2,1,0:T(8,128)} %param.18) | copy-start | bytes 9437188
  90.6 7.8 %copy-start.6 = (f32[1024,768]{1,0:T(8,128)S(1)}, f32[1024,768]{1,0:T(8,128)}, u32[]{:S(2)}) copy-start(f32[1024,768]{1,0:T(8,128)} %get-tuple-element.120.refs_3_) | copy-start | bytes 9437188
  90.6 7.7 %copy-start.9 = (f32[768]{0:T(1024)S(1)}, f32[768]{0:T(1024)}, u32[]{:S(2)}) copy-start(f32[768]{0:T(1024)} %param.20) | copy-start | bytes 9220
  92.6 5.7 %collective-permute-start.6 = (f32[1024,768]{1,0:T(8,128)S(1)}, f32[1024,768]{1,0:T(8,128)S(1)}, u32[]{:S(2)}, u32[]{:S(2)}) collective-permute-start(f32[1024,768]{1,0:T(8,128)S(1)} %get-tuple-element.119.refs_0_), channel_id=1, source_target_pairs={{0,1},{1,0},{2,3},{3,2},{4,5},{5,4},{6,7},{7,6},{8,9},{9,8},{10,11... | collective-permute-start | bytes 9437192 | tf_op jit(solution)/shard_map/ppermute | solution.py:629
  92.7 47.2 %collective-permute-start.11 = (f32[4,48,2048]{2,1,0:T(8,128)S(1)}, f32[4,48,2048]{2,1,0:T(8,128)S(1)}, u32[]{:S(2)}, u32[]{:S(2)}) collective-permute-start(f32[4,48,2048]{2,1,0:T(8,128)S(1)} %get-tuple-element.135), channel_id=1, source_target_pairs={{0,8},{1,17},{2,10},{3,19},{4,12},{5,21},{6,14},{7,23},{8,0},{9,25... | collective-permute-start | bytes 4718600 | tf_op jit(solution)/shard_map/ppermute | solution.py:665
  94.2 28.8 %collective-permute-start.9 = (f32[8,48,768]{2,1,0:T(8,128)S(1)}, f32[8,48,768]{2,1,0:T(8,128)S(1)}, u32[]{:S(2)}, u32[]{:S(2)}) collective-permute-start(f32[8,48,768]{2,1,0:T(8,128)S(1)} %get-tuple-element.132), channel_id=1, source_target_pairs={{0,2},{1,3},{2,0},{3,1},{4,6},{5,7},{6,4},{7,5},{8,10},{9,11},{10,... | collective-permute-start | bytes 3538952 | tf_op jit(solution)/shard_map/ppermute | solution.py:665
  95.1 28.7 %collective-permute-start.8 = (f32[8,48,768]{2,1,0:T(8,128)S(1)}, f32[8,48,768]{2,1,0:T(8,128)S(1)}, u32[]{:S(2)}, u32[]{:S(2)}) collective-permute-start(f32[8,48,768]{2,1,0:T(8,128)S(1)} %get-tuple-element.129), channel_id=1, source_target_pairs={{0,4},{1,5},{2,6},{3,7},{4,0},{5,1},{6,2},{7,3},{8,12},{9,13},{10,... | collective-permute-start | bytes 3538952 | tf_op jit(solution)/shard_map/ppermute | solution.py:665
  96.6 43.3 %collective-permute-start.12 = (f32[4,48,1024]{2,1,0:T(8,128)S(1)}, f32[4,48,1024]{2,1,0:T(8,128)S(1)}, u32[]{:S(2)}, u32[]{:S(2)}) collective-permute-start(f32[4,48,1024]{2,1,0:T(8,128)S(1)} %get-tuple-element.137), channel_id=1, source_target_pairs={{0,2},{1,3},{2,0},{3,1},{4,6},{5,7},{6,4},{7,5},{8,10},{9,11},{10,... | collective-permute-start | bytes 2359304 | tf_op jit(solution)/shard_map/ppermute | solution.py:665
  98.4 28.3 %copy-start.3 = (f32[8,48,768]{2,1,0:T(8,128)S(1)}, f32[8,48,768]{2,1,0:T(8,128)}, u32[]{:S(2)}) copy-start(f32[8,48,768]{2,1,0:T(8,128)} %get-tuple-element.128.refs_2_) | copy-start | bytes 3538948
  98.4 28.3 %copy-start.4 = (f32[8,48,768]{2,1,0:T(8,128)S(1)}, f32[8,48,768]{2,1,0:T(8,128)}, u32[]{:S(2)}) copy-start(f32[8,48,768]{2,1,0:T(8,128)} %get-tuple-element.131.refs_4_.refs_5_.refs_6_.refs_7_) | copy-start | bytes 3538948
  102.3 24.4 %collective-permute-start.7 = (f32[1,48,768]{2,1,0:T(8,128)S(1)}, f32[1,48,768]{2,1,0:T(8,128)S(1)}, u32[]{:S(2)}, u32[]{:S(2)}) collective-permute-start(f32[1,48,768]{2,1,0:T(8,128)S(1)} %get-tuple-element.127.refs_0_), channel_id=1, source_target_pairs={{0,4},{1,5},{2,6},{3,7},{4,0},{5,1},{6,2},{7,3},{8,12},{9,13},{10,... | collective-permute-start | bytes 442376 | tf_op jit(solution)/shard_map/ppermute | solution.py:665
  126.9 21.0 %collective-permute-start.10 = (f32[5,48,768]{2,1,0:T(8,128)S(1)}, f32[5,48,768]{2,1,0:T(8,128)S(1)}, u32[]{:S(2)}, u32[]{:S(2)}) collective-permute-start(f32[5,48,768]{2,1,0:T(8,128)S(1)} %get-tuple-element.134.refs_0_), channel_id=1, source_target_pairs={{0,16},{1,3},{2,18},{3,1},{4,20},{5,7},{6,22},{7,5},{8,24},{9,11},... | collective-permute-start | bytes 2211848 | tf_op jit(solution)/shard_map/ppermute | solution.py:665
  127.3 18.3 %collective-permute-start.13 = (f32[4,48,768]{2,1,0:T(8,128)S(1)}, f32[4,48,768]{2,1,0:T(8,128)S(1)}, u32[]{:S(2)}, u32[]{:S(2)}) collective-permute-start(f32[4,48,768]{2,1,0:T(8,128)S(1)} %get-tuple-element.141), channel_id=1, source_target_pairs={{0,8},{1,5},{2,10},{3,7},{4,12},{5,1},{6,14},{7,3},{8,0},{9,13},{1... | collective-permute-start | bytes 1769480 | tf_op jit(solution)/shard_map/ppermute | solution.py:665
  141.4 20.6 %collective-permute-start.15 = (f32[2,48,2048]{2,1,0:T(8,128)S(1)}, f32[2,48,2048]{2,1,0:T(8,128)S(1)}, u32[]{:S(2)}, u32[]{:S(2)}) collective-permute-start(f32[2,48,2048]{2,1,0:T(8,128)S(1)} %get-tuple-element.139), channel_id=1, source_target_pairs={{0,2},{1,5},{2,0},{3,7},{4,6},{5,1},{6,4},{7,3},{8,10},{9,13},{10,... | collective-permute-start | bytes 2359304 | tf_op jit(solution)/shard_map/ppermute | solution.py:665
  142.3 19.7 %collective-permute-start.16 = (f32[2,48,1024]{2,1,0:T(8,128)S(1)}, f32[2,48,1024]{2,1,0:T(8,128)S(1)}, u32[]{:S(2)}, u32[]{:S(2)}) collective-permute-start(f32[2,48,1024]{2,1,0:T(8,128)S(1)} %get-tuple-element.145), channel_id=1, source_target_pairs={{0,16},{1,9},{2,18},{3,11},{4,20},{5,13},{6,22},{7,15},{8,24},{9,1... | collective-permute-start | bytes 1179656 | tf_op jit(solution)/shard_map/ppermute | solution.py:665
  148.0 15.3 %collective-permute-start.14 = (f32[3,48,768]{2,1,0:T(8,128)S(1)}, f32[3,48,768]{2,1,0:T(8,128)S(1)}, u32[]{:S(2)}, u32[]{:S(2)}) collective-permute-start(f32[3,48,768]{2,1,0:T(8,128)S(1)} %get-tuple-element.143.refs_0_), channel_id=1, source_target_pairs={{0,2},{1,17},{2,0},{3,19},{4,6},{5,21},{6,4},{7,23},{8,10},{9,25},... | collective-permute-start | bytes 1327112 | tf_op jit(solution)/shard_map/ppermute | solution.py:665
  149.1 14.1 %collective-permute-start.17 = (f32[2,48,768]{2,1,0:T(8,128)S(1)}, f32[2,48,768]{2,1,0:T(8,128)S(1)}, u32[]{:S(2)}, u32[]{:S(2)}) collective-permute-start(f32[2,48,768]{2,1,0:T(8,128)S(1)} %get-tuple-element.149), channel_id=1, source_target_pairs={{0,4},{1,9},{2,6},{3,11},{4,0},{5,13},{6,2},{7,15},{8,12},{9,1},{1... | collective-permute-start | bytes 884744 | tf_op jit(solution)/shard_map/ppermute | solution.py:665
  163.2 16.0 %collective-permute-start.19 = (f32[1,48,2048]{2,1,0:T(8,128)S(1)}, f32[1,48,2048]{2,1,0:T(8,128)S(1)}, u32[]{:S(2)}, u32[]{:S(2)}) collective-permute-start(f32[1,48,2048]{2,1,0:T(8,128)S(1)} %get-tuple-element.147), channel_id=1, source_target_pairs={{0,16},{1,9},{2,18},{3,11},{4,20},{5,13},{6,22},{7,15},{8,24},{9,1... | collective-permute-start | bytes 1179656 | tf_op jit(solution)/shard_map/ppermute | solution.py:665
  163.4 19.0 %collective-permute-start.18 = (f32[2,48,768]{2,1,0:T(8,128)S(1)}, f32[2,48,768]{2,1,0:T(8,128)S(1)}, u32[]{:S(2)}, u32[]{:S(2)}) collective-permute-start(f32[2,48,768]{2,1,0:T(8,128)S(1)} %get-tuple-element.151.refs_0_), channel_id=1, source_target_pairs={{0,8},{1,9},{2,10},{3,11},{4,12},{5,13},{6,14},{7,15},{8,0},{9,1},... | collective-permute-start | bytes 884744 | tf_op jit(solution)/shard_map/ppermute | solution.py:665
  166.5 5.7 %collective-permute-start.20 = (f32[1,48,1024]{2,1,0:T(8,128)S(1)}, f32[1,48,1024]{2,1,0:T(8,128)S(1)}, u32[]{:S(2)}, u32[]{:S(2)}) collective-permute-start(f32[1,48,1024]{2,1,0:T(8,128)S(1)} %get-tuple-element.153), channel_id=1, source_target_pairs={{0,4},{1,5},{2,6},{3,7},{4,0},{5,1},{6,2},{7,3},{8,12},{9,13},{10,... | collective-permute-start | bytes 589832 | tf_op jit(solution)/shard_map/ppermute | solution.py:665
  168.0 14.4 %collective-permute-start.21 = (f32[1,48,768]{2,1,0:T(8,128)S(1)}, f32[1,48,768]{2,1,0:T(8,128)S(1)}, u32[]{:S(2)}, u32[]{:S(2)}) collective-permute-start(f32[1,48,768]{2,1,0:T(8,128)S(1)} %get-tuple-element.157), channel_id=1, source_target_pairs={{0,16},{1,17},{2,18},{3,19},{4,20},{5,21},{6,22},{7,23},{8,24},{9,... | collective-permute-start | bytes 442376 | tf_op jit(solution)/shard_map/ppermute | solution.py:665
  (6 other events, 46.4 us)

commit v7 on v6

--- a/solution.py
+++ b/solution.py
@@ -629,7 +629,7 @@
     return lax.ppermute(part, "mp", [(0, 1), (1, 0)])
 
 
-ORDERS = {"a": ("ynxf", "xfyn"), "b": ("nxfy", "fxny"), "q": ("yfxn", "yxfn"), "r": ("xnyf", "xynf")}
+ORDERS = {"a": ("yfxn", "xnyf"), "b": ("nxfy", "fxny"), "q": ("ynxf", "yfxn"), "r": ("xyfn", "xynf")}
 SIXTHS = {"a": 4, "b": 2, "q": 3, "r": 3}
 
 

time: 184 us -> 182 us (0.989)
  waiting for transfers between devices: 68.6 us -> 62.1 us
  starting transfers between devices: 25 us -> 28.7 us
    ppermute x17, waiting for transfers between devices: 64 us -> 58.1 us  [exchange(): return lax.ppermute(array, ('dp', 'mp'), pairs)]
    ppermute x17, starting transfers between devices: 23.7 us -> 27.4 us  [exchange(): return lax.ppermute(array, ('dp', 'mp'), pairs)]
  transfers between devices with their start and end apart: 22 -> 22, of which waited for: 13 -> 14; matrix products, arithmetic and copies ran while one was open for 3% -> 3% of each run, Pallas kernels for 21% -> 22%
where the time goes in v7:
time: 182 us; the launch traced here: 181 us
  Pallas kernels  82.3 us (45%)
  waiting for transfers between devices  62.1 us (34%)
  starting transfers between devices  28.7 us (16%)
  other arithmetic  6.18 us (3%)
    ppermute x17, waiting for transfers between devices, exchange(): return lax.ppermute(array, ('dp', 'mp'), pairs)  58.1 us
    pallas_call x1, Pallas kernels, forward(): pl.pallas_call(lambda *refs: forward_kernel(*refs, tables=tables, rows=ro...  29.9 us
    ppermute x17, starting transfers between devices, exchange(): return lax.ppermute(array, ('dp', 'mp'), pairs)  27.4 us
    pallas_call x1, Pallas kernels, attend_back(): pl.pallas_call(lambda *refs: attend_back_kernel(*refs, tables=tables, wid...  24.8 us
    pallas_call x2, Pallas kernels, attend(): pl.pallas_call(lambda *refs: attend_kernel(*refs, first_row=first_row), g...  16 us
    add x1, other arithmetic, on_device(): outcome = pin(middle, sum_qkv) + (down_mine + down_other) + b_down  6.18 us
    pallas_call x6, Pallas kernels, advance(): pl.pallas_call(lambda *refs: add_kernel(*refs[:len(flat)], *refs[len(flat...  4.93 us
    ppermute x5, waiting for transfers between devices, from_partner(): return lax.ppermute(part, 'mp', [(0, 1), (1, 0)])  4.03 us
  transfers between devices with their start and end apart: 22, of which 14 were waited for; matrix products, arithmetic and copies ran while one was open for 3% of the time, Pallas kernels for 22%

profile of v7, /device:TPU:0, one launch (start us, length us, event | category | flops | bytes accessed | tf_op | source)
XLA Modules:
  0.0 180.5 jit_solution(5614410353201683291)
XLA Ops:
  0.7 10.3 %attend.2 = (bf16[1024,768]{1,0:T(8,128)(2,1)}, bf16[1024,1152]{1,0:T(8,128)(2,1)}, bf16[4,6,256,256]{3,2,1,0:T(8,128)(2,1)}, bf16[1024,384]{1,0:T(8,128)(2,1)}, f32[768,768]{1,0:T(8,128)}) custom-call(s32[4,256]{1,0:T(4,128)} %refs_0_.3, f32[6,128]{1,0:T(8,128)} %bitcast.26, f32[6,128]{1,0:T(8,128)} %bitcast.32, f32[3,128]{1,0:T(4,128)} %bitcast.39, ...), custom_call_target="tpu_custom_call" | custom-call | flops 21139292 | bytes 129761 | tf_op jit(solution)/shard_map/attend/pallas_call | solution.py:283
  11.5 5.6 %attend.3 = (bf16[1024,768]{1,0:T(8,128)(2,1)}, bf16[1024,1152]{1,0:T(8,128)(2,1)}, bf16[4,6,256,256]{3,2,1,0:T(8,128)(2,1)}, bf16[1024,384]{1,0:T(8,128)(2,1)}, f32[256,768]{1,0:T(8,128)}) custom-call(s32[4,256]{1,0:T(4,128)} %refs_0_.3, f32[6,128]{1,0:T(8,128)} %bitcast.27, ...), custom_call_target="tpu_custom_call", output_to_operand_aliasing={{0}: (11, {}), {1}: (12, {}), {2}: (13, {}), {3}: (14, {})} | custom-call | flops 7046430 | bytes 58982 | tf_op jit(solution)/shard_map/attend/pallas_call | solution.py:283
  17.3 2.6 %collective-permute-done.1.refs_3_ = f32[256,768]{1,0:T(8,128)} collective-permute-done((f32[256,768]{1,0:T(8,128)}, f32[256,768]{1,0:T(8,128)}, u32[]{:S(2)}, u32[]{:S(2)}) %collective-permute-start.1) | collective-permute-done | bytes 786464 | tf_op jit(solution)/shard_map/ppermute | solution.py:629
  19.9 29.9 %forward.1 = (f32[1024,768]{1,0:T(8,128)}, f32[1024,768]{1,0:T(8,128)}, f32[1024,768]{1,0:T(8,128)}, f32[1,768]{1,0:T(1,128)}, f32[1,1536]{1,0:T(1,128)}, /*inde...) custom-call(f32[768,768]{1,0:T(8,128)} %get-tuple-element.95.refs_0_, ...), custom_call_target="tpu_custom_call" | custom-call | flops 144955152 | bytes 330301 | tf_op jit(solution)/shard_map/forward/pallas_call | solution.py:404
  50.3 2.6 %collective-permute-start.4 = (f32[8,48,2048]{2,1,0:T(8,128)}, f32[8,48,2048]{2,1,0:T(8,128)}, u32[]{:S(2)}, u32[]{:S(2)}) collective-permute-start(f32[8,48,2048]{2,1,0:T(8,128)} %get-tuple-element.111), channel_id=1, source_target_pairs={{0,4},{1,3},{2,6},{3,1},{4,0},{5,7},{6,2},{7,5},{8,12},{9,11},{10,... | collective-permute-start | bytes 9437192 | tf_op jit(solution)/shard_map/ppermute | solution.py:665
  53.0 1.6 collective-permute-start.5
  54.6 1.3 collective-permute-done.2.refs_1_
  55.8 24.8 %back.1 = (f32[1024,768]{1,0:T(8,128)}, f32[1024,768]{1,0:T(8,128)}, f32[1,768]{1,0:T(1,128)}, f32[1,768]{1,0:T(1,128)}, f32[1,768]{1,0:T(1,128)}, /*index=5*/f3...) custom-call(f32[1024,768]{1,0:T(8,128)} %get-tuple-element.102.refs_, ...), custom_call_target="tpu_custom_call" | custom-call | flops 56371444 | bytes 338165 | tf_op jit(solution)/shard_map/back/pallas_call | solution.py:528
  80.7 6.2 %add_add_fusion = f32[1024,768]{1,0:T(8,128)} fusion(f32[1024,768]{1,0:T(8,128)} %get-tuple-element.108.refs_3_, f32[1024,768]{1,0:T(8,128)} %get-tuple-element.109, f32[1024,768]{1,0:T(8,128)} %collective-permute-done.3, f32[768]{0:T(1024)} %param.34), kind=kLoop, calls=%fused_computation | loop fusion | flops 2359296 | bytes 12585984 | tf_op jit(solution)/shard_map/add | solution.py:868
  86.9 3.6 %collective-permute-done.5.refs_3_.refs_4_.refs_5_.refs_6_ = f32[8,48,1024]{2,1,0:T(8,128)} collective-permute-done((f32[8,48,1024]{2,1,0:T(8,128)}, f32[8,48,1024]{2,1,0:T(8,128)}, u32[]{:S(2)}, u32[]{:S(2)}) %collective-permute-start.5) | collective-permute-done | bytes 1572896 | tf_op jit(solution)/shard_map/ppermute | solution.py:665
  90.7 1.9 %add.28 = (f32[4,48,2048]{2,1,0:T(8,128)S(1)}, f32[4,48,1024]{2,1,0:T(8,128)S(1)}, f32[1024,768]{1,0:T(8,128)S(1)}, f32[8,48,768]{2,1,0:T(8,128)S(1)}, f32[8,48,768]{2,1,0:T(8,128)S(1)}) custom-call(f32[8,48,2048]{2,1,0:T(8,128)S(1)} %copy-done, ...), custom_call_target="tpu_custom_call", output_to_operand_aliasing={{2}: (4, {}), {3}: (5, {}), {4}: (6, {})} | custom-call | bytes 23592 | tf_op jit(solution)/shard_map/add/pallas_call | solution.py:718
  92.7 2.4 %collective-permute-start.11 = (f32[4,48,2048]{2,1,0:T(8,128)S(1)}, f32[4,48,2048]{2,1,0:T(8,128)S(1)}, u32[]{:S(2)}, u32[]{:S(2)}) collective-permute-start(f32[4,48,2048]{2,1,0:T(8,128)S(1)} %get-tuple-element.135), channel_id=1, source_target_pairs={{0,16},{1,9},{2,18},{3,11},{4,20},{5,13},{6,22},{7,15},{8,24},{9,1... | collective-permute-start | bytes 4718600 | tf_op jit(solution)/shard_map/ppermute | solution.py:665
  95.1 1.0 collective-permute-start.9
  96.1 1.5 collective-permute-start.8
  98.4 3.8 %first.1 = (f32[1024,768]{1,0:T(8,128)}, f32[1,48,768]{2,1,0:T(8,128)S(1)}) custom-call(f32[1024,768]{1,0:T(8,128)S(1)} %get-tuple-element.119.refs_0_, f32[1024,768]{1,0:T(8,128)S(1)} %collective-permute-done.6.refs_1_, f32[1024,768]{1,0:T(8,128)S(1)} %bitcast.25, f32[1024,768]{1,0:T(8,128)S(1)} %copy-done.6, f32[6,128]{1,0:T(8,128)S(1)} %bitcast.28, ...), custom_call_target="tpu_custom_call" | custom-call | flops 157286 | bytes 157286 | tf_op jit(solution)/shard_map/first/pallas_call | solution.py:610
  103.1 20.9 %collective-permute-done.9.refs_5_.refs_6_.refs_7_.refs_8_ = f32[8,48,768]{2,1,0:T(8,128)S(1)} collective-permute-done((f32[8,48,768]{2,1,0:T(8,128)S(1)}, f32[8,48,768]{2,1,0:T(8,128)S(1)}, u32[]{:S(2)}, u32[]{:S(2)}) %collective-permute-start.9) | collective-permute-done | bytes 1179680 | tf_op jit(solution)/shard_map/ppermute | solution.py:665
  124.3 1.6 collective-permute-done.7.refs_1_
  126.4 1.5 collective-permute-start.13
  127.9 11.2 %collective-permute-done.12.refs_5_.refs_6_.refs_7_ = f32[4,48,1024]{2,1,0:T(8,128)S(1)} collective-permute-done((f32[4,48,1024]{2,1,0:T(8,128)S(1)}, f32[4,48,1024]{2,1,0:T(8,128)S(1)}, u32[]{:S(2)}, u32[]{:S(2)}) %collective-permute-start.12) | collective-permute-done | bytes 786464 | tf_op jit(solution)/shard_map/ppermute | solution.py:665
  139.1 1.4 add.30
  141.4 1.2 collective-permute-start.16
  142.6 4.2 %collective-permute-done.10.refs_1_.refs_4_ = f32[5,48,768]{2,1,0:T(8,128)S(1)} collective-permute-done((f32[5,48,768]{2,1,0:T(8,128)S(1)}, f32[5,48,768]{2,1,0:T(8,128)S(1)}, u32[]{:S(2)}, u32[]{:S(2)}) %collective-permute-start.10) | collective-permute-done | bytes 737312 | tf_op jit(solution)/shard_map/ppermute | solution.py:665
  146.9 3.2 %collective-permute-start.14 = (f32[3,48,768]{2,1,0:T(8,128)S(1)}, f32[3,48,768]{2,1,0:T(8,128)S(1)}, u32[]{:S(2)}, u32[]{:S(2)}) collective-permute-start(f32[3,48,768]{2,1,0:T(8,128)S(1)} %get-tuple-element.143.refs_0_), channel_id=1, source_target_pairs={{0,2},{1,3},{2,0},{3,1},{4,6},{5,7},{6,4},{7,5},{8,10},{9,11},{10,... | collective-permute-start | bytes 1327112 | tf_op jit(solution)/shard_map/ppermute | solution.py:665
  150.1 4.2 %collective-permute-done.16.refs_7_.refs_8_ = f32[2,48,1024]{2,1,0:T(8,128)S(1)} collective-permute-done((f32[2,48,1024]{2,1,0:T(8,128)S(1)}, f32[2,48,1024]{2,1,0:T(8,128)S(1)}, u32[]{:S(2)}, u32[]{:S(2)}) %collective-permute-start.16) | collective-permute-done | bytes 393248 | tf_op jit(solution)/shard_map/ppermute | solution.py:665
  155.1 1.2 add.32
  156.3 2.6 %collective-permute-start.19 = (f32[1,48,2048]{2,1,0:T(8,128)S(1)}, f32[1,48,2048]{2,1,0:T(8,128)S(1)}, u32[]{:S(2)}, u32[]{:S(2)}) collective-permute-start(f32[1,48,2048]{2,1,0:T(8,128)S(1)} %get-tuple-element.147), channel_id=1, source_target_pairs={{0,8},{1,17},{2,10},{3,19},{4,12},{5,21},{6,14},{7,23},{8,0},{9,25... | collective-permute-start | bytes 1179656 | tf_op jit(solution)/shard_map/ppermute | solution.py:665
  159.0 7.8 %collective-permute-done.17.refs_9_.refs_10_ = f32[2,48,768]{2,1,0:T(8,128)S(1)} collective-permute-done((f32[2,48,768]{2,1,0:T(8,128)S(1)}, f32[2,48,768]{2,1,0:T(8,128)S(1)}, u32[]{:S(2)}, u32[]{:S(2)}) %collective-permute-start.17) | collective-permute-done | bytes 294944 | tf_op jit(solution)/shard_map/ppermute | solution.py:665
  167.0 2.2 %collective-permute-start.20 = (f32[1,48,1024]{2,1,0:T(8,128)S(1)}, f32[1,48,1024]{2,1,0:T(8,128)S(1)}, u32[]{:S(2)}, u32[]{:S(2)}) collective-permute-start(f32[1,48,1024]{2,1,0:T(8,128)S(1)} %get-tuple-element.153), channel_id=1, source_target_pairs={{0,4},{1,5},{2,6},{3,7},{4,0},{5,1},{6,2},{7,3},{8,12},{9,13},{10,... | collective-permute-start | bytes 589832 | tf_op jit(solution)/shard_map/ppermute | solution.py:665
  169.2 4.9 %collective-permute-start.21 = (f32[1,48,768]{2,1,0:T(8,128)S(1)}, f32[1,48,768]{2,1,0:T(8,128)S(1)}, u32[]{:S(2)}, u32[]{:S(2)}) collective-permute-start(f32[1,48,768]{2,1,0:T(8,128)S(1)} %get-tuple-element.157), channel_id=1, source_target_pairs={{0,8},{1,17},{2,10},{3,19},{4,12},{5,21},{6,14},{7,23},{8,0},{9,25... | collective-permute-start | bytes 442376 | tf_op jit(solution)/shard_map/ppermute | solution.py:665
  174.1 2.3 %collective-permute-done.19.refs_4_ = f32[1,48,2048]{2,1,0:T(8,128)S(1)} collective-permute-done((f32[1,48,2048]{2,1,0:T(8,128)S(1)}, f32[1,48,2048]{2,1,0:T(8,128)S(1)}, u32[]{:S(2)}, u32[]{:S(2)}) %collective-permute-start.19) | collective-permute-done | bytes 393248 | tf_op jit(solution)/shard_map/ppermute | solution.py:665
  176.4 2.1 %finish.2 = (f32[48,1536]{1,0:T(8,128)}, f32[48,1536]{1,0:T(8,128)}) custom-call(f32[8,48,2048]{2,1,0:T(8,128)S(1)} %copy-done, f32[8,48,2048]{2,1,0:T(8,128)} %collective-permute-done.4.refs_1_, f32[4,48,2048]{2,1,0:T(8,128)S(1)} %collective-permute-done.11.refs_2_, f32[2,48,2048]{2,1,0:T(8,128)S(1)} %collective-permute-done.15.refs_3_, ...), custom_call_target="tpu_custom_call" | custom-call | bytes 39321 | tf_op jit(solution)/shard_map/finish/pallas_call | solution.py:780
  178.4 1.2 collective-permute-done.18.refs_1_.refs_6_
  (58 shorter events, 6.5 us)
Async XLA Ops:
  11.0 8.9 %collective-permute-start = (f32[768,768]{1,0:T(8,128)}, f32[768,768]{1,0:T(8,128)}, u32[]{:S(2)}, u32[]{:S(2)}) collective-permute-start(f32[768,768]{1,0:T(8,128)} %get-tuple-element.95.refs_0_), channel_id=1, source_target_pairs={{0,1},{1,0},{2,3},{3,2},{4,5},{5,4},{6,7},{7,6},{8,9},{9,8},{10,11... | collective-permute-start | bytes 7077896 | tf_op jit(solution)/shard_map/ppermute | solution.py:629
  17.2 2.7 %collective-permute-start.1 = (f32[256,768]{1,0:T(8,128)}, f32[256,768]{1,0:T(8,128)}, u32[]{:S(2)}, u32[]{:S(2)}) collective-permute-start(f32[256,768]{1,0:T(8,128)} %get-tuple-element.100.refs_1_), channel_id=1, source_target_pairs={{0,1},{1,0},{2,3},{3,2},{4,5},{5,4},{6,7},{7,6},{8,9},{9,8},{10,11... | collective-permute-start | bytes 2359304 | tf_op jit(solution)/shard_map/ppermute | solution.py:629
  49.8 6.1 %collective-permute-start.2 = (f32[1024,768]{1,0:T(8,128)}, f32[1024,768]{1,0:T(8,128)}, u32[]{:S(2)}, u32[]{:S(2)}) collective-permute-start(f32[1024,768]{1,0:T(8,128)} %get-tuple-element.102.refs_0_), channel_id=1, source_target_pairs={{0,1},{1,0},{2,3},{3,2},{4,5},{5,4},{6,7},{7,6},{8,9},{9,8},{10,11... | collective-permute-start | bytes 9437192 | tf_op jit(solution)/shard_map/ppermute | solution.py:629
  49.9 30.8 %collective-permute-start.3 = (f32[1024,768]{1,0:T(8,128)}, f32[1024,768]{1,0:T(8,128)}, u32[]{:S(2)}, u32[]{:S(2)}) collective-permute-start(f32[1024,768]{1,0:T(8,128)} %get-tuple-element.109), channel_id=1, source_target_pairs={{0,1},{1,0},{2,3},{3,2},{4,5},{5,4},{6,7},{7,6},{8,9},{9,8},{10,11... | collective-permute-start | bytes 9437192 | tf_op jit(solution)/shard_map/ppermute | solution.py:629
  50.3 40.2 %collective-permute-start.4 = (f32[8,48,2048]{2,1,0:T(8,128)}, f32[8,48,2048]{2,1,0:T(8,128)}, u32[]{:S(2)}, u32[]{:S(2)}) collective-permute-start(f32[8,48,2048]{2,1,0:T(8,128)} %get-tuple-element.111), channel_id=1, source_target_pairs={{0,4},{1,3},{2,6},{3,1},{4,0},{5,7},{6,2},{7,5},{8,12},{9,11},{10,... | collective-permute-start | bytes 9437192 | tf_op jit(solution)/shard_map/ppermute | solution.py:665
  53.0 37.6 %collective-permute-start.5 = (f32[8,48,1024]{2,1,0:T(8,128)}, f32[8,48,1024]{2,1,0:T(8,128)}, u32[]{:S(2)}, u32[]{:S(2)}) collective-permute-start(f32[8,48,1024]{2,1,0:T(8,128)} %get-tuple-element.114), channel_id=1, source_target_pairs={{0,8},{1,17},{2,10},{3,19},{4,12},{5,21},{6,14},{7,23},{8,0},{9,25... | collective-permute-start | bytes 4718600 | tf_op jit(solution)/shard_map/ppermute | solution.py:665
  80.7 9.9 %copy-start = (f32[8,48,2048]{2,1,0:T(8,128)S(1)}, f32[8,48,2048]{2,1,0:T(8,128)}, u32[]{:S(2)}) copy-start(f32[8,48,2048]{2,1,0:T(8,128)} %get-tuple-element.110.refs_0_) | copy-start | bytes 9437188
  80.7 9.9 %copy-start.2 = (f32[8,48,1024]{2,1,0:T(8,128)S(1)}, f32[8,48,1024]{2,1,0:T(8,128)}, u32[]{:S(2)}) copy-start(f32[8,48,1024]{2,1,0:T(8,128)} %get-tuple-element.113.refs_2_.refs_3_.refs_4_.refs_5_) | copy-start | bytes 4718596
  80.7 9.9 %copy-start.5 = (f32[1024,768]{1,0:T(8,128)S(1)}, f32[1024,768]{1,0:T(8,128)}, u32[]{:S(2)}) copy-start(f32[1024,768]{1,0:T(8,128)} %get-tuple-element.116.refs_4_) | copy-start | bytes 9437188
  80.7 9.9 %copy-start.7 = (f32[8,48,768]{2,1,0:T(8,128)S(1)}, f32[8,48,768]{2,1,0:T(8,128)}, u32[]{:S(2)}) copy-start(f32[8,48,768]{2,1,0:T(8,128)} %get-tuple-element.117.refs_5_) | copy-start | bytes 3538948
  80.7 9.9 %copy-start.8 = (f32[8,48,768]{2,1,0:T(8,128)S(1)}, f32[8,48,768]{2,1,0:T(8,128)}, u32[]{:S(2)}) copy-start(f32[8,48,768]{2,1,0:T(8,128)} %get-tuple-element.118.refs_6_) | copy-start | bytes 3538948
  90.6 7.8 %copy-start.1 = (f32[4,256,768]{2,1,0:T(8,128)S(1)}, f32[4,256,768]{2,1,0:T(8,128)}, u32[]{:S(2)}) copy-start(f32[4,256,768]{2,1,0:T(8,128)} %param.18) | copy-start | bytes 9437188
  90.6 7.8 %copy-start.6 = (f32[1024,768]{1,0:T(8,128)S(1)}, f32[1024,768]{1,0:T(8,128)}, u32[]{:S(2)}) copy-start(f32[1024,768]{1,0:T(8,128)} %get-tuple-element.120.refs_3_) | copy-start | bytes 9437188
  90.6 7.7 %copy-start.9 = (f32[768]{0:T(1024)S(1)}, f32[768]{0:T(1024)}, u32[]{:S(2)}) copy-start(f32[768]{0:T(1024)} %param.20) | copy-start | bytes 9220
  92.6 5.7 %collective-permute-start.6 = (f32[1024,768]{1,0:T(8,128)S(1)}, f32[1024,768]{1,0:T(8,128)S(1)}, u32[]{:S(2)}, u32[]{:S(2)}) collective-permute-start(f32[1024,768]{1,0:T(8,128)S(1)} %get-tuple-element.119.refs_0_), channel_id=1, source_target_pairs={{0,1},{1,0},{2,3},{3,2},{4,5},{5,4},{6,7},{7,6},{8,9},{9,8},{10,11... | collective-permute-start | bytes 9437192 | tf_op jit(solution)/shard_map/ppermute | solution.py:629
  92.7 46.4 %collective-permute-start.11 = (f32[4,48,2048]{2,1,0:T(8,128)S(1)}, f32[4,48,2048]{2,1,0:T(8,128)S(1)}, u32[]{:S(2)}, u32[]{:S(2)}) collective-permute-start(f32[4,48,2048]{2,1,0:T(8,128)S(1)} %get-tuple-element.135), channel_id=1, source_target_pairs={{0,16},{1,9},{2,18},{3,11},{4,20},{5,13},{6,22},{7,15},{8,24},{9,1... | collective-permute-start | bytes 4718600 | tf_op jit(solution)/shard_map/ppermute | solution.py:665
  95.1 28.9 %collective-permute-start.9 = (f32[8,48,768]{2,1,0:T(8,128)S(1)}, f32[8,48,768]{2,1,0:T(8,128)S(1)}, u32[]{:S(2)}, u32[]{:S(2)}) collective-permute-start(f32[8,48,768]{2,1,0:T(8,128)S(1)} %get-tuple-element.132), channel_id=1, source_target_pairs={{0,2},{1,3},{2,0},{3,1},{4,6},{5,7},{6,4},{7,5},{8,10},{9,11},{10,... | collective-permute-start | bytes 3538952 | tf_op jit(solution)/shard_map/ppermute | solution.py:665
  96.1 28.2 %collective-permute-start.8 = (f32[8,48,768]{2,1,0:T(8,128)S(1)}, f32[8,48,768]{2,1,0:T(8,128)S(1)}, u32[]{:S(2)}, u32[]{:S(2)}) collective-permute-start(f32[8,48,768]{2,1,0:T(8,128)S(1)} %get-tuple-element.129), channel_id=1, source_target_pairs={{0,4},{1,5},{2,6},{3,7},{4,0},{5,1},{6,2},{7,3},{8,12},{9,13},{10,... | collective-permute-start | bytes 3538952 | tf_op jit(solution)/shard_map/ppermute | solution.py:665
  97.6 41.5 %collective-permute-start.12 = (f32[4,48,1024]{2,1,0:T(8,128)S(1)}, f32[4,48,1024]{2,1,0:T(8,128)S(1)}, u32[]{:S(2)}, u32[]{:S(2)}) collective-permute-start(f32[4,48,1024]{2,1,0:T(8,128)S(1)} %get-tuple-element.137), channel_id=1, source_target_pairs={{0,2},{1,3},{2,0},{3,1},{4,6},{5,7},{6,4},{7,5},{8,10},{9,11},{10,... | collective-permute-start | bytes 2359304 | tf_op jit(solution)/shard_map/ppermute | solution.py:665
  98.4 27.5 %copy-start.3 = (f32[8,48,768]{2,1,0:T(8,128)S(1)}, f32[8,48,768]{2,1,0:T(8,128)}, u32[]{:S(2)}) copy-start(f32[8,48,768]{2,1,0:T(8,128)} %get-tuple-element.128.refs_2_) | copy-start | bytes 3538948
  98.4 27.5 %copy-start.4 = (f32[8,48,768]{2,1,0:T(8,128)S(1)}, f32[8,48,768]{2,1,0:T(8,128)}, u32[]{:S(2)}) copy-start(f32[8,48,768]{2,1,0:T(8,128)} %get-tuple-element.131.refs_4_.refs_5_.refs_6_.refs_7_) | copy-start | bytes 3538948
  102.3 23.6 %collective-permute-start.7 = (f32[1,48,768]{2,1,0:T(8,128)S(1)}, f32[1,48,768]{2,1,0:T(8,128)S(1)}, u32[]{:S(2)}, u32[]{:S(2)}) collective-permute-start(f32[1,48,768]{2,1,0:T(8,128)S(1)} %get-tuple-element.127.refs_0_), channel_id=1, source_target_pairs={{0,4},{1,5},{2,6},{3,7},{4,0},{5,1},{6,2},{7,3},{8,12},{9,13},{10,... | collective-permute-start | bytes 442376 | tf_op jit(solution)/shard_map/ppermute | solution.py:665
  126.1 20.8 %collective-permute-start.10 = (f32[5,48,768]{2,1,0:T(8,128)S(1)}, f32[5,48,768]{2,1,0:T(8,128)S(1)}, u32[]{:S(2)}, u32[]{:S(2)}) collective-permute-start(f32[5,48,768]{2,1,0:T(8,128)S(1)} %get-tuple-element.134.refs_0_), channel_id=1, source_target_pairs={{0,8},{1,17},{2,10},{3,19},{4,12},{5,21},{6,14},{7,23},{8,0},{9,25... | collective-permute-start | bytes 2211848 | tf_op jit(solution)/shard_map/ppermute | solution.py:665
  126.4 16.2 %collective-permute-start.13 = (f32[4,48,768]{2,1,0:T(8,128)S(1)}, f32[4,48,768]{2,1,0:T(8,128)S(1)}, u32[]{:S(2)}, u32[]{:S(2)}) collective-permute-start(f32[4,48,768]{2,1,0:T(8,128)S(1)} %get-tuple-element.141), channel_id=1, source_target_pairs={{0,4},{1,5},{2,6},{3,7},{4,0},{5,1},{6,2},{7,3},{8,12},{9,13},{10,... | collective-permute-start | bytes 1769480 | tf_op jit(solution)/shard_map/ppermute | solution.py:665
  140.6 14.6 %collective-permute-start.15 = (f32[2,48,2048]{2,1,0:T(8,128)S(1)}, f32[2,48,2048]{2,1,0:T(8,128)S(1)}, u32[]{:S(2)}, u32[]{:S(2)}) collective-permute-start(f32[2,48,2048]{2,1,0:T(8,128)S(1)} %get-tuple-element.139), channel_id=1, source_target_pairs={{0,2},{1,5},{2,0},{3,7},{4,6},{5,1},{6,4},{7,3},{8,10},{9,13},{10,... | collective-permute-start | bytes 2359304 | tf_op jit(solution)/shard_map/ppermute | solution.py:665
  141.4 12.9 %collective-permute-start.16 = (f32[2,48,1024]{2,1,0:T(8,128)S(1)}, f32[2,48,1024]{2,1,0:T(8,128)S(1)}, u32[]{:S(2)}, u32[]{:S(2)}) collective-permute-start(f32[2,48,1024]{2,1,0:T(8,128)S(1)} %get-tuple-element.145), channel_id=1, source_target_pairs={{0,16},{1,9},{2,18},{3,11},{4,20},{5,13},{6,22},{7,15},{8,24},{9,1... | collective-permute-start | bytes 1179656 | tf_op jit(solution)/shard_map/ppermute | solution.py:665
  146.9 19.8 %collective-permute-start.14 = (f32[3,48,768]{2,1,0:T(8,128)S(1)}, f32[3,48,768]{2,1,0:T(8,128)S(1)}, u32[]{:S(2)}, u32[]{:S(2)}) collective-permute-start(f32[3,48,768]{2,1,0:T(8,128)S(1)} %get-tuple-element.143.refs_0_), channel_id=1, source_target_pairs={{0,2},{1,3},{2,0},{3,1},{4,6},{5,7},{6,4},{7,5},{8,10},{9,11},{10,... | collective-permute-start | bytes 1327112 | tf_op jit(solution)/shard_map/ppermute | solution.py:665
  150.1 16.7 %collective-permute-start.17 = (f32[2,48,768]{2,1,0:T(8,128)S(1)}, f32[2,48,768]{2,1,0:T(8,128)S(1)}, u32[]{:S(2)}, u32[]{:S(2)}) collective-permute-start(f32[2,48,768]{2,1,0:T(8,128)S(1)} %get-tuple-element.149), channel_id=1, source_target_pairs={{0,16},{1,9},{2,18},{3,11},{4,20},{5,13},{6,22},{7,15},{8,24},{9,1... | collective-permute-start | bytes 884744 | tf_op jit(solution)/shard_map/ppermute | solution.py:665
  156.3 20.0 %collective-permute-start.19 = (f32[1,48,2048]{2,1,0:T(8,128)S(1)}, f32[1,48,2048]{2,1,0:T(8,128)S(1)}, u32[]{:S(2)}, u32[]{:S(2)}) collective-permute-start(f32[1,48,2048]{2,1,0:T(8,128)S(1)} %get-tuple-element.147), channel_id=1, source_target_pairs={{0,8},{1,17},{2,10},{3,19},{4,12},{5,21},{6,14},{7,23},{8,0},{9,25... | collective-permute-start | bytes 1179656 | tf_op jit(solution)/shard_map/ppermute | solution.py:665
  166.9 12.7 %collective-permute-start.18 = (f32[2,48,768]{2,1,0:T(8,128)S(1)}, f32[2,48,768]{2,1,0:T(8,128)S(1)}, u32[]{:S(2)}, u32[]{:S(2)}) collective-permute-start(f32[2,48,768]{2,1,0:T(8,128)S(1)} %get-tuple-element.151.refs_0_), channel_id=1, source_target_pairs={{0,16},{1,9},{2,18},{3,11},{4,20},{5,13},{6,22},{7,15},{8,24},{9,1... | collective-permute-start | bytes 884744 | tf_op jit(solution)/shard_map/ppermute | solution.py:665
  167.0 7.1 %collective-permute-start.20 = (f32[1,48,1024]{2,1,0:T(8,128)S(1)}, f32[1,48,1024]{2,1,0:T(8,128)S(1)}, u32[]{:S(2)}, u32[]{:S(2)}) collective-permute-start(f32[1,48,1024]{2,1,0:T(8,128)S(1)} %get-tuple-element.153), channel_id=1, source_target_pairs={{0,4},{1,5},{2,6},{3,7},{4,0},{5,1},{6,2},{7,3},{8,12},{9,13},{10,... | collective-permute-start | bytes 589832 | tf_op jit(solution)/shard_map/ppermute | solution.py:665
  169.2 9.3 %collective-permute-start.21 = (f32[1,48,768]{2,1,0:T(8,128)S(1)}, f32[1,48,768]{2,1,0:T(8,128)S(1)}, u32[]{:S(2)}, u32[]{:S(2)}) collective-permute-start(f32[1,48,768]{2,1,0:T(8,128)S(1)} %get-tuple-element.157), channel_id=1, source_target_pairs={{0,8},{1,17},{2,10},{3,19},{4,12},{5,21},{6,14},{7,23},{8,0},{9,25... | collective-permute-start | bytes 442376 | tf_op jit(solution)/shard_map/ppermute | solution.py:665
  (6 other events, 46.4 us)

commit v8 on v7

--- a/solution.py
+++ b/solution.py
@@ -630,7 +630,7 @@
 
 
 ORDERS = {"a": ("yfxn", "xnyf"), "b": ("nxfy", "fxny"), "q": ("ynxf", "yfxn"), "r": ("xyfn", "xynf")}
-SIXTHS = {"a": 4, "b": 2, "q": 3, "r": 3}
+SHARES = {"a": 17, "b": 7, "q": 12, "r": 12}
 
 
 def orders_for(kind, bits):
@@ -837,7 +837,7 @@
     bits = butterfly_bits(width)
 
     orders = {key: orders_for(ORDERS[key], bits) for key in ORDERS}
-    widths = [2 * hidden * SIXTHS[key] // 6 for key in "ab"] + [4 * cols * SIXTHS[key] // 6 for key in "qr"]
+    widths = [2 * hidden * SHARES[key] // 24 for key in "ab"] + [4 * cols * SHARES[key] // 24 for key in "qr"]
     tables = {key: block_masks(orders[key], bits) for key in ORDERS} if bits else {}
 
     most = rows - 1

time: 182 us -> 184 us (1.011)
  waiting for transfers between devices: 62.1 us -> 66.8 us
    ppermute x17, waiting for transfers between devices: 58.1 us -> 63 us  [exchange(): return lax.ppermute(array, ('dp', 'mp'), pairs)]
  transfers between devices with their start and end apart: 22 -> 22, of which waited for: 14 -> 13; matrix products, arithmetic and copies ran while one was open for 3% -> 3% of each run, Pallas kernels for 22% -> 21%
where the time goes in v8:
time: 184 us
  Pallas kernels  82.5 us (45%)
  waiting for transfers between devices  66.8 us (36%)
  starting transfers between devices  27.2 us (15%)
  other arithmetic  6.18 us (3%)
    ppermute x17, waiting for transfers between devices, exchange(): return lax.ppermute(array, ('dp', 'mp'), pairs)  63 us
    pallas_call x1, Pallas kernels, forward(): pl.pallas_call(lambda *refs: forward_kernel(*refs, tables=tables, rows=ro...  30.2 us
    ppermute x17, starting transfers between devices, exchange(): return lax.ppermute(array, ('dp', 'mp'), pairs)  25.9 us
    pallas_call x1, Pallas kernels, attend_back(): pl.pallas_call(lambda *refs: attend_back_kernel(*refs, tables=tables, wid...  24.8 us
    pallas_call x2, Pallas kernels, attend(): pl.pallas_call(lambda *refs: attend_kernel(*refs, first_row=first_row), g...  15.9 us
    add x1, other arithmetic, on_device(): outcome = pin(middle, sum_qkv) + (down_mine + down_other) + b_down  6.18 us
    pallas_call x6, Pallas kernels, advance(): pl.pallas_call(lambda *refs: add_kernel(*refs[:len(flat)], *refs[len(flat...  4.91 us
    ppermute x5, waiting for transfers between devices, from_partner(): return lax.ppermute(part, 'mp', [(0, 1), (1, 0)])  3.86 us
  transfers between devices with their start and end apart: 22, of which 13 were waited for; matrix products, arithmetic and copies ran while one was open for 3% of the time, Pallas kernels for 21%

profile of v8, /device:TPU:0, one launch (start us, length us, event | category | flops | bytes accessed | tf_op | source)
XLA Modules:
  0.0 183.9 jit_solution(4181781940639491219)
XLA Ops:
  0.7 10.3 %attend.2 = (bf16[1024,768]{1,0:T(8,128)(2,1)}, bf16[1024,1152]{1,0:T(8,128)(2,1)}, bf16[4,6,256,256]{3,2,1,0:T(8,128)(2,1)}, bf16[1024,384]{1,0:T(8,128)(2,1)}, f32[768,768]{1,0:T(8,128)}) custom-call(s32[4,256]{1,0:T(4,128)} %refs_0_.3, f32[6,128]{1,0:T(8,128)} %bitcast.26, f32[6,128]{1,0:T(8,128)} %bitcast.32, f32[3,128]{1,0:T(4,128)} %bitcast.39, ...), custom_call_target="tpu_custom_call" | custom-call | flops 21139292 | bytes 129761 | tf_op jit(solution)/shard_map/attend/pallas_call | solution.py:283
  11.5 5.6 %attend.3 = (bf16[1024,768]{1,0:T(8,128)(2,1)}, bf16[1024,1152]{1,0:T(8,128)(2,1)}, bf16[4,6,256,256]{3,2,1,0:T(8,128)(2,1)}, bf16[1024,384]{1,0:T(8,128)(2,1)}, f32[256,768]{1,0:T(8,128)}) custom-call(s32[4,256]{1,0:T(4,128)} %refs_0_.3, f32[6,128]{1,0:T(8,128)} %bitcast.27, ...), custom_call_target="tpu_custom_call", output_to_operand_aliasing={{0}: (11, {}), {1}: (12, {}), {2}: (13, {}), {3}: (14, {})} | custom-call | flops 7046430 | bytes 58982 | tf_op jit(solution)/shard_map/attend/pallas_call | solution.py:283
  17.2 2.6 %collective-permute-done.1.refs_3_ = f32[256,768]{1,0:T(8,128)} collective-permute-done((f32[256,768]{1,0:T(8,128)}, f32[256,768]{1,0:T(8,128)}, u32[]{:S(2)}, u32[]{:S(2)}) %collective-permute-start.1) | collective-permute-done | bytes 786464 | tf_op jit(solution)/shard_map/ppermute | solution.py:629
  19.8 30.2 %forward.1 = (f32[1024,768]{1,0:T(8,128)}, f32[1024,768]{1,0:T(8,128)}, f32[1024,768]{1,0:T(8,128)}, f32[1,768]{1,0:T(1,128)}, f32[1,1536]{1,0:T(1,128)}, /*inde...) custom-call(f32[768,768]{1,0:T(8,128)} %get-tuple-element.95.refs_0_, ...), custom_call_target="tpu_custom_call" | custom-call | flops 144955152 | bytes 330301 | tf_op jit(solution)/shard_map/forward/pallas_call | solution.py:404
  50.6 2.6 %collective-permute-start.4 = (f32[8,48,2176]{2,1,0:T(8,128)}, f32[8,48,2176]{2,1,0:T(8,128)}, u32[]{:S(2)}, u32[]{:S(2)}) collective-permute-start(f32[8,48,2176]{2,1,0:T(8,128)} %get-tuple-element.111), channel_id=1, source_target_pairs={{0,4},{1,3},{2,6},{3,1},{4,0},{5,7},{6,2},{7,5},{8,12},{9,11},{10,... | collective-permute-start | bytes 10027016 | tf_op jit(solution)/shard_map/ppermute | solution.py:665
  53.2 1.6 collective-permute-start.5
  54.8 1.3 collective-permute-done.2.refs_1_
  56.1 24.8 %back.1 = (f32[1024,768]{1,0:T(8,128)}, f32[1024,768]{1,0:T(8,128)}, f32[1,768]{1,0:T(1,128)}, f32[1,768]{1,0:T(1,128)}, f32[1,768]{1,0:T(1,128)}, /*index=5*/f3...) custom-call(f32[1024,768]{1,0:T(8,128)} %get-tuple-element.102.refs_, ...), custom_call_target="tpu_custom_call" | custom-call | flops 56371444 | bytes 338165 | tf_op jit(solution)/shard_map/back/pallas_call | solution.py:528
  81.0 6.2 %add_add_fusion = f32[1024,768]{1,0:T(8,128)} fusion(f32[1024,768]{1,0:T(8,128)} %get-tuple-element.108.refs_3_, f32[1024,768]{1,0:T(8,128)} %get-tuple-element.109, f32[1024,768]{1,0:T(8,128)} %collective-permute-done.3, f32[768]{0:T(1024)} %param.34), kind=kLoop, calls=%fused_computation | loop fusion | flops 2359296 | bytes 12585984 | tf_op jit(solution)/shard_map/add | solution.py:868
  87.1 3.7 %collective-permute-done.4.refs_1_ = f32[8,48,2176]{2,1,0:T(8,128)} collective-permute-done((f32[8,48,2176]{2,1,0:T(8,128)}, f32[8,48,2176]{2,1,0:T(8,128)}, u32[]{:S(2)}, u32[]{:S(2)}) %collective-permute-start.4) | collective-permute-done | bytes 3342368 | tf_op jit(solution)/shard_map/ppermute | solution.py:665
  91.0 1.9 %add.28 = (f32[4,48,2176]{2,1,0:T(8,128)S(1)}, f32[4,48,896]{2,1,0:T(8,128)S(1)}, f32[1024,768]{1,0:T(8,128)S(1)}, f32[8,48,768]{2,1,0:T(8,128)S(1)}, f32[8,48,768]{2,1,0:T(8,128)S(1)}) custom-call(f32[8,48,2176]{2,1,0:T(8,128)S(1)} %copy-done, ...), custom_call_target="tpu_custom_call", output_to_operand_aliasing={{2}: (4, {}), {3}: (5, {}), {4}: (6, {})} | custom-call | bytes 23592 | tf_op jit(solution)/shard_map/add/pallas_call | solution.py:718
  93.0 3.2 %collective-permute-start.11 = (f32[4,48,2176]{2,1,0:T(8,128)S(1)}, f32[4,48,2176]{2,1,0:T(8,128)S(1)}, u32[]{:S(2)}, u32[]{:S(2)}) collective-permute-start(f32[4,48,2176]{2,1,0:T(8,128)S(1)} %get-tuple-element.135), channel_id=1, source_target_pairs={{0,16},{1,9},{2,18},{3,11},{4,20},{5,13},{6,22},{7,15},{8,24},{9,1... | collective-permute-start | bytes 5013512 | tf_op jit(solution)/shard_map/ppermute | solution.py:665
  96.2 1.5 collective-permute-start.9
  97.7 1.5 collective-permute-start.8
  99.8 3.8 %first.1 = (f32[1024,768]{1,0:T(8,128)}, f32[1,48,768]{2,1,0:T(8,128)S(1)}) custom-call(f32[1024,768]{1,0:T(8,128)S(1)} %get-tuple-element.119.refs_0_, f32[1024,768]{1,0:T(8,128)S(1)} %collective-permute-done.6.refs_1_, f32[1024,768]{1,0:T(8,128)S(1)} %bitcast.25, f32[1024,768]{1,0:T(8,128)S(1)} %copy-done.6, f32[6,128]{1,0:T(8,128)S(1)} %bitcast.28, ...), custom_call_target="tpu_custom_call" | custom-call | flops 157286 | bytes 157286 | tf_op jit(solution)/shard_map/first/pallas_call | solution.py:610
  103.7 1.0 collective-permute-start.7
  104.6 20.5 %collective-permute-done.9.refs_5_.refs_6_.refs_7_.refs_8_ = f32[8,48,768]{2,1,0:T(8,128)S(1)} collective-permute-done((f32[8,48,768]{2,1,0:T(8,128)S(1)}, f32[8,48,768]{2,1,0:T(8,128)S(1)}, u32[]{:S(2)}, u32[]{:S(2)}) %collective-permute-start.9) | collective-permute-done | bytes 1179680 | tf_op jit(solution)/shard_map/ppermute | solution.py:665
  126.0 1.6 collective-permute-done.7.refs_1_
  128.2 1.5 collective-permute-start.13
  129.7 8.2 %collective-permute-done.12.refs_5_.refs_6_.refs_7_ = f32[4,48,896]{2,1,0:T(8,128)S(1)} collective-permute-done((f32[4,48,896]{2,1,0:T(8,128)S(1)}, f32[4,48,896]{2,1,0:T(8,128)S(1)}, u32[]{:S(2)}, u32[]{:S(2)}) %collective-permute-start.12) | collective-permute-done | bytes 688160 | tf_op jit(solution)/shard_map/ppermute | solution.py:665
  137.9 1.4 add.30
  139.4 1.6 collective-permute-start.15
  140.9 1.8 collective-permute-start.16
  143.6 10.0 %collective-permute-done.10.refs_1_.refs_4_ = f32[5,48,768]{2,1,0:T(8,128)S(1)} collective-permute-done((f32[5,48,768]{2,1,0:T(8,128)S(1)}, f32[5,48,768]{2,1,0:T(8,128)S(1)}, u32[]{:S(2)}, u32[]{:S(2)}) %collective-permute-start.10) | collective-permute-done | bytes 737312 | tf_op jit(solution)/shard_map/ppermute | solution.py:665
  153.7 0.9 collective-permute-start.14
  155.5 1.2 add.32
  156.7 2.9 %collective-permute-start.19 = (f32[1,48,2176]{2,1,0:T(8,128)S(1)}, f32[1,48,2176]{2,1,0:T(8,128)S(1)}, u32[]{:S(2)}, u32[]{:S(2)}) collective-permute-start(f32[1,48,2176]{2,1,0:T(8,128)S(1)} %get-tuple-element.147), channel_id=1, source_target_pairs={{0,8},{1,17},{2,10},{3,19},{4,12},{5,21},{6,14},{7,23},{8,0},{9,25... | collective-permute-start | bytes 1253384 | tf_op jit(solution)/shard_map/ppermute | solution.py:665
  159.6 10.9 %collective-permute-done.17.refs_9_.refs_10_ = f32[2,48,768]{2,1,0:T(8,128)S(1)} collective-permute-done((f32[2,48,768]{2,1,0:T(8,128)S(1)}, f32[2,48,768]{2,1,0:T(8,128)S(1)}, u32[]{:S(2)}, u32[]{:S(2)}) %collective-permute-start.17) | collective-permute-done | bytes 294944 | tf_op jit(solution)/shard_map/ppermute | solution.py:665
  170.7 4.5 %collective-permute-start.20 = (f32[1,48,896]{2,1,0:T(8,128)S(1)}, f32[1,48,896]{2,1,0:T(8,128)S(1)}, u32[]{:S(2)}, u32[]{:S(2)}) collective-permute-start(f32[1,48,896]{2,1,0:T(8,128)S(1)} %get-tuple-element.153), channel_id=1, source_target_pairs={{0,4},{1,5},{2,6},{3,7},{4,0},{5,1},{6,2},{7,3},{8,12},{9,13},{10,... | collective-permute-start | bytes 516104 | tf_op jit(solution)/shard_map/ppermute | solution.py:665
  175.4 3.2 %collective-permute-done.20.refs_9_ = f32[1,48,896]{2,1,0:T(8,128)S(1)} collective-permute-done((f32[1,48,896]{2,1,0:T(8,128)S(1)}, f32[1,48,896]{2,1,0:T(8,128)S(1)}, u32[]{:S(2)}, u32[]{:S(2)}) %collective-permute-start.20) | collective-permute-done | bytes 172064 | tf_op jit(solution)/shard_map/ppermute | solution.py:665
  178.6 2.0 %finish.2 = (f32[48,1536]{1,0:T(8,128)}, f32[48,1536]{1,0:T(8,128)}) custom-call(f32[8,48,2176]{2,1,0:T(8,128)S(1)} %copy-done, f32[8,48,2176]{2,1,0:T(8,128)} %collective-permute-done.4.refs_1_, f32[4,48,2176]{2,1,0:T(8,128)S(1)} %collective-permute-done.11.refs_2_, f32[2,48,2176]{2,1,0:T(8,128)S(1)} %collective-permute-done.15.refs_3_, ...), custom_call_target="tpu_custom_call" | custom-call | bytes 41779 | tf_op jit(solution)/shard_map/finish/pallas_call | solution.py:780
  180.6 2.3 %collective-permute-done.18.refs_1_.refs_6_ = f32[2,48,768]{2,1,0:T(8,128)S(1)} collective-permute-done((f32[2,48,768]{2,1,0:T(8,128)S(1)}, f32[2,48,768]{2,1,0:T(8,128)S(1)}, u32[]{:S(2)}, u32[]{:S(2)}) %collective-permute-start.18) | collective-permute-done | bytes 294944 | tf_op jit(solution)/shard_map/ppermute | solution.py:665
  (58 shorter events, 6.6 us)
Async XLA Ops:
  11.0 8.9 %collective-permute-start = (f32[768,768]{1,0:T(8,128)}, f32[768,768]{1,0:T(8,128)}, u32[]{:S(2)}, u32[]{:S(2)}) collective-permute-start(f32[768,768]{1,0:T(8,128)} %get-tuple-element.95.refs_0_), channel_id=1, source_target_pairs={{0,1},{1,0},{2,3},{3,2},{4,5},{5,4},{6,7},{7,6},{8,9},{9,8},{10,11... | collective-permute-start | bytes 7077896 | tf_op jit(solution)/shard_map/ppermute | solution.py:629
  17.1 2.7 %collective-permute-start.1 = (f32[256,768]{1,0:T(8,128)}, f32[256,768]{1,0:T(8,128)}, u32[]{:S(2)}, u32[]{:S(2)}) collective-permute-start(f32[256,768]{1,0:T(8,128)} %get-tuple-element.100.refs_1_), channel_id=1, source_target_pairs={{0,1},{1,0},{2,3},{3,2},{4,5},{5,4},{6,7},{7,6},{8,9},{9,8},{10,11... | collective-permute-start | bytes 2359304 | tf_op jit(solution)/shard_map/ppermute | solution.py:629
  50.0 6.1 %collective-permute-start.2 = (f32[1024,768]{1,0:T(8,128)}, f32[1024,768]{1,0:T(8,128)}, u32[]{:S(2)}, u32[]{:S(2)}) collective-permute-start(f32[1024,768]{1,0:T(8,128)} %get-tuple-element.102.refs_0_), channel_id=1, source_target_pairs={{0,1},{1,0},{2,3},{3,2},{4,5},{5,4},{6,7},{7,6},{8,9},{9,8},{10,11... | collective-permute-start | bytes 9437192 | tf_op jit(solution)/shard_map/ppermute | solution.py:629
  50.2 30.7 %collective-permute-start.3 = (f32[1024,768]{1,0:T(8,128)}, f32[1024,768]{1,0:T(8,128)}, u32[]{:S(2)}, u32[]{:S(2)}) collective-permute-start(f32[1024,768]{1,0:T(8,128)} %get-tuple-element.109), channel_id=1, source_target_pairs={{0,1},{1,0},{2,3},{3,2},{4,5},{5,4},{6,7},{7,6},{8,9},{9,8},{10,11... | collective-permute-start | bytes 9437192 | tf_op jit(solution)/shard_map/ppermute | solution.py:629
  50.6 40.3 %collective-permute-start.4 = (f32[8,48,2176]{2,1,0:T(8,128)}, f32[8,48,2176]{2,1,0:T(8,128)}, u32[]{:S(2)}, u32[]{:S(2)}) collective-permute-start(f32[8,48,2176]{2,1,0:T(8,128)} %get-tuple-element.111), channel_id=1, source_target_pairs={{0,4},{1,3},{2,6},{3,1},{4,0},{5,7},{6,2},{7,5},{8,12},{9,11},{10,... | collective-permute-start | bytes 10027016 | tf_op jit(solution)/shard_map/ppermute | solution.py:665
  53.2 33.9 %collective-permute-start.5 = (f32[8,48,896]{2,1,0:T(8,128)}, f32[8,48,896]{2,1,0:T(8,128)}, u32[]{:S(2)}, u32[]{:S(2)}) collective-permute-start(f32[8,48,896]{2,1,0:T(8,128)} %get-tuple-element.114), channel_id=1, source_target_pairs={{0,8},{1,17},{2,10},{3,19},{4,12},{5,21},{6,14},{7,23},{8,0},{9,25... | collective-permute-start | bytes 4128776 | tf_op jit(solution)/shard_map/ppermute | solution.py:665
  80.9 10.0 %copy-start = (f32[8,48,2176]{2,1,0:T(8,128)S(1)}, f32[8,48,2176]{2,1,0:T(8,128)}, u32[]{:S(2)}) copy-start(f32[8,48,2176]{2,1,0:T(8,128)} %get-tuple-element.110.refs_0_) | copy-start | bytes 10027012
  80.9 10.0 %copy-start.2 = (f32[8,48,896]{2,1,0:T(8,128)S(1)}, f32[8,48,896]{2,1,0:T(8,128)}, u32[]{:S(2)}) copy-start(f32[8,48,896]{2,1,0:T(8,128)} %get-tuple-element.113.refs_2_.refs_3_.refs_4_.refs_5_) | copy-start | bytes 4128772
  80.9 10.0 %copy-start.5 = (f32[1024,768]{1,0:T(8,128)S(1)}, f32[1024,768]{1,0:T(8,128)}, u32[]{:S(2)}) copy-start(f32[1024,768]{1,0:T(8,128)} %get-tuple-element.116.refs_4_) | copy-start | bytes 9437188
  80.9 10.0 %copy-start.7 = (f32[8,48,768]{2,1,0:T(8,128)S(1)}, f32[8,48,768]{2,1,0:T(8,128)}, u32[]{:S(2)}) copy-start(f32[8,48,768]{2,1,0:T(8,128)} %get-tuple-element.117.refs_5_) | copy-start | bytes 3538948
  80.9 10.0 %copy-start.8 = (f32[8,48,768]{2,1,0:T(8,128)S(1)}, f32[8,48,768]{2,1,0:T(8,128)}, u32[]{:S(2)}) copy-start(f32[8,48,768]{2,1,0:T(8,128)} %get-tuple-element.118.refs_6_) | copy-start | bytes 3538948
  90.9 8.8 %copy-start.1 = (f32[4,256,768]{2,1,0:T(8,128)S(1)}, f32[4,256,768]{2,1,0:T(8,128)}, u32[]{:S(2)}) copy-start(f32[4,256,768]{2,1,0:T(8,128)} %param.18) | copy-start | bytes 9437188
  90.9 8.8 %copy-start.6 = (f32[1024,768]{1,0:T(8,128)S(1)}, f32[1024,768]{1,0:T(8,128)}, u32[]{:S(2)}) copy-start(f32[1024,768]{1,0:T(8,128)} %get-tuple-element.120.refs_3_) | copy-start | bytes 9437188
  90.9 8.8 %copy-start.9 = (f32[768]{0:T(1024)S(1)}, f32[768]{0:T(1024)}, u32[]{:S(2)}) copy-start(f32[768]{0:T(1024)} %param.20) | copy-start | bytes 9220
  92.9 6.8 %collective-permute-start.6 = (f32[1024,768]{1,0:T(8,128)S(1)}, f32[1024,768]{1,0:T(8,128)S(1)}, u32[]{:S(2)}, u32[]{:S(2)}) collective-permute-start(f32[1024,768]{1,0:T(8,128)S(1)} %get-tuple-element.119.refs_0_), channel_id=1, source_target_pairs={{0,1},{1,0},{2,3},{3,2},{4,5},{5,4},{6,7},{7,6},{8,9},{9,8},{10,11... | collective-permute-start | bytes 9437192 | tf_op jit(solution)/shard_map/ppermute | solution.py:629
  93.0 44.9 %collective-permute-start.11 = (f32[4,48,2176]{2,1,0:T(8,128)S(1)}, f32[4,48,2176]{2,1,0:T(8,128)S(1)}, u32[]{:S(2)}, u32[]{:S(2)}) collective-permute-start(f32[4,48,2176]{2,1,0:T(8,128)S(1)} %get-tuple-element.135), channel_id=1, source_target_pairs={{0,16},{1,9},{2,18},{3,11},{4,20},{5,13},{6,22},{7,15},{8,24},{9,1... | collective-permute-start | bytes 5013512 | tf_op jit(solution)/shard_map/ppermute | solution.py:665
  96.2 28.9 %collective-permute-start.9 = (f32[8,48,768]{2,1,0:T(8,128)S(1)}, f32[8,48,768]{2,1,0:T(8,128)S(1)}, u32[]{:S(2)}, u32[]{:S(2)}) collective-permute-start(f32[8,48,768]{2,1,0:T(8,128)S(1)} %get-tuple-element.132), channel_id=1, source_target_pairs={{0,2},{1,3},{2,0},{3,1},{4,6},{5,7},{6,4},{7,5},{8,10},{9,11},{10,... | collective-permute-start | bytes 3538952 | tf_op jit(solution)/shard_map/ppermute | solution.py:665
  97.7 28.3 %collective-permute-start.8 = (f32[8,48,768]{2,1,0:T(8,128)S(1)}, f32[8,48,768]{2,1,0:T(8,128)S(1)}, u32[]{:S(2)}, u32[]{:S(2)}) collective-permute-start(f32[8,48,768]{2,1,0:T(8,128)S(1)} %get-tuple-element.129), channel_id=1, source_target_pairs={{0,4},{1,5},{2,6},{3,7},{4,0},{5,1},{6,2},{7,3},{8,12},{9,13},{10,... | collective-permute-start | bytes 3538952 | tf_op jit(solution)/shard_map/ppermute | solution.py:665
  99.2 38.7 %collective-permute-start.12 = (f32[4,48,896]{2,1,0:T(8,128)S(1)}, f32[4,48,896]{2,1,0:T(8,128)S(1)}, u32[]{:S(2)}, u32[]{:S(2)}) collective-permute-start(f32[4,48,896]{2,1,0:T(8,128)S(1)} %get-tuple-element.137), channel_id=1, source_target_pairs={{0,2},{1,3},{2,0},{3,1},{4,6},{5,7},{6,4},{7,5},{8,10},{9,11},{10,... | collective-permute-start | bytes 2064392 | tf_op jit(solution)/shard_map/ppermute | solution.py:665
  99.8 27.8 %copy-start.3 = (f32[8,48,768]{2,1,0:T(8,128)S(1)}, f32[8,48,768]{2,1,0:T(8,128)}, u32[]{:S(2)}) copy-start(f32[8,48,768]{2,1,0:T(8,128)} %get-tuple-element.128.refs_2_) | copy-start | bytes 3538948
  99.8 27.8 %copy-start.4 = (f32[8,48,768]{2,1,0:T(8,128)S(1)}, f32[8,48,768]{2,1,0:T(8,128)}, u32[]{:S(2)}) copy-start(f32[8,48,768]{2,1,0:T(8,128)} %get-tuple-element.131.refs_4_.refs_5_.refs_6_.refs_7_) | copy-start | bytes 3538948
  103.7 23.9 %collective-permute-start.7 = (f32[1,48,768]{2,1,0:T(8,128)S(1)}, f32[1,48,768]{2,1,0:T(8,128)S(1)}, u32[]{:S(2)}, u32[]{:S(2)}) collective-permute-start(f32[1,48,768]{2,1,0:T(8,128)S(1)} %get-tuple-element.127.refs_0_), channel_id=1, source_target_pairs={{0,4},{1,5},{2,6},{3,7},{4,0},{5,1},{6,2},{7,3},{8,12},{9,13},{10,... | collective-permute-start | bytes 442376 | tf_op jit(solution)/shard_map/ppermute | solution.py:665
  127.7 25.9 %collective-permute-start.10 = (f32[5,48,768]{2,1,0:T(8,128)S(1)}, f32[5,48,768]{2,1,0:T(8,128)S(1)}, u32[]{:S(2)}, u32[]{:S(2)}) collective-permute-start(f32[5,48,768]{2,1,0:T(8,128)S(1)} %get-tuple-element.134.refs_0_), channel_id=1, source_target_pairs={{0,8},{1,17},{2,10},{3,19},{4,12},{5,21},{6,14},{7,23},{8,0},{9,25... | collective-permute-start | bytes 2211848 | tf_op jit(solution)/shard_map/ppermute | solution.py:665
  128.2 15.4 %collective-permute-start.13 = (f32[4,48,768]{2,1,0:T(8,128)S(1)}, f32[4,48,768]{2,1,0:T(8,128)S(1)}, u32[]{:S(2)}, u32[]{:S(2)}) collective-permute-start(f32[4,48,768]{2,1,0:T(8,128)S(1)} %get-tuple-element.141), channel_id=1, source_target_pairs={{0,4},{1,5},{2,6},{3,7},{4,0},{5,1},{6,2},{7,3},{8,12},{9,13},{10,... | collective-permute-start | bytes 1769480 | tf_op jit(solution)/shard_map/ppermute | solution.py:665
  139.4 16.2 %collective-permute-start.15 = (f32[2,48,2176]{2,1,0:T(8,128)S(1)}, f32[2,48,2176]{2,1,0:T(8,128)S(1)}, u32[]{:S(2)}, u32[]{:S(2)}) collective-permute-start(f32[2,48,2176]{2,1,0:T(8,128)S(1)} %get-tuple-element.139), channel_id=1, source_target_pairs={{0,2},{1,5},{2,0},{3,7},{4,6},{5,1},{6,4},{7,3},{8,10},{9,13},{10,... | collective-permute-start | bytes 2506760 | tf_op jit(solution)/shard_map/ppermute | solution.py:665
  140.9 14.6 %collective-permute-start.16 = (f32[2,48,896]{2,1,0:T(8,128)S(1)}, f32[2,48,896]{2,1,0:T(8,128)S(1)}, u32[]{:S(2)}, u32[]{:S(2)}) collective-permute-start(f32[2,48,896]{2,1,0:T(8,128)S(1)} %get-tuple-element.145), channel_id=1, source_target_pairs={{0,16},{1,9},{2,18},{3,11},{4,20},{5,13},{6,22},{7,15},{8,24},{9,1... | collective-permute-start | bytes 1032200 | tf_op jit(solution)/shard_map/ppermute | solution.py:665
  153.7 16.7 %collective-permute-start.14 = (f32[3,48,768]{2,1,0:T(8,128)S(1)}, f32[3,48,768]{2,1,0:T(8,128)S(1)}, u32[]{:S(2)}, u32[]{:S(2)}) collective-permute-start(f32[3,48,768]{2,1,0:T(8,128)S(1)} %get-tuple-element.143.refs_0_), channel_id=1, source_target_pairs={{0,2},{1,3},{2,0},{3,1},{4,6},{5,7},{6,4},{7,5},{8,10},{9,11},{10,... | collective-permute-start | bytes 1327112 | tf_op jit(solution)/shard_map/ppermute | solution.py:665
  154.7 15.8 %collective-permute-start.17 = (f32[2,48,768]{2,1,0:T(8,128)S(1)}, f32[2,48,768]{2,1,0:T(8,128)S(1)}, u32[]{:S(2)}, u32[]{:S(2)}) collective-permute-start(f32[2,48,768]{2,1,0:T(8,128)S(1)} %get-tuple-element.149), channel_id=1, source_target_pairs={{0,16},{1,9},{2,18},{3,11},{4,20},{5,13},{6,22},{7,15},{8,24},{9,1... | collective-permute-start | bytes 884744 | tf_op jit(solution)/shard_map/ppermute | solution.py:665
  156.7 21.8 %collective-permute-start.19 = (f32[1,48,2176]{2,1,0:T(8,128)S(1)}, f32[1,48,2176]{2,1,0:T(8,128)S(1)}, u32[]{:S(2)}, u32[]{:S(2)}) collective-permute-start(f32[1,48,2176]{2,1,0:T(8,128)S(1)} %get-tuple-element.147), channel_id=1, source_target_pairs={{0,8},{1,17},{2,10},{3,19},{4,12},{5,21},{6,14},{7,23},{8,0},{9,25... | collective-permute-start | bytes 1253384 | tf_op jit(solution)/shard_map/ppermute | solution.py:665
  170.6 12.3 %collective-permute-start.18 = (f32[2,48,768]{2,1,0:T(8,128)S(1)}, f32[2,48,768]{2,1,0:T(8,128)S(1)}, u32[]{:S(2)}, u32[]{:S(2)}) collective-permute-start(f32[2,48,768]{2,1,0:T(8,128)S(1)} %get-tuple-element.151.refs_0_), channel_id=1, source_target_pairs={{0,16},{1,9},{2,18},{3,11},{4,20},{5,13},{6,22},{7,15},{8,24},{9,1... | collective-permute-start | bytes 884744 | tf_op jit(solution)/shard_map/ppermute | solution.py:665
  170.7 7.9 %collective-permute-start.20 = (f32[1,48,896]{2,1,0:T(8,128)S(1)}, f32[1,48,896]{2,1,0:T(8,128)S(1)}, u32[]{:S(2)}, u32[]{:S(2)}) collective-permute-start(f32[1,48,896]{2,1,0:T(8,128)S(1)} %get-tuple-element.153), channel_id=1, source_target_pairs={{0,4},{1,5},{2,6},{3,7},{4,0},{5,1},{6,2},{7,3},{8,12},{9,13},{10,... | collective-permute-start | bytes 516104 | tf_op jit(solution)/shard_map/ppermute | solution.py:665
  175.2 5.5 %collective-permute-start.21 = (f32[1,48,768]{2,1,0:T(8,128)S(1)}, f32[1,48,768]{2,1,0:T(8,128)S(1)}, u32[]{:S(2)}, u32[]{:S(2)}) collective-permute-start(f32[1,48,768]{2,1,0:T(8,128)S(1)} %get-tuple-element.157), channel_id=1, source_target_pairs={{0,8},{1,17},{2,10},{3,19},{4,12},{5,21},{6,14},{7,23},{8,0},{9,25... | collective-permute-start | bytes 442376 | tf_op jit(solution)/shard_map/ppermute | solution.py:665
  (6 other events, 52.8 us)
